TPU v7x, 128 devices: a whole 4x4x4 slice. The times are simulated.
128 devices in a mesh: group: 4 (over z_lo, core), dp: 2 (over z_hi), tensor: 16 (over x, y).
Axes of the slice: x: 4, y: 4, z: 4 (z_hi: 2, z_lo: 2; z = z_hi * 2 + z_lo), core: 2. Of those that a mesh axis runs over, the one named last changes fastest.
Arguments:
- tokens: bfloat16 [2048, 8, 2048], P('tensor', ('group', 'dp')), may hold values from -6 to 6
- cotangent: bfloat16 [2048, 8, 2048], P('tensor', ('group', 'dp')), may hold values from -6 to 6
- lengths: int32 [8], replicated, may hold values from 1 to 2048, 9830 in all
- ln1_gain: float32 [2048], replicated, may hold values from 0.25 to 1.75
- ln1_bias: float32 [2048], replicated, may hold values from -1.75 to 1.75
- w_qkv: bfloat16 [2048, 3, 16, 128], P(None, None, 'tensor'), may hold values from -0.125 to 0.125
- b_qv: float32 [2, 2048], P(None, 'tensor'), may hold values from -1.75 to 1.75
- w_o: bfloat16 [16, 128, 2048], P('tensor'), may hold values from -0.75 to 0.75
- b_o: float32 [2048], replicated, may hold values from -1.75 to 1.75
- ln2_gain: float32 [2048], replicated, may hold values from 0.25 to 1.75
- ln2_bias: float32 [2048], replicated, may hold values from -1.75 to 1.75
- w_in: bfloat16 [2048, 8192], P(None, 'tensor'), may hold values from -0.125 to 0.125
- b_in: float32 [8192], P('tensor'), may hold values from -1.75 to 1.75
- w_out: bfloat16 [8192, 2048], P('tensor'), may hold values from -0.0625 to 0.0625
- b_out: float32 [2048], replicated, may hold values from -1.75 to 1.75
Outputs:
- output: bfloat16 [2048, 8, 2048], P('tensor', ('group', 'dp'))
- input_grad: bfloat16 [2048, 8, 2048], P('tensor', ('group', 'dp'))
- d_ln1_gain: float32 [2048], P(('group', 'dp', 'tensor'))
- d_ln1_bias: float32 [2048], P(('group', 'dp', 'tensor'))
- d_w_qkv: float32 [2048, 3, 16, 128], P(('group', 'dp'), None, 'tensor')
- d_b_qv: float32 [2, 2048], P(None, ('group', 'dp', 'tensor'))
- d_w_o: float32 [16, 128, 2048], P('tensor', None, ('group', 'dp'))
- d_b_o: float32 [2048], P(('group', 'dp', 'tensor'))
- d_ln2_gain: float32 [2048], P(('group', 'dp', 'tensor'))
- d_ln2_bias: float32 [2048], P(('group', 'dp', 'tensor'))
- d_w_in: float32 [2048, 8192], P(('group', 'dp'), 'tensor')
- d_b_in: float32 [8192], P(('group', 'dp', 'tensor'))
- d_w_out: float32 [8192, 2048], P('tensor', ('group', 'dp'))
- d_b_out: float32 [2048], P(('group', 'dp', 'tensor'))
Inputs may be any that keep to these rules, and one draw needn't show every extreme that they name: The true lengths of the 8 sequences sum to 9830.
All inputs are finite; a program needn't handle non-finite values.
Results may differ from a plain program's by a relative error of at most 0.02.
Values may be sent and summed in bfloat16 or wider, within the bound.
No kernel may reach another device: no remote copies, remote signals or barrier semaphores. Data moves between devices by JAX's collectives and lax.ppermute only.
A program may use at most 192 MiB of HBM per device.

v0:
```python
from functools import partial
import math

import jax
import jax.numpy as jnp
from jax import lax
from jax.sharding import PartitionSpec as P

EPS = 1e-05
NEGATIVE = -1e30


def layer_norm(value, gain, shift):
    mean = jnp.mean(value, axis=-1, keepdims=True)
    centred = value - mean
    spread = jnp.mean(centred * centred, axis=-1, keepdims=True)
    return centred * lax.rsqrt(spread + EPS) * gain + shift


def gelu_tanh(value):
    return jax.nn.gelu(value, approximate=True)


def block_scores(rows_query, key_rows, first, length, score_scale):
    count = rows_query.shape[0]
    key_pos = jnp.arange(key_rows.shape[0], dtype=jnp.int32)
    query_pos = first + jnp.arange(count, dtype=jnp.int32)
    valid = (key_pos[None, :] <= query_pos[:, None]) & (key_pos[None, :] < length)
    scores = (
        lax.dot_general(
            rows_query, key_rows, (((1,), (1,)), ((), ())), preferred_element_type=jnp.float32
        )
        * score_scale
    )
    return (jnp.where(valid, scores, NEGATIVE), valid)


def attend_forward(item, block_rows, score_scale):
    query, key_rows, value_rows, length = item
    outputs = []
    log_parts = []
    for first in range(0, query.shape[0], block_rows):
        rows_query = query[first : first + block_rows]
        scores, valid = block_scores(rows_query, key_rows, first, length, score_scale)
        peak = jnp.max(scores, axis=-1, keepdims=True)
        expo = jnp.exp(scores - peak)
        weight_sum = jnp.sum(expo, axis=-1, keepdims=True)
        probs = (expo / weight_sum).astype(jnp.bfloat16)
        outputs.append(
            jnp.dot(probs, value_rows, preferred_element_type=jnp.float32).astype(jnp.bfloat16)
        )
        log_parts.append((peak + jnp.log(weight_sum))[:, 0])
    return (jnp.concatenate(outputs, 0), jnp.concatenate(log_parts, 0))


def attend_backward(item, block_rows, score_scale):
    query, key_rows, value_rows, length, grad_out, log_sums = item
    key_grad = jnp.zeros(key_rows.shape, jnp.float32)
    value_grad = jnp.zeros(value_rows.shape, jnp.float32)
    query_parts = []
    for first in range(0, query.shape[0], block_rows):
        rows_query = query[first : first + block_rows]
        scores, valid = block_scores(rows_query, key_rows, first, length, score_scale)
        probs = jnp.where(valid, jnp.exp(scores - log_sums[first : first + block_rows, None]), 0.0)
        grad_rows = grad_out[first : first + block_rows]
        probs_grad = lax.dot_general(
            grad_rows, value_rows, (((1,), (1,)), ((), ())), preferred_element_type=jnp.float32
        )
        inner = jnp.sum(probs * probs_grad, axis=-1, keepdims=True)
        score_grad = (probs * (probs_grad - inner)).astype(jnp.bfloat16)
        query_parts.append(
            jnp.dot(score_grad, key_rows, preferred_element_type=jnp.float32) * score_scale
        )
        key_grad = (
            key_grad
            + lax.dot_general(
                score_grad, rows_query, (((0,), (0,)), ((), ())), preferred_element_type=jnp.float32
            )
            * score_scale
        )
        value_grad = value_grad + lax.dot_general(
            probs.astype(jnp.bfloat16),
            grad_rows,
            (((0,), (0,)), ((), ())),
            preferred_element_type=jnp.float32,
        )
    return (
        jnp.concatenate(query_parts, 0).astype(jnp.bfloat16),
        key_grad.astype(jnp.bfloat16),
        value_grad.astype(jnp.bfloat16),
    )


def shards(
    tokens,
    cotangent,
    lengths,
    ln1_gain,
    ln1_bias,
    w_qkv,
    b_qv,
    w_o,
    b_o,
    ln2_gain,
    ln2_bias,
    w_in,
    b_in,
    w_out,
    b_out,
):
    row_count, seq_count, model_width = tokens.shape
    tensor_count = lax.axis_size("tensor")
    tensor_rank = lax.axis_index("tensor")
    seq_total = row_count * tensor_count
    local_heads = w_qkv.shape[2]
    head_size = w_qkv.shape[3]
    local_width = local_heads * head_size
    hidden = w_in.shape[1]
    block_rows = min(512, seq_total)
    score_scale = 1.0 / math.sqrt(head_size)
    group_count = lax.axis_size("group")
    group_rank = lax.axis_index("group")
    member = group_rank * lax.axis_size("dp") + lax.axis_index("dp")
    seq_lengths = lax.dynamic_slice_in_dim(lengths, member * seq_count, seq_count, 0)
    group_totals = jnp.sum(lengths.reshape(group_count, -1), axis=1).astype(jnp.float32)
    factor = (
        group_count
        * lax.dynamic_index_in_dim(group_totals, group_rank, 0, keepdims=False)
        / jnp.sum(group_totals)
    )
    inputs = tokens.astype(jnp.float32)
    normed_low = layer_norm(inputs, ln1_gain, ln1_bias).astype(jnp.bfloat16)
    normed_full = lax.all_gather(normed_low, "tensor", axis=0, tiled=True)
    joint_weight = w_qkv.reshape(model_width, 3 * local_width)
    projected = jnp.dot(
        normed_full.reshape(seq_total * seq_count, model_width),
        joint_weight,
        preferred_element_type=jnp.float32,
    )
    projected = projected.reshape(seq_total, seq_count, 3, local_width)
    query = (projected[:, :, 0] + b_qv[0]).astype(jnp.bfloat16)
    keys = projected[:, :, 1].astype(jnp.bfloat16)
    values = (projected[:, :, 2] + b_qv[1]).astype(jnp.bfloat16)

    def per_item(array):
        shaped = array.reshape(seq_total, seq_count, local_heads, head_size)
        return jnp.transpose(shaped, (1, 2, 0, 3)).reshape(
            seq_count * local_heads, seq_total, head_size
        )

    def per_row(array):
        shaped = array.reshape(seq_count, local_heads, seq_total, head_size)
        return jnp.transpose(shaped, (2, 0, 1, 3)).reshape(seq_total, seq_count, local_width)

    query_items = per_item(query)
    key_items = per_item(keys)
    value_items = per_item(values)
    item_lengths = jnp.repeat(seq_lengths, local_heads)
    heads_out, log_sums = lax.map(
        partial(attend_forward, block_rows=block_rows, score_scale=score_scale),
        (query_items, key_items, value_items, item_lengths),
    )
    attended = per_row(heads_out)
    out_weight = w_o.reshape(local_width, model_width)
    piece = attended
    attention = (
        lax.psum_scatter(
            jnp.einsum("rse,ed->rsd", piece, out_weight, preferred_element_type=jnp.float32),
            "tensor",
            scatter_dimension=0,
            tiled=True,
        )
        + b_o
    )
    middle = inputs + attention
    second_low = layer_norm(middle, ln2_gain, ln2_bias).astype(jnp.bfloat16)
    second_full = lax.all_gather(second_low, "tensor", axis=0, tiled=True)
    pre_act = (
        jnp.dot(
            second_full.reshape(seq_total * seq_count, model_width),
            w_in,
            preferred_element_type=jnp.float32,
        )
        + b_in
    )
    activated = gelu_tanh(pre_act).astype(jnp.bfloat16).reshape(seq_total, seq_count, hidden)
    piece = activated
    feed = (
        lax.psum_scatter(
            jnp.einsum("rsf,fd->rsd", piece, w_out, preferred_element_type=jnp.float32).astype(
                jnp.bfloat16
            ),
            "tensor",
            scatter_dimension=0,
            tiled=True,
        ).astype(jnp.float32)
        + b_out
    )
    output = (middle + feed).astype(jnp.bfloat16)
    positions = tensor_rank * row_count + jnp.arange(row_count, dtype=jnp.int32)
    live = positions[:, None] < seq_lengths[None, :]
    upstream = jnp.where(live[:, :, None], cotangent, jnp.zeros_like(cotangent))
    piece = lax.all_gather(upstream, "tensor", axis=0, tiled=True)
    weight_grad = jnp.einsum("rsf,rsd->fd", activated, piece, preferred_element_type=jnp.float32)
    part = jnp.einsum("rsd,fd->rsf", piece, w_out, preferred_element_type=jnp.float32)
    act_grad = part
    grad_w_out = weight_grad
    gelu_back = jax.vjp(gelu_tanh, pre_act)[1]
    pre_low = gelu_back(act_grad.reshape(seq_total * seq_count, hidden))[0].astype(jnp.bfloat16)
    grad_b_in = jnp.sum(pre_low, axis=0, dtype=jnp.float32)
    grad_w_in = jnp.einsum(
        "rd,rf->df",
        second_full.reshape(seq_total * seq_count, model_width),
        pre_low,
        preferred_element_type=jnp.float32,
    )
    pre_rows = pre_low.reshape(seq_total, seq_count, hidden)
    piece = pre_rows
    second_grad = lax.psum_scatter(
        jnp.einsum("rsf,df->rsd", piece, w_in, preferred_element_type=jnp.float32),
        "tensor",
        scatter_dimension=0,
        tiled=True,
    )
    norm_two_back = jax.vjp(layer_norm, middle, ln2_gain, ln2_bias)[1]
    middle_part, grad_ln2_gain, grad_ln2_bias = norm_two_back(second_grad)
    middle_grad = upstream.astype(jnp.float32) + middle_part
    branch_low = middle_grad.astype(jnp.bfloat16)
    grad_b_o = jnp.sum(branch_low, axis=(0, 1), dtype=jnp.float32)
    grad_b_out = jnp.sum(upstream, axis=(0, 1), dtype=jnp.float32)
    piece = lax.all_gather(branch_low, "tensor", axis=0, tiled=True)
    weight_grad = jnp.einsum("rse,rsd->ed", attended, piece, preferred_element_type=jnp.float32)
    part = jnp.einsum("rsd,ed->rse", piece, out_weight, preferred_element_type=jnp.float32)
    head_items = per_item(part.astype(jnp.bfloat16))
    grads_query, grads_keys, grads_values = lax.map(
        partial(attend_backward, block_rows=block_rows, score_scale=score_scale),
        (query_items, key_items, value_items, item_lengths, head_items, log_sums),
    )
    joint_grad = jnp.stack(
        (per_row(grads_query), per_row(grads_keys), per_row(grads_values)), axis=2
    )
    grad_b_qv = jnp.sum(joint_grad[:, :, 0::2], axis=(0, 1), dtype=jnp.float32)
    joint_rows = joint_grad.reshape(seq_total, seq_count, 3 * local_width)
    grad_w_qkv = jnp.einsum(
        "rd,rc->dc",
        normed_full.reshape(seq_total * seq_count, model_width),
        joint_rows.reshape(seq_total * seq_count, 3 * local_width),
        preferred_element_type=jnp.float32,
    )
    piece = joint_rows
    normed_grad = lax.psum_scatter(
        jnp.einsum("rsc,dc->rsd", piece, joint_weight, preferred_element_type=jnp.float32).astype(
            jnp.bfloat16
        ),
        "tensor",
        scatter_dimension=0,
        tiled=True,
    ).astype(jnp.float32)
    norm_one_back = jax.vjp(layer_norm, inputs, ln1_gain, ln1_bias)[1]
    input_part, grad_ln1_gain, grad_ln1_bias = norm_one_back(normed_grad)
    input_grad = (middle_grad + input_part).astype(jnp.bfloat16)
    matrices = (
        grad_w_qkv.reshape(model_width, 3, local_heads, head_size) * factor,
        weight_grad.reshape(local_heads, head_size, model_width) * factor,
        grad_w_in * factor,
        grad_w_out * factor,
    )
    summed = (
        lax.psum_scatter(
            matrices[0].astype(jnp.bfloat16), ("group", "dp"), scatter_dimension=0, tiled=True
        ).astype(jnp.float32),
        lax.psum_scatter(
            matrices[1].astype(jnp.bfloat16), ("group", "dp"), scatter_dimension=2, tiled=True
        ).astype(jnp.float32),
        lax.psum_scatter(
            matrices[2].astype(jnp.bfloat16), ("group", "dp"), scatter_dimension=0, tiled=True
        ).astype(jnp.float32),
        lax.psum_scatter(
            matrices[3].astype(jnp.bfloat16), ("group", "dp"), scatter_dimension=1, tiled=True
        ).astype(jnp.float32),
    )
    in_full = lax.dynamic_update_slice_in_dim(
        jnp.zeros((hidden * tensor_count,), jnp.float32), grad_b_in, tensor_rank * hidden, 0
    )
    joint_full = lax.dynamic_update_slice_in_dim(
        jnp.zeros((2, local_width * tensor_count), jnp.float32),
        grad_b_qv,
        tensor_rank * local_width,
        1,
    )
    stacked = (
        jnp.concatenate(
            (
                jnp.stack(
                    (
                        grad_ln1_gain,
                        grad_ln1_bias,
                        grad_b_o,
                        grad_ln2_gain,
                        grad_ln2_bias,
                        grad_b_out,
                    )
                ),
                joint_full,
            ),
            0,
        )
        * factor
    )
    vector_sums, in_sums = (
        lax.psum_scatter(stacked, ("group", "dp", "tensor"), scatter_dimension=1, tiled=True),
        lax.psum_scatter(
            in_full * factor, ("group", "dp", "tensor"), scatter_dimension=0, tiled=True
        ),
    )
    return (
        output,
        input_grad,
        vector_sums[0],
        vector_sums[1],
        summed[0],
        vector_sums[6:8],
        summed[1],
        vector_sums[2],
        vector_sums[3],
        vector_sums[4],
        summed[2],
        in_sums,
        summed[3],
        vector_sums[5],
    )


def solution(mesh):
    in_specs = (
        P("tensor", ("group", "dp"), None),
        P("tensor", ("group", "dp"), None),
        P(),
        P(),
        P(),
        P(None, None, "tensor", None),
        P(None, "tensor"),
        P("tensor", None, None),
        P(),
        P(),
        P(),
        P(None, "tensor"),
        P("tensor"),
        P("tensor", None),
        P(),
    )
    out_specs = (
        P("tensor", ("group", "dp"), None),
        P("tensor", ("group", "dp"), None),
        P(("group", "dp", "tensor")),
        P(("group", "dp", "tensor")),
        P(("group", "dp"), None, "tensor", None),
        P(None, ("group", "dp", "tensor")),
        P("tensor", None, ("group", "dp")),
        P(("group", "dp", "tensor")),
        P(("group", "dp", "tensor")),
        P(("group", "dp", "tensor")),
        P(("group", "dp"), "tensor"),
        P(("group", "dp", "tensor")),
        P("tensor", ("group", "dp")),
        P(("group", "dp", "tensor")),
    )
    return jax.shard_map(shards, mesh=mesh, in_specs=in_specs, out_specs=out_specs, check_vma=False)
```

profile of v0, /device:TPU:96, one launch (start us, length us, event | category | flops | bytes accessed | tf_op | source)
XLA Modules:
  0.0 1724.0 jit_solution(11324964571885417214)
XLA Ops:
  16.8 68.1 %all-gather.5.cloned.1.call-done = bf16[2048,1,2048]{2,0,1:T(8,128)(2,1)} async-done(((bf16[128,1,2048]{2,0,1:T(8,128)(2,1)}), bf16[2048,1,2048]{2,0,1:T(8,128)(2,1)}) %all-gather.5.cloned.1.call-update) | async-done | bytes 8388624 | tf_op jit(solution)/shard_map/all_gather | solution.py:133
  84.8 7.4 fusion.31
  131.9 8.1 convolution_bitcast_fusion.1
  140.1 110.3 %reduce-scatter.12.cloned.1.call-done = f32[128,1,2048]{2,0,1:T(8,128)} async-done(((f32[2048,1,2048]{2,0,1:T(8,128)}), f32[128,1,2048]{2,0,1:T(8,128)}) %reduce-scatter.12.cloned.1.call-update) | async-done | bytes 1048592 | tf_op jit(solution)/shard_map/reduce_scatter | solution.py:167
  258.5 67.0 %all-gather.7.cloned.1.call-done = bf16[2048,1,2048]{2,0,1:T(8,128)(2,1)} async-done(((bf16[128,1,2048]{2,0,1:T(8,128)(2,1)}), bf16[2048,1,2048]{2,0,1:T(8,128)(2,1)}) %all-gather.7.cloned.1.call-update) | async-done | bytes 8388624 | tf_op jit(solution)/shard_map/all_gather | solution.py:177
  325.4 10.5 fusion.10
  335.9 62.4 %all-gather.9.cloned.1.call-done = bf16[2048,1,2048]{2,0,1:T(8,128)(2,1)} async-done(((bf16[128,1,2048]{2,0,1:T(8,128)(2,1)}), bf16[2048,1,2048]{2,0,1:T(8,128)(2,1)}) %all-gather.9.cloned.1.call-update) | async-done | bytes 8388624 | tf_op jit(solution)/shard_map/all_gather | solution.py:203
  398.4 12.4 convert_reduce_fusion
  412.2 8.2 convolution_bitcast_fusion
  420.5 10.3 convert_bitcast_fusion.1
  430.9 99.9 %reduce-scatter.16.cloned.1.call-done = f32[128,1,2048]{2,0,1:T(8,128)} async-done(((f32[2048,1,2048]{2,0,1:T(8,128)}), f32[128,1,2048]{2,0,1:T(8,128)}) %reduce-scatter.16.cloned.1.call-update) | async-done | bytes 1048592 | tf_op jit(solution)/shard_map/reduce_scatter | solution.py:219
  533.0 85.7 %reduce-scatter.14.cloned.1.call-done = bf16[128,1,2048]{2,0,1:T(8,128)(2,1)} async-done(((bf16[2048,1,2048]{2,0,1:T(8,128)(2,1)}), bf16[128,1,2048]{2,0,1:T(8,128)(2,1)}) %reduce-scatter.14.cloned.1.call-update) | async-done | bytes 524304 | tf_op jit(solution)/shard_map/reduce_scatter | solution.py:189
  625.7 11.3 multiply_convert_fusion
  645.5 9.6 multiply_convert_fusion.1
  655.3 37.3 %all-gather.11.cloned.1.call-done = bf16[2048,1,2048]{2,0,1:T(8,128)(2,1)} async-done(((bf16[128,1,2048]{2,0,1:T(8,128)(2,1)}), bf16[2048,1,2048]{2,0,1:T(8,128)(2,1)}) %all-gather.11.cloned.1.call-update) | async-done | bytes 8388624 | tf_op jit(solution)/shard_map/all_gather | solution.py:231
  692.6 5.9 fusion.45
  707.7 9.5 multiply_reduce_fusion
  721.8 9.5 multiply_convert_fusion.2
  755.0 8.3 fusion.38
  763.4 9.7 convert_bitcast_fusion
  773.9 76.5 %all-reduce = f32[8192]{0:T(1024)S(1)} all-reduce(f32[8192]{0:T(1024)S(1)} %broadcast_multiply_fusion.1), channel_id=10, replica_groups=mesh['group'=4,'dp'=2,'tensor'=16] {'group','dp','tensor'}, use_global_device_ids=true, to_apply=%region_38.39.clone | all-reduce | flops 8192 | bytes 65536
  857.3 45.5 %reduce-scatter.20.cloned.1.call-done = bf16[256,3,1,128]{3,0,1,2:T(8,128)(2,1)} async-done(((bf16[2048,3,1,128]{3,0,1,2:T(8,128)(2,1)}), bf16[256,3,1,128]{3,0,1,2:T(8,128)(2,1)}) %reduce-scatter.20.cloned.1.call-update) | async-done | bytes 196624 | tf_op jit(solution)/shard_map/reduce_scatter | solution.py:269
  904.8 90.1 %reduce-scatter.18.cloned.1.call-done = bf16[128,1,2048]{2,0,1:T(8,128)(2,1)} async-done(((bf16[2048,1,2048]{2,0,1:T(8,128)(2,1)}), bf16[128,1,2048]{2,0,1:T(8,128)(2,1)}) %reduce-scatter.18.cloned.1.call-update) | async-done | bytes 524304 | tf_op jit(solution)/shard_map/reduce_scatter | solution.py:251
  1002.2 708.9 %reduce-scatter.28.cloned.1.call-done = f32[16,8]{1,0:T(8,128)} async-done(((f32[2048,8]{1,0:T(8,128)}), f32[16,8]{1,0:T(8,128)}) %reduce-scatter.28.cloned.1.call-update) | async-done | bytes 528
  (279 shorter events, 134.9 us)
Async XLA Ops:
  7.2 391.2 %copy-start = (bf16[512,2048]{1,0:T(8,128)(2,1)S(1)}, bf16[512,2048]{1,0:T(8,128)(2,1)}, u32[]{:S(2)}) copy-start(bf16[512,2048]{1,0:T(8,128)(2,1)} %param.28) | copy-start | bytes 6291460
  7.2 77.6 %all-gather.5.cloned.1.call-start = ((), (), s32[]{:S(2)}) async-start(), calls=%async_computation.9 | async-start | bytes 8912896 | tf_op jit(solution)/shard_map/all_gather | solution.py:133
  12.8 237.6 %reduce-scatter.12.cloned.1.call-start = ((), (), s32[]{:S(2)}) async-start(), calls=%async_computation.10 | async-start | bytes 17825792 | tf_op jit(solution)/shard_map/reduce_scatter | solution.py:167
  140.0 185.4 %all-gather.7.cloned.1.call-start = ((), (), s32[]{:S(2)}) async-start(), calls=%async_computation.11 | async-start | bytes 8912896 | tf_op jit(solution)/shard_map/all_gather | solution.py:177
  255.1 143.3 %all-gather.9.cloned.1.call-start = ((), (), s32[]{:S(2)}) async-start(), calls=%async_computation.13 | async-start | bytes 8912896 | tf_op jit(solution)/shard_map/all_gather | solution.py:203
  258.4 272.4 %reduce-scatter.16.cloned.1.call-start = ((), (), s32[]{:S(2)}) async-start(), calls=%async_computation.14 | async-start | bytes 17825792 | tf_op jit(solution)/shard_map/reduce_scatter | solution.py:219
  420.5 198.3 %reduce-scatter.14.cloned.1.call-start = ((), (), s32[]{:S(2)}) async-start(), calls=%async_computation.12 | async-start | bytes 8912896 | tf_op jit(solution)/shard_map/reduce_scatter | solution.py:189
  430.8 261.8 %all-gather.11.cloned.1.call-start = ((), (), s32[]{:S(2)}) async-start(), calls=%async_computation.15 | async-start | bytes 8912896 | tf_op jit(solution)/shard_map/all_gather | solution.py:231
  622.5 228.6 %reduce-scatter.26.cloned.1.call-start = ((), (), s32[]{:S(2)}) async-start(), calls=%async_computation.20 | async-start | bytes 2359296 | tf_op jit(solution)/shard_map/reduce_scatter | solution.py:278
  637.0 215.8 %reduce-scatter.24.cloned.1.call-start = ((), (), s32[]{:S(2)}) async-start(), calls=%async_computation.19 | async-start | bytes 2359296 | tf_op jit(solution)/shard_map/reduce_scatter | solution.py:275
  655.1 200.5 %reduce-scatter.22.cloned.1.call-start = ((), (), s32[]{:S(2)}) async-start(), calls=%async_computation.18 | async-start | bytes 589824 | tf_op jit(solution)/shard_map/reduce_scatter | solution.py:272
  752.1 150.7 %reduce-scatter.20.cloned.1.call-start = ((), (), s32[]{:S(2)}) async-start(), calls=%async_computation.17 | async-start | bytes 1769472 | tf_op jit(solution)/shard_map/reduce_scatter | solution.py:269
  763.4 231.5 %reduce-scatter.18.cloned.1.call-start = ((), (), s32[]{:S(2)}) async-start(), calls=%async_computation.16 | async-start | bytes 8912896 | tf_op jit(solution)/shard_map/reduce_scatter | solution.py:251
  773.1 221.8 %copy-start.28 = (f32[2048]{0:T(1024)S(1)}, f32[2048]{0:T(1024)}, u32[]{:S(2)}) copy-start(f32[2048]{0:T(1024)} %param.18) | copy-start | bytes 24580
  773.1 221.8 %copy-start.46 = (f32[128]{0:T(128)S(1)}, f32[128]{0:T(128)}, u32[]{:S(2)}) copy-start(f32[128]{0:T(128)} %copy-done.45) | copy-start | bytes 1540
  773.1 223.2 %copy-start.69 = (f32[128]{0:T(128)S(1)}, f32[128]{0:T(128)}, u32[]{:S(2)}) copy-start(f32[128]{0:T(128)} %copy-done.68) | copy-start | bytes 1540
  773.1 223.2 %copy-start.55 = (f32[128]{0:T(128)S(1)}, f32[128]{0:T(128)}, u32[]{:S(2)}) copy-start(f32[128]{0:T(128)} %copy-done.54) | copy-start | bytes 1540
  773.1 224.8 %copy-start.30 = (f32[2048]{0:T(1024)S(1)}, f32[2048]{0:T(1024)}, u32[]{:S(2)}) copy-start(f32[2048]{0:T(1024)} %get-tuple-element.118) | copy-start | bytes 24580
  773.1 224.8 %copy-start.31 = (f32[2048]{0:T(1024)S(1)}, f32[2048]{0:T(1024)}, u32[]{:S(2)}) copy-start(f32[2048]{0:T(1024)} %get-tuple-element.107) | copy-start | bytes 24580
  773.1 224.8 %copy-start.32 = (f32[2048]{0:T(1024)S(1)}, f32[2048]{0:T(1024)}, u32[]{:S(2)}) copy-start(f32[2048]{0:T(1024)} %get-tuple-element.111) | copy-start | bytes 24580
  773.2 226.3 %copy-start.16 = (bf16[128,1,2048]{2,0,1:T(8,128)(2,1)S(1)}, bf16[128,1,2048]{2,0,1:T(8,128)(2,1)}, u32[]{:S(2)}) copy-start(bf16[128,1,2048]{2,0,1:T(8,128)(2,1)} %get-tuple-element.119) | copy-start | bytes 1572868
  773.2 226.3 %copy-start.61 = (f32[128]{0:T(128)S(1)}, f32[128]{0:T(128)}, u32[]{:S(2)}) copy-start(f32[128]{0:T(128)} %copy-done.60) | copy-start | bytes 1540
  773.2 937.9 %reduce-scatter.28.cloned.1.call-start = ((), (), s32[]{:S(2)}) async-start(), calls=%async_computation.21 | async-start | bytes 1056768
  855.6 861.4 %copy-start.1 = (bf16[512,2048]{1,0:T(8,128)(2,1)S(1)}, bf16[512,2048]{1,0:T(8,128)(2,1)}, u32[]{:S(2)}) copy-start(bf16[512,2048]{1,0:T(8,128)(2,1)} %param.28) | copy-start | bytes 6291460
  (65 other events, 2354.3 us)
Sparse Core Ops, SparseCore 0:
  12.9 71.8 all-gather.4
  140.2 110.1 reduce-scatter.11
  255.2 70.2 all-gather.6
  328.0 70.3 all-gather.8
  420.6 110.1 reduce-scatter.15
  534.1 84.6 reduce-scatter.13
  622.6 69.9 all-gather.10
  695.0 56.5 reduce-scatter.25
  754.0 60.3 reduce-scatter.23
  816.6 39.0 reduce-scatter.21
  858.2 44.5 reduce-scatter.19
  906.5 88.3 reduce-scatter.17
  999.6 711.5 reduce-scatter.27
where the time goes:
time: 1730 us; the launch traced here: 1720 us
  waiting for transfers between devices  1380 us (80%)
  matrix products  158 us (9%)
  blocking collectives  76.5 us (4%)
  other arithmetic  57.3 us (3%)
  local copies, waits for them, and re-layouts  22.4 us (1%)
    unnamed x14, waiting for transfers between devices  709 us
    reduce_scatter x1, waiting for transfers between devices, shards(): lax.psum_scatter(jnp.einsum('rse,ed->rsd', piece, out_weight, preferred_e...  110 us
    reduce_scatter x1, waiting for transfers between devices, shards(): lax.psum_scatter(jnp.einsum('rsf,df->rsd', piece, w_in, preferred_element...  99.9 us
    reduce_scatter x1, waiting for transfers between devices, shards(): lax.psum_scatter(jnp.einsum('rsc,dc->rsd', piece, joint_weight, preferred...  90.1 us
    reduce_scatter x1, waiting for transfers between devices, shards(): lax.psum_scatter(jnp.einsum('rsf,fd->rsd', piece, w_out, preferred_elemen...  85.7 us
    unnamed x1, blocking collectives  76.5 us
    all_gather x1, waiting for transfers between devices, shards(): normed_full = lax.all_gather(normed_low, 'tensor', axis=0, tiled=True)  68.1 us
    all_gather x1, waiting for transfers between devices, shards(): second_full = lax.all_gather(second_low, 'tensor', axis=0, tiled=True)  67 us
  transfers between devices with their start and end apart: 13, of which 11 were waited for; matrix products, arithmetic and copies ran while one was open for 9% of the time, Pallas kernels for 0%

commit v1 on v0

--- a/solution.py
+++ b/solution.py
@@ -259,25 +259,11 @@
     norm_one_back = jax.vjp(layer_norm, inputs, ln1_gain, ln1_bias)[1]
     input_part, grad_ln1_gain, grad_ln1_bias = norm_one_back(normed_grad)
     input_grad = (middle_grad + input_part).astype(jnp.bfloat16)
-    matrices = (
-        grad_w_qkv.reshape(model_width, 3, local_heads, head_size) * factor,
-        weight_grad.reshape(local_heads, head_size, model_width) * factor,
-        grad_w_in * factor,
-        grad_w_out * factor,
-    )
     summed = (
-        lax.psum_scatter(
-            matrices[0].astype(jnp.bfloat16), ("group", "dp"), scatter_dimension=0, tiled=True
-        ).astype(jnp.float32),
-        lax.psum_scatter(
-            matrices[1].astype(jnp.bfloat16), ("group", "dp"), scatter_dimension=2, tiled=True
-        ).astype(jnp.float32),
-        lax.psum_scatter(
-            matrices[2].astype(jnp.bfloat16), ("group", "dp"), scatter_dimension=0, tiled=True
-        ).astype(jnp.float32),
-        lax.psum_scatter(
-            matrices[3].astype(jnp.bfloat16), ("group", "dp"), scatter_dimension=1, tiled=True
-        ).astype(jnp.float32),
+        halving_sum(grad_w_qkv.reshape(model_width, 3, local_heads, head_size) * factor, 0),
+        halving_sum(weight_grad.reshape(local_heads, head_size, model_width) * factor, 2),
+        halving_sum(grad_w_in * factor, 0),
+        halving_sum(grad_w_out * factor, 1),
     )
     in_full = lax.dynamic_update_slice_in_dim(
         jnp.zeros((hidden * tensor_count,), jnp.float32), grad_b_in, tensor_rank * hidden, 0
@@ -288,47 +274,79 @@
         tensor_rank * local_width,
         1,
     )
-    stacked = (
-        jnp.concatenate(
-            (
-                jnp.stack(
-                    (
-                        grad_ln1_gain,
-                        grad_ln1_bias,
-                        grad_b_o,
-                        grad_ln2_gain,
-                        grad_ln2_bias,
-                        grad_b_out,
-                    )
-                ),
-                joint_full,
-            ),
-            0,
-        )
-        * factor
-    )
-    vector_sums, in_sums = (
-        lax.psum_scatter(stacked, ("group", "dp", "tensor"), scatter_dimension=1, tiled=True),
-        lax.psum_scatter(
-            in_full * factor, ("group", "dp", "tensor"), scatter_dimension=0, tiled=True
-        ),
-    )
+    shard_count = group_count * lax.axis_size("dp")
+    vectors = (
+        grad_ln1_gain,
+        grad_ln1_bias,
+        grad_b_o,
+        grad_ln2_gain,
+        grad_ln2_bias,
+        grad_b_out,
+        joint_full[0],
+        joint_full[1],
+        in_full,
+    )
+    pieces = [
+        jnp.transpose(
+            (item * factor).reshape(shard_count, tensor_count, -1), (1, 0, 2)
+        )
+        for item in vectors
+    ]
+    widths = [piece.shape[2] for piece in pieces]
+    packed = jnp.concatenate(pieces, 2)
+    packed = halving_steps(packed, 0, [("tensor", tensor_count, 8), ("tensor", tensor_count, 4),
+                                       ("tensor", tensor_count, 2), ("tensor", tensor_count, 1)])
+    packed = halving_steps(packed, 1, [("group", group_count, 2), ("group", group_count, 1),
+                                       ("dp", lax.axis_size("dp"), 1)])
+    flat = packed.reshape(-1)
+    parts = []
+    offset = 0
+    for width in widths:
+        parts.append(flat[offset : offset + width])
+        offset += width
     return (
         output,
         input_grad,
-        vector_sums[0],
-        vector_sums[1],
+        parts[0],
+        parts[1],
         summed[0],
-        vector_sums[6:8],
+        jnp.stack((parts[6], parts[7])),
         summed[1],
-        vector_sums[2],
-        vector_sums[3],
-        vector_sums[4],
+        parts[2],
+        parts[3],
+        parts[4],
         summed[2],
-        in_sums,
+        parts[8],
         summed[3],
-        vector_sums[5],
-    )
+        parts[5],
+    )
+
+
+def halving_steps(value, dim, steps, send_type=None):
+    for axis, size, bit in steps:
+        half = value.shape[dim] // 2
+        low_half = lax.slice_in_dim(value, 0, half, axis=dim)
+        high_half = lax.slice_in_dim(value, half, 2 * half, axis=dim)
+        upper = (lax.axis_index(axis) // bit) % 2 == 1
+        keep = jnp.where(upper, high_half, low_half)
+        send = jnp.where(upper, low_half, high_half)
+        if send_type is not None:
+            send = send.astype(send_type)
+        got = lax.ppermute(send, axis, [(i, i ^ bit) for i in range(size)])
+        value = keep + got.astype(keep.dtype)
+    return value
+
+
+def halving_sum(value, dim):
+    shape = value.shape
+    groups = lax.axis_size("group")
+    dps = lax.axis_size("dp")
+    split = shape[:dim] + (groups * dps, shape[dim] // (groups * dps)) + shape[dim + 1 :]
+    value = value.reshape(split)
+    value = halving_steps(
+        value, dim, [("group", groups, 2), ("group", groups, 1), ("dp", dps, 1)], jnp.bfloat16
+    )
+    return value.reshape(shape[:dim] + (shape[dim] // (groups * dps),) + shape[dim + 1 :])
 
 
 def solution(mesh):

time: 1730 us -> 957 us (0.55)
  waiting for transfers between devices: 1380 us -> 640 us
  blocking collectives: 76.5 us -> 0 us
  starting transfers between devices: 1.12 us -> 24.9 us
    unnamed x14 -> x8, waiting for transfers between devices: 709 us -> 0.13 us
    reduce_scatter x1, waiting for transfers between devices: 90.1 us -> 0.01 us  [shards(): lax.psum_scatter(jnp.einsum('rsc,dc->rsd', piece, joint_weight, preferred...]
    ppermute x0 -> x19, waiting for transfers between devices: none -> 84.3 us  [halving_steps(): got = lax.ppermute(send, axis, [(i, i ^ bit) for i in range(size)])]
    unnamed x1 -> x0, blocking collectives: 76.5 us -> none
    reduce_scatter x4 -> x0, waiting for transfers between devices: 46.2 us -> none  [the longest x1 45.5 us: shards(): lax.psum_scatter(matrices[0].astype(jnp.bfloat16), ('group', 'dp'), scatt...]
    all_gather x1, waiting for transfers between devices: 37.3 us -> 61.8 us  [shards(): piece = lax.all_gather(branch_low, 'tensor', axis=0, tiled=True)]
    ppermute x0 -> x19, starting transfers between devices: none -> 24.4 us  [halving_steps(): got = lax.ppermute(send, axis, [(i, i ^ bit) for i in range(size)])]
  transfers between devices with their start and end apart: 13 -> 27, of which waited for: 11 -> 20; matrix products, arithmetic and copies ran while one was open for 9% -> 11% of each run, Pallas kernels for 0% -> 0%
where the time goes in v1:
time: 957 us; the launch traced here: 944 us
  waiting for transfers between devices  640 us (67%)
  matrix products  149 us (16%)
  other arithmetic  72.5 us (8%)
  starting transfers between devices  24.9 us (3%)
  local copies, waits for them, and re-layouts  24.2 us (3%)
  between operations  17.3 us (2%)
  Pallas kernels  16.2 us (2%)
    reduce_scatter x1, waiting for transfers between devices, shards(): lax.psum_scatter(jnp.einsum('rse,ed->rsd', piece, out_weight, preferred_e...  110 us
    reduce_scatter x1, waiting for transfers between devices, shards(): lax.psum_scatter(jnp.einsum('rsf,df->rsd', piece, w_in, preferred_element...  100 us
    reduce_scatter x1, waiting for transfers between devices, shards(): lax.psum_scatter(jnp.einsum('rsf,fd->rsd', piece, w_out, preferred_elemen...  85.7 us
    ppermute x19, waiting for transfers between devices, halving_steps(): got = lax.ppermute(send, axis, [(i, i ^ bit) for i in range(size)])  84.3 us
    all_gather x1, waiting for transfers between devices, shards(): normed_full = lax.all_gather(normed_low, 'tensor', axis=0, tiled=True)  68.1 us
    all_gather x1, waiting for transfers between devices, shards(): second_full = lax.all_gather(second_low, 'tensor', axis=0, tiled=True)  67.6 us
    all_gather x1, waiting for transfers between devices, shards(): piece = lax.all_gather(upstream, 'tensor', axis=0, tiled=True)  62.4 us
    all_gather x1, waiting for transfers between devices, shards(): piece = lax.all_gather(branch_low, 'tensor', axis=0, tiled=True)  61.8 us
  transfers between devices with their start and end apart: 27, of which 20 were waited for; matrix products, arithmetic and copies ran while one was open for 11% of the time, Pallas kernels for 0%

profile of v1, /device:TPU:96, one launch (start us, length us, event | category | flops | bytes accessed | tf_op | source)
XLA Modules:
  0.0 944.1 jit_solution(5569445801283736321)
XLA Ops:
  16.8 68.1 %all-gather.5.cloned.1.call-done = bf16[2048,1,2048]{2,0,1:T(8,128)(2,1)} async-done(((bf16[128,1,2048]{2,0,1:T(8,128)(2,1)}), bf16[2048,1,2048]{2,0,1:T(8,128)(2,1)}) %all-gather.5.cloned.1.call-update) | async-done | bytes 8388624 | tf_op jit(solution)/shard_map/all_gather | solution.py:133
  84.8 7.4 fusion.33
  129.3 8.1 convolution_bitcast_fusion.1
  137.5 110.3 %reduce-scatter.5.cloned.1.call-done = f32[128,1,2048]{2,0,1:T(8,128)} async-done(((f32[2048,1,2048]{2,0,1:T(8,128)}), f32[128,1,2048]{2,0,1:T(8,128)}) %reduce-scatter.5.cloned.1.call-update) | async-done | bytes 1048592 | tf_op jit(solution)/shard_map/reduce_scatter | solution.py:167
  253.5 67.6 %all-gather.7.cloned.1.call-done = bf16[2048,1,2048]{2,0,1:T(8,128)(2,1)} async-done(((bf16[128,1,2048]{2,0,1:T(8,128)(2,1)}), bf16[2048,1,2048]{2,0,1:T(8,128)(2,1)}) %all-gather.7.cloned.1.call-update) | async-done | bytes 8388624 | tf_op jit(solution)/shard_map/all_gather | solution.py:177
  321.1 10.5 %fusion.10 = f32[2048,512]{1,0:T(8,128)} fusion(bf16[2048,512]{1,0:T(8,128)(2,1)} %param.26, bf16[2048,1,2048]{2,0,1:T(8,128)(2,1)} %all-gather.7.cloned.1.call-done), kind=kOutput, calls=%fused_computation.12 | convolution fusion | flops 4294967296 | bytes 14680064 | tf_op jit(solution)/shard_map/dot_general | solution.py:179
  331.7 62.4 %all-gather.9.cloned.1.call-done = bf16[2048,1,2048]{2,0,1:T(8,128)(2,1)} async-done(((bf16[128,1,2048]{2,0,1:T(8,128)(2,1)}), bf16[2048,1,2048]{2,0,1:T(8,128)(2,1)}) %all-gather.9.cloned.1.call-update) | async-done | bytes 8388624 | tf_op jit(solution)/shard_map/all_gather | solution.py:203
  394.0 12.7 %convert_reduce_fusion = (f32[512]{0:T(512)}, bf16[2048,512]{1,0:T(8,128)(2,1)S(1)}) fusion(f32[2048,512]{1,0:T(8,128)} %fusion.10, f32[512]{0:T(512)S(1)} %copy-done.72, bf16[512,2048]{1,0:T(8,128)(2,1)S(1)} %copy-done, bf16[2048,1,2048]{2,0,1:T(8,128)(2,1)} %all-gather.9.cloned.1.call-done), kind=kOutput, calls=%fused_computation.29 | convolution fusion | flops 4319084032 | bytes 16781312 | tf_op jit(solution)/shard_map/rsd,fd->rsf/dot_general | solution.py:205
  408.1 8.3 convolution_bitcast_fusion
  416.5 10.2 %convert_bitcast_fusion.1 = bf16[2048,1,2048]{2,0,1:T(8,128)(2,1)} fusion(bf16[512,2048]{1,0:T(8,128)(2,1)S(1)} %copy-done, f32[2048,512]{1,0:T(8,128)} %fusion.10, f32[512]{0:T(512)S(1)} %copy-done.72), kind=kOutput, calls=%fused_computation.19 | convolution fusion | flops 4309647360 | bytes 14682112 | tf_op jit(solution)/shard_map/rsf,fd->rsd/dot_general | solution.py:190
  426.8 100.0 %reduce-scatter.9.cloned.1.call-done = f32[128,1,2048]{2,0,1:T(8,128)} async-done(((f32[2048,1,2048]{2,0,1:T(8,128)}), f32[128,1,2048]{2,0,1:T(8,128)}) %reduce-scatter.9.cloned.1.call-update) | async-done | bytes 1048592 | tf_op jit(solution)/shard_map/reduce_scatter | solution.py:219
  529.1 85.7 %reduce-scatter.7.cloned.1.call-done = bf16[128,1,2048]{2,0,1:T(8,128)(2,1)} async-done(((bf16[2048,1,2048]{2,0,1:T(8,128)(2,1)}), bf16[128,1,2048]{2,0,1:T(8,128)(2,1)}) %reduce-scatter.7.cloned.1.call-update) | async-done | bytes 524304 | tf_op jit(solution)/shard_map/reduce_scatter | solution.py:189
  626.9 61.8 %all-gather.11.cloned.1.call-done = bf16[2048,1,2048]{2,0,1:T(8,128)(2,1)} async-done(((bf16[128,1,2048]{2,0,1:T(8,128)(2,1)}), bf16[2048,1,2048]{2,0,1:T(8,128)(2,1)}) %all-gather.11.cloned.1.call-update) | async-done | bytes 8388624 | tf_op jit(solution)/shard_map/all_gather | solution.py:231
  688.7 5.7 fusion.45
  706.5 10.2 %multiply_reduce_fusion = (f32[512]{0:T(512)}, f32[512]{0:T(512)}, f32[512]{0:T(512)}, f32[512]{0:T(512)}, f32[512,2048]{1,0:T(8,128)}) fusion(f32[512,2048]{1,0:T(8,128)S(1)} %copy-done.2, f32[512]{0:T(512)S(1)} %get-tuple-element.117, pred[2048]{0:T(1024)(128)(4,1)S(1)} %iota_compare_fusion.4, s32[512]{0:T(512)S(1)} %iota_add_fusion, ...), kind=kOutput, calls=%fused_computation.31 | convolution fusion | flops 293599232 | bytes 34234368 | tf_op jit(solution)/shard_map/while/body/eval_jaxpr/dot_general | solution.py:66
  716.7 9.4 multiply_convert_fusion
  743.3 9.7 %convert_bitcast_fusion = bf16[2048,1,2048]{2,0,1:T(8,128)(2,1)} fusion(bf16[2048,384]{0,1:T(8,128)(2,1)} %bitcast.201, bf16[2048,384]{0,1:T(8,128)(2,1)} %bitcast.202), kind=kOutput, calls=%fused_computation.18 | convolution fusion | flops 3225419776 | bytes 11534336 | tf_op jit(solution)/shard_map/rsc,dc->rsd/dot_general | solution.py:252
  756.4 8.7 fusion.27
  767.2 7.1 fusion.30
  784.4 17.5 %collective-permute-done.13 = bf16[4,256,512]{2,1,0:T(8,128)(2,1)S(1)} collective-permute-done((bf16[4,256,512]{2,1,0:T(8,128)(2,1)}, bf16[4,256,512]{2,1,0:T(8,128)(2,1)S(1)}, u32[]{:S(2)}, u32[]{:S(2)}) %collective-permute-start.13) | collective-permute-done | bytes 1048608 | tf_op jit(solution)/shard_map/ppermute | solution.py:335
  802.4 20.9 %collective-permute-done.16 = bf16[512,4,256]{2,0,1:T(8,128)(2,1)} collective-permute-done((bf16[512,4,256]{2,0,1:T(8,128)(2,1)}, bf16[512,4,256]{2,0,1:T(8,128)(2,1)}, u32[]{:S(2)}, u32[]{:S(2)}) %collective-permute-start.16) | collective-permute-done | bytes 1048608 | tf_op jit(solution)/shard_map/ppermute | solution.py:335
  851.7 7.0 fusion.36
  878.5 23.7 %collective-permute-done.7 = bf16[4,256,3,1,128]{4,3,2,1,0:T(2,128)(2,1)} collective-permute-done((bf16[4,256,3,1,128]{4,3,2,1,0:T(2,128)(2,1)S(1)}, bf16[4,256,3,1,128]{4,3,2,1,0:T(2,128)(2,1)}, u32[]{:S(2)}, u32[]{:S(2)}) %collective-permute-start.7) | collective-permute-done | bytes 786464 | tf_op jit(solution)/shard_map/ppermute | solution.py:335
  921.7 5.5 collective-permute-done.9
  (349 shorter events, 188.3 us)
Async XLA Ops:
  7.2 77.6 %all-gather.5.cloned.1.call-start = ((), (), s32[]{:S(2)}) async-start(), calls=%async_computation.4 | async-start | bytes 8912896 | tf_op jit(solution)/shard_map/all_gather | solution.py:133
  12.8 235.0 %reduce-scatter.5.cloned.1.call-start = ((), (), s32[]{:S(2)}) async-start(), calls=%async_computation.5 | async-start | bytes 17825792 | tf_op jit(solution)/shard_map/reduce_scatter | solution.py:167
  137.4 183.7 %all-gather.7.cloned.1.call-start = ((), (), s32[]{:S(2)}) async-start(), calls=%async_computation.6 | async-start | bytes 8912896 | tf_op jit(solution)/shard_map/all_gather | solution.py:177
  250.7 143.3 %all-gather.9.cloned.1.call-start = ((), (), s32[]{:S(2)}) async-start(), calls=%async_computation.8 | async-start | bytes 8912896 | tf_op jit(solution)/shard_map/all_gather | solution.py:203
  253.5 273.4 %reduce-scatter.9.cloned.1.call-start = ((), (), s32[]{:S(2)}) async-start(), calls=%async_computation.9 | async-start | bytes 17825792 | tf_op jit(solution)/shard_map/reduce_scatter | solution.py:219
  416.4 198.4 %reduce-scatter.7.cloned.1.call-start = ((), (), s32[]{:S(2)}) async-start(), calls=%async_computation.7 | async-start | bytes 8912896 | tf_op jit(solution)/shard_map/reduce_scatter | solution.py:189
  426.8 261.9 %all-gather.11.cloned.1.call-start = ((), (), s32[]{:S(2)}) async-start(), calls=%async_computation.10 | async-start | bytes 8912896 | tf_op jit(solution)/shard_map/all_gather | solution.py:231
  618.5 251.7 %reduce-scatter.11.cloned.1.call-start = ((), (), s32[]{:S(2)}) async-start(), calls=%async_computation.11 | async-start | bytes 8912896 | tf_op jit(solution)/shard_map/reduce_scatter | solution.py:251
  775.6 26.3 %collective-permute-start.13 = (bf16[4,256,512]{2,1,0:T(8,128)(2,1)}, bf16[4,256,512]{2,1,0:T(8,128)(2,1)S(1)}, u32[]{:S(2)}, u32[]{:S(2)}) collective-permute-start(bf16[4,256,512]{2,1,0:T(8,128)(2,1)} %bitcast.57), channel_id=1, source_target_pairs={{0,64},{32,96},{64,0},{96,32},{1,65},{33,97},{65,1},{97,33},{2,66}... | collective-permute-start | bytes 3145736 | tf_op jit(solution)/shard_map/ppermute | solution.py:335
  780.1 43.2 %collective-permute-start.16 = (bf16[512,4,256]{2,0,1:T(8,128)(2,1)}, bf16[512,4,256]{2,0,1:T(8,128)(2,1)}, u32[]{:S(2)}, u32[]{:S(2)}) collective-permute-start(bf16[512,4,256]{2,0,1:T(8,128)(2,1)} %select_convert_fusion), channel_id=1, source_target_pairs={{0,64},{32,96},{64,0},{96,32},{1,65},{33,97},{65,1},{97,33},{2,66}... | collective-permute-start | bytes 3145736 | tf_op jit(solution)/shard_map/ppermute | solution.py:335
  802.3 23.1 %collective-permute-start.14 = (bf16[2,256,512]{2,1,0:T(8,128)(2,1)S(1)}, bf16[2,256,512]{2,1,0:T(8,128)(2,1)S(1)}, u32[]{:S(2)}, u32[]{:S(2)}) collective-permute-start(bf16[2,256,512]{2,1,0:T(8,128)(2,1)S(1)} %select_convert_fusion.4), channel_id=1, source_target_pairs={{0,32},{32,0},{64,96},{96,64},{1,33},{33,1},{65,97},{97,65},{2,34}... | collective-permute-start | bytes 1572872 | tf_op jit(solution)/shard_map/ppermute | solution.py:335
  825.8 10.7 %collective-permute-start.15 = (bf16[1,256,512]{2,1,0:T(8,128)(2,1)S(1)}, bf16[1,256,512]{2,1,0:T(8,128)(2,1)S(1)}, u32[]{:S(2)}, u32[]{:S(2)}) collective-permute-start(bf16[1,256,512]{2,1,0:T(8,128)(2,1)S(1)} %select_convert_fusion.6), channel_id=1, source_target_pairs={{0,16},{16,0},{1,17},{17,1},{2,18},{18,2},{3,19},{19,3},{4,20},{20... | collective-permute-start | bytes 786440 | tf_op jit(solution)/shard_map/ppermute | solution.py:335
  828.3 13.4 %collective-permute-start.18 = (bf16[512,1,256]{2,0,1:T(8,128)(2,1)}, bf16[512,1,256]{2,0,1:T(8,128)(2,1)S(1)}, u32[]{:S(2)}, u32[]{:S(2)}) collective-permute-start(bf16[512,1,256]{2,0,1:T(8,128)(2,1)} %select_convert_fusion.5), channel_id=1, source_target_pairs={{0,16},{16,0},{1,17},{17,1},{2,18},{18,2},{3,19},{19,3},{4,20},{20... | collective-permute-start | bytes 786440 | tf_op jit(solution)/shard_map/ppermute | solution.py:335
  850.8 9.4 collective-permute-start.10
  862.6 6.1 collective-permute-start.12
  865.8 36.4 %collective-permute-start.7 = (bf16[4,256,3,1,128]{4,3,2,1,0:T(2,128)(2,1)S(1)}, bf16[4,256,3,1,128]{4,3,2,1,0:T(2,128)(2,1)}, u32[]{:S(2)}, u32[]{:S(2)}) collective-permute-start(bf16[4,256,3,1,128]{4,3,2,1,0:T(2,128)(2,1)S(1)} %copy.55), channel_id=1, source_target_pairs={{0,64},{32,96},{64,0},{96,32},{1,65},{33,97},{65,1},{97,33},{2,66}... | collective-permute-start | bytes 2359304 | tf_op jit(solution)/shard_map/ppermute | solution.py:335
  875.2 31.2 %collective-permute-start = (f32[8,8,192]{2,0,1:T(8,128)S(1)}, f32[8,8,192]{2,0,1:T(8,128)S(1)}, u32[]{:S(2)}, u32[]{:S(2)}) collective-permute-start(f32[8,8,192]{2,0,1:T(8,128)S(1)} %slice_select_fusion.2), channel_id=1, source_target_pairs={{0,8},{1,9},{2,10},{3,11},{4,12},{5,13},{6,14},{7,15},{8,0},{9,1},... | collective-permute-start | bytes 147464 | tf_op jit(solution)/shard_map/ppermute | solution.py:335
  906.6 4.0 collective-permute-start.1
  908.9 4.8 collective-permute-start.8
  910.6 5.3 collective-permute-start.2
  916.0 4.5 collective-permute-start.3
  917.9 9.4 collective-permute-start.9
  920.5 8.2 collective-permute-start.4
  929.9 5.2 collective-permute-start.6
  (80 other events, 3688.8 us)
Sparse Core Ops, SparseCore 0:
  12.9 71.8 all-gather.4
  137.5 110.1 reduce-scatter.4
  250.8 70.2 all-gather.6
  323.7 70.3 all-gather.8
  416.6 110.2 reduce-scatter.8
  530.1 84.6 reduce-scatter.6
  618.7 70.0 all-gather.10
  753.2 84.7 reduce-scatter.10

commit v2 on v1

--- a/solution.py
+++ b/solution.py
@@ -162,13 +162,17 @@
     )
     attended = per_row(heads_out)
     out_weight = w_o.reshape(local_width, model_width)
-    piece = attended
+    positions = tensor_rank * row_count + jnp.arange(row_count, dtype=jnp.int32)
+    live = positions[:, None] < seq_lengths[None, :]
+    upstream = jnp.where(live[:, :, None], cotangent, jnp.zeros_like(cotangent))
+    upstream_full = lax.all_gather(upstream, "tensor", axis=0, tiled=True)
+    attention_part = jnp.einsum(
+        "rse,ed->rsd", attended, out_weight, preferred_element_type=jnp.float32
+    ).astype(jnp.bfloat16)
+    attention_part, upstream_full = lax.optimization_barrier((attention_part, upstream_full))
     attention = (
-        lax.psum_scatter(
-            jnp.einsum("rse,ed->rsd", piece, out_weight, preferred_element_type=jnp.float32),
-            "tensor",
-            scatter_dimension=0,
-            tiled=True,
+        lax.psum_scatter(attention_part, "tensor", scatter_dimension=0, tiled=True).astype(
+            jnp.float32
         )
         + b_o
     )
@@ -184,23 +188,10 @@
         + b_in
     )
     activated = gelu_tanh(pre_act).astype(jnp.bfloat16).reshape(seq_total, seq_count, hidden)
-    piece = activated
-    feed = (
-        lax.psum_scatter(
-            jnp.einsum("rsf,fd->rsd", piece, w_out, preferred_element_type=jnp.float32).astype(
-                jnp.bfloat16
-            ),
-            "tensor",
-            scatter_dimension=0,
-            tiled=True,
-        ).astype(jnp.float32)
-        + b_out
-    )
-    output = (middle + feed).astype(jnp.bfloat16)
-    positions = tensor_rank * row_count + jnp.arange(row_count, dtype=jnp.int32)
-    live = positions[:, None] < seq_lengths[None, :]
-    upstream = jnp.where(live[:, :, None], cotangent, jnp.zeros_like(cotangent))
-    piece = lax.all_gather(upstream, "tensor", axis=0, tiled=True)
+    feed_part = jnp.einsum(
+        "rsf,fd->rsd", activated, w_out, preferred_element_type=jnp.float32
+    ).astype(jnp.bfloat16)
+    piece = upstream_full
     weight_grad = jnp.einsum("rsf,rsd->fd", activated, piece, preferred_element_type=jnp.float32)
     part = jnp.einsum("rsd,fd->rsf", piece, w_out, preferred_element_type=jnp.float32)
     act_grad = part
@@ -217,11 +208,13 @@
     pre_rows = pre_low.reshape(seq_total, seq_count, hidden)
     piece = pre_rows
     second_grad = lax.psum_scatter(
-        jnp.einsum("rsf,df->rsd", piece, w_in, preferred_element_type=jnp.float32),
+        jnp.einsum("rsf,df->rsd", piece, w_in, preferred_element_type=jnp.float32).astype(
+            jnp.bfloat16
+        ),
         "tensor",
         scatter_dimension=0,
         tiled=True,
-    )
+    ).astype(jnp.float32)
     norm_two_back = jax.vjp(layer_norm, middle, ln2_gain, ln2_bias)[1]
     middle_part, grad_ln2_gain, grad_ln2_bias = norm_two_back(second_grad)
     middle_grad = upstream.astype(jnp.float32) + middle_part
@@ -229,6 +222,14 @@
     grad_b_o = jnp.sum(branch_low, axis=(0, 1), dtype=jnp.float32)
     grad_b_out = jnp.sum(upstream, axis=(0, 1), dtype=jnp.float32)
     piece = lax.all_gather(branch_low, "tensor", axis=0, tiled=True)
+    feed_part, piece = lax.optimization_barrier((feed_part, piece))
+    feed = (
+        lax.psum_scatter(feed_part, "tensor", scatter_dimension=0, tiled=True).astype(
+            jnp.float32
+        )
+        + b_out
+    )
+    output = (middle + feed).astype(jnp.bfloat16)
     weight_grad = jnp.einsum("rse,rsd->ed", attended, piece, preferred_element_type=jnp.float32)
     part = jnp.einsum("rsd,ed->rse", piece, out_weight, preferred_element_type=jnp.float32)
     head_items = per_item(part.astype(jnp.bfloat16))

time: 957 us -> 789 us (0.82)
  waiting for transfers between devices: 640 us -> 456 us
    reduce_scatter x2, waiting for transfers between devices: 196 us -> 88.1 us  [the longest x1 88.1 us: shards(): lax.psum_scatter(attention_part, 'tensor', scatter_dimension=0, tiled=True)]
    all_gather x1, waiting for transfers between devices: 62.4 us -> 19.1 us  [shards(): upstream_full = lax.all_gather(upstream, 'tensor', axis=0, tiled=True)]
    all_gather x1, waiting for transfers between devices: 61.8 us -> 45.5 us  [shards(): piece = lax.all_gather(branch_low, 'tensor', axis=0, tiled=True)]
    reduce_scatter x1, waiting for transfers between devices: 100 us -> 84.9 us  [shards(): lax.psum_scatter(jnp.einsum('rsf,df->rsd', piece, w_in, preferred_element...]
  transfers between devices with their start and end apart: 27 -> 27, of which waited for: 20 -> 17; matrix products, arithmetic and copies ran while one was open for 11% -> 18% of each run, Pallas kernels for 0% -> 2%
where the time goes in v2:
time: 789 us; the launch traced here: 777 us
  waiting for transfers between devices  456 us (58%)
  matrix products  155 us (20%)
  other arithmetic  77.7 us (10%)
  local copies, waits for them, and re-layouts  28.2 us (4%)
  starting transfers between devices  26.2 us (3%)
  between operations  17.3 us (2%)
  Pallas kernels  16.6 us (2%)
    reduce_scatter x1, waiting for transfers between devices, shards(): lax.psum_scatter(attention_part, 'tensor', scatter_dimension=0, tiled=True)  88.1 us
    reduce_scatter x1, waiting for transfers between devices, shards(): lax.psum_scatter(jnp.einsum('rsf,df->rsd', piece, w_in, preferred_element...  84.9 us
    ppermute x19, waiting for transfers between devices, halving_steps(): got = lax.ppermute(send, axis, [(i, i ^ bit) for i in range(size)])  84 us
    all_gather x1, waiting for transfers between devices, shards(): second_full = lax.all_gather(second_low, 'tensor', axis=0, tiled=True)  70.1 us
    all_gather x1, waiting for transfers between devices, shards(): normed_full = lax.all_gather(normed_low, 'tensor', axis=0, tiled=True)  64 us
    all_gather x1, waiting for transfers between devices, shards(): piece = lax.all_gather(branch_low, 'tensor', axis=0, tiled=True)  45.5 us
    ppermute x19, starting transfers between devices, halving_steps(): got = lax.ppermute(send, axis, [(i, i ^ bit) for i in range(size)])  25.8 us
    dot_general x4, matrix products, attend_backward(): lax.dot_general(grad_rows, value_rows, (((1,), (1,)), ((), ())), preferre...  21.5 us
  transfers between devices with their start and end apart: 27, of which 17 were waited for; matrix products, arithmetic and copies ran while one was open for 18% of the time, Pallas kernels for 2%

profile of v2, /device:TPU:96, one launch (start us, length us, event | category | flops | bytes accessed | tf_op | source)
XLA Modules:
  0.0 777.0 jit_solution(8731599573753859071)
XLA Ops:
  20.3 64.0 %all-gather.5.cloned.1.call-done = bf16[2048,1,2048]{2,0,1:T(8,128)(2,1)} async-done(((bf16[128,1,2048]{2,0,1:T(8,128)(2,1)}), bf16[2048,1,2048]{2,0,1:T(8,128)(2,1)}) %all-gather.5.cloned.1.call-update) | async-done | bytes 8388624 | tf_op jit(solution)/shard_map/all_gather | solution.py:133
  84.3 7.4 fusion.33
  132.6 5.6 convert_bitcast_fusion.3
  138.2 19.1 %all-gather.7.cloned.1.call-done = bf16[2048,1,2048]{2,0,1:T(8,128)(2,1)} async-done(((bf16[128,1,2048]{2,0,1:T(8,128)(2,1)}), bf16[2048,1,2048]{2,0,1:T(8,128)(2,1)}) %all-gather.7.cloned.1.call-update) | async-done | bytes 8388624 | tf_op jit(solution)/shard_map/all_gather | solution.py:168
  157.4 88.1 %reduce-scatter.5.cloned.1.call-done = bf16[128,1,2048]{2,0,1:T(8,128)(2,1)} async-done(((bf16[2048,1,2048]{2,0,1:T(8,128)(2,1)}), bf16[128,1,2048]{2,0,1:T(8,128)(2,1)}) %reduce-scatter.5.cloned.1.call-update) | async-done | bytes 524304 | tf_op jit(solution)/shard_map/reduce_scatter | solution.py:174
  250.5 70.1 %all-gather.9.cloned.1.call-done = bf16[2048,1,2048]{2,0,1:T(8,128)(2,1)} async-done(((bf16[128,1,2048]{2,0,1:T(8,128)(2,1)}), bf16[2048,1,2048]{2,0,1:T(8,128)(2,1)}) %all-gather.9.cloned.1.call-update) | async-done | bytes 8388624 | tf_op jit(solution)/shard_map/all_gather | solution.py:181
  320.7 7.5 fusion.10
  328.3 13.1 %convert_reduce_fusion = (f32[512]{0:T(512)}, bf16[2048,512]{1,0:T(8,128)(2,1)S(1)}) fusion(f32[2048,512]{1,0:T(8,128)S(1)} %fusion.10, f32[512]{0:T(512)S(1)} %copy-done.85, bf16[512,2048]{1,0:T(8,128)(2,1)S(1)} %copy-done, bf16[2048,1,2048]{2,0,1:T(8,128)(2,1)} %all-gather.7.cloned.1.call-done), kind=kOutput, calls=%fused_computation.29 | convolution fusion | flops 4319084032 | bytes 16781312 | tf_op jit(solution)/shard_map/rsd,fd->rsf/dot_general | solution.py:196
  342.8 6.9 convert_bitcast_fusion.1
  349.7 84.9 %reduce-scatter.7.cloned.1.call-done = bf16[128,1,2048]{2,0,1:T(8,128)(2,1)} async-done(((bf16[2048,1,2048]{2,0,1:T(8,128)(2,1)}), bf16[128,1,2048]{2,0,1:T(8,128)(2,1)}) %reduce-scatter.7.cloned.1.call-update) | async-done | bytes 524304 | tf_op jit(solution)/shard_map/reduce_scatter | solution.py:210
  449.3 15.8 %convert_bitcast_fusion.2 = bf16[2048,1,2048]{2,0,1:T(8,128)(2,1)} fusion(bf16[512,2048]{1,0:T(8,128)(2,1)S(1)} %copy-done, f32[2048,512]{1,0:T(8,128)S(1)} %copy-done.89, f32[512]{0:T(512)S(1)} %copy-done.85), kind=kOutput, calls=%fused_computation.18 | convolution fusion | flops 4309647360 | bytes 14682112 | tf_op jit(solution)/shard_map/rsf,fd->rsd/dot_general | solution.py:191
  465.1 45.5 %all-gather.11.cloned.1.call-done = bf16[2048,1,2048]{2,0,1:T(8,128)(2,1)} async-done(((bf16[128,1,2048]{2,0,1:T(8,128)(2,1)}), bf16[2048,1,2048]{2,0,1:T(8,128)(2,1)}) %all-gather.11.cloned.1.call-update) | async-done | bytes 8388624 | tf_op jit(solution)/shard_map/all_gather | solution.py:224
  510.6 5.8 fusion.45
  529.6 10.9 %multiply_reduce_fusion = (f32[512]{0:T(512)}, f32[512]{0:T(512)}, f32[512]{0:T(512)}, f32[512]{0:T(512)}, f32[512,2048]{1,0:T(8,128)}) fusion(f32[512,2048]{1,0:T(8,128)S(1)} %copy-done.2, f32[512]{0:T(512)S(1)} %copy-done.59, pred[2048]{0:T(1024)(128)(4,1)S(1)} %iota_compare_fusion.4, s32[512]{0:T(512)S(1)} %copy-done.52, f32[512,2048]{1,0:T(8,128)} %fusion.108, ...), kind=kOutput, calls=%fused_computation.31 | convolution fusion | flops 293599232 | bytes 34234368 | tf_op jit(solution)/shard_map/while/body/eval_jaxpr/dot_general | solution.py:66
  540.5 9.5 %multiply_convert_fusion = (bf16[512,2048]{1,0:T(8,128)(2,1)S(1)}, bf16[512,2048]{1,0:T(8,128)(2,1)}, bf16[512,2048]{1,0:T(8,128)(2,1)S(1)}) fusion(f32[512,2048]{1,0:T(8,128)} %get-tuple-element.119, f32[512]{0:T(512)} %get-tuple-element.82, f32[512,2048]{1,0:T(8,128)S(1)} %copy-done.2, f32[512]{0:T(512)} %get-tuple-element.124, ...), kind=kLoop, calls=%fused_computation.30 | loop fusion | flops 22020096 | bytes 31475712 | tf_op jit(solution)/shard_map/while/body/eval_jaxpr/convert_element_type | solution.py:70
  568.2 9.7 %convert_bitcast_fusion = bf16[2048,1,2048]{2,0,1:T(8,128)(2,1)} fusion(bf16[2048,384]{0,1:T(8,128)(2,1)} %bitcast.201, bf16[2048,384]{0,1:T(8,128)(2,1)} %bitcast.202), kind=kOutput, calls=%fused_computation.16 | convolution fusion | flops 3225419776 | bytes 11534336 | tf_op jit(solution)/shard_map/rsc,dc->rsd/dot_general | solution.py:253
  581.3 8.5 %fusion.27 = f32[512,2048]{1,0:T(8,128)S(1)} fusion(bf16[2048,1,2048]{2,0,1:T(8,128)(2,1)} %all-gather.7.cloned.1.call-done, f32[]{:T(128)S(6)} %div.167, f32[2048,512]{1,0:T(8,128)} %copy-done.88, f32[512]{0:T(512)S(1)} %copy-done.86), kind=kOutput, calls=%fused_computation.59 | convolution fusion | flops 4306501632 | bytes 16779268 | tf_op jit(solution)/shard_map/rsf,rsd->fd/dot_general | solution.py:195
  595.4 7.1 fusion.30
  612.9 17.5 %collective-permute-done.13 = bf16[4,256,512]{2,1,0:T(8,128)(2,1)} collective-permute-done((bf16[4,256,512]{2,1,0:T(8,128)(2,1)}, bf16[4,256,512]{2,1,0:T(8,128)(2,1)}, u32[]{:S(2)}, u32[]{:S(2)}) %collective-permute-start.13) | collective-permute-done | bytes 1048608 | tf_op jit(solution)/shard_map/ppermute | solution.py:336
  632.2 19.6 %collective-permute-done.16 = bf16[512,4,256]{2,0,1:T(8,128)(2,1)} collective-permute-done((bf16[512,4,256]{2,0,1:T(8,128)(2,1)}, bf16[512,4,256]{2,0,1:T(8,128)(2,1)}, u32[]{:S(2)}, u32[]{:S(2)}) %collective-permute-start.16) | collective-permute-done | bytes 1048608 | tf_op jit(solution)/shard_map/ppermute | solution.py:336
  660.3 5.6 collective-permute-done.15
  681.5 7.0 fusion.36
  707.9 25.0 %collective-permute-done.7 = bf16[4,256,3,1,128]{4,3,2,1,0:T(2,128)(2,1)} collective-permute-done((bf16[4,256,3,1,128]{4,3,2,1,0:T(2,128)(2,1)S(1)}, bf16[4,256,3,1,128]{4,3,2,1,0:T(2,128)(2,1)}, u32[]{:S(2)}, u32[]{:S(2)}) %collective-permute-start.7) | collective-permute-done | bytes 786464 | tf_op jit(solution)/shard_map/ppermute | solution.py:336
  753.4 5.6 collective-permute-done.9
  (379 shorter events, 199.8 us)
Async XLA Ops:
  7.2 77.1 %all-gather.5.cloned.1.call-start = ((), (), s32[]{:S(2)}) async-start(), calls=%async_computation.4 | async-start | bytes 8912896 | tf_op jit(solution)/shard_map/all_gather | solution.py:133
  12.2 145.1 %all-gather.7.cloned.1.call-start = ((), (), s32[]{:S(2)}) async-start(), calls=%async_computation.5 | async-start | bytes 8912896 | tf_op jit(solution)/shard_map/all_gather | solution.py:168
  16.8 228.7 %reduce-scatter.5.cloned.1.call-start = ((), (), s32[]{:S(2)}) async-start(), calls=%async_computation.6 | async-start | bytes 8912896 | tf_op jit(solution)/shard_map/reduce_scatter | solution.py:174
  157.4 163.3 %all-gather.9.cloned.1.call-start = ((), (), s32[]{:S(2)}) async-start(), calls=%async_computation.7 | async-start | bytes 8912896 | tf_op jit(solution)/shard_map/all_gather | solution.py:181
  250.5 184.1 %reduce-scatter.7.cloned.1.call-start = ((), (), s32[]{:S(2)}) async-start(), calls=%async_computation.8 | async-start | bytes 8912896 | tf_op jit(solution)/shard_map/reduce_scatter | solution.py:210
  349.7 160.9 %all-gather.11.cloned.1.call-start = ((), (), s32[]{:S(2)}) async-start(), calls=%async_computation.9 | async-start | bytes 8912896 | tf_op jit(solution)/shard_map/all_gather | solution.py:224
  440.5 259.8 %reduce-scatter.11.cloned.1.call-start = ((), (), s32[]{:S(2)}) async-start(), calls=%async_computation.11 | async-start | bytes 8912896 | tf_op jit(solution)/shard_map/reduce_scatter | solution.py:252
  577.9 186.7 %reduce-scatter.9.cloned.1.call-start = ((), (), s32[]{:S(2)}) async-start(), calls=%async_computation.10 | async-start | bytes 8912896 | tf_op jit(solution)/shard_map/reduce_scatter | solution.py:227
  603.9 26.5 %collective-permute-start.13 = (bf16[4,256,512]{2,1,0:T(8,128)(2,1)}, bf16[4,256,512]{2,1,0:T(8,128)(2,1)}, u32[]{:S(2)}, u32[]{:S(2)}) collective-permute-start(bf16[4,256,512]{2,1,0:T(8,128)(2,1)} %bitcast.57), channel_id=1, source_target_pairs={{0,64},{32,96},{64,0},{96,32},{1,65},{33,97},{65,1},{97,33},{2,66}... | collective-permute-start | bytes 3145736 | tf_op jit(solution)/shard_map/ppermute | solution.py:336
  608.5 43.3 %collective-permute-start.16 = (bf16[512,4,256]{2,0,1:T(8,128)(2,1)}, bf16[512,4,256]{2,0,1:T(8,128)(2,1)}, u32[]{:S(2)}, u32[]{:S(2)}) collective-permute-start(bf16[512,4,256]{2,0,1:T(8,128)(2,1)} %select_convert_fusion), channel_id=1, source_target_pairs={{0,64},{32,96},{64,0},{96,32},{1,65},{33,97},{65,1},{97,33},{2,66}... | collective-permute-start | bytes 3145736 | tf_op jit(solution)/shard_map/ppermute | solution.py:336
  632.1 21.9 %collective-permute-start.14 = (bf16[2,256,512]{2,1,0:T(8,128)(2,1)S(1)}, bf16[2,256,512]{2,1,0:T(8,128)(2,1)S(1)}, u32[]{:S(2)}, u32[]{:S(2)}) collective-permute-start(bf16[2,256,512]{2,1,0:T(8,128)(2,1)S(1)} %select_convert_fusion.4), channel_id=1, source_target_pairs={{0,32},{32,0},{64,96},{96,64},{1,33},{33,1},{65,97},{97,65},{2,34}... | collective-permute-start | bytes 1572872 | tf_op jit(solution)/shard_map/ppermute | solution.py:336
  655.0 10.9 %collective-permute-start.15 = (bf16[1,256,512]{2,1,0:T(8,128)(2,1)}, bf16[1,256,512]{2,1,0:T(8,128)(2,1)S(1)}, u32[]{:S(2)}, u32[]{:S(2)}) collective-permute-start(bf16[1,256,512]{2,1,0:T(8,128)(2,1)} %select_convert_fusion.6), channel_id=1, source_target_pairs={{0,16},{16,0},{1,17},{17,1},{2,18},{18,2},{3,19},{19,3},{4,20},{20... | collective-permute-start | bytes 786440 | tf_op jit(solution)/shard_map/ppermute | solution.py:336
  657.4 13.9 %collective-permute-start.18 = (bf16[512,1,256]{2,0,1:T(8,128)(2,1)}, bf16[512,1,256]{2,0,1:T(8,128)(2,1)}, u32[]{:S(2)}, u32[]{:S(2)}) collective-permute-start(bf16[512,1,256]{2,0,1:T(8,128)(2,1)} %select_convert_fusion.5), channel_id=1, source_target_pairs={{0,16},{16,0},{1,17},{17,1},{2,18},{18,2},{3,19},{19,3},{4,20},{20... | collective-permute-start | bytes 786440 | tf_op jit(solution)/shard_map/ppermute | solution.py:336
  680.7 9.4 %collective-permute-start.10 = (bf16[1,128,4,256]{3,1,2,0:T(8,128)(2,1)S(1)}, bf16[1,128,4,256]{3,1,2,0:T(8,128)(2,1)S(1)}, u32[]{:S(2)}, u32[]{:S(2)}) collective-permute-start(bf16[1,128,4,256]{3,1,2,0:T(8,128)(2,1)S(1)} %select_convert_fusion.7), channel_id=1, source_target_pairs={{0,64},{32,96},{64,0},{96,32},{1,65},{33,97},{65,1},{97,33},{2,66}... | collective-permute-start | bytes 786440 | tf_op jit(solution)/shard_map/ppermute | solution.py:336
  692.5 6.3 collective-permute-start.12
  696.5 36.4 %collective-permute-start.7 = (bf16[4,256,3,1,128]{4,3,2,1,0:T(2,128)(2,1)S(1)}, bf16[4,256,3,1,128]{4,3,2,1,0:T(2,128)(2,1)}, u32[]{:S(2)}, u32[]{:S(2)}) collective-permute-start(bf16[4,256,3,1,128]{4,3,2,1,0:T(2,128)(2,1)S(1)} %copy.55), channel_id=1, source_target_pairs={{0,64},{32,96},{64,0},{96,32},{1,65},{33,97},{65,1},{97,33},{2,66}... | collective-permute-start | bytes 2359304 | tf_op jit(solution)/shard_map/ppermute | solution.py:336
  704.8 32.4 %collective-permute-start = (f32[8,8,192]{2,0,1:T(8,128)S(1)}, f32[8,8,192]{2,0,1:T(8,128)S(1)}, u32[]{:S(2)}, u32[]{:S(2)}) collective-permute-start(f32[8,8,192]{2,0,1:T(8,128)S(1)} %slice_select_fusion.2), channel_id=1, source_target_pairs={{0,8},{1,9},{2,10},{3,11},{4,12},{5,13},{6,14},{7,15},{8,0},{9,1},... | collective-permute-start | bytes 147464 | tf_op jit(solution)/shard_map/ppermute | solution.py:336
  737.3 4.4 collective-permute-start.1
  739.6 5.4 collective-permute-start.8
  741.7 5.5 collective-permute-start.2
  747.2 4.6 collective-permute-start.3
  749.3 9.6 %collective-permute-start.9 = (bf16[1,256,3,1,128]{4,3,2,1,0:T(2,128)(2,1)S(1)}, bf16[1,256,3,1,128]{4,3,2,1,0:T(2,128)(2,1)S(1)}, u32[]{:S(2)}, u32[]{:S(2)}) collective-permute-start(bf16[1,256,3,1,128]{4,3,2,1,0:T(2,128)(2,1)S(1)} %fusion.96), channel_id=1, source_target_pairs={{0,16},{16,0},{1,17},{17,1},{2,18},{18,2},{3,19},{19,3},{4,20},{20... | collective-permute-start | bytes 589832 | tf_op jit(solution)/shard_map/ppermute | solution.py:336
  751.8 8.6 %collective-permute-start.4 = (f32[1,4,192]{2,0,1:T(1,128)S(1)}, f32[1,4,192]{2,0,1:T(1,128)S(1)}, u32[]{:S(2)}, u32[]{:S(2)}) collective-permute-start(f32[1,4,192]{2,0,1:T(1,128)S(1)} %broadcast_select_fusion.8), channel_id=1, source_target_pairs={{0,64},{32,96},{64,0},{96,32},{1,65},{33,97},{65,1},{97,33},{2,66}... | collective-permute-start | bytes 9224 | tf_op jit(solution)/shard_map/ppermute | solution.py:336
  761.7 6.4 collective-permute-start.6
  (95 other events, 2200.2 us)
Sparse Core Ops, SparseCore 0:
  12.4 71.8 all-gather.4
  87.0 70.3 all-gather.6
  160.8 84.6 reduce-scatter.4
  250.6 70.0 all-gather.8
  349.8 84.7 reduce-scatter.6
  440.6 69.9 all-gather.10
  578.0 84.9 reduce-scatter.10
  666.4 85.7 reduce-scatter.8

commit v3 on v2

--- a/solution.py
+++ b/solution.py
@@ -4,6 +4,8 @@
 import jax
 import jax.numpy as jnp
 from jax import lax
+from jax.experimental import pallas as pl
+from jax.experimental.pallas import tpu as pltpu
 from jax.sharding import PartitionSpec as P
 
 EPS = 1e-05
@@ -21,74 +23,171 @@
     return jax.nn.gelu(value, approximate=True)
 
 
-def block_scores(rows_query, key_rows, first, length, score_scale):
-    count = rows_query.shape[0]
-    key_pos = jnp.arange(key_rows.shape[0], dtype=jnp.int32)
-    query_pos = first + jnp.arange(count, dtype=jnp.int32)
-    valid = (key_pos[None, :] <= query_pos[:, None]) & (key_pos[None, :] < length)
-    scores = (
-        lax.dot_general(
-            rows_query, key_rows, (((1,), (1,)), ((), ())), preferred_element_type=jnp.float32
-        )
-        * score_scale
-    )
-    return (jnp.where(valid, scores, NEGATIVE), valid)
-
-
-def attend_forward(item, block_rows, score_scale):
-    query, key_rows, value_rows, length = item
-    outputs = []
-    log_parts = []
-    for first in range(0, query.shape[0], block_rows):
-        rows_query = query[first : first + block_rows]
-        scores, valid = block_scores(rows_query, key_rows, first, length, score_scale)
-        peak = jnp.max(scores, axis=-1, keepdims=True)
-        expo = jnp.exp(scores - peak)
-        weight_sum = jnp.sum(expo, axis=-1, keepdims=True)
-        probs = (expo / weight_sum).astype(jnp.bfloat16)
-        outputs.append(
-            jnp.dot(probs, value_rows, preferred_element_type=jnp.float32).astype(jnp.bfloat16)
-        )
-        log_parts.append((peak + jnp.log(weight_sum))[:, 0])
-    return (jnp.concatenate(outputs, 0), jnp.concatenate(log_parts, 0))
-
-
-def attend_backward(item, block_rows, score_scale):
-    query, key_rows, value_rows, length, grad_out, log_sums = item
-    key_grad = jnp.zeros(key_rows.shape, jnp.float32)
-    value_grad = jnp.zeros(value_rows.shape, jnp.float32)
-    query_parts = []
-    for first in range(0, query.shape[0], block_rows):
-        rows_query = query[first : first + block_rows]
-        scores, valid = block_scores(rows_query, key_rows, first, length, score_scale)
-        probs = jnp.where(valid, jnp.exp(scores - log_sums[first : first + block_rows, None]), 0.0)
-        grad_rows = grad_out[first : first + block_rows]
-        probs_grad = lax.dot_general(
-            grad_rows, value_rows, (((1,), (1,)), ((), ())), preferred_element_type=jnp.float32
-        )
-        inner = jnp.sum(probs * probs_grad, axis=-1, keepdims=True)
-        score_grad = (probs * (probs_grad - inner)).astype(jnp.bfloat16)
-        query_parts.append(
-            jnp.dot(score_grad, key_rows, preferred_element_type=jnp.float32) * score_scale
-        )
-        key_grad = (
-            key_grad
-            + lax.dot_general(
-                score_grad, rows_query, (((0,), (0,)), ((), ())), preferred_element_type=jnp.float32
-            )
-            * score_scale
-        )
-        value_grad = value_grad + lax.dot_general(
-            probs.astype(jnp.bfloat16),
-            grad_rows,
-            (((0,), (0,)), ((), ())),
-            preferred_element_type=jnp.float32,
-        )
-    return (
-        jnp.concatenate(query_parts, 0).astype(jnp.bfloat16),
-        key_grad.astype(jnp.bfloat16),
-        value_grad.astype(jnp.bfloat16),
-    )
+def _valid(first_q, first_k, rows, cols, length):
+    q_pos = first_q + lax.broadcasted_iota(jnp.int32, (rows, cols), 0)
+    k_pos = first_k + lax.broadcasted_iota(jnp.int32, (rows, cols), 1)
+    return (k_pos <= q_pos) & (k_pos < length)
+
+
+def _key_blocks(i, block_q, block_k, length):
+    causal = (i * block_q + block_q + block_k - 1) // block_k
+    live = (length + block_k - 1) // block_k
+    return jnp.minimum(causal, live)
+
+
+def _attn_fwd_kernel(len_ref, q_ref, k_ref, v_ref, o_ref, lse_ref, s_buf, *, block_q, block_k, scale):
+    i = pl.program_id(0)
+    length = len_ref[0]
+    count = _key_blocks(i, block_q, block_k, length)
+    q = q_ref[...]
+
+    def scores(j, m):
+        first = pl.multiple_of(j * block_k, block_k)
+        k = k_ref[pl.ds(first, block_k), :]
+        s = lax.dot_general(q, k, (((1,), (1,)), ((), ())), preferred_element_type=jnp.float32)
+        s = jnp.where(_valid(i * block_q, first, block_q, block_k, length), s * scale, NEGATIVE)
+        s_buf[:, pl.ds(first, block_k)] = s
+        return jnp.maximum(m, jnp.max(s, axis=1, keepdims=True))
+
+    peak = lax.fori_loop(0, count, scores, jnp.full((block_q, 1), NEGATIVE, jnp.float32))
+
+    def exps(j, total):
+        first = pl.multiple_of(j * block_k, block_k)
+        e = jnp.exp(s_buf[:, pl.ds(first, block_k)] - peak)
+        s_buf[:, pl.ds(first, block_k)] = e
+        return total + jnp.sum(e, axis=1, keepdims=True)
+
+    total = lax.fori_loop(0, count, exps, jnp.zeros((block_q, 1), jnp.float32))
+
+    def mix(j, acc):
+        first = pl.multiple_of(j * block_k, block_k)
+        probs = (s_buf[:, pl.ds(first, block_k)] / total).astype(jnp.bfloat16)
+        return acc + jnp.dot(probs, v_ref[pl.ds(first, block_k), :], preferred_element_type=jnp.float32)
+
+    acc = lax.fori_loop(0, count, mix, jnp.zeros(o_ref.shape, jnp.float32))
+    o_ref[...] = acc.astype(o_ref.dtype)
+    lse_ref[...] = peak + jnp.log(total)
+
+
+def attention_forward(q, k, v, length, *, block_q=256, block_k=256):
+    n, d = q.shape
+    scale = 1.0 / math.sqrt(d)
+    kernel = partial(_attn_fwd_kernel, block_q=block_q, block_k=block_k, scale=scale)
+    pairs = (n // block_q) * (n // block_k + 1) // 2
+    return pl.pallas_call(
+        kernel,
+        out_shape=(jax.ShapeDtypeStruct((n, d), jnp.bfloat16), jax.ShapeDtypeStruct((n, 1), jnp.float32)),
+        grid_spec=pltpu.PrefetchScalarGridSpec(
+            num_scalar_prefetch=1,
+            grid=(n // block_q,),
+            in_specs=[
+                pl.BlockSpec((block_q, d), lambda i, lens: (i, 0)),
+                pl.BlockSpec((n, d), lambda i, lens: (0, 0)),
+                pl.BlockSpec((n, d), lambda i, lens: (0, 0)),
+            ],
+            out_specs=[
+                pl.BlockSpec((block_q, d), lambda i, lens: (i, 0)),
+                pl.BlockSpec((block_q, 1), lambda i, lens: (i, 0)),
+            ],
+            scratch_shapes=[pltpu.VMEM((block_q, n), jnp.float32)],
+        ),
+        compiler_params=pltpu.CompilerParams(dimension_semantics=("arbitrary",)),
+        cost_estimate=pl.CostEstimate(
+            flops=4 * pairs * block_q * block_k * d,
+            transcendentals=pairs * block_q * block_k,
+            bytes_accessed=4 * n * d * 2,
+        ),
+    )(length, q, k, v)
+
+
+def _attn_bwd_kernel(len_ref, q_ref, k_ref, v_ref, do_ref, lse_ref, dq_ref, dk_ref, dv_ref,
+                     p_buf, dp_buf, dk_acc, dv_acc, *, block_q, block_k, scale):
+    i = pl.program_id(0)
+    length = len_ref[0]
+
+    @pl.when(i == 0)
+    def _():
+        dk_acc[...] = jnp.zeros_like(dk_acc)
+        dv_acc[...] = jnp.zeros_like(dv_acc)
+
+    live = i * block_q < length
+
+    @pl.when(live)
+    def _():
+        count = _key_blocks(i, block_q, block_k, length)
+        q = q_ref[...]
+        do = do_ref[...]
+        lse = lse_ref[...]
+
+        def first_pass(j, inner):
+            first = pl.multiple_of(j * block_k, block_k)
+            k = k_ref[pl.ds(first, block_k), :]
+            v = v_ref[pl.ds(first, block_k), :]
+            s = lax.dot_general(q, k, (((1,), (1,)), ((), ())), preferred_element_type=jnp.float32)
+            valid = _valid(i * block_q, first, block_q, block_k, length)
+            s = jnp.where(valid, s * scale, NEGATIVE)
+            p = jnp.where(valid, jnp.exp(s - lse), 0.0)
+            dp = lax.dot_general(do, v, (((1,), (1,)), ((), ())), preferred_element_type=jnp.float32)
+            p_buf[:, pl.ds(first, block_k)] = p
+            dp_buf[:, pl.ds(first, block_k)] = dp
+            return inner + jnp.sum(p * dp, axis=1, keepdims=True)
+
+        inner = lax.fori_loop(0, count, first_pass, jnp.zeros((block_q, 1), jnp.float32))
+
+        def second_pass(j, dq):
+            first = pl.multiple_of(j * block_k, block_k)
+            p = p_buf[:, pl.ds(first, block_k)]
+            dp = dp_buf[:, pl.ds(first, block_k)]
+            ds = (p * (dp - inner)).astype(jnp.bfloat16)
+            k = k_ref[pl.ds(first, block_k), :]
+            dk_acc[pl.ds(first, block_k), :] += lax.dot_general(
+                ds, q, (((0,), (0,)), ((), ())), preferred_element_type=jnp.float32)
+            dv_acc[pl.ds(first, block_k), :] += lax.dot_general(
+                p.astype(jnp.bfloat16), do, (((0,), (0,)), ((), ())), preferred_element_type=jnp.float32)
+            return dq + jnp.dot(ds, k, preferred_element_type=jnp.float32)
+
+        dq = lax.fori_loop(0, count, second_pass, jnp.zeros(dq_ref.shape, jnp.float32))
+        dq_ref[...] = (dq * scale).astype(dq_ref.dtype)
+
+    @pl.when(jnp.logical_not(live))
+    def _():
+        dq_ref[...] = jnp.zeros_like(dq_ref)
+
+    @pl.when(i == pl.num_programs(0) - 1)
+    def _():
+        dk_ref[...] = (dk_acc[...] * scale).astype(dk_ref.dtype)
+        dv_ref[...] = dv_acc[...].astype(dv_ref.dtype)
+
+
+def attention_backward(q, k, v, do, lse, length, *, block_q=256, block_k=256):
+    n, d = q.shape
+    scale = 1.0 / math.sqrt(d)
+    kernel = partial(_attn_bwd_kernel, block_q=block_q, block_k=block_k, scale=scale)
+    pairs = (n // block_q) * (n // block_k + 1) // 2
+    full = pl.BlockSpec((n, d), lambda i, lens: (0, 0))
+    rows = pl.BlockSpec((block_q, d), lambda i, lens: (i, 0))
+    return pl.pallas_call(
+        kernel,
+        out_shape=tuple(jax.ShapeDtypeStruct((n, d), jnp.bfloat16) for _ in range(3)),
+        grid_spec=pltpu.PrefetchScalarGridSpec(
+            num_scalar_prefetch=1,
+            grid=(n // block_q,),
+            in_specs=[rows, full, full, rows, pl.BlockSpec((block_q, 1), lambda i, lens: (i, 0))],
+            out_specs=[rows, full, full],
+            scratch_shapes=[
+                pltpu.VMEM((block_q, n), jnp.float32),
+                pltpu.VMEM((block_q, n), jnp.float32),
+                pltpu.VMEM((n, d), jnp.float32),
+                pltpu.VMEM((n, d), jnp.float32),
+            ],
+        ),
+        compiler_params=pltpu.CompilerParams(dimension_semantics=("arbitrary",)),
+        cost_estimate=pl.CostEstimate(
+            flops=8 * pairs * block_q * block_k * d,
+            transcendentals=pairs * block_q * block_k,
+            bytes_accessed=8 * n * d * 2,
+        ),
+    )(length, q, k, v, do, lse)
 
 
 def shards(
@@ -116,8 +215,6 @@
     head_size = w_qkv.shape[3]
     local_width = local_heads * head_size
     hidden = w_in.shape[1]
-    block_rows = min(512, seq_total)
-    score_scale = 1.0 / math.sqrt(head_size)
     group_count = lax.axis_size("group")
     group_rank = lax.axis_index("group")
     member = group_rank * lax.axis_size("dp") + lax.axis_index("dp")
@@ -142,25 +239,21 @@
     keys = projected[:, :, 1].astype(jnp.bfloat16)
     values = (projected[:, :, 2] + b_qv[1]).astype(jnp.bfloat16)
 
-    def per_item(array):
-        shaped = array.reshape(seq_total, seq_count, local_heads, head_size)
-        return jnp.transpose(shaped, (1, 2, 0, 3)).reshape(
-            seq_count * local_heads, seq_total, head_size
-        )
-
-    def per_row(array):
-        shaped = array.reshape(seq_count, local_heads, seq_total, head_size)
-        return jnp.transpose(shaped, (2, 0, 1, 3)).reshape(seq_total, seq_count, local_width)
-
-    query_items = per_item(query)
-    key_items = per_item(keys)
-    value_items = per_item(values)
-    item_lengths = jnp.repeat(seq_lengths, local_heads)
-    heads_out, log_sums = lax.map(
-        partial(attend_forward, block_rows=block_rows, score_scale=score_scale),
-        (query_items, key_items, value_items, item_lengths),
-    )
-    attended = per_row(heads_out)
+    def item(array, s, h):
+        return array[:, s, h * head_size : (h + 1) * head_size]
+
+    def per_row(items):
+        stacked = jnp.stack(items).reshape(seq_count, local_heads, seq_total, head_size)
+        return jnp.transpose(stacked, (2, 0, 1, 3)).reshape(seq_total, seq_count, local_width)
+
+    pairs = [(s, h) for s in range(seq_count) for h in range(local_heads)]
+    forward_items = [
+        attention_forward(
+            item(query, s, h), item(keys, s, h), item(values, s, h), seq_lengths[s : s + 1]
+        )
+        for s, h in pairs
+    ]
+    attended = per_row([o for o, _ in forward_items])
     out_weight = w_o.reshape(local_width, model_width)
     positions = tensor_rank * row_count + jnp.arange(row_count, dtype=jnp.int32)
     live = positions[:, None] < seq_lengths[None, :]
@@ -232,13 +325,20 @@
     output = (middle + feed).astype(jnp.bfloat16)
     weight_grad = jnp.einsum("rse,rsd->ed", attended, piece, preferred_element_type=jnp.float32)
     part = jnp.einsum("rsd,ed->rse", piece, out_weight, preferred_element_type=jnp.float32)
-    head_items = per_item(part.astype(jnp.bfloat16))
-    grads_query, grads_keys, grads_values = lax.map(
-        partial(attend_backward, block_rows=block_rows, score_scale=score_scale),
-        (query_items, key_items, value_items, item_lengths, head_items, log_sums),
-    )
+    attended_grad = part.astype(jnp.bfloat16)
+    backward_items = [
+        attention_backward(
+            item(query, s, h),
+            item(keys, s, h),
+            item(values, s, h),
+            item(attended_grad, s, h),
+            lse,
+            seq_lengths[s : s + 1],
+        )
+        for (s, h), (_, lse) in zip(pairs, forward_items)
+    ]
     joint_grad = jnp.stack(
-        (per_row(grads_query), per_row(grads_keys), per_row(grads_values)), axis=2
+        [per_row([grads[kind] for grads in backward_items]) for kind in range(3)], axis=2
     )
     grad_b_qv = jnp.sum(joint_grad[:, :, 0::2], axis=(0, 1), dtype=jnp.float32)
     joint_rows = joint_grad.reshape(seq_total, seq_count, 3 * local_width)

time: 789 us -> 757 us (0.959)
  matrix products: 155 us -> 94.7 us
  Pallas kernels: 16.6 us -> 46.4 us
  other arithmetic: 77.7 us -> 56.9 us
  waiting for transfers between devices: 456 us -> 474 us
  starting transfers between devices: 26.2 us -> 34.7 us
    dot_general x20 -> x0, matrix products: 56 us -> none  [the longest x4 21.5 us: attend_backward(): lax.dot_general(grad_rows, value_rows, (((1,), (1,)), ((), ())), preferre...]
    pallas_call x0 -> x2, Pallas kernels: none -> 46.4 us  [the longest x1 23.7 us: attention_forward(): pl.pallas_call(kernel, out_shape=(jax.ShapeDtypeStruct((n, d), jnp.bfloat...]
    unnamed x4 -> x0, Pallas kernels: 16.6 us -> none
    convert_element_type x7 -> x0, other arithmetic: 15.4 us -> none  [the longest x2 11.5 us: attend_backward(): score_grad = (probs * (probs_grad - inner)).astype(jnp.bfloat16)]
    all_gather x1, waiting for transfers between devices: 45.5 us -> 59.7 us  [shards(): piece = lax.all_gather(branch_low, 'tensor', axis=0, tiled=True)]
    all_gather x1, waiting for transfers between devices: 19.1 us -> 32.8 us  [shards(): upstream_full = lax.all_gather(upstream, 'tensor', axis=0, tiled=True)]
    ppermute x19, waiting for transfers between devices: 84 us -> 73.6 us  [halving_steps(): got = lax.ppermute(send, axis, [(i, i ^ bit) for i in range(size)])]
  transfers between devices with their start and end apart: 27 -> 27, of which waited for: 17 -> 18; matrix products, arithmetic and copies ran while one was open for 18% -> 14% of each run, Pallas kernels for 2% -> 3%
where the time goes in v3:
time: 757 us; the launch traced here: 748 us
  waiting for transfers between devices  474 us (63%)
  matrix products  94.7 us (13%)
  other arithmetic  56.9 us (8%)
  Pallas kernels  46.4 us (6%)
  starting transfers between devices  34.7 us (5%)
  local copies, waits for them, and re-layouts  24.7 us (3%)
  between operations  16.7 us (2%)
    reduce_scatter x1, waiting for transfers between devices, shards(): lax.psum_scatter(attention_part, 'tensor', scatter_dimension=0, tiled=True)  88.1 us
    reduce_scatter x1, waiting for transfers between devices, shards(): lax.psum_scatter(jnp.einsum('rsf,df->rsd', piece, w_in, preferred_element...  84.4 us
    ppermute x19, waiting for transfers between devices, halving_steps(): got = lax.ppermute(send, axis, [(i, i ^ bit) for i in range(size)])  73.6 us
    all_gather x1, waiting for transfers between devices, shards(): second_full = lax.all_gather(second_low, 'tensor', axis=0, tiled=True)  69.9 us
    all_gather x1, waiting for transfers between devices, shards(): normed_full = lax.all_gather(normed_low, 'tensor', axis=0, tiled=True)  65.3 us
    all_gather x1, waiting for transfers between devices, shards(): piece = lax.all_gather(branch_low, 'tensor', axis=0, tiled=True)  59.7 us
    ppermute x19, starting transfers between devices, halving_steps(): got = lax.ppermute(send, axis, [(i, i ^ bit) for i in range(size)])  33.6 us
    all_gather x1, waiting for transfers between devices, shards(): upstream_full = lax.all_gather(upstream, 'tensor', axis=0, tiled=True)  32.8 us
  transfers between devices with their start and end apart: 27, of which 18 were waited for; matrix products, arithmetic and copies ran while one was open for 14% of the time, Pallas kernels for 3%

profile of v3, /device:TPU:96, one launch (start us, length us, event | category | flops | bytes accessed | tf_op | source)
XLA Modules:
  0.0 748.1 jit_solution(4797995963102717022)
XLA Ops:
  19.0 65.3 %all-gather.5.cloned.1.call-done = bf16[2048,1,2048]{2,0,1:T(8,128)(2,1)} async-done(((bf16[128,1,2048]{2,0,1:T(8,128)(2,1)}), bf16[2048,1,2048]{2,0,1:T(8,128)(2,1)}) %all-gather.5.cloned.1.call-update) | async-done | bytes 8388624 | tf_op jit(solution)/shard_map/all_gather | solution.py:230
  84.3 7.4 fusion.29
  93.7 23.7 %shard_map.254 = (bf16[2048,128]{1,0:T(8,128)(2,1)}, f32[2048,1]{1,0:T(8,128)}) custom-call(s32[1]{0:T(128)} %dynamic_slice.7.len_ref, bf16[2048,128]{1,0:T(8,128)(2,1)} %get-tuple-element.50.q_ref, bf16[2048,128]{1,0:T(8,128)(2,1)} %fusion.70.k_ref, bf16[2048,128]{1,0:T(8,128)(2,1)} %get-tuple-element.49.v_ref), custom_call_target="tpu_custom_call" | custom-call | flops 1207959552 | bytes 2097152 | tf_op jit(solution)/shard_map/pallas_call | solution.py:77
  117.4 6.6 convert_bitcast_fusion.3
  124.0 32.8 %all-gather.7.cloned.1.call-done = bf16[2048,1,2048]{2,0,1:T(8,128)(2,1)} async-done(((bf16[128,1,2048]{2,0,1:T(8,128)(2,1)}), bf16[2048,1,2048]{2,0,1:T(8,128)(2,1)}) %all-gather.7.cloned.1.call-update) | async-done | bytes 8388624 | tf_op jit(solution)/shard_map/all_gather | solution.py:261
  156.9 88.1 %reduce-scatter.5.cloned.1.call-done = bf16[128,1,2048]{2,0,1:T(8,128)(2,1)} async-done(((bf16[2048,1,2048]{2,0,1:T(8,128)(2,1)}), bf16[128,1,2048]{2,0,1:T(8,128)(2,1)}) %reduce-scatter.5.cloned.1.call-update) | async-done | bytes 524304 | tf_op jit(solution)/shard_map/reduce_scatter | solution.py:267
  250.3 69.9 %all-gather.9.cloned.1.call-done = bf16[2048,1,2048]{2,0,1:T(8,128)(2,1)} async-done(((bf16[128,1,2048]{2,0,1:T(8,128)(2,1)}), bf16[2048,1,2048]{2,0,1:T(8,128)(2,1)}) %all-gather.9.cloned.1.call-update) | async-done | bytes 8388624 | tf_op jit(solution)/shard_map/all_gather | solution.py:274
  320.2 7.6 %fusion.10 = f32[2048,512]{1,0:T(8,128)S(1)} fusion(bf16[2048,512]{1,0:T(8,128)(2,1)} %param.26, bf16[2048,1,2048]{2,0,1:T(8,128)(2,1)} %all-gather.9.cloned.1.call-done), kind=kOutput, calls=%fused_computation.10 | convolution fusion | flops 4294967296 | bytes 14680064 | tf_op jit(solution)/shard_map/dot_general | solution.py:276
  327.8 12.5 %convert_reduce_fusion = (f32[512]{0:T(512)S(1)}, bf16[2048,512]{1,0:T(8,128)(2,1)S(1)}) fusion(f32[2048,512]{1,0:T(8,128)S(1)} %fusion.10, f32[512]{0:T(512)S(1)} %copy-done.32, bf16[512,2048]{1,0:T(8,128)(2,1)S(1)} %copy-done, bf16[2048,1,2048]{2,0,1:T(8,128)(2,1)} %all-gather.7.cloned.1.call-done), kind=kOutput, calls=%fused_computation.29 | convolution fusion | flops 4319084032 | bytes 16781312 | tf_op jit(solution)/shard_map/rsd,fd->rsf/dot_general | solution.py:289
  341.6 6.9 convert_bitcast_fusion.1
  348.6 84.4 %reduce-scatter.7.cloned.1.call-done = bf16[128,1,2048]{2,0,1:T(8,128)(2,1)} async-done(((bf16[2048,1,2048]{2,0,1:T(8,128)(2,1)}), bf16[128,1,2048]{2,0,1:T(8,128)(2,1)}) %reduce-scatter.7.cloned.1.call-update) | async-done | bytes 524304 | tf_op jit(solution)/shard_map/reduce_scatter | solution.py:303
  439.3 10.1 %convert_bitcast_fusion.2 = bf16[2048,1,2048]{2,0,1:T(8,128)(2,1)} fusion(bf16[512,2048]{1,0:T(8,128)(2,1)S(1)} %copy-done, f32[2048,512]{1,0:T(8,128)} %copy-done.33, f32[512]{0:T(512)S(1)} %copy-done.32), kind=kOutput, calls=%fused_computation.18 | convolution fusion | flops 4309647360 | bytes 14682112 | tf_op jit(solution)/shard_map/rsf,fd->rsd/dot_general | solution.py:284
  449.3 59.7 %all-gather.11.cloned.1.call-done = bf16[2048,1,2048]{2,0,1:T(8,128)(2,1)} async-done(((bf16[128,1,2048]{2,0,1:T(8,128)(2,1)}), bf16[2048,1,2048]{2,0,1:T(8,128)(2,1)}) %all-gather.11.cloned.1.call-update) | async-done | bytes 8388624 | tf_op jit(solution)/shard_map/all_gather | solution.py:317
  509.0 6.6 fusion.40.do_ref
  515.6 22.7 %shard_map.255 = (bf16[2048,128]{1,0:T(8,128)(2,1)}, bf16[2048,128]{1,0:T(8,128)(2,1)}, bf16[2048,128]{1,0:T(8,128)(2,1)}) custom-call(s32[1]{0:T(128)} %dynamic_slice.7.len_ref, bf16[2048,128]{1,0:T(8,128)(2,1)} %get-tuple-element.50.q_ref, bf16[2048,128]{1,0:T(8,128)(2,1)} %fusion.70.k_ref, bf16[2048,128]{1,0:T(8,128)(2,1)} %get-tuple-element.49.v_ref, ...), custom_call_target="tpu_custom_call" | custom-call | flops 2415919104 | bytes 4194304 | tf_op jit(solution)/shard_map/pallas_call | solution.py:169
  541.5 9.7 %convert_bitcast_fusion = bf16[2048,1,2048]{2,0,1:T(8,128)(2,1)} fusion(bf16[2048,384]{0,1:T(8,128)(2,1)} %bitcast.152, bf16[2048,384]{0,1:T(8,128)(2,1)} %bitcast.153), kind=kOutput, calls=%fused_computation.16 | convolution fusion | flops 3225419776 | bytes 11534336 | tf_op jit(solution)/shard_map/rsc,dc->rsd/dot_general | solution.py:353
  554.5 8.5 %fusion.23 = f32[512,2048]{1,0:T(8,128)S(1)} fusion(bf16[2048,1,2048]{2,0,1:T(8,128)(2,1)} %all-gather.7.cloned.1.call-done, f32[]{:T(128)S(6)} %div.111, f32[2048,512]{1,0:T(8,128)} %copy-done.33, f32[512]{0:T(512)S(1)} %copy-done.32), kind=kOutput, calls=%fused_computation.31 | convolution fusion | flops 4306501632 | bytes 16779268 | tf_op jit(solution)/shard_map/rsf,rsd->fd/dot_general | solution.py:288
  568.6 7.1 fusion.26
  585.9 14.2 %collective-permute-done.13 = bf16[4,256,512]{2,1,0:T(8,128)(2,1)} collective-permute-done((bf16[4,256,512]{2,1,0:T(8,128)(2,1)}, bf16[4,256,512]{2,1,0:T(8,128)(2,1)}, u32[]{:S(2)}, u32[]{:S(2)}) %collective-permute-start.13) | collective-permute-done | bytes 1048608 | tf_op jit(solution)/shard_map/ppermute | solution.py:436
  601.8 6.9 collective-permute-start.14
  608.7 13.8 %collective-permute-done.16 = bf16[512,4,256]{2,0,1:T(8,128)(2,1)} collective-permute-done((bf16[512,4,256]{2,0,1:T(8,128)(2,1)}, bf16[512,4,256]{2,0,1:T(8,128)(2,1)}, u32[]{:S(2)}, u32[]{:S(2)}) %collective-permute-start.16) | collective-permute-done | bytes 1048608 | tf_op jit(solution)/shard_map/ppermute | solution.py:436
  635.0 5.0 collective-permute-done.15
  654.1 7.0 fusion.32
  679.6 25.0 %collective-permute-done.7 = bf16[4,256,3,1,128]{4,3,2,1,0:T(2,128)(2,1)} collective-permute-done((bf16[4,256,3,1,128]{4,3,2,1,0:T(2,128)(2,1)S(1)}, bf16[4,256,3,1,128]{4,3,2,1,0:T(2,128)(2,1)}, u32[]{:S(2)}, u32[]{:S(2)}) %collective-permute-start.7) | collective-permute-done | bytes 786464 | tf_op jit(solution)/shard_map/ppermute | solution.py:436
  (227 shorter events, 130.0 us)
Async XLA Ops:
  7.2 77.1 %all-gather.5.cloned.1.call-start = ((), (), s32[]{:S(2)}) async-start(), calls=%async_computation.4 | async-start | bytes 8912896 | tf_op jit(solution)/shard_map/all_gather | solution.py:230
  12.2 144.6 %all-gather.7.cloned.1.call-start = ((), (), s32[]{:S(2)}) async-start(), calls=%async_computation.5 | async-start | bytes 8912896 | tf_op jit(solution)/shard_map/all_gather | solution.py:261
  16.2 228.8 %reduce-scatter.5.cloned.1.call-start = ((), (), s32[]{:S(2)}) async-start(), calls=%async_computation.6 | async-start | bytes 8912896 | tf_op jit(solution)/shard_map/reduce_scatter | solution.py:267
  156.9 163.3 %all-gather.9.cloned.1.call-start = ((), (), s32[]{:S(2)}) async-start(), calls=%async_computation.7 | async-start | bytes 8912896 | tf_op jit(solution)/shard_map/all_gather | solution.py:274
  250.0 183.0 %reduce-scatter.7.cloned.1.call-start = ((), (), s32[]{:S(2)}) async-start(), calls=%async_computation.8 | async-start | bytes 8912896 | tf_op jit(solution)/shard_map/reduce_scatter | solution.py:303
  348.5 160.5 %all-gather.11.cloned.1.call-start = ((), (), s32[]{:S(2)}) async-start(), calls=%async_computation.9 | async-start | bytes 8912896 | tf_op jit(solution)/shard_map/all_gather | solution.py:317
  438.8 232.8 %reduce-scatter.11.cloned.1.call-start = ((), (), s32[]{:S(2)}) async-start(), calls=%async_computation.11 | async-start | bytes 8912896 | tf_op jit(solution)/shard_map/reduce_scatter | solution.py:352
  551.2 184.5 %reduce-scatter.9.cloned.1.call-start = ((), (), s32[]{:S(2)}) async-start(), calls=%async_computation.10 | async-start | bytes 8912896 | tf_op jit(solution)/shard_map/reduce_scatter | solution.py:320
  577.1 23.0 %collective-permute-start.13 = (bf16[4,256,512]{2,1,0:T(8,128)(2,1)}, bf16[4,256,512]{2,1,0:T(8,128)(2,1)}, u32[]{:S(2)}, u32[]{:S(2)}) collective-permute-start(bf16[4,256,512]{2,1,0:T(8,128)(2,1)} %bitcast.49), channel_id=1, source_target_pairs={{0,64},{32,96},{64,0},{96,32},{1,65},{33,97},{65,1},{97,33},{2,66}... | collective-permute-start | bytes 3145736 | tf_op jit(solution)/shard_map/ppermute | solution.py:436
  581.6 41.0 %collective-permute-start.16 = (bf16[512,4,256]{2,0,1:T(8,128)(2,1)}, bf16[512,4,256]{2,0,1:T(8,128)(2,1)}, u32[]{:S(2)}, u32[]{:S(2)}) collective-permute-start(bf16[512,4,256]{2,0,1:T(8,128)(2,1)} %select_convert_fusion), channel_id=1, source_target_pairs={{0,64},{32,96},{64,0},{96,32},{1,65},{33,97},{65,1},{97,33},{2,66}... | collective-permute-start | bytes 3145736 | tf_op jit(solution)/shard_map/ppermute | solution.py:436
  601.8 26.1 %collective-permute-start.14 = (bf16[2,256,512]{2,1,0:T(8,128)(2,1)S(1)}, bf16[2,256,512]{2,1,0:T(8,128)(2,1)S(1)}, u32[]{:S(2)}, u32[]{:S(2)}) collective-permute-start(bf16[2,256,512]{2,1,0:T(8,128)(2,1)S(1)} %select_convert_fusion.4), channel_id=1, source_target_pairs={{0,32},{32,0},{64,96},{96,64},{1,33},{33,1},{65,97},{97,65},{2,34}... | collective-permute-start | bytes 1572872 | tf_op jit(solution)/shard_map/ppermute | solution.py:436
  624.6 4.8 collective-permute-start.17
  628.9 11.1 %collective-permute-start.15 = (bf16[1,256,512]{2,1,0:T(8,128)(2,1)}, bf16[1,256,512]{2,1,0:T(8,128)(2,1)S(1)}, u32[]{:S(2)}, u32[]{:S(2)}) collective-permute-start(bf16[1,256,512]{2,1,0:T(8,128)(2,1)} %select_convert_fusion.6), channel_id=1, source_target_pairs={{0,16},{16,0},{1,17},{17,1},{2,18},{18,2},{3,19},{19,3},{4,20},{20... | collective-permute-start | bytes 786440 | tf_op jit(solution)/shard_map/ppermute | solution.py:436
  630.4 14.4 %collective-permute-start.18 = (bf16[512,1,256]{2,0,1:T(8,128)(2,1)}, bf16[512,1,256]{2,0,1:T(8,128)(2,1)}, u32[]{:S(2)}, u32[]{:S(2)}) collective-permute-start(bf16[512,1,256]{2,0,1:T(8,128)(2,1)} %select_convert_fusion.5), channel_id=1, source_target_pairs={{0,16},{16,0},{1,17},{17,1},{2,18},{18,2},{3,19},{19,3},{4,20},{20... | collective-permute-start | bytes 786440 | tf_op jit(solution)/shard_map/ppermute | solution.py:436
  653.2 10.2 %collective-permute-start.10 = (bf16[1,128,4,256]{3,1,2,0:T(8,128)(2,1)S(1)}, bf16[1,128,4,256]{3,1,2,0:T(8,128)(2,1)S(1)}, u32[]{:S(2)}, u32[]{:S(2)}) collective-permute-start(bf16[1,128,4,256]{3,1,2,0:T(8,128)(2,1)S(1)} %select_convert_fusion.7), channel_id=1, source_target_pairs={{0,64},{32,96},{64,0},{96,32},{1,65},{33,97},{65,1},{97,33},{2,66}... | collective-permute-start | bytes 786440 | tf_op jit(solution)/shard_map/ppermute | solution.py:436
  665.1 5.8 collective-permute-start.12
  668.2 36.4 %collective-permute-start.7 = (bf16[4,256,3,1,128]{4,3,2,1,0:T(2,128)(2,1)S(1)}, bf16[4,256,3,1,128]{4,3,2,1,0:T(2,128)(2,1)}, u32[]{:S(2)}, u32[]{:S(2)}) collective-permute-start(bf16[4,256,3,1,128]{4,3,2,1,0:T(2,128)(2,1)S(1)} %copy.39), channel_id=1, source_target_pairs={{0,64},{32,96},{64,0},{96,32},{1,65},{33,97},{65,1},{97,33},{2,66}... | collective-permute-start | bytes 2359304 | tf_op jit(solution)/shard_map/ppermute | solution.py:436
  676.3 32.6 %collective-permute-start = (f32[8,8,192]{2,0,1:T(8,128)S(1)}, f32[8,8,192]{2,0,1:T(8,128)S(1)}, u32[]{:S(2)}, u32[]{:S(2)}) collective-permute-start(f32[8,8,192]{2,0,1:T(8,128)S(1)} %slice_select_fusion.2), channel_id=1, source_target_pairs={{0,8},{1,9},{2,10},{3,11},{4,12},{5,13},{6,14},{7,15},{8,0},{9,1},... | collective-permute-start | bytes 147464 | tf_op jit(solution)/shard_map/ppermute | solution.py:436
  711.4 4.8 collective-permute-start.8
  713.1 5.4 collective-permute-start.2
  718.5 5.0 collective-permute-start.3
  720.5 9.4 %collective-permute-start.9 = (bf16[1,256,3,1,128]{4,3,2,1,0:T(2,128)(2,1)S(1)}, bf16[1,256,3,1,128]{4,3,2,1,0:T(2,128)(2,1)S(1)}, u32[]{:S(2)}, u32[]{:S(2)}) collective-permute-start(bf16[1,256,3,1,128]{4,3,2,1,0:T(2,128)(2,1)S(1)} %fusion.75), channel_id=1, source_target_pairs={{0,16},{16,0},{1,17},{17,1},{2,18},{18,2},{3,19},{19,3},{4,20},{20... | collective-permute-start | bytes 589832 | tf_op jit(solution)/shard_map/ppermute | solution.py:436
  723.6 7.7 %collective-permute-start.4 = (f32[1,4,192]{2,0,1:T(1,128)S(1)}, f32[1,4,192]{2,0,1:T(1,128)S(1)}, u32[]{:S(2)}, u32[]{:S(2)}) collective-permute-start(f32[1,4,192]{2,0,1:T(1,128)S(1)} %broadcast_select_fusion.8), channel_id=1, source_target_pairs={{0,64},{32,96},{64,0},{96,32},{1,65},{33,97},{65,1},{97,33},{2,66}... | collective-permute-start | bytes 9224 | tf_op jit(solution)/shard_map/ppermute | solution.py:436
  732.6 6.5 collective-permute-start.6
  (39 other events, 1578.0 us)
Sparse Core Ops, SparseCore 0:
  12.4 71.8 all-gather.4
  86.4 70.3 all-gather.6
  160.3 84.6 reduce-scatter.4
  250.1 70.0 all-gather.8
  348.6 84.3 reduce-scatter.6
  439.0 70.0 all-gather.10
  551.3 89.3 reduce-scatter.10
  644.1 85.8 reduce-scatter.8

commit v4 on v3

--- a/solution.py
+++ b/solution.py
@@ -188,6 +188,75 @@
             bytes_accessed=8 * n * d * 2,
         ),
     )(length, q, k, v, do, lse)
+
+
+GRID = 4
+
+
+def grid_pairs(axis_of, delta):
+    out = []
+    for s in range(GRID * GRID):
+        x, y = divmod(s, GRID)
+        if axis_of == "x":
+            out.append((s, ((x + delta) % GRID) * GRID + y))
+        else:
+            out.append((s, x * GRID + (y + delta) % GRID))
+    return out
+
+
+def grid_position(axis_of):
+    t = lax.axis_index("tensor")
+    return t // GRID if axis_of == "x" else t % GRID
+
+
+def gather_line(block, axis_of):
+    pos = grid_position(axis_of)
+    from_left = lax.ppermute(block, "tensor", grid_pairs(axis_of, 1))
+    from_right = lax.ppermute(block, "tensor", grid_pairs(axis_of, -1))
+    half = block.shape[0] // 2
+    far_low = lax.ppermute(from_left[:half], "tensor", grid_pairs(axis_of, 1))
+    far_high = lax.ppermute(from_right[half:], "tensor", grid_pairs(axis_of, -1))
+    far = jnp.concatenate([far_low, far_high], 0)
+    ring = jnp.stack([block, from_right, far, from_left, block, from_right, far, from_left])
+    return lax.dynamic_slice_in_dim(ring, (GRID - pos) % GRID, GRID, 0)
+
+
+def gather_tensor(block):
+    rows, cols = block.shape
+    mid = cols // 2
+    first = gather_line(block[:, :mid], "y").reshape(GRID * rows, mid)
+    first = gather_line(first, "x").reshape(GRID * GRID * rows, mid)
+    second = gather_line(block[:, mid:], "x").reshape(GRID * rows, cols - mid)
+    second = gather_line(second, "y").reshape(GRID, GRID, rows, cols - mid)
+    second = jnp.transpose(second, (1, 0, 2, 3)).reshape(GRID * GRID * rows, cols - mid)
+    return jnp.concatenate([first, second], 1)
+
+
+def scatter_line(blocks, axis_of, wire):
+    pos = grid_position(axis_of)
+    ring = jnp.concatenate([blocks, blocks], 0)
+    rel = lax.dynamic_slice_in_dim(ring, pos, GRID, 0)
+    half = blocks.shape[1] // 2
+    got_left = lax.ppermute(rel[2, :half].astype(wire), "tensor", grid_pairs(axis_of, 1))
+    got_right = lax.ppermute(rel[2, half:].astype(wire), "tensor", grid_pairs(axis_of, -1))
+    to_right = rel[1].at[:half].add(got_left.astype(rel.dtype))
+    to_left = rel[3].at[half:].add(got_right.astype(rel.dtype))
+    got_left = lax.ppermute(to_right.astype(wire), "tensor", grid_pairs(axis_of, 1))
+    got_right = lax.ppermute(to_left.astype(wire), "tensor", grid_pairs(axis_of, -1))
+    return rel[0] + got_left.astype(rel.dtype) + got_right.astype(rel.dtype)
+
+
+def scatter_tensor(partial, wire=jnp.bfloat16):
+    total, cols = partial.shape
+    rows = total // (GRID * GRID)
+    mid = cols // 2
+    grid = partial.reshape(GRID, GRID, rows, cols)
+    first = scatter_line(grid[..., :mid].reshape(GRID, GRID * rows, mid), "x", wire)
+    first = scatter_line(first.reshape(GRID, rows, mid), "y", wire)
+    second = jnp.transpose(grid[..., mid:], (1, 0, 2, 3)).reshape(GRID, GRID * rows, cols - mid)
+    second = scatter_line(second, "y", wire)
+    second = scatter_line(second.reshape(GRID, rows, cols - mid), "x", wire)
+    return jnp.concatenate([first, second], 1)
 
 
 def shards(
@@ -227,7 +296,9 @@
     )
     inputs = tokens.astype(jnp.float32)
     normed_low = layer_norm(inputs, ln1_gain, ln1_bias).astype(jnp.bfloat16)
-    normed_full = lax.all_gather(normed_low, "tensor", axis=0, tiled=True)
+    normed_full = gather_tensor(normed_low.reshape(row_count, seq_count * model_width)).reshape(
+        seq_total, seq_count, model_width
+    )
     joint_weight = w_qkv.reshape(model_width, 3 * local_width)
     projected = jnp.dot(
         normed_full.reshape(seq_total * seq_count, model_width),
@@ -258,20 +329,22 @@
     positions = tensor_rank * row_count + jnp.arange(row_count, dtype=jnp.int32)
     live = positions[:, None] < seq_lengths[None, :]
     upstream = jnp.where(live[:, :, None], cotangent, jnp.zeros_like(cotangent))
+    upstream, normed_full = lax.optimization_barrier((upstream, normed_full))
     upstream_full = lax.all_gather(upstream, "tensor", axis=0, tiled=True)
     attention_part = jnp.einsum(
         "rse,ed->rsd", attended, out_weight, preferred_element_type=jnp.float32
-    ).astype(jnp.bfloat16)
-    attention_part, upstream_full = lax.optimization_barrier((attention_part, upstream_full))
+    )
     attention = (
-        lax.psum_scatter(attention_part, "tensor", scatter_dimension=0, tiled=True).astype(
-            jnp.float32
+        scatter_tensor(attention_part.reshape(seq_total, seq_count * model_width)).reshape(
+            row_count, seq_count, model_width
         )
         + b_o
     )
     middle = inputs + attention
     second_low = layer_norm(middle, ln2_gain, ln2_bias).astype(jnp.bfloat16)
-    second_full = lax.all_gather(second_low, "tensor", axis=0, tiled=True)
+    second_full = gather_tensor(second_low.reshape(row_count, seq_count * model_width)).reshape(
+        seq_total, seq_count, model_width
+    )
     pre_act = (
         jnp.dot(
             second_full.reshape(seq_total * seq_count, model_width),
@@ -300,21 +373,20 @@
     )
     pre_rows = pre_low.reshape(seq_total, seq_count, hidden)
     piece = pre_rows
-    second_grad = lax.psum_scatter(
-        jnp.einsum("rsf,df->rsd", piece, w_in, preferred_element_type=jnp.float32).astype(
-            jnp.bfloat16
-        ),
-        "tensor",
-        scatter_dimension=0,
-        tiled=True,
-    ).astype(jnp.float32)
+    second_grad = scatter_tensor(
+        jnp.einsum("rsf,df->rsd", piece, w_in, preferred_element_type=jnp.float32).reshape(
+            seq_total, seq_count * model_width
+        )
+    ).reshape(row_count, seq_count, model_width)
     norm_two_back = jax.vjp(layer_norm, middle, ln2_gain, ln2_bias)[1]
     middle_part, grad_ln2_gain, grad_ln2_bias = norm_two_back(second_grad)
     middle_grad = upstream.astype(jnp.float32) + middle_part
     branch_low = middle_grad.astype(jnp.bfloat16)
     grad_b_o = jnp.sum(branch_low, axis=(0, 1), dtype=jnp.float32)
     grad_b_out = jnp.sum(upstream, axis=(0, 1), dtype=jnp.float32)
-    piece = lax.all_gather(branch_low, "tensor", axis=0, tiled=True)
+    piece = gather_tensor(branch_low.reshape(row_count, seq_count * model_width)).reshape(
+        seq_total, seq_count, model_width
+    )
     feed_part, piece = lax.optimization_barrier((feed_part, piece))
     feed = (
         lax.psum_scatter(feed_part, "tensor", scatter_dimension=0, tiled=True).astype(
@@ -349,14 +421,11 @@
         preferred_element_type=jnp.float32,
     )
     piece = joint_rows
-    normed_grad = lax.psum_scatter(
-        jnp.einsum("rsc,dc->rsd", piece, joint_weight, preferred_element_type=jnp.float32).astype(
-            jnp.bfloat16
-        ),
-        "tensor",
-        scatter_dimension=0,
-        tiled=True,
-    ).astype(jnp.float32)
+    normed_grad = scatter_tensor(
+        jnp.einsum("rsc,dc->rsd", piece, joint_weight, preferred_element_type=jnp.float32).reshape(
+            seq_total, seq_count * model_width
+        )
+    ).reshape(row_count, seq_count, model_width)
     norm_one_back = jax.vjp(layer_norm, inputs, ln1_gain, ln1_bias)[1]
     input_part, grad_ln1_gain, grad_ln1_bias = norm_one_back(normed_grad)
     input_grad = (middle_grad + input_part).astype(jnp.bfloat16)

time: 757 us -> 787 us (1.040)
  waiting for transfers between devices: 474 us -> 172 us
  local copies, waits for them, and re-layouts: 24.7 us -> 170 us
  starting transfers between devices: 34.7 us -> 175 us
  other arithmetic: 56.9 us -> 117 us
  matrix products: 94.7 us -> 77.8 us
    all_gather x3 -> x0, waiting for transfers between devices: 195 us -> none  [the longest x1 69.9 us: shards(): second_full = lax.all_gather(second_low, 'tensor', axis=0, tiled=True)]
    reduce_scatter x3 -> x0, waiting for transfers between devices: 173 us -> none  [the longest x1 88.1 us: shards(): lax.psum_scatter(attention_part, 'tensor', scatter_dimension=0, tiled=True)]
    ppermute x0 -> x96, waiting for transfers between devices: none -> 156 us  [the longest x12 70.5 us: scatter_line(): lax.ppermute(to_right.astype(wire), 'tensor', grid_pairs(axis_of, 1))]
    ppermute x0 -> x96, starting transfers between devices: none -> 150 us  [the longest x12 35.2 us: scatter_line(): lax.ppermute(rel[2, half:].astype(wire), 'tensor', grid_pairs(axis_of, -1))]
    ppermute x19, waiting for transfers between devices: 73.6 us -> 15.5 us  [halving_steps(): got = lax.ppermute(send, axis, [(i, i ^ bit) for i in range(size)])]
    unnamed x75 -> x168, local copies, waits for them, and re-layouts: 14 us -> 55.3 us
    another operation x0 -> x12, other arithmetic: none -> 35.8 us
    slice x0 -> x30, local copies, waits for them, and re-layouts: none -> 35.1 us  [the longest x3 20.2 us: scatter_tensor(): grid[..., :mid].reshape(GRID, GRID * rows, mid)]
  transfers between devices with their start and end apart: 27 -> 117, of which waited for: 18 -> 41; matrix products, arithmetic and copies ran while one was open for 14% -> 32% of each run, Pallas kernels for 3% -> 0%
where the time goes in v4:
time: 787 us; the launch traced here: 776 us
  starting transfers between devices  175 us (22%)
  waiting for transfers between devices  172 us (22%)
  local copies, waits for them, and re-layouts  170 us (22%)
  other arithmetic  117 us (15%)
  matrix products  77.8 us (10%)
  Pallas kernels  46.5 us (6%)
  between operations  18.1 us (2%)
    ppermute x12, waiting for transfers between devices, scatter_line(): lax.ppermute(to_right.astype(wire), 'tensor', grid_pairs(axis_of, 1))  70.5 us
    unnamed x168, local copies, waits for them, and re-layouts  55.3 us
    ppermute x12, waiting for transfers between devices, gather_line(): from_left = lax.ppermute(block, 'tensor', grid_pairs(axis_of, 1))  47.8 us
    another operation x12, other arithmetic  35.8 us
    ppermute x12, starting transfers between devices, scatter_line(): lax.ppermute(rel[2, half:].astype(wire), 'tensor', grid_pairs(axis_of, -1))  35.2 us
    ppermute x12, starting transfers between devices, gather_line(): lax.ppermute(from_right[half:], 'tensor', grid_pairs(axis_of, -1))  33.3 us
    ppermute x12, starting transfers between devices, scatter_line(): lax.ppermute(to_left.astype(wire), 'tensor', grid_pairs(axis_of, -1))  31.4 us
    ppermute x19, starting transfers between devices, halving_steps(): got = lax.ppermute(send, axis, [(i, i ^ bit) for i in range(size)])  24.4 us
  transfers between devices with their start and end apart: 117, of which 41 were waited for; matrix products, arithmetic and copies ran while one was open for 32% of the time, Pallas kernels for 0%

profile of v4, /device:TPU:96, one launch (start us, length us, event | category | flops | bytes accessed | tf_op | source)
XLA Modules:
  0.0 775.6 jit_solution(3423237511387313463)
XLA Ops:
  43.4 15.6 %collective-permute-done.5 = bf16[512,1024]{1,0:T(8,128)(2,1)} collective-permute-done((bf16[512,1024]{1,0:T(8,128)(2,1)}, bf16[512,1024]{1,0:T(8,128)(2,1)}, u32[]{:S(2)}, u32[]{:S(2)}) %collective-permute-start.5) | collective-permute-done | bytes 1048608 | tf_op jit(solution)/shard_map/ppermute | solution.py:214
  88.0 8.3 %fusion.20 = bf16[2048,1,2048]{2,0,1:T(8,128)(2,1)} fusion(bf16[2048,1024]{1,0:T(8,128)(2,1)} %bitcast.741, bf16[2048,1024]{1,0:T(8,128)(2,1)} %bitcast.739), kind=kLoop, calls=%fused_computation.41 | loop fusion | flops 16777216 | bytes 16777216 | tf_op jit(solution)/shard_map/reshape | solution.py:299
  96.3 7.4 fusion.32
  105.7 23.7 %shard_map.254 = (bf16[2048,128]{1,0:T(8,128)(2,1)}, f32[2048,1]{1,0:T(8,128)}) custom-call(s32[1]{0:T(128)} %dynamic_slice.79.len_ref, bf16[2048,128]{1,0:T(8,128)(2,1)} %get-tuple-element.401.q_ref, bf16[2048,128]{1,0:T(8,128)(2,1)} %fusion.126.k_ref, bf16[2048,128]{1,0:T(8,128)(2,1)} %get-tuple-element.400.v_ref), custom_call_target="tpu_custom_call" | custom-call | flops 1207959552 | bytes 2097152 | tf_op jit(solution)/shard_map/pallas_call | solution.py:77
  132.8 6.8 fusion.213
  139.6 7.8 %fusion.205 = (bf16[4,512,1024]{2,1,0:T(8,128)(2,1)S(1)}, f32[4,512,1024]{2,1,0:T(8,128)}) fusion(s32[]{:T(128)S(6)} %select_n.457, f32[4,512,1024]{2,1,0:T(8,128)} %bitcast.723), kind=kLoop, calls=%fused_computation.507 | loop fusion | flops 4194304 | bytes 20971524 | tf_op jit(solution)/shard_map/convert.23
  176.1 19.1 %collective-permute-done.17 = bf16[512,1024]{1,0:T(8,128)(2,1)S(1)} collective-permute-done((bf16[512,1024]{1,0:T(8,128)(2,1)S(1)}, bf16[512,1024]{1,0:T(8,128)(2,1)S(1)}, u32[]{:S(2)}, u32[]{:S(2)}) %collective-permute-start.17) | collective-permute-done | bytes 1048608 | tf_op jit(solution)/shard_map/ppermute | solution.py:244
  227.0 7.9 %collective-permute-done.29 = bf16[128,1024]{1,0:T(8,128)(2,1)S(1)} collective-permute-done((bf16[128,1024]{1,0:T(8,128)(2,1)S(1)}, bf16[128,1024]{1,0:T(8,128)(2,1)S(1)}, u32[]{:S(2)}, u32[]{:S(2)}) %collective-permute-start.29) | collective-permute-done | bytes 262176 | tf_op jit(solution)/shard_map/ppermute | solution.py:244
  274.2 10.1 %collective-permute-done.37 = bf16[512,1024]{1,0:T(8,128)(2,1)} collective-permute-done((bf16[512,1024]{1,0:T(8,128)(2,1)}, bf16[512,1024]{1,0:T(8,128)(2,1)}, u32[]{:S(2)}, u32[]{:S(2)}) %collective-permute-start.37) | collective-permute-done | bytes 1048608 | tf_op jit(solution)/shard_map/ppermute | solution.py:214
  324.5 7.4 convert_bitcast_fusion
  331.9 8.5 %fusion.28 = f32[512,2048]{1,0:T(8,128)S(1)} fusion(bf16[2048,1,2048]{2,0,1:T(8,128)(2,1)} %all-gather.2.cloned.1.call-done, f32[]{:T(128)S(6)} %div.123, f32[2048,512]{1,0:T(8,128)} %copy-done.47, f32[512]{0:T(512)S(1)} %copy-done.46), kind=kOutput, calls=%fused_computation.63 | convolution fusion | flops 4306501632 | bytes 16779268 | tf_op jit(solution)/shard_map/rsf,rsd->fd/dot_general | solution.py:361
  345.9 10.2 %convert_reduce_fusion = (f32[512]{0:T(512)S(1)}, bf16[2048,512]{1,0:T(8,128)(2,1)S(1)}) fusion(f32[2048,512]{1,0:T(8,128)} %copy-done.47, f32[512]{0:T(512)S(1)} %copy-done.46, bf16[512,2048]{1,0:T(8,128)(2,1)S(1)} %copy-done, bf16[2048,1,2048]{2,0,1:T(8,128)(2,1)S(1)} %bitcast.791), kind=kOutput, calls=%fused_computation.61 | convolution fusion | flops 4319084032 | bytes 16781312 | tf_op jit(solution)/shard_map/rsd,fd->rsf/dot_general | solution.py:362
  364.1 8.2 %fusion.64 = f32[4,4,128,2048]{3,2,1,0:T(8,128)} fusion(bf16[4,4,128,512]{3,2,1,0:T(8,128)(2,1)S(1)} %bitcast.792, bf16[2048,512]{1,0:T(8,128)(2,1)S(1)} %copy-done.45), kind=kOutput, calls=%fused_computation.105 | convolution fusion | flops 4294967296 | bytes 20971520 | tf_op jit(solution)/shard_map/rsf,df->rsd/dot_general | solution.py:377
  372.3 6.7 fusion.212
  492.4 12.5 %collective-permute-done.69 = bf16[512,1024]{1,0:T(8,128)(2,1)} collective-permute-done((bf16[512,1024]{1,0:T(8,128)(2,1)}, bf16[512,1024]{1,0:T(8,128)(2,1)}, u32[]{:S(2)}, u32[]{:S(2)}) %collective-permute-start.69) | collective-permute-done | bytes 1048608 | tf_op jit(solution)/shard_map/ppermute | solution.py:214
  533.9 8.3 %maximum_bitcast_fusion = bf16[2048,1,2048]{2,0,1:T(8,128)(2,1)} fusion(bf16[2048,1024]{1,0:T(8,128)(2,1)} %bitcast.743, bf16[2048,1024]{1,0:T(8,128)(2,1)} %bitcast.738), kind=kLoop, calls=%fused_computation.23 | loop fusion | flops 16777216 | bytes 16777216 | tf_op jit(solution)/shard_map/reshape | solution.py:387
  551.5 22.9 %shard_map.255 = (bf16[2048,128]{1,0:T(8,128)(2,1)}, bf16[2048,128]{1,0:T(8,128)(2,1)}, bf16[2048,128]{1,0:T(8,128)(2,1)}) custom-call(s32[1]{0:T(128)} %dynamic_slice.79.len_ref, bf16[2048,128]{1,0:T(8,128)(2,1)} %get-tuple-element.401.q_ref, bf16[2048,128]{1,0:T(8,128)(2,1)} %fusion.126.k_ref, bf16[2048,128]{1,0:T(8,128)(2,1)} %get-tuple-element.400.v_ref, ...), custom_call_target="tpu_custom_call" | custom-call | flops 2415919104 | bytes 4194304 | tf_op jit(solution)/shard_map/pallas_call | solution.py:169
  575.9 10.7 %copy.75 = bf16[2048,1,3,128]{3,2,0,1:T(4,128)(2,1)} copy(bf16[2048,1,3,128]{3,0,2,1:T(8,128)(2,1)S(1)} %pad_maximum_fusion.7) | data formatting | bytes 3145728 | tf_op jit(solution)/shard_map/rsc,dc->rsd/dot_general | solution.py:425
  609.6 8.0 %fusion.187 = (bf16[4,512,1024]{2,1,0:T(8,128)(2,1)S(1)}, f32[4,512,1024]{2,1,0:T(8,128)}) fusion(s32[]{:T(128)S(6)} %select_n.457, f32[4,512,1024]{2,1,0:T(8,128)} %bitcast.725), kind=kLoop, calls=%fused_computation.497 | loop fusion | flops 4194304 | bytes 20971524 | tf_op jit(solution)/shard_map/convert.7
  634.3 7.9 %fusion.35 = f32[2048,3,128]{2,0,1:T(8,128)S(1)} fusion(bf16[2048,1,2048]{2,0,1:T(8,128)(2,1)} %fusion.20, bf16[2048,1,3,128]{0,3,2,1:T(8,128)(2,1)} %copy.59, f32[]{:T(128)S(6)} %div.123), kind=kOutput, calls=%fused_computation.66 | convolution fusion | flops 3222011904 | bytes 13107204 | tf_op jit(solution)/shard_map/rd,rc->dc/dot_general | solution.py:417
  666.1 18.0 %collective-permute-done.81 = bf16[512,1024]{1,0:T(8,128)(2,1)S(1)} collective-permute-done((bf16[512,1024]{1,0:T(8,128)(2,1)S(1)}, bf16[512,1024]{1,0:T(8,128)(2,1)S(1)}, u32[]{:S(2)}, u32[]{:S(2)}) %collective-permute-start.81) | collective-permute-done | bytes 1048608 | tf_op jit(solution)/shard_map/ppermute | solution.py:244
  691.5 7.4 collective-permute-done.89
  724.4 7.4 collective-permute-start.108
  754.1 9.4 %collective-permute-done.105 = bf16[1,256,3,1,128]{4,3,2,1,0:T(2,128)(2,1)S(1)} collective-permute-done((bf16[1,256,3,1,128]{4,3,2,1,0:T(2,128)(2,1)S(1)}, bf16[1,256,3,1,128]{4,3,2,1,0:T(2,128)(2,1)S(1)}, u32[]{:S(2)}, u32[]{:S(2)}) %collective-permute-start.105) | collective-permute-done | bytes 196640 | tf_op jit(solution)/shard_map/ppermute | solution.py:505
  (651 shorter events, 497.5 us)
Async XLA Ops:
  7.2 324.6 %all-gather.2.cloned.1.call-start = ((), (), s32[]{:S(2)}) async-start(), calls=%async_computation.1 | async-start | bytes 8912896 | tf_op jit(solution)/shard_map/all_gather | solution.py:333
  35.1 25.3 %collective-permute-start.4 = (bf16[512,1024]{1,0:T(8,128)(2,1)}, bf16[512,1024]{1,0:T(8,128)(2,1)}, u32[]{:S(2)}, u32[]{:S(2)}) collective-permute-start(bf16[512,1024]{1,0:T(8,128)(2,1)} %bitcast.6), channel_id=1, source_target_pairs={{0,12},{1,13},{2,14},{3,15},{4,0},{5,1},{6,2},{7,3},{8,4},{9,5},{1... | collective-permute-start | bytes 3145736 | tf_op jit(solution)/shard_map/ppermute | solution.py:215
  37.3 30.0 %collective-permute-start.12 = (bf16[512,1024]{1,0:T(8,128)(2,1)S(1)}, bf16[512,1024]{1,0:T(8,128)(2,1)}, u32[]{:S(2)}, u32[]{:S(2)}) collective-permute-start(bf16[512,1024]{1,0:T(8,128)(2,1)S(1)} %bitcast.752), channel_id=1, source_target_pairs={{0,3},{1,0},{2,1},{3,2},{4,7},{5,4},{6,5},{7,6},{8,11},{9,8},{10,9... | collective-permute-start | bytes 3145736 | tf_op jit(solution)/shard_map/ppermute | solution.py:215
  162.4 604.2 %reduce-scatter.2.cloned.1.call-start = ((), (), s32[]{:S(2)}) async-start(), calls=%async_computation.2 | async-start | bytes 8912896 | tf_op jit(solution)/shard_map/reduce_scatter | solution.py:392
  167.5 27.7 %collective-permute-start.17 = (bf16[512,1024]{1,0:T(8,128)(2,1)S(1)}, bf16[512,1024]{1,0:T(8,128)(2,1)S(1)}, u32[]{:S(2)}, u32[]{:S(2)}) collective-permute-start(bf16[512,1024]{1,0:T(8,128)(2,1)S(1)} %get-tuple-element.378), channel_id=1, source_target_pairs={{0,4},{1,5},{2,6},{3,7},{4,8},{5,9},{6,10},{7,11},{8,12},{9,13},{1... | collective-permute-start | bytes 3145736 | tf_op jit(solution)/shard_map/ppermute | solution.py:244
  167.6 27.6 %collective-permute-start.19 = (bf16[512,1024]{1,0:T(8,128)(2,1)S(1)}, bf16[512,1024]{1,0:T(8,128)(2,1)S(1)}, u32[]{:S(2)}, u32[]{:S(2)}) collective-permute-start(bf16[512,1024]{1,0:T(8,128)(2,1)S(1)} %get-tuple-element.379), channel_id=1, source_target_pairs={{0,12},{1,13},{2,14},{3,15},{4,0},{5,1},{6,2},{7,3},{8,4},{9,5},{1... | collective-permute-start | bytes 3145736 | tf_op jit(solution)/shard_map/ppermute | solution.py:245
  172.8 29.3 %collective-permute-start.25 = (bf16[512,1024]{1,0:T(8,128)(2,1)S(1)}, bf16[512,1024]{1,0:T(8,128)(2,1)S(1)}, u32[]{:S(2)}, u32[]{:S(2)}) collective-permute-start(bf16[512,1024]{1,0:T(8,128)(2,1)S(1)} %get-tuple-element.382), channel_id=1, source_target_pairs={{0,1},{1,2},{2,3},{3,0},{4,5},{5,6},{6,7},{7,4},{8,9},{9,10},{10,1... | collective-permute-start | bytes 3145736 | tf_op jit(solution)/shard_map/ppermute | solution.py:244
  173.8 33.6 %collective-permute-start.27 = (bf16[512,1024]{1,0:T(8,128)(2,1)S(1)}, bf16[512,1024]{1,0:T(8,128)(2,1)S(1)}, u32[]{:S(2)}, u32[]{:S(2)}) collective-permute-start(bf16[512,1024]{1,0:T(8,128)(2,1)S(1)} %get-tuple-element.383), channel_id=1, source_target_pairs={{0,3},{1,0},{2,1},{3,2},{4,7},{5,4},{6,5},{7,6},{8,11},{9,8},{10,9... | collective-permute-start | bytes 3145736 | tf_op jit(solution)/shard_map/ppermute | solution.py:245
  267.0 25.5 %collective-permute-start.44 = (bf16[512,1024]{1,0:T(8,128)(2,1)}, bf16[512,1024]{1,0:T(8,128)(2,1)}, u32[]{:S(2)}, u32[]{:S(2)}) collective-permute-start(bf16[512,1024]{1,0:T(8,128)(2,1)} %bitcast.88), channel_id=1, source_target_pairs={{0,3},{1,0},{2,1},{3,2},{4,7},{5,4},{6,5},{7,6},{8,11},{9,8},{10,9... | collective-permute-start | bytes 3145736 | tf_op jit(solution)/shard_map/ppermute | solution.py:215
  344.7 77.4 %collective-permute-start.112 = (bf16[512,4,256]{2,0,1:T(8,128)(2,1)}, bf16[512,4,256]{2,0,1:T(8,128)(2,1)}, u32[]{:S(2)}, u32[]{:S(2)}) collective-permute-start(bf16[512,4,256]{2,0,1:T(8,128)(2,1)} %select_convert_fusion), channel_id=1, source_target_pairs={{0,64},{32,96},{64,0},{96,32},{1,65},{33,97},{65,1},{97,33},{2,66}... | collective-permute-start | bytes 3145736 | tf_op jit(solution)/shard_map/ppermute | solution.py:505
  428.6 35.9 %collective-permute-start.114 = (bf16[512,1,256]{2,0,1:T(8,128)(2,1)S(1)}, bf16[512,1,256]{2,0,1:T(8,128)(2,1)S(1)}, u32[]{:S(2)}, u32[]{:S(2)}) collective-permute-start(bf16[512,1,256]{2,0,1:T(8,128)(2,1)S(1)} %select_convert_fusion.5), channel_id=1, source_target_pairs={{0,16},{16,0},{1,17},{17,1},{2,18},{18,2},{3,19},{19,3},{4,20},{20... | collective-permute-start | bytes 786440 | tf_op jit(solution)/shard_map/ppermute | solution.py:505
  448.1 40.4 %collective-permute-start.111 = (bf16[1,256,512]{2,1,0:T(8,128)(2,1)S(1)}, bf16[1,256,512]{2,1,0:T(8,128)(2,1)S(1)}, u32[]{:S(2)}, u32[]{:S(2)}) collective-permute-start(bf16[1,256,512]{2,1,0:T(8,128)(2,1)S(1)} %select_convert_fusion.6), channel_id=1, source_target_pairs={{0,16},{16,0},{1,17},{17,1},{2,18},{18,2},{3,19},{19,3},{4,20},{20... | collective-permute-start | bytes 786440 | tf_op jit(solution)/shard_map/ppermute | solution.py:505
  482.6 24.9 %collective-permute-start.68 = (bf16[512,1024]{1,0:T(8,128)(2,1)}, bf16[512,1024]{1,0:T(8,128)(2,1)}, u32[]{:S(2)}, u32[]{:S(2)}) collective-permute-start(bf16[512,1024]{1,0:T(8,128)(2,1)} %bitcast.143), channel_id=1, source_target_pairs={{0,12},{1,13},{2,14},{3,15},{4,0},{5,1},{6,2},{7,3},{8,4},{9,5},{1... | collective-permute-start | bytes 3145736 | tf_op jit(solution)/shard_map/ppermute | solution.py:215
  484.7 27.2 %collective-permute-start.76 = (bf16[512,1024]{1,0:T(8,128)(2,1)S(1)}, bf16[512,1024]{1,0:T(8,128)(2,1)}, u32[]{:S(2)}, u32[]{:S(2)}) collective-permute-start(bf16[512,1024]{1,0:T(8,128)(2,1)S(1)} %bitcast.748), channel_id=1, source_target_pairs={{0,3},{1,0},{2,1},{3,2},{4,7},{5,4},{6,5},{7,6},{8,11},{9,8},{10,9... | collective-permute-start | bytes 3145736 | tf_op jit(solution)/shard_map/ppermute | solution.py:215
  591.0 65.6 %collective-permute-start.106 = (bf16[1,128,4,256]{3,1,2,0:T(8,128)(2,1)S(1)}, bf16[1,128,4,256]{3,1,2,0:T(8,128)(2,1)}, u32[]{:S(2)}, u32[]{:S(2)}) collective-permute-start(bf16[1,128,4,256]{3,1,2,0:T(8,128)(2,1)S(1)} %select_convert_fusion.7), channel_id=1, source_target_pairs={{0,64},{32,96},{64,0},{96,32},{1,65},{33,97},{65,1},{97,33},{2,66}... | collective-permute-start | bytes 786440 | tf_op jit(solution)/shard_map/ppermute | solution.py:505
  618.7 33.4 %collective-permute-start.80 = (bf16[256,1024]{1,0:T(8,128)(2,1)}, bf16[256,1024]{1,0:T(8,128)(2,1)}, u32[]{:S(2)}, u32[]{:S(2)}) collective-permute-start(bf16[256,1024]{1,0:T(8,128)(2,1)} %get-tuple-element.388), channel_id=1, source_target_pairs={{0,4},{1,5},{2,6},{3,7},{4,8},{5,9},{6,10},{7,11},{8,12},{9,13},{1... | collective-permute-start | bytes 1572872 | tf_op jit(solution)/shard_map/ppermute | solution.py:240
  618.7 35.6 %collective-permute-start.82 = (bf16[256,1024]{1,0:T(8,128)(2,1)}, bf16[256,1024]{1,0:T(8,128)(2,1)}, u32[]{:S(2)}, u32[]{:S(2)}) collective-permute-start(bf16[256,1024]{1,0:T(8,128)(2,1)} %get-tuple-element.389), channel_id=1, source_target_pairs={{0,12},{1,13},{2,14},{3,15},{4,0},{5,1},{6,2},{7,3},{8,4},{9,5},{1... | collective-permute-start | bytes 1572872 | tf_op jit(solution)/shard_map/ppermute | solution.py:241
  629.3 31.7 %collective-permute-start.88 = (bf16[256,1024]{1,0:T(8,128)(2,1)}, bf16[256,1024]{1,0:T(8,128)(2,1)}, u32[]{:S(2)}, u32[]{:S(2)}) collective-permute-start(bf16[256,1024]{1,0:T(8,128)(2,1)} %get-tuple-element.390), channel_id=1, source_target_pairs={{0,1},{1,2},{2,3},{3,0},{4,5},{5,6},{6,7},{7,4},{8,9},{9,10},{10,1... | collective-permute-start | bytes 1572872 | tf_op jit(solution)/shard_map/ppermute | solution.py:240
  629.3 31.9 %collective-permute-start.90 = (bf16[256,1024]{1,0:T(8,128)(2,1)}, bf16[256,1024]{1,0:T(8,128)(2,1)}, u32[]{:S(2)}, u32[]{:S(2)}) collective-permute-start(bf16[256,1024]{1,0:T(8,128)(2,1)} %get-tuple-element.391), channel_id=1, source_target_pairs={{0,3},{1,0},{2,1},{3,2},{4,7},{5,4},{6,5},{7,6},{8,11},{9,8},{10,9... | collective-permute-start | bytes 1572872 | tf_op jit(solution)/shard_map/ppermute | solution.py:241
  652.1 85.2 %collective-permute-start.103 = (bf16[4,256,3,1,128]{4,3,2,1,0:T(2,128)(2,1)}, bf16[4,256,3,1,128]{4,3,2,1,0:T(2,128)(2,1)}, u32[]{:S(2)}, u32[]{:S(2)}) collective-permute-start(bf16[4,256,3,1,128]{4,3,2,1,0:T(2,128)(2,1)} %copy.65), channel_id=1, source_target_pairs={{0,64},{32,96},{64,0},{96,32},{1,65},{33,97},{65,1},{97,33},{2,66}... | collective-permute-start | bytes 2359304 | tf_op jit(solution)/shard_map/ppermute | solution.py:505
  656.5 27.6 %collective-permute-start.81 = (bf16[512,1024]{1,0:T(8,128)(2,1)S(1)}, bf16[512,1024]{1,0:T(8,128)(2,1)S(1)}, u32[]{:S(2)}, u32[]{:S(2)}) collective-permute-start(bf16[512,1024]{1,0:T(8,128)(2,1)S(1)} %get-tuple-element.362), channel_id=1, source_target_pairs={{0,4},{1,5},{2,6},{3,7},{4,8},{5,9},{6,10},{7,11},{8,12},{9,13},{1... | collective-permute-start | bytes 3145736 | tf_op jit(solution)/shard_map/ppermute | solution.py:244
  656.6 28.7 %collective-permute-start.83 = (bf16[512,1024]{1,0:T(8,128)(2,1)S(1)}, bf16[512,1024]{1,0:T(8,128)(2,1)S(1)}, u32[]{:S(2)}, u32[]{:S(2)}) collective-permute-start(bf16[512,1024]{1,0:T(8,128)(2,1)S(1)} %get-tuple-element.363), channel_id=1, source_target_pairs={{0,12},{1,13},{2,14},{3,15},{4,0},{5,1},{6,2},{7,3},{8,4},{9,5},{1... | collective-permute-start | bytes 3145736 | tf_op jit(solution)/shard_map/ppermute | solution.py:245
  662.8 36.1 %collective-permute-start.89 = (bf16[512,1024]{1,0:T(8,128)(2,1)S(1)}, bf16[512,1024]{1,0:T(8,128)(2,1)S(1)}, u32[]{:S(2)}, u32[]{:S(2)}) collective-permute-start(bf16[512,1024]{1,0:T(8,128)(2,1)S(1)} %get-tuple-element.366), channel_id=1, source_target_pairs={{0,1},{1,2},{2,3},{3,0},{4,5},{5,6},{6,7},{7,4},{8,9},{9,10},{10,1... | collective-permute-start | bytes 3145736 | tf_op jit(solution)/shard_map/ppermute | solution.py:244
  662.9 36.2 %collective-permute-start.91 = (bf16[512,1024]{1,0:T(8,128)(2,1)S(1)}, bf16[512,1024]{1,0:T(8,128)(2,1)S(1)}, u32[]{:S(2)}, u32[]{:S(2)}) collective-permute-start(bf16[512,1024]{1,0:T(8,128)(2,1)S(1)} %get-tuple-element.367), channel_id=1, source_target_pairs={{0,3},{1,0},{2,1},{3,2},{4,7},{5,4},{6,5},{7,6},{8,11},{9,8},{10,9... | collective-permute-start | bytes 3145736 | tf_op jit(solution)/shard_map/ppermute | solution.py:245
  (149 other events, 1957.1 us)
Sparse Core Ops, SparseCore 0:
  162.5 87.9 all-gather.1
  596.6 105.9 reduce-scatter.1

commit v5 on v3

--- a/solution.py
+++ b/solution.py
@@ -59,9 +59,11 @@
 
     total = lax.fori_loop(0, count, exps, jnp.zeros((block_q, 1), jnp.float32))
 
+    inverse = 1.0 / total
+
     def mix(j, acc):
         first = pl.multiple_of(j * block_k, block_k)
-        probs = (s_buf[:, pl.ds(first, block_k)] / total).astype(jnp.bfloat16)
+        probs = (s_buf[:, pl.ds(first, block_k)] * inverse).astype(jnp.bfloat16)
         return acc + jnp.dot(probs, v_ref[pl.ds(first, block_k), :], preferred_element_type=jnp.float32)
 
     acc = lax.fori_loop(0, count, mix, jnp.zeros(o_ref.shape, jnp.float32))
@@ -270,6 +272,8 @@
         + b_o
     )
     middle = inputs + attention
+    act_grad = jnp.einsum("rsd,fd->rsf", upstream_full, w_out, preferred_element_type=jnp.float32)
+    middle, act_grad = lax.optimization_barrier((middle, act_grad))
     second_low = layer_norm(middle, ln2_gain, ln2_bias).astype(jnp.bfloat16)
     second_full = lax.all_gather(second_low, "tensor", axis=0, tiled=True)
     pre_act = (
@@ -281,14 +285,8 @@
         + b_in
     )
     activated = gelu_tanh(pre_act).astype(jnp.bfloat16).reshape(seq_total, seq_count, hidden)
-    feed_part = jnp.einsum(
-        "rsf,fd->rsd", activated, w_out, preferred_element_type=jnp.float32
-    ).astype(jnp.bfloat16)
     piece = upstream_full
-    weight_grad = jnp.einsum("rsf,rsd->fd", activated, piece, preferred_element_type=jnp.float32)
-    part = jnp.einsum("rsd,fd->rsf", piece, w_out, preferred_element_type=jnp.float32)
-    act_grad = part
-    grad_w_out = weight_grad
+    grad_w_out = jnp.einsum("rsf,rsd->fd", activated, piece, preferred_element_type=jnp.float32)
     gelu_back = jax.vjp(gelu_tanh, pre_act)[1]
     pre_low = gelu_back(act_grad.reshape(seq_total * seq_count, hidden))[0].astype(jnp.bfloat16)
     grad_b_in = jnp.sum(pre_low, axis=0, dtype=jnp.float32)
@@ -300,14 +298,16 @@
     )
     pre_rows = pre_low.reshape(seq_total, seq_count, hidden)
     piece = pre_rows
+    second_part = jnp.einsum("rsf,df->rsd", piece, w_in, preferred_element_type=jnp.float32)
+    second_part = second_part.astype(jnp.bfloat16)
+    feed_input, second_part = lax.optimization_barrier((activated, second_part))
     second_grad = lax.psum_scatter(
-        jnp.einsum("rsf,df->rsd", piece, w_in, preferred_element_type=jnp.float32).astype(
-            jnp.bfloat16
-        ),
-        "tensor",
-        scatter_dimension=0,
-        tiled=True,
+        second_part, "tensor", scatter_dimension=0, tiled=True
     ).astype(jnp.float32)
+    feed_part = jnp.einsum(
+        "rsf,fd->rsd", feed_input, w_out, preferred_element_type=jnp.float32
+    ).astype(jnp.bfloat16)
+    feed_part, second_grad = lax.optimization_barrier((feed_part, second_grad))
     norm_two_back = jax.vjp(layer_norm, middle, ln2_gain, ln2_bias)[1]
     middle_part, grad_ln2_gain, grad_ln2_bias = norm_two_back(second_grad)
     middle_grad = upstream.astype(jnp.float32) + middle_part
@@ -315,14 +315,6 @@
     grad_b_o = jnp.sum(branch_low, axis=(0, 1), dtype=jnp.float32)
     grad_b_out = jnp.sum(upstream, axis=(0, 1), dtype=jnp.float32)
     piece = lax.all_gather(branch_low, "tensor", axis=0, tiled=True)
-    feed_part, piece = lax.optimization_barrier((feed_part, piece))
-    feed = (
-        lax.psum_scatter(feed_part, "tensor", scatter_dimension=0, tiled=True).astype(
-            jnp.float32
-        )
-        + b_out
-    )
-    output = (middle + feed).astype(jnp.bfloat16)
     weight_grad = jnp.einsum("rse,rsd->ed", attended, piece, preferred_element_type=jnp.float32)
     part = jnp.einsum("rsd,ed->rse", piece, out_weight, preferred_element_type=jnp.float32)
     attended_grad = part.astype(jnp.bfloat16)
@@ -349,14 +341,15 @@
         preferred_element_type=jnp.float32,
     )
     piece = joint_rows
-    normed_grad = lax.psum_scatter(
-        jnp.einsum("rsc,dc->rsd", piece, joint_weight, preferred_element_type=jnp.float32).astype(
-            jnp.bfloat16
-        ),
-        "tensor",
-        scatter_dimension=0,
-        tiled=True,
+    normed_part = jnp.einsum(
+        "rsc,dc->rsd", piece, joint_weight, preferred_element_type=jnp.float32
+    ).astype(jnp.bfloat16)
+    both = lax.psum_scatter(
+        jnp.concatenate([normed_part, feed_part], 2), "tensor", scatter_dimension=0, tiled=True
     ).astype(jnp.float32)
+    normed_grad = both[:, :, :model_width]
+    feed = both[:, :, model_width:] + b_out
+    output = (middle + feed).astype(jnp.bfloat16)
     norm_one_back = jax.vjp(layer_norm, inputs, ln1_gain, ln1_bias)[1]
     input_part, grad_ln1_gain, grad_ln1_bias = norm_one_back(normed_grad)
     input_grad = (middle_grad + input_part).astype(jnp.bfloat16)

time: 757 us -> 756 us (level)
  starting transfers between devices: 34.7 us -> 55.2 us
  Pallas kernels: 46.4 us -> 31.5 us
  other arithmetic: 56.9 us -> 65.3 us
    ppermute x19, starting transfers between devices: 33.6 us -> 54.7 us  [halving_steps(): got = lax.ppermute(send, axis, [(i, i ^ bit) for i in range(size)])]
    reduce_scatter x1, waiting for transfers between devices: 88.1 us -> 77.4 us  [shards(): lax.psum_scatter(attention_part, 'tensor', scatter_dimension=0, tiled=True)]
    concatenate x0 -> x1, other arithmetic: none -> 10.6 us  [shards(): jnp.concatenate([normed_part, feed_part], 2)]
    all_gather x1, waiting for transfers between devices: 59.7 us -> 70.1 us  [shards(): piece = lax.all_gather(branch_low, 'tensor', axis=0, tiled=True)]
    pallas_call x1, Pallas kernels: 22.7 us -> 12.9 us  [attention_backward(): pl.pallas_call(kernel, out_shape=tuple((jax.ShapeDtypeStruct((n, d), jnp....]
    reduce_scatter x3 -> x2, waiting for transfers between devices: 84.4 us -> 75.1 us  [the longest x1 75.1 us: shards(): lax.psum_scatter(second_part, 'tensor', scatter_dimension=0, tiled=True)]
  transfers between devices with their start and end apart: 27 -> 26, of which waited for: 18 -> 18; matrix products, arithmetic and copies ran while one was open for 14% -> 15% of each run, Pallas kernels for 3% -> 2%
where the time goes in v5:
time: 756 us; the launch traced here: 746 us
  waiting for transfers between devices  468 us (62%)
  matrix products  87.5 us (12%)
  other arithmetic  65.3 us (9%)
  starting transfers between devices  55.2 us (7%)
  Pallas kernels  31.5 us (4%)
  local copies, waits for them, and re-layouts  21.7 us (3%)
  between operations  16.8 us (2%)
    reduce_scatter x1, waiting for transfers between devices, shards(): lax.psum_scatter(attention_part, 'tensor', scatter_dimension=0, tiled=True)  77.4 us
    reduce_scatter x1, waiting for transfers between devices, shards(): lax.psum_scatter(second_part, 'tensor', scatter_dimension=0, tiled=True)  75.1 us
    ppermute x19, waiting for transfers between devices, halving_steps(): got = lax.ppermute(send, axis, [(i, i ^ bit) for i in range(size)])  71.7 us
    all_gather x1, waiting for transfers between devices, shards(): piece = lax.all_gather(branch_low, 'tensor', axis=0, tiled=True)  70.1 us
    all_gather x1, waiting for transfers between devices, shards(): second_full = lax.all_gather(second_low, 'tensor', axis=0, tiled=True)  69.9 us
    all_gather x1, waiting for transfers between devices, shards(): normed_full = lax.all_gather(normed_low, 'tensor', axis=0, tiled=True)  65.3 us
    ppermute x19, starting transfers between devices, halving_steps(): got = lax.ppermute(send, axis, [(i, i ^ bit) for i in range(size)])  54.7 us
    all_gather x1, waiting for transfers between devices, shards(): upstream_full = lax.all_gather(upstream, 'tensor', axis=0, tiled=True)  37.9 us
  transfers between devices with their start and end apart: 26, of which 18 were waited for; matrix products, arithmetic and copies ran while one was open for 15% of the time, Pallas kernels for 2%

profile of v5, /device:TPU:96, one launch (start us, length us, event | category | flops | bytes accessed | tf_op | source)
XLA Modules:
  0.0 745.7 jit_solution(18432758682621753856)
XLA Ops:
  19.0 65.3 %all-gather.5.cloned.1.call-done = bf16[2048,1,2048]{2,0,1:T(8,128)(2,1)} async-done(((bf16[128,1,2048]{2,0,1:T(8,128)(2,1)}), bf16[2048,1,2048]{2,0,1:T(8,128)(2,1)}) %all-gather.5.cloned.1.call-update) | async-done | bytes 8388624 | tf_op jit(solution)/shard_map/all_gather | solution.py:232
  84.3 7.4 fusion.35
  93.7 18.6 %shard_map.254 = (bf16[2048,128]{1,0:T(8,128)(2,1)}, f32[2048,1]{1,0:T(8,128)}) custom-call(s32[1]{0:T(128)} %dynamic_slice.7.len_ref, bf16[2048,128]{1,0:T(8,128)(2,1)} %get-tuple-element.60.q_ref, bf16[2048,128]{1,0:T(8,128)(2,1)} %fusion.70.k_ref, bf16[2048,128]{1,0:T(8,128)(2,1)} %get-tuple-element.59.v_ref), custom_call_target="tpu_custom_call" | custom-call | flops 1207959552 | bytes 2097152 | tf_op jit(solution)/shard_map/pallas_call | solution.py:79
  112.3 6.6 convert_bitcast_fusion.3
  119.0 37.9 %all-gather.7.cloned.1.call-done = bf16[2048,1,2048]{2,0,1:T(8,128)(2,1)} async-done(((bf16[128,1,2048]{2,0,1:T(8,128)(2,1)}), bf16[2048,1,2048]{2,0,1:T(8,128)(2,1)}) %all-gather.7.cloned.1.call-update) | async-done | bytes 8388624 | tf_op jit(solution)/shard_map/all_gather | solution.py:263
  156.9 10.5 %fusion.32 = f32[2048,1,512]{2,0,1:T(8,128)} fusion(bf16[512,2048]{1,0:T(8,128)(2,1)} %param.28, bf16[2048,1,2048]{2,0,1:T(8,128)(2,1)} %all-gather.7.cloned.1.call-done), kind=kOutput, calls=%fused_computation.39 | convolution fusion | flops 4294967296 | bytes 14680064 | tf_op jit(solution)/shard_map/rsd,fd->rsf/dot_general | solution.py:275
  167.5 77.4 %reduce-scatter.4.cloned.1.call-done = bf16[128,1,2048]{2,0,1:T(8,128)(2,1)} async-done(((bf16[2048,1,2048]{2,0,1:T(8,128)(2,1)}), bf16[128,1,2048]{2,0,1:T(8,128)(2,1)}) %reduce-scatter.4.cloned.1.call-update) | async-done | bytes 524304 | tf_op jit(solution)/shard_map/reduce_scatter | solution.py:269
  248.1 69.9 %all-gather.9.cloned.1.call-done = bf16[2048,1,2048]{2,0,1:T(8,128)(2,1)} async-done(((bf16[128,1,2048]{2,0,1:T(8,128)(2,1)}), bf16[2048,1,2048]{2,0,1:T(8,128)(2,1)}) %all-gather.9.cloned.1.call-update) | async-done | bytes 8388624 | tf_op jit(solution)/shard_map/all_gather | solution.py:278
  318.0 7.0 fusion.6
  330.8 6.9 convert_bitcast_fusion.2
  339.3 8.3 %convert_bitcast_fusion.1 = bf16[2048,1,2048]{2,0,1:T(8,128)(2,1)} fusion(bf16[512,2048]{1,0:T(8,128)(2,1)} %param.28, bf16[2048,1,512]{2,0,1:T(8,128)(2,1)S(1)} %copy-done.19), kind=kOutput, calls=%fused_computation.18 | convolution fusion | flops 4299161600 | bytes 12582912 | tf_op jit(solution)/shard_map/rsf,fd->rsd/dot_general | solution.py:307
  347.6 75.1 %reduce-scatter.6.cloned.1.call-done = bf16[128,1,2048]{2,0,1:T(8,128)(2,1)} async-done(((bf16[2048,1,2048]{2,0,1:T(8,128)(2,1)}), bf16[128,1,2048]{2,0,1:T(8,128)(2,1)}) %reduce-scatter.6.cloned.1.call-update) | async-done | bytes 524304 | tf_op jit(solution)/shard_map/reduce_scatter | solution.py:304
  426.5 70.1 %all-gather.11.cloned.1.call-done = bf16[2048,1,2048]{2,0,1:T(8,128)(2,1)} async-done(((bf16[128,1,2048]{2,0,1:T(8,128)(2,1)}), bf16[2048,1,2048]{2,0,1:T(8,128)(2,1)}) %all-gather.11.cloned.1.call-update) | async-done | bytes 8388624 | tf_op jit(solution)/shard_map/all_gather | solution.py:317
  503.1 12.9 %shard_map.255 = (bf16[2048,128]{1,0:T(8,128)(2,1)}, bf16[2048,128]{1,0:T(8,128)(2,1)}, bf16[2048,128]{1,0:T(8,128)(2,1)}) custom-call(s32[1]{0:T(128)} %dynamic_slice.7.len_ref, bf16[2048,128]{1,0:T(8,128)(2,1)} %get-tuple-element.60.q_ref, bf16[2048,128]{1,0:T(8,128)(2,1)} %fusion.70.k_ref, bf16[2048,128]{1,0:T(8,128)(2,1)} %get-tuple-element.59.v_ref, ...), custom_call_target="tpu_custom_call" | custom-call | flops 2415919104 | bytes 4194304 | tf_op jit(solution)/shard_map/pallas_call | solution.py:171
  525.6 10.6 %pad_maximum_fusion = bf16[2048,1,4096]{2,0,1:T(8,128)(2,1)} fusion(bf16[2048,1,2048]{2,0,1:T(8,128)(2,1)} %convert_bitcast_fusion.1, bf16[2048,1,2048]{2,0,1:T(8,128)(2,1)S(1)} %convert_bitcast_fusion), kind=kLoop, calls=%fused_computation | loop fusion | flops 33554432 | bytes 33554432 | tf_op jit(solution)/shard_map/concatenate | solution.py:348
  539.6 8.5 %fusion.26 = f32[512,2048]{1,0:T(8,128)S(1)} fusion(bf16[2048,1,2048]{2,0,1:T(8,128)(2,1)} %all-gather.7.cloned.1.call-done, f32[]{:T(128)S(6)} %div.111, f32[2048,512]{1,0:T(8,128)} %copy-done.15, f32[512]{0:T(512)S(1)} %copy-done.32), kind=kOutput, calls=%fused_computation.37 | convolution fusion | flops 4306501632 | bytes 16779268 | tf_op jit(solution)/shard_map/rsf,rsd->fd/dot_general | solution.py:289
  550.2 7.1 fusion.29
  570.1 10.4 %collective-permute-done.13 = bf16[4,256,512]{2,1,0:T(8,128)(2,1)} collective-permute-done((bf16[4,256,512]{2,1,0:T(8,128)(2,1)}, bf16[4,256,512]{2,1,0:T(8,128)(2,1)}, u32[]{:S(2)}, u32[]{:S(2)}) %collective-permute-start.13) | collective-permute-done | bytes 1048608 | tf_op jit(solution)/shard_map/ppermute | solution.py:429
  582.3 14.1 %collective-permute-start.14 = (bf16[2,256,512]{2,1,0:T(8,128)(2,1)S(1)}, bf16[2,256,512]{2,1,0:T(8,128)(2,1)S(1)}, u32[]{:S(2)}, u32[]{:S(2)}) collective-permute-start(bf16[2,256,512]{2,1,0:T(8,128)(2,1)S(1)} %select_convert_fusion.4), channel_id=1, source_target_pairs={{0,32},{32,0},{64,96},{96,64},{1,33},{33,1},{65,97},{97,65},{2,34}... | collective-permute-start | bytes 1572872 | tf_op jit(solution)/shard_map/ppermute | solution.py:429
  596.3 6.6 collective-permute-done.16
  612.5 12.9 %collective-permute-start.15 = (bf16[1,256,512]{2,1,0:T(8,128)(2,1)}, bf16[1,256,512]{2,1,0:T(8,128)(2,1)S(1)}, u32[]{:S(2)}, u32[]{:S(2)}) collective-permute-start(bf16[1,256,512]{2,1,0:T(8,128)(2,1)} %select_convert_fusion.6), channel_id=1, source_target_pairs={{0,16},{16,0},{1,17},{17,1},{2,18},{18,2},{3,19},{19,3},{4,20},{20... | collective-permute-start | bytes 786440 | tf_op jit(solution)/shard_map/ppermute | solution.py:429
  647.9 7.2 fusion.38
  674.1 29.5 %collective-permute-done.7 = bf16[4,256,3,1,128]{4,3,2,1,0:T(2,128)(2,1)} collective-permute-done((bf16[4,256,3,1,128]{4,3,2,1,0:T(2,128)(2,1)}, bf16[4,256,3,1,128]{4,3,2,1,0:T(2,128)(2,1)}, u32[]{:S(2)}, u32[]{:S(2)}) %collective-permute-start.7) | collective-permute-done | bytes 786464 | tf_op jit(solution)/shard_map/ppermute | solution.py:429
  721.8 7.1 collective-permute-done.9
  (241 shorter events, 140.8 us)
Async XLA Ops:
  7.2 77.1 %all-gather.5.cloned.1.call-start = ((), (), s32[]{:S(2)}) async-start(), calls=%async_computation.3 | async-start | bytes 8912896 | tf_op jit(solution)/shard_map/all_gather | solution.py:232
  12.2 144.6 %all-gather.7.cloned.1.call-start = ((), (), s32[]{:S(2)}) async-start(), calls=%async_computation.4 | async-start | bytes 8912896 | tf_op jit(solution)/shard_map/all_gather | solution.py:263
  16.3 228.6 %reduce-scatter.4.cloned.1.call-start = ((), (), s32[]{:S(2)}) async-start(), calls=%async_computation.5 | async-start | bytes 8912896 | tf_op jit(solution)/shard_map/reduce_scatter | solution.py:269
  156.9 161.1 %all-gather.9.cloned.1.call-start = ((), (), s32[]{:S(2)}) async-start(), calls=%async_computation.6 | async-start | bytes 8912896 | tf_op jit(solution)/shard_map/all_gather | solution.py:278
  247.8 174.9 %reduce-scatter.6.cloned.1.call-start = ((), (), s32[]{:S(2)}) async-start(), calls=%async_computation.7 | async-start | bytes 8912896 | tf_op jit(solution)/shard_map/reduce_scatter | solution.py:304
  337.7 158.9 %all-gather.11.cloned.1.call-start = ((), (), s32[]{:S(2)}) async-start(), calls=%async_computation.8 | async-start | bytes 8912896 | tf_op jit(solution)/shard_map/all_gather | solution.py:317
  426.4 241.4 %reduce-scatter.8.cloned.1.call-start = ((), (), s32[]{:S(2)}) async-start(), calls=%async_computation.9 | async-start | bytes 17825792 | tf_op jit(solution)/shard_map/reduce_scatter | solution.py:347
  558.7 21.8 %collective-permute-start.13 = (bf16[4,256,512]{2,1,0:T(8,128)(2,1)}, bf16[4,256,512]{2,1,0:T(8,128)(2,1)}, u32[]{:S(2)}, u32[]{:S(2)}) collective-permute-start(bf16[4,256,512]{2,1,0:T(8,128)(2,1)} %bitcast.53), channel_id=1, source_target_pairs={{0,64},{32,96},{64,0},{96,32},{1,65},{33,97},{65,1},{97,33},{2,66}... | collective-permute-start | bytes 3145736 | tf_op jit(solution)/shard_map/ppermute | solution.py:429
  566.0 37.0 %collective-permute-start.16 = (bf16[512,4,256]{2,0,1:T(8,128)(2,1)}, bf16[512,4,256]{2,0,1:T(8,128)(2,1)}, u32[]{:S(2)}, u32[]{:S(2)}) collective-permute-start(bf16[512,4,256]{2,0,1:T(8,128)(2,1)} %select_convert_fusion), channel_id=1, source_target_pairs={{0,64},{32,96},{64,0},{96,32},{1,65},{33,97},{65,1},{97,33},{2,66}... | collective-permute-start | bytes 3145736 | tf_op jit(solution)/shard_map/ppermute | solution.py:429
  582.3 29.2 %collective-permute-start.14 = (bf16[2,256,512]{2,1,0:T(8,128)(2,1)S(1)}, bf16[2,256,512]{2,1,0:T(8,128)(2,1)S(1)}, u32[]{:S(2)}, u32[]{:S(2)}) collective-permute-start(bf16[2,256,512]{2,1,0:T(8,128)(2,1)S(1)} %select_convert_fusion.4), channel_id=1, source_target_pairs={{0,32},{32,0},{64,96},{96,64},{1,33},{33,1},{65,97},{97,65},{2,34}... | collective-permute-start | bytes 1572872 | tf_op jit(solution)/shard_map/ppermute | solution.py:429
  605.1 20.3 %collective-permute-start.17 = (bf16[512,2,256]{2,0,1:T(8,128)(2,1)S(1)}, bf16[512,2,256]{2,0,1:T(8,128)(2,1)S(1)}, u32[]{:S(2)}, u32[]{:S(2)}) collective-permute-start(bf16[512,2,256]{2,0,1:T(8,128)(2,1)S(1)} %select_convert_fusion.3), channel_id=1, source_target_pairs={{0,32},{32,0},{64,96},{96,64},{1,33},{33,1},{65,97},{97,65},{2,34}... | collective-permute-start | bytes 1572872 | tf_op jit(solution)/shard_map/ppermute | solution.py:429
  612.5 20.2 %collective-permute-start.15 = (bf16[1,256,512]{2,1,0:T(8,128)(2,1)}, bf16[1,256,512]{2,1,0:T(8,128)(2,1)S(1)}, u32[]{:S(2)}, u32[]{:S(2)}) collective-permute-start(bf16[1,256,512]{2,1,0:T(8,128)(2,1)} %select_convert_fusion.6), channel_id=1, source_target_pairs={{0,16},{16,0},{1,17},{17,1},{2,18},{18,2},{3,19},{19,3},{4,20},{20... | collective-permute-start | bytes 786440 | tf_op jit(solution)/shard_map/ppermute | solution.py:429
  626.3 12.0 %collective-permute-start.18 = (bf16[512,1,256]{2,0,1:T(8,128)(2,1)}, bf16[512,1,256]{2,0,1:T(8,128)(2,1)}, u32[]{:S(2)}, u32[]{:S(2)}) collective-permute-start(bf16[512,1,256]{2,0,1:T(8,128)(2,1)} %select_convert_fusion.5), channel_id=1, source_target_pairs={{0,16},{16,0},{1,17},{17,1},{2,18},{18,2},{3,19},{19,3},{4,20},{20... | collective-permute-start | bytes 786440 | tf_op jit(solution)/shard_map/ppermute | solution.py:429
  646.7 10.9 %collective-permute-start.10 = (bf16[1,128,4,256]{3,1,2,0:T(8,128)(2,1)S(1)}, bf16[1,128,4,256]{3,1,2,0:T(8,128)(2,1)S(1)}, u32[]{:S(2)}, u32[]{:S(2)}) collective-permute-start(bf16[1,128,4,256]{3,1,2,0:T(8,128)(2,1)S(1)} %select_convert_fusion.7), channel_id=1, source_target_pairs={{0,64},{32,96},{64,0},{96,32},{1,65},{33,97},{65,1},{97,33},{2,66}... | collective-permute-start | bytes 786440 | tf_op jit(solution)/shard_map/ppermute | solution.py:429
  659.3 7.8 %collective-permute-start.12 = (bf16[1,128,1,256]{3,1,2,0:T(8,128)(2,1)S(1)}, bf16[1,128,1,256]{3,1,2,0:T(8,128)(2,1)S(1)}, u32[]{:S(2)}, u32[]{:S(2)}) collective-permute-start(bf16[1,128,1,256]{3,1,2,0:T(8,128)(2,1)S(1)} %select_convert_fusion.9), channel_id=1, source_target_pairs={{0,16},{16,0},{1,17},{17,1},{2,18},{18,2},{3,19},{19,3},{4,20},{20... | collective-permute-start | bytes 196616 | tf_op jit(solution)/shard_map/ppermute | solution.py:429
  667.1 36.5 %collective-permute-start.7 = (bf16[4,256,3,1,128]{4,3,2,1,0:T(2,128)(2,1)}, bf16[4,256,3,1,128]{4,3,2,1,0:T(2,128)(2,1)}, u32[]{:S(2)}, u32[]{:S(2)}) collective-permute-start(bf16[4,256,3,1,128]{4,3,2,1,0:T(2,128)(2,1)} %copy.41), channel_id=1, source_target_pairs={{0,64},{32,96},{64,0},{96,32},{1,65},{33,97},{65,1},{97,33},{2,66}... | collective-permute-start | bytes 2359304 | tf_op jit(solution)/shard_map/ppermute | solution.py:429
  671.1 36.8 %collective-permute-start = (f32[8,8,192]{2,0,1:T(8,128)S(1)}, f32[8,8,192]{2,0,1:T(8,128)S(1)}, u32[]{:S(2)}, u32[]{:S(2)}) collective-permute-start(f32[8,8,192]{2,0,1:T(8,128)S(1)} %slice_select_fusion.2), channel_id=1, source_target_pairs={{0,8},{1,9},{2,10},{3,11},{4,12},{5,13},{6,14},{7,15},{8,0},{9,1},... | collective-permute-start | bytes 147464 | tf_op jit(solution)/shard_map/ppermute | solution.py:429
  708.0 4.0 collective-permute-start.1
  710.3 5.0 collective-permute-start.8
  712.1 5.6 collective-permute-start.2
  717.7 3.7 collective-permute-start.3
  719.5 9.4 %collective-permute-start.9 = (bf16[1,256,3,1,128]{4,3,2,1,0:T(2,128)(2,1)S(1)}, bf16[1,256,3,1,128]{4,3,2,1,0:T(2,128)(2,1)S(1)}, u32[]{:S(2)}, u32[]{:S(2)}) collective-permute-start(bf16[1,256,3,1,128]{4,3,2,1,0:T(2,128)(2,1)S(1)} %fusion.75), channel_id=1, source_target_pairs={{0,16},{16,0},{1,17},{17,1},{2,18},{18,2},{3,19},{19,3},{4,20},{20... | collective-permute-start | bytes 589832 | tf_op jit(solution)/shard_map/ppermute | solution.py:429
  721.4 8.9 %collective-permute-start.4 = (f32[1,4,192]{2,0,1:T(1,128)S(1)}, f32[1,4,192]{2,0,1:T(1,128)S(1)}, u32[]{:S(2)}, u32[]{:S(2)}) collective-permute-start(f32[1,4,192]{2,0,1:T(1,128)S(1)} %broadcast_select_fusion.8), channel_id=1, source_target_pairs={{0,64},{32,96},{64,0},{96,32},{1,65},{33,97},{65,1},{97,33},{2,66}... | collective-permute-start | bytes 9224 | tf_op jit(solution)/shard_map/ppermute | solution.py:429
  731.6 5.2 collective-permute-start.6
  (44 other events, 1391.3 us)
Sparse Core Ops, SparseCore 0:
  12.4 71.8 all-gather.4
  86.4 70.3 all-gather.6
  160.3 84.6 reduce-scatter.3
  247.9 70.0 all-gather.8
  337.8 84.7 reduce-scatter.5
  426.6 69.9 all-gather.10
  536.4 123.2 reduce-scatter.7

commit v6 on v5

--- a/solution.py
+++ b/solution.py
@@ -307,7 +307,8 @@
     feed_part = jnp.einsum(
         "rsf,fd->rsd", feed_input, w_out, preferred_element_type=jnp.float32
     ).astype(jnp.bfloat16)
-    feed_part, second_grad = lax.optimization_barrier((feed_part, second_grad))
+    feed_buffer = jnp.concatenate([jnp.zeros_like(feed_part), feed_part], 2)
+    feed_buffer, second_grad = lax.optimization_barrier((feed_buffer, second_grad))
     norm_two_back = jax.vjp(layer_norm, middle, ln2_gain, ln2_bias)[1]
     middle_part, grad_ln2_gain, grad_ln2_bias = norm_two_back(second_grad)
     middle_grad = upstream.astype(jnp.float32) + middle_part
@@ -340,19 +341,15 @@
         joint_rows.reshape(seq_total * seq_count, 3 * local_width),
         preferred_element_type=jnp.float32,
     )
-    piece = joint_rows
     normed_part = jnp.einsum(
-        "rsc,dc->rsd", piece, joint_weight, preferred_element_type=jnp.float32
+        "rsc,dc->rsd", joint_rows, joint_weight, preferred_element_type=jnp.float32
     ).astype(jnp.bfloat16)
-    both = lax.psum_scatter(
-        jnp.concatenate([normed_part, feed_part], 2), "tensor", scatter_dimension=0, tiled=True
-    ).astype(jnp.float32)
-    normed_grad = both[:, :, :model_width]
-    feed = both[:, :, model_width:] + b_out
-    output = (middle + feed).astype(jnp.bfloat16)
-    norm_one_back = jax.vjp(layer_norm, inputs, ln1_gain, ln1_bias)[1]
-    input_part, grad_ln1_gain, grad_ln1_bias = norm_one_back(normed_grad)
-    input_grad = (middle_grad + input_part).astype(jnp.bfloat16)
+    joint_sums = jnp.sum(joint_rows, axis=(0, 1), dtype=jnp.float32)
+    grad_ln1_bias = jnp.dot(
+        joint_weight.astype(jnp.float32), joint_sums, precision=lax.Precision.HIGHEST
+    )
+    merged = lax.dynamic_update_slice(feed_buffer, normed_part, (0, 0, 0))
+    both = lax.psum_scatter(merged, "tensor", scatter_dimension=0, tiled=True)
     summed = (
         halving_sum(grad_w_qkv.reshape(model_width, 3, local_heads, head_size) * factor, 0),
         halving_sum(weight_grad.reshape(local_heads, head_size, model_width) * factor, 2),
@@ -368,52 +365,69 @@
         tensor_rank * local_width,
         1,
     )
-    shard_count = group_count * lax.axis_size("dp")
-    vectors = (
-        grad_ln1_gain,
-        grad_ln1_bias,
-        grad_b_o,
-        grad_ln2_gain,
-        grad_ln2_bias,
-        grad_b_out,
-        joint_full[0],
-        joint_full[1],
-        in_full,
-    )
+    early = reduce_vectors(
+        (
+            grad_ln1_bias,
+            grad_b_o,
+            grad_ln2_gain,
+            grad_ln2_bias,
+            grad_b_out,
+            joint_full[0],
+            joint_full[1],
+            in_full,
+        ),
+        factor,
+    )
+    both, summed, early = lax.optimization_barrier((both, summed, early))
+    both = both.astype(jnp.float32)
+    normed_grad = both[:, :, :model_width]
+    feed = both[:, :, model_width:] + b_out
+    output = (middle + feed).astype(jnp.bfloat16)
+    norm_one_back = jax.vjp(layer_norm, inputs, ln1_gain, ln1_bias)[1]
+    input_part, grad_ln1_gain, _ = norm_one_back(normed_grad)
+    input_grad = (middle_grad + input_part).astype(jnp.bfloat16)
+    (late,) = reduce_vectors((grad_ln1_gain,), factor)
+    return (
+        output,
+        input_grad,
+        late,
+        early[0],
+        summed[0],
+        jnp.stack((early[5], early[6])),
+        summed[1],
+        early[1],
+        early[2],
+        early[3],
+        summed[2],
+        early[7],
+        summed[3],
+        early[4],
+    )
+
+
+def reduce_vectors(vectors, factor):
+    tensor_count = lax.axis_size("tensor")
+    group_count = lax.axis_size("group")
+    dp_count = lax.axis_size("dp")
     pieces = [
-        jnp.transpose(
-            (item * factor).reshape(shard_count, tensor_count, -1), (1, 0, 2)
-        )
+        jnp.transpose((item * factor).reshape(group_count * dp_count, tensor_count, -1), (1, 0, 2))
         for item in vectors
     ]
     widths = [piece.shape[2] for piece in pieces]
     packed = jnp.concatenate(pieces, 2)
-    packed = halving_steps(packed, 0, [("tensor", tensor_count, 8), ("tensor", tensor_count, 4),
-                                       ("tensor", tensor_count, 2), ("tensor", tensor_count, 1)])
-    packed = halving_steps(packed, 1, [("group", group_count, 2), ("group", group_count, 1),
-                                       ("dp", lax.axis_size("dp"), 1)])
+    packed = halving_steps(
+        packed, 0, [("tensor", tensor_count, bit) for bit in (8, 4, 2, 1)]
+    )
+    packed = halving_steps(
+        packed, 1, [("group", group_count, 2), ("group", group_count, 1), ("dp", dp_count, 1)]
+    )
     flat = packed.reshape(-1)
     parts = []
     offset = 0
     for width in widths:
         parts.append(flat[offset : offset + width])
         offset += width
-    return (
-        output,
-        input_grad,
-        parts[0],
-        parts[1],
-        summed[0],
-        jnp.stack((parts[6], parts[7])),
-        summed[1],
-        parts[2],
-        parts[3],
-        parts[4],
-        summed[2],
-        parts[8],
-        summed[3],
-        parts[5],
-    )
+    return tuple(parts)
 
 
 def halving_steps(value, dim, steps, send_type=None):

time: 756 us -> 783 us (1.036)
  waiting for transfers between devices: 468 us -> 493 us
  other arithmetic: 65.3 us -> 51 us
    ppermute x19 -> x26, waiting for transfers between devices: 71.7 us -> 104 us  [halving_steps(): got = lax.ppermute(send, axis, [(i, i ^ bit) for i in range(size)])]
    concatenate x1 -> x0, other arithmetic: 10.6 us -> none  [shards(): jnp.concatenate([normed_part, feed_part], 2)]
    ppermute x19 -> x26, starting transfers between devices: 54.7 us -> 56.7 us  [halving_steps(): got = lax.ppermute(send, axis, [(i, i ^ bit) for i in range(size)])]
  transfers between devices with their start and end apart: 26 -> 33, of which waited for: 18 -> 25; matrix products, arithmetic and copies ran while one was open for 15% -> 14% of each run, Pallas kernels for 2% -> 3%
where the time goes in v6:
time: 783 us; the launch traced here: 773 us
  waiting for transfers between devices  493 us (63%)
  matrix products  89 us (11%)
  starting transfers between devices  57.2 us (7%)
  other arithmetic  51 us (7%)
  Pallas kernels  36.8 us (5%)
  local copies, waits for them, and re-layouts  29.2 us (4%)
  between operations  16.9 us (2%)
    ppermute x26, waiting for transfers between devices, halving_steps(): got = lax.ppermute(send, axis, [(i, i ^ bit) for i in range(size)])  104 us
    reduce_scatter x1, waiting for transfers between devices, shards(): lax.psum_scatter(attention_part, 'tensor', scatter_dimension=0, tiled=True)  77.5 us
    all_gather x1, waiting for transfers between devices, shards(): piece = lax.all_gather(branch_low, 'tensor', axis=0, tiled=True)  70 us
    reduce_scatter x1, waiting for transfers between devices, shards(): lax.psum_scatter(second_part, 'tensor', scatter_dimension=0, tiled=True)  70 us
    all_gather x1, waiting for transfers between devices, shards(): second_full = lax.all_gather(second_low, 'tensor', axis=0, tiled=True)  69.9 us
    all_gather x1, waiting for transfers between devices, shards(): normed_full = lax.all_gather(normed_low, 'tensor', axis=0, tiled=True)  65.3 us
    ppermute x26, starting transfers between devices, halving_steps(): got = lax.ppermute(send, axis, [(i, i ^ bit) for i in range(size)])  56.7 us
    all_gather x1, waiting for transfers between devices, shards(): upstream_full = lax.all_gather(upstream, 'tensor', axis=0, tiled=True)  35.5 us
  transfers between devices with their start and end apart: 33, of which 25 were waited for; matrix products, arithmetic and copies ran while one was open for 14% of the time, Pallas kernels for 3%

profile of v6, /device:TPU:96, one launch (start us, length us, event | category | flops | bytes accessed | tf_op | source)
XLA Modules:
  0.0 772.8 jit_solution(1990684222432848289)
XLA Ops:
  19.5 65.3 %all-gather.5.cloned.1.call-done = bf16[2048,1,2048]{2,0,1:T(8,128)(2,1)} async-done(((bf16[128,1,2048]{2,0,1:T(8,128)(2,1)}), bf16[2048,1,2048]{2,0,1:T(8,128)(2,1)}) %all-gather.5.cloned.1.call-update) | async-done | bytes 8388624 | tf_op jit(solution)/shard_map/all_gather | solution.py:232
  84.8 7.4 fusion.35
  94.2 21.0 %shard_map.254 = (bf16[2048,128]{1,0:T(8,128)(2,1)}, f32[2048,1]{1,0:T(8,128)}) custom-call(s32[1]{0:T(128)} %dynamic_slice.7.len_ref, bf16[2048,128]{1,0:T(8,128)(2,1)} %get-tuple-element.87.q_ref, bf16[2048,128]{1,0:T(8,128)(2,1)} %fusion.70.k_ref, bf16[2048,128]{1,0:T(8,128)(2,1)} %get-tuple-element.86.v_ref), custom_call_target="tpu_custom_call" | custom-call | flops 1207959552 | bytes 2097152 | tf_op jit(solution)/shard_map/pallas_call | solution.py:79
  115.2 6.9 convert_bitcast_fusion.2
  122.0 35.5 %all-gather.7.cloned.1.call-done = bf16[2048,1,2048]{2,0,1:T(8,128)(2,1)} async-done(((bf16[128,1,2048]{2,0,1:T(8,128)(2,1)}), bf16[2048,1,2048]{2,0,1:T(8,128)(2,1)}) %all-gather.7.cloned.1.call-update) | async-done | bytes 8388624 | tf_op jit(solution)/shard_map/all_gather | solution.py:263
  157.7 10.5 %fusion.32 = f32[2048,1,512]{2,0,1:T(8,128)} fusion(bf16[512,2048]{1,0:T(8,128)(2,1)} %param.28, bf16[2048,1,2048]{2,0,1:T(8,128)(2,1)} %all-gather.7.cloned.1.call-done), kind=kOutput, calls=%fused_computation.38 | convolution fusion | flops 4294967296 | bytes 14680064 | tf_op jit(solution)/shard_map/rsd,fd->rsf/dot_general | solution.py:275
  168.2 77.5 %reduce-scatter.4.cloned.1.call-done = bf16[128,1,2048]{2,0,1:T(8,128)(2,1)} async-done(((bf16[2048,1,2048]{2,0,1:T(8,128)(2,1)}), bf16[128,1,2048]{2,0,1:T(8,128)(2,1)}) %reduce-scatter.4.cloned.1.call-update) | async-done | bytes 524304 | tf_op jit(solution)/shard_map/reduce_scatter | solution.py:269
  248.9 69.9 %all-gather.9.cloned.1.call-done = bf16[2048,1,2048]{2,0,1:T(8,128)(2,1)} async-done(((bf16[128,1,2048]{2,0,1:T(8,128)(2,1)}), bf16[2048,1,2048]{2,0,1:T(8,128)(2,1)}) %all-gather.9.cloned.1.call-update) | async-done | bytes 8388624 | tf_op jit(solution)/shard_map/all_gather | solution.py:278
  318.8 7.0 fusion.6
  331.5 6.9 convert_bitcast_fusion.1
  346.4 7.0 concatenate.12
  353.4 70.0 %reduce-scatter.6.cloned.1.call-done = bf16[128,1,2048]{2,0,1:T(8,128)(2,1)} async-done(((bf16[2048,1,2048]{2,0,1:T(8,128)(2,1)}), bf16[128,1,2048]{2,0,1:T(8,128)(2,1)}) %reduce-scatter.6.cloned.1.call-update) | async-done | bytes 524304 | tf_op jit(solution)/shard_map/reduce_scatter | solution.py:304
  427.2 70.0 %all-gather.11.cloned.1.call-done = bf16[2048,1,2048]{2,0,1:T(8,128)(2,1)} async-done(((bf16[128,1,2048]{2,0,1:T(8,128)(2,1)}), bf16[2048,1,2048]{2,0,1:T(8,128)(2,1)}) %all-gather.11.cloned.1.call-update) | async-done | bytes 8388624 | tf_op jit(solution)/shard_map/all_gather | solution.py:318
  503.8 15.9 %shard_map.255 = (bf16[2048,128]{1,0:T(8,128)(2,1)}, bf16[2048,128]{1,0:T(8,128)(2,1)}, bf16[2048,128]{1,0:T(8,128)(2,1)}) custom-call(s32[1]{0:T(128)} %dynamic_slice.7.len_ref, bf16[2048,128]{1,0:T(8,128)(2,1)} %get-tuple-element.87.q_ref, bf16[2048,128]{1,0:T(8,128)(2,1)} %fusion.70.k_ref, bf16[2048,128]{1,0:T(8,128)(2,1)} %get-tuple-element.86.v_ref, ...), custom_call_target="tpu_custom_call" | custom-call | flops 2415919104 | bytes 4194304 | tf_op jit(solution)/shard_map/pallas_call | solution.py:171
  523.7 9.8 %bitcast_dynamic-update-slice_fusion = bf16[2048,1,4096]{2,0,1:T(8,128)(2,1)} fusion(bf16[2048,1,4096]{2,0,1:T(8,128)(2,1)} %concatenate.12, bf16[2048,384]{0,1:T(8,128)(2,1)} %bitcast.181, bf16[2048,384]{0,1:T(8,128)(2,1)} %bitcast.174), kind=kOutput, calls=%fused_computation | convolution fusion | flops 3225419776 | bytes 11534336 | tf_op jit(solution)/shard_map/rsc,dc->rsd/dot_general | solution.py:344
  536.9 8.5 %fusion.26 = f32[512,2048]{1,0:T(8,128)S(1)} fusion(bf16[2048,1,2048]{2,0,1:T(8,128)(2,1)} %all-gather.7.cloned.1.call-done, f32[]{:T(128)S(6)} %div.106, f32[2048,512]{1,0:T(8,128)} %copy-done.14, f32[512]{0:T(512)S(1)} %copy-done.30), kind=kOutput, calls=%fused_computation.36 | convolution fusion | flops 4306501632 | bytes 16779268 | tf_op jit(solution)/shard_map/rsf,rsd->fd/dot_general | solution.py:289
  547.5 7.1 fusion.29
  564.6 11.3 %collective-permute-done.6 = bf16[4,256,512]{2,1,0:T(8,128)(2,1)} collective-permute-done((bf16[4,256,512]{2,1,0:T(8,128)(2,1)}, bf16[4,256,512]{2,1,0:T(8,128)(2,1)}, u32[]{:S(2)}, u32[]{:S(2)}) %collective-permute-start.6) | collective-permute-done | bytes 1048608 | tf_op jit(solution)/shard_map/ppermute | solution.py:443
  577.8 13.0 %collective-permute-start.7 = (bf16[2,256,512]{2,1,0:T(8,128)(2,1)S(1)}, bf16[2,256,512]{2,1,0:T(8,128)(2,1)S(1)}, u32[]{:S(2)}, u32[]{:S(2)}) collective-permute-start(bf16[2,256,512]{2,1,0:T(8,128)(2,1)S(1)} %select_convert_fusion.4), channel_id=1, source_target_pairs={{0,32},{32,0},{64,96},{96,64},{1,33},{33,1},{65,97},{97,65},{2,34}... | collective-permute-start | bytes 1572872 | tf_op jit(solution)/shard_map/ppermute | solution.py:443
  590.8 7.6 collective-permute-done.9
  607.5 12.5 %collective-permute-start.8 = (bf16[1,256,512]{2,1,0:T(8,128)(2,1)S(1)}, bf16[1,256,512]{2,1,0:T(8,128)(2,1)S(1)}, u32[]{:S(2)}, u32[]{:S(2)}) collective-permute-start(bf16[1,256,512]{2,1,0:T(8,128)(2,1)S(1)} %select_convert_fusion.6), channel_id=1, source_target_pairs={{0,16},{16,0},{1,17},{17,1},{2,18},{18,2},{3,19},{19,3},{4,20},{20... | collective-permute-start | bytes 786440 | tf_op jit(solution)/shard_map/ppermute | solution.py:443
  640.7 8.5 %fusion.38 = f32[2048,3,128]{2,0,1:T(8,128)S(1)} fusion(bf16[2048,1,2048]{2,0,1:T(8,128)(2,1)} %all-gather.5.cloned.1.call-done, bf16[2048,1,3,128]{0,3,2,1:T(8,128)(2,1)} %copy.37, f32[]{:T(128)S(6)} %div.106), kind=kOutput, calls=%fused_computation.41 | convolution fusion | flops 3222011904 | bytes 13107204 | tf_op jit(solution)/shard_map/rd,rc->dc/dot_general | solution.py:338
  677.4 32.1 %collective-permute-done = bf16[4,256,3,1,128]{4,3,2,1,0:T(2,128)(2,1)S(1)} collective-permute-done((bf16[4,256,3,1,128]{4,3,2,1,0:T(2,128)(2,1)S(1)}, bf16[4,256,3,1,128]{4,3,2,1,0:T(2,128)(2,1)S(1)}, u32[]{:S(2)}, u32[]{:S(2)}) %collective-permute-start) | collective-permute-done | bytes 786464 | tf_op jit(solution)/shard_map/ppermute | solution.py:443
  719.6 10.0 %collective-permute-done.2 = bf16[1,256,3,1,128]{4,3,2,1,0:T(2,128)(2,1)S(1)} collective-permute-done((bf16[1,256,3,1,128]{4,3,2,1,0:T(2,128)(2,1)S(1)}, bf16[1,256,3,1,128]{4,3,2,1,0:T(2,128)(2,1)S(1)}, u32[]{:S(2)}, u32[]{:S(2)}) %collective-permute-start.2) | collective-permute-done | bytes 196640 | tf_op jit(solution)/shard_map/ppermute | solution.py:443
  (267 shorter events, 164.7 us)
Async XLA Ops:
  7.2 77.6 %all-gather.5.cloned.1.call-start = ((), (), s32[]{:S(2)}) async-start(), calls=%async_computation.3 | async-start | bytes 8912896 | tf_op jit(solution)/shard_map/all_gather | solution.py:232
  12.8 144.8 %all-gather.7.cloned.1.call-start = ((), (), s32[]{:S(2)}) async-start(), calls=%async_computation.4 | async-start | bytes 8912896 | tf_op jit(solution)/shard_map/all_gather | solution.py:263
  16.8 228.9 %reduce-scatter.4.cloned.1.call-start = ((), (), s32[]{:S(2)}) async-start(), calls=%async_computation.5 | async-start | bytes 8912896 | tf_op jit(solution)/shard_map/reduce_scatter | solution.py:269
  157.6 161.2 %all-gather.9.cloned.1.call-start = ((), (), s32[]{:S(2)}) async-start(), calls=%async_computation.6 | async-start | bytes 8912896 | tf_op jit(solution)/shard_map/all_gather | solution.py:278
  248.6 174.8 %reduce-scatter.6.cloned.1.call-start = ((), (), s32[]{:S(2)}) async-start(), calls=%async_computation.7 | async-start | bytes 8912896 | tf_op jit(solution)/shard_map/reduce_scatter | solution.py:304
  338.5 158.7 %all-gather.11.cloned.1.call-start = ((), (), s32[]{:S(2)}) async-start(), calls=%async_computation.8 | async-start | bytes 8912896 | tf_op jit(solution)/shard_map/all_gather | solution.py:318
  427.1 303.9 %reduce-scatter.8.cloned.1.call-start = ((), (), s32[]{:S(2)}) async-start(), calls=%async_computation.9 | async-start | bytes 17825792 | tf_op jit(solution)/shard_map/reduce_scatter | solution.py:352
  556.0 20.0 %collective-permute-start.6 = (bf16[4,256,512]{2,1,0:T(8,128)(2,1)}, bf16[4,256,512]{2,1,0:T(8,128)(2,1)}, u32[]{:S(2)}, u32[]{:S(2)}) collective-permute-start(bf16[4,256,512]{2,1,0:T(8,128)(2,1)} %bitcast.37), channel_id=1, source_target_pairs={{0,64},{32,96},{64,0},{96,32},{1,65},{33,97},{65,1},{97,33},{2,66}... | collective-permute-start | bytes 3145736 | tf_op jit(solution)/shard_map/ppermute | solution.py:443
  560.5 37.9 %collective-permute-start.9 = (bf16[512,4,256]{2,0,1:T(8,128)(2,1)}, bf16[512,4,256]{2,0,1:T(8,128)(2,1)}, u32[]{:S(2)}, u32[]{:S(2)}) collective-permute-start(bf16[512,4,256]{2,0,1:T(8,128)(2,1)} %select_convert_fusion), channel_id=1, source_target_pairs={{0,64},{32,96},{64,0},{96,32},{1,65},{33,97},{65,1},{97,33},{2,66}... | collective-permute-start | bytes 3145736 | tf_op jit(solution)/shard_map/ppermute | solution.py:443
  577.8 29.4 %collective-permute-start.7 = (bf16[2,256,512]{2,1,0:T(8,128)(2,1)S(1)}, bf16[2,256,512]{2,1,0:T(8,128)(2,1)S(1)}, u32[]{:S(2)}, u32[]{:S(2)}) collective-permute-start(bf16[2,256,512]{2,1,0:T(8,128)(2,1)S(1)} %select_convert_fusion.4), channel_id=1, source_target_pairs={{0,32},{32,0},{64,96},{96,64},{1,33},{33,1},{65,97},{97,65},{2,34}... | collective-permute-start | bytes 1572872 | tf_op jit(solution)/shard_map/ppermute | solution.py:443
  600.5 19.5 %collective-permute-start.10 = (bf16[512,2,256]{2,0,1:T(8,128)(2,1)S(1)}, bf16[512,2,256]{2,0,1:T(8,128)(2,1)S(1)}, u32[]{:S(2)}, u32[]{:S(2)}) collective-permute-start(bf16[512,2,256]{2,0,1:T(8,128)(2,1)S(1)} %select_convert_fusion.3), channel_id=1, source_target_pairs={{0,32},{32,0},{64,96},{96,64},{1,33},{33,1},{65,97},{97,65},{2,34}... | collective-permute-start | bytes 1572872 | tf_op jit(solution)/shard_map/ppermute | solution.py:443
  607.5 19.4 %collective-permute-start.8 = (bf16[1,256,512]{2,1,0:T(8,128)(2,1)S(1)}, bf16[1,256,512]{2,1,0:T(8,128)(2,1)S(1)}, u32[]{:S(2)}, u32[]{:S(2)}) collective-permute-start(bf16[1,256,512]{2,1,0:T(8,128)(2,1)S(1)} %select_convert_fusion.6), channel_id=1, source_target_pairs={{0,16},{16,0},{1,17},{17,1},{2,18},{18,2},{3,19},{19,3},{4,20},{20... | collective-permute-start | bytes 786440 | tf_op jit(solution)/shard_map/ppermute | solution.py:443
  622.0 12.9 %collective-permute-start.11 = (bf16[512,1,256]{2,0,1:T(8,128)(2,1)}, bf16[512,1,256]{2,0,1:T(8,128)(2,1)S(1)}, u32[]{:S(2)}, u32[]{:S(2)}) collective-permute-start(bf16[512,1,256]{2,0,1:T(8,128)(2,1)} %select_convert_fusion.5), channel_id=1, source_target_pairs={{0,16},{16,0},{1,17},{17,1},{2,18},{18,2},{3,19},{19,3},{4,20},{20... | collective-permute-start | bytes 786440 | tf_op jit(solution)/shard_map/ppermute | solution.py:443
  631.9 6.9 collective-permute-start.12
  638.8 10.3 %collective-permute-start.13 = (f32[4,8,176]{2,0,1:T(4,128)S(1)}, f32[4,8,176]{2,0,1:T(4,128)S(1)}, u32[]{:S(2)}, u32[]{:S(2)}) collective-permute-start(f32[4,8,176]{2,0,1:T(4,128)S(1)} %slice_select_fusion.4), channel_id=1, source_target_pairs={{0,4},{1,5},{2,6},{3,7},{4,0},{5,1},{6,2},{7,3},{8,12},{9,13},{10,... | collective-permute-start | bytes 67592 | tf_op jit(solution)/shard_map/ppermute | solution.py:443
  649.2 5.3 collective-permute-start.14
  663.3 7.7 collective-permute-start.18
  667.6 9.3 %collective-permute-start.3 = (bf16[1,128,4,256]{3,1,2,0:T(8,128)(2,1)S(1)}, bf16[1,128,4,256]{3,1,2,0:T(8,128)(2,1)S(1)}, u32[]{:S(2)}, u32[]{:S(2)}) collective-permute-start(bf16[1,128,4,256]{3,1,2,0:T(8,128)(2,1)S(1)} %select_convert_fusion.7), channel_id=1, source_target_pairs={{0,64},{32,96},{64,0},{96,32},{1,65},{33,97},{65,1},{97,33},{2,66}... | collective-permute-start | bytes 786440 | tf_op jit(solution)/shard_map/ppermute | solution.py:443
  668.9 40.5 %collective-permute-start = (bf16[4,256,3,1,128]{4,3,2,1,0:T(2,128)(2,1)S(1)}, bf16[4,256,3,1,128]{4,3,2,1,0:T(2,128)(2,1)S(1)}, u32[]{:S(2)}, u32[]{:S(2)}) collective-permute-start(bf16[4,256,3,1,128]{4,3,2,1,0:T(2,128)(2,1)S(1)} %copy.39), channel_id=1, source_target_pairs={{0,64},{32,96},{64,0},{96,32},{1,65},{33,97},{65,1},{97,33},{2,66}... | collective-permute-start | bytes 2359304 | tf_op jit(solution)/shard_map/ppermute | solution.py:443
  677.0 35.7 %collective-permute-start.4 = (bf16[1,128,2,256]{3,1,2,0:T(8,128)(2,1)S(1)}, bf16[1,128,2,256]{3,1,2,0:T(8,128)(2,1)S(1)}, u32[]{:S(2)}, u32[]{:S(2)}) collective-permute-start(bf16[1,128,2,256]{3,1,2,0:T(8,128)(2,1)S(1)} %select_convert_fusion.8), channel_id=1, source_target_pairs={{0,32},{32,0},{64,96},{96,64},{1,33},{33,1},{65,97},{97,65},{2,34}... | collective-permute-start | bytes 393224 | tf_op jit(solution)/shard_map/ppermute | solution.py:443
  712.9 6.1 collective-permute-start.5
  716.9 12.7 %collective-permute-start.2 = (bf16[1,256,3,1,128]{4,3,2,1,0:T(2,128)(2,1)S(1)}, bf16[1,256,3,1,128]{4,3,2,1,0:T(2,128)(2,1)S(1)}, u32[]{:S(2)}, u32[]{:S(2)}) collective-permute-start(bf16[1,256,3,1,128]{4,3,2,1,0:T(2,128)(2,1)S(1)} %fusion.75), channel_id=1, source_target_pairs={{0,16},{16,0},{1,17},{17,1},{2,18},{18,2},{3,19},{19,3},{4,20},{20... | collective-permute-start | bytes 589832 | tf_op jit(solution)/shard_map/ppermute | solution.py:443
  734.0 5.5 collective-permute-start.19
  743.3 5.2 collective-permute-start.21
  (48 other events, 1150.8 us)
Sparse Core Ops, SparseCore 0:
  12.9 71.8 all-gather.4
  87.0 70.5 all-gather.6
  161.0 84.6 reduce-scatter.3
  248.8 70.0 all-gather.8
  338.6 84.7 reduce-scatter.5
  427.2 69.9 all-gather.10
  533.6 121.5 reduce-scatter.7

commit v7 on v6

--- a/solution.py
+++ b/solution.py
@@ -315,6 +315,11 @@
     branch_low = middle_grad.astype(jnp.bfloat16)
     grad_b_o = jnp.sum(branch_low, axis=(0, 1), dtype=jnp.float32)
     grad_b_out = jnp.sum(upstream, axis=(0, 1), dtype=jnp.float32)
+    summed_in = halving_sum(grad_w_in * factor, 0)
+    summed_out = halving_sum(grad_w_out * factor, 1)
+    summed_in, summed_out, branch_low = lax.optimization_barrier(
+        (summed_in, summed_out, branch_low)
+    )
     piece = lax.all_gather(branch_low, "tensor", axis=0, tiled=True)
     weight_grad = jnp.einsum("rse,rsd->ed", attended, piece, preferred_element_type=jnp.float32)
     part = jnp.einsum("rsd,ed->rse", piece, out_weight, preferred_element_type=jnp.float32)
@@ -351,10 +356,10 @@
     merged = lax.dynamic_update_slice(feed_buffer, normed_part, (0, 0, 0))
     both = lax.psum_scatter(merged, "tensor", scatter_dimension=0, tiled=True)
     summed = (
-        halving_sum(grad_w_qkv.reshape(model_width, 3, local_heads, head_size) * factor, 0),
+        halving_sum(grad_w_qkv * factor, 0).reshape(-1, 3, local_heads, head_size),
         halving_sum(weight_grad.reshape(local_heads, head_size, model_width) * factor, 2),
-        halving_sum(grad_w_in * factor, 0),
-        halving_sum(grad_w_out * factor, 1),
+        summed_in,
+        summed_out,
     )
     in_full = lax.dynamic_update_slice_in_dim(
         jnp.zeros((hidden * tensor_count,), jnp.float32), grad_b_in, tensor_rank * hidden, 0

time: 783 us -> 713 us (0.911)
  waiting for transfers between devices: 493 us -> 451 us
  starting transfers between devices: 57.2 us -> 45.9 us
    reduce_scatter x1, waiting for transfers between devices: 70 us -> 0.01 us  [shards(): lax.psum_scatter(second_part, 'tensor', scatter_dimension=0, tiled=True)]
    reduce_scatter x1, waiting for transfers between devices: 0.01 us -> 35.6 us  [shards(): both = lax.psum_scatter(merged, 'tensor', scatter_dimension=0, tiled=True)]
    ppermute x26, starting transfers between devices: 56.7 us -> 45.1 us  [halving_steps(): got = lax.ppermute(send, axis, [(i, i ^ bit) for i in range(size)])]
    ppermute x26, waiting for transfers between devices: 104 us -> 94.5 us  [halving_steps(): got = lax.ppermute(send, axis, [(i, i ^ bit) for i in range(size)])]
where the time goes in v7:
time: 713 us; the launch traced here: 701 us
  waiting for transfers between devices  451 us (63%)
  matrix products  86.7 us (12%)
  starting transfers between devices  45.9 us (6%)
  other arithmetic  45.3 us (6%)
  Pallas kernels  31.1 us (4%)
  local copies, waits for them, and re-layouts  25 us (4%)
  between operations  16.6 us (2%)
    ppermute x26, waiting for transfers between devices, halving_steps(): got = lax.ppermute(send, axis, [(i, i ^ bit) for i in range(size)])  94.5 us
    reduce_scatter x1, waiting for transfers between devices, shards(): lax.psum_scatter(attention_part, 'tensor', scatter_dimension=0, tiled=True)  77.4 us
    all_gather x1, waiting for transfers between devices, shards(): piece = lax.all_gather(branch_low, 'tensor', axis=0, tiled=True)  70 us
    all_gather x1, waiting for transfers between devices, shards(): second_full = lax.all_gather(second_low, 'tensor', axis=0, tiled=True)  70 us
    all_gather x1, waiting for transfers between devices, shards(): normed_full = lax.all_gather(normed_low, 'tensor', axis=0, tiled=True)  65.4 us
    ppermute x26, starting transfers between devices, halving_steps(): got = lax.ppermute(send, axis, [(i, i ^ bit) for i in range(size)])  45.1 us
    all_gather x1, waiting for transfers between devices, shards(): upstream_full = lax.all_gather(upstream, 'tensor', axis=0, tiled=True)  37.8 us
    reduce_scatter x1, waiting for transfers between devices, shards(): both = lax.psum_scatter(merged, 'tensor', scatter_dimension=0, tiled=True)  35.6 us
  transfers between devices with their start and end apart: 33, of which 25 were waited for; matrix products, arithmetic and copies ran while one was open for 14% of the time, Pallas kernels for 3%

profile of v7, /device:TPU:96, one launch (start us, length us, event | category | flops | bytes accessed | tf_op | source)
XLA Modules:
  0.0 701.4 jit_solution(6677150995167023007)
XLA Ops:
  18.9 65.4 %all-gather.5.cloned.1.call-done = bf16[2048,1,2048]{2,0,1:T(8,128)(2,1)} async-done(((bf16[128,1,2048]{2,0,1:T(8,128)(2,1)}), bf16[2048,1,2048]{2,0,1:T(8,128)(2,1)}) %all-gather.5.cloned.1.call-update) | async-done | bytes 8388624 | tf_op jit(solution)/shard_map/all_gather | solution.py:232
  84.3 7.4 %fusion.38 = f32[2048,1,3,128]{3,0,2,1:T(8,128)S(1)} fusion(bf16[2048,1,2048]{2,0,1:T(8,128)(2,1)} %all-gather.5.cloned.1.call-done, bf16[2048,3,1,128]{0,3,1,2:T(8,128)(2,1)} %copy.33), kind=kOutput, calls=%fused_computation.41 | convolution fusion | flops 3221225472 | bytes 13107200 | tf_op jit(solution)/shard_map/dot_general | solution.py:234
  93.7 18.6 %shard_map.254 = (bf16[2048,128]{1,0:T(8,128)(2,1)}, f32[2048,1]{1,0:T(8,128)}) custom-call(s32[1]{0:T(128)} %dynamic_slice.7.len_ref, bf16[2048,128]{1,0:T(8,128)(2,1)} %get-tuple-element.93.q_ref, bf16[2048,128]{1,0:T(8,128)(2,1)} %fusion.67.k_ref, bf16[2048,128]{1,0:T(8,128)(2,1)} %get-tuple-element.92.v_ref), custom_call_target="tpu_custom_call" | custom-call | flops 1207959552 | bytes 2097152 | tf_op jit(solution)/shard_map/pallas_call | solution.py:79
  112.3 6.6 convert_bitcast_fusion.2
  118.9 37.8 %all-gather.7.cloned.1.call-done = bf16[2048,1,2048]{2,0,1:T(8,128)(2,1)} async-done(((bf16[128,1,2048]{2,0,1:T(8,128)(2,1)}), bf16[2048,1,2048]{2,0,1:T(8,128)(2,1)}) %all-gather.7.cloned.1.call-update) | async-done | bytes 8388624 | tf_op jit(solution)/shard_map/all_gather | solution.py:263
  156.8 10.5 %fusion.32 = f32[2048,1,512]{2,0,1:T(8,128)} fusion(bf16[512,2048]{1,0:T(8,128)(2,1)} %param.28, bf16[2048,1,2048]{2,0,1:T(8,128)(2,1)} %all-gather.7.cloned.1.call-done), kind=kOutput, calls=%fused_computation.38 | convolution fusion | flops 4294967296 | bytes 14680064 | tf_op jit(solution)/shard_map/rsd,fd->rsf/dot_general | solution.py:275
  167.4 77.4 %reduce-scatter.4.cloned.1.call-done = bf16[128,1,2048]{2,0,1:T(8,128)(2,1)} async-done(((bf16[2048,1,2048]{2,0,1:T(8,128)(2,1)}), bf16[128,1,2048]{2,0,1:T(8,128)(2,1)}) %reduce-scatter.4.cloned.1.call-update) | async-done | bytes 524304 | tf_op jit(solution)/shard_map/reduce_scatter | solution.py:269
  247.9 70.0 %all-gather.9.cloned.1.call-done = bf16[2048,1,2048]{2,0,1:T(8,128)(2,1)} async-done(((bf16[128,1,2048]{2,0,1:T(8,128)(2,1)}), bf16[2048,1,2048]{2,0,1:T(8,128)(2,1)}) %all-gather.9.cloned.1.call-update) | async-done | bytes 8388624 | tf_op jit(solution)/shard_map/all_gather | solution.py:278
  317.9 7.0 fusion.6
  330.7 6.9 convert_bitcast_fusion.1
  341.0 8.5 %fusion.26 = f32[512,2048]{1,0:T(8,128)S(1)} fusion(bf16[2048,1,2048]{2,0,1:T(8,128)(2,1)} %all-gather.7.cloned.1.call-done, f32[]{:T(128)S(6)} %div.103, f32[2048,512]{1,0:T(8,128)} %copy-done.9, f32[512]{0:T(512)S(1)} %copy-done.20), kind=kOutput, calls=%fused_computation.36 | convolution fusion | flops 4306501632 | bytes 16779268 | tf_op jit(solution)/shard_map/rsf,rsd->fd/dot_general | solution.py:289
  351.5 7.0 %fusion.29 = f32[2048,512]{1,0:T(8,128)S(1)} fusion(bf16[2048,512]{1,0:T(8,128)(2,1)S(1)} %copy-done.13, bf16[2048,1,2048]{2,0,1:T(8,128)(2,1)} %all-gather.9.cloned.1.call-done, f32[]{:T(128)S(6)} %div.103), kind=kOutput, calls=%fused_computation.37 | convolution fusion | flops 4296015872 | bytes 14680068 | tf_op jit(solution)/shard_map/rd,rf->df/dot_general | solution.py:293
  368.6 17.9 %collective-permute-done = bf16[4,256,512]{2,1,0:T(8,128)(2,1)} collective-permute-done((bf16[4,256,512]{2,1,0:T(8,128)(2,1)}, bf16[4,256,512]{2,1,0:T(8,128)(2,1)}, u32[]{:S(2)}, u32[]{:S(2)}) %collective-permute-start) | collective-permute-done | bytes 1048608 | tf_op jit(solution)/shard_map/ppermute | solution.py:448
  388.4 19.5 %collective-permute-done.3 = bf16[512,4,256]{2,0,1:T(8,128)(2,1)} collective-permute-done((bf16[512,4,256]{2,0,1:T(8,128)(2,1)}, bf16[512,4,256]{2,0,1:T(8,128)(2,1)}, u32[]{:S(2)}, u32[]{:S(2)}) %collective-permute-start.3) | collective-permute-done | bytes 1048608 | tf_op jit(solution)/shard_map/ppermute | solution.py:448
  419.1 7.0 concatenate.12
  432.8 70.0 %all-gather.11.cloned.1.call-done = bf16[2048,1,2048]{2,0,1:T(8,128)(2,1)} async-done(((bf16[128,1,2048]{2,0,1:T(8,128)(2,1)}), bf16[2048,1,2048]{2,0,1:T(8,128)(2,1)}) %all-gather.11.cloned.1.call-update) | async-done | bytes 8388624 | tf_op jit(solution)/shard_map/all_gather | solution.py:323
  502.8 6.6 fusion.44.do_ref
  509.4 12.4 %shard_map.255 = (bf16[2048,128]{1,0:T(8,128)(2,1)}, bf16[2048,128]{1,0:T(8,128)(2,1)}, bf16[2048,128]{1,0:T(8,128)(2,1)}) custom-call(s32[1]{0:T(128)} %dynamic_slice.7.len_ref, bf16[2048,128]{1,0:T(8,128)(2,1)} %get-tuple-element.93.q_ref, bf16[2048,128]{1,0:T(8,128)(2,1)} %fusion.67.k_ref, bf16[2048,128]{1,0:T(8,128)(2,1)} %get-tuple-element.92.v_ref, ...), custom_call_target="tpu_custom_call" | custom-call | flops 2415919104 | bytes 4194304 | tf_op jit(solution)/shard_map/pallas_call | solution.py:171
  525.2 9.8 %bitcast_dynamic-update-slice_fusion = bf16[2048,1,4096]{2,0,1:T(8,128)(2,1)} fusion(bf16[2048,1,4096]{2,0,1:T(8,128)(2,1)} %concatenate.12, bf16[2048,384]{0,1:T(8,128)(2,1)} %bitcast.171, bf16[2048,384]{0,1:T(8,128)(2,1)} %bitcast.165), kind=kOutput, calls=%fused_computation | convolution fusion | flops 3225419776 | bytes 11534336 | tf_op jit(solution)/shard_map/rsc,dc->rsd/dot_general | solution.py:349
  546.4 8.2 %fusion.35 = f32[2048,384]{1,0:T(8,128)S(1)} fusion(bf16[2048,384]{0,1:T(8,128)(2,1)} %bitcast.172, bf16[2048,1,2048]{2,0,1:T(8,128)(2,1)} %all-gather.5.cloned.1.call-done, f32[]{:T(128)S(6)} %div.103), kind=kOutput, calls=%fused_computation.40 | convolution fusion | flops 3222011904 | bytes 13107204 | tf_op jit(solution)/shard_map/rd,rc->dc/dot_general | solution.py:343
  567.7 7.1 %collective-permute-start.17 = (f32[1,2,176]{2,0,1:T(1,128)S(1)}, f32[1,2,176]{2,0,1:T(1,128)S(1)}, u32[]{:S(2)}, u32[]{:S(2)}) collective-permute-start(f32[1,2,176]{2,0,1:T(1,128)S(1)} %broadcast_select_fusion.11), channel_id=1, source_target_pairs={{0,32},{32,0},{64,96},{96,64},{1,33},{33,1},{65,97},{97,65},{2,34}... | collective-permute-start | bytes 4232 | tf_op jit(solution)/shard_map/ppermute | solution.py:448
  575.6 10.1 %collective-permute-start.18 = (f32[1,1,176]{2,0,1:T(1,128)S(1)}, f32[1,1,176]{2,0,1:T(1,128)S(1)}, u32[]{:S(2)}, u32[]{:S(2)}) collective-permute-start(f32[1,1,176]{2,0,1:T(1,128)S(1)} %broadcast_select_fusion.15), channel_id=1, source_target_pairs={{0,16},{16,0},{1,17},{17,1},{2,18},{18,2},{3,19},{19,3},{4,20},{20... | collective-permute-start | bytes 2120 | tf_op jit(solution)/shard_map/ppermute | solution.py:448
  595.5 15.5 %collective-permute-done.6 = bf16[4,256,384]{2,1,0:T(8,128)(2,1)S(1)} collective-permute-done((bf16[4,256,384]{2,1,0:T(8,128)(2,1)S(1)}, bf16[4,256,384]{2,1,0:T(8,128)(2,1)S(1)}, u32[]{:S(2)}, u32[]{:S(2)}) %collective-permute-start.6) | collective-permute-done | bytes 786464 | tf_op jit(solution)/shard_map/ppermute | solution.py:448
  622.8 35.6 %reduce-scatter.8.cloned.1.call-done = bf16[128,1,4096]{2,0,1:T(8,128)(2,1)} async-done(((bf16[2048,1,4096]{2,0,1:T(8,128)(2,1)}), bf16[128,1,4096]{2,0,1:T(8,128)(2,1)}) %reduce-scatter.8.cloned.1.call-update) | async-done | bytes 1048592 | tf_op jit(solution)/shard_map/reduce_scatter | solution.py:357
  (240 shorter events, 141.9 us)
Async XLA Ops:
  7.2 77.1 %all-gather.5.cloned.1.call-start = ((), (), s32[]{:S(2)}) async-start(), calls=%async_computation.3 | async-start | bytes 8912896 | tf_op jit(solution)/shard_map/all_gather | solution.py:232
  12.2 144.5 %all-gather.7.cloned.1.call-start = ((), (), s32[]{:S(2)}) async-start(), calls=%async_computation.4 | async-start | bytes 8912896 | tf_op jit(solution)/shard_map/all_gather | solution.py:263
  16.2 228.5 %reduce-scatter.4.cloned.1.call-start = ((), (), s32[]{:S(2)}) async-start(), calls=%async_computation.5 | async-start | bytes 8912896 | tf_op jit(solution)/shard_map/reduce_scatter | solution.py:269
  156.8 161.1 %all-gather.9.cloned.1.call-start = ((), (), s32[]{:S(2)}) async-start(), calls=%async_computation.6 | async-start | bytes 8912896 | tf_op jit(solution)/shard_map/all_gather | solution.py:278
  247.6 180.3 %reduce-scatter.6.cloned.1.call-start = ((), (), s32[]{:S(2)}) async-start(), calls=%async_computation.7 | async-start | bytes 8912896 | tf_op jit(solution)/shard_map/reduce_scatter | solution.py:304
  337.6 165.2 %all-gather.11.cloned.1.call-start = ((), (), s32[]{:S(2)}) async-start(), calls=%async_computation.8 | async-start | bytes 8912896 | tf_op jit(solution)/shard_map/all_gather | solution.py:323
  359.9 26.6 %collective-permute-start = (bf16[4,256,512]{2,1,0:T(8,128)(2,1)}, bf16[4,256,512]{2,1,0:T(8,128)(2,1)}, u32[]{:S(2)}, u32[]{:S(2)}) collective-permute-start(bf16[4,256,512]{2,1,0:T(8,128)(2,1)} %bitcast.24), channel_id=1, source_target_pairs={{0,64},{32,96},{64,0},{96,32},{1,65},{33,97},{65,1},{97,33},{2,66}... | collective-permute-start | bytes 3145736 | tf_op jit(solution)/shard_map/ppermute | solution.py:448
  364.6 43.3 %collective-permute-start.3 = (bf16[512,4,256]{2,0,1:T(8,128)(2,1)}, bf16[512,4,256]{2,0,1:T(8,128)(2,1)}, u32[]{:S(2)}, u32[]{:S(2)}) collective-permute-start(bf16[512,4,256]{2,0,1:T(8,128)(2,1)} %select_convert_fusion), channel_id=1, source_target_pairs={{0,64},{32,96},{64,0},{96,32},{1,65},{33,97},{65,1},{97,33},{2,66}... | collective-permute-start | bytes 3145736 | tf_op jit(solution)/shard_map/ppermute | solution.py:448
  388.3 21.8 %collective-permute-start.1 = (bf16[2,256,512]{2,1,0:T(8,128)(2,1)S(1)}, bf16[2,256,512]{2,1,0:T(8,128)(2,1)S(1)}, u32[]{:S(2)}, u32[]{:S(2)}) collective-permute-start(bf16[2,256,512]{2,1,0:T(8,128)(2,1)S(1)} %select_convert_fusion.4), channel_id=1, source_target_pairs={{0,32},{32,0},{64,96},{96,64},{1,33},{33,1},{65,97},{97,65},{2,34}... | collective-permute-start | bytes 1572872 | tf_op jit(solution)/shard_map/ppermute | solution.py:448
  410.4 15.7 %collective-permute-start.2 = (bf16[1,256,512]{2,1,0:T(8,128)(2,1)S(1)}, bf16[1,256,512]{2,1,0:T(8,128)(2,1)S(1)}, u32[]{:S(2)}, u32[]{:S(2)}) collective-permute-start(bf16[1,256,512]{2,1,0:T(8,128)(2,1)S(1)} %select_convert_fusion.8), channel_id=1, source_target_pairs={{0,16},{16,0},{1,17},{17,1},{2,18},{18,2},{3,19},{19,3},{4,20},{20... | collective-permute-start | bytes 786440 | tf_op jit(solution)/shard_map/ppermute | solution.py:448
  412.2 14.8 %collective-permute-start.5 = (bf16[512,1,256]{2,0,1:T(8,128)(2,1)S(1)}, bf16[512,1,256]{2,0,1:T(8,128)(2,1)S(1)}, u32[]{:S(2)}, u32[]{:S(2)}) collective-permute-start(bf16[512,1,256]{2,0,1:T(8,128)(2,1)S(1)} %select_convert_fusion.7), channel_id=1, source_target_pairs={{0,16},{16,0},{1,17},{17,1},{2,18},{18,2},{3,19},{19,3},{4,20},{20... | collective-permute-start | bytes 786440 | tf_op jit(solution)/shard_map/ppermute | solution.py:448
  432.3 226.1 %reduce-scatter.8.cloned.1.call-start = ((), (), s32[]{:S(2)}) async-start(), calls=%async_computation.9 | async-start | bytes 17825792 | tf_op jit(solution)/shard_map/reduce_scatter | solution.py:357
  538.8 5.8 collective-permute-start.12
  544.7 10.0 %collective-permute-start.13 = (f32[4,8,176]{2,0,1:T(4,128)S(1)}, f32[4,8,176]{2,0,1:T(4,128)S(1)}, u32[]{:S(2)}, u32[]{:S(2)}) collective-permute-start(f32[4,8,176]{2,0,1:T(4,128)S(1)} %slice_select_fusion.4), channel_id=1, source_target_pairs={{0,4},{1,5},{2,6},{3,7},{4,0},{5,1},{6,2},{7,3},{8,12},{9,13},{10,... | collective-permute-start | bytes 67592 | tf_op jit(solution)/shard_map/ppermute | solution.py:448
  554.7 5.3 collective-permute-start.14
  567.7 7.9 %collective-permute-start.17 = (f32[1,2,176]{2,0,1:T(1,128)S(1)}, f32[1,2,176]{2,0,1:T(1,128)S(1)}, u32[]{:S(2)}, u32[]{:S(2)}) collective-permute-start(f32[1,2,176]{2,0,1:T(1,128)S(1)} %broadcast_select_fusion.11), channel_id=1, source_target_pairs={{0,32},{32,0},{64,96},{96,64},{1,33},{33,1},{65,97},{97,65},{2,34}... | collective-permute-start | bytes 4232 | tf_op jit(solution)/shard_map/ppermute | solution.py:448
  575.6 12.3 %collective-permute-start.18 = (f32[1,1,176]{2,0,1:T(1,128)S(1)}, f32[1,1,176]{2,0,1:T(1,128)S(1)}, u32[]{:S(2)}, u32[]{:S(2)}) collective-permute-start(f32[1,1,176]{2,0,1:T(1,128)S(1)} %broadcast_select_fusion.15), channel_id=1, source_target_pairs={{0,16},{16,0},{1,17},{17,1},{2,18},{18,2},{3,19},{19,3},{4,20},{20... | collective-permute-start | bytes 2120 | tf_op jit(solution)/shard_map/ppermute | solution.py:448
  585.9 9.3 %collective-permute-start.9 = (bf16[1,128,4,256]{3,1,2,0:T(8,128)(2,1)S(1)}, bf16[1,128,4,256]{3,1,2,0:T(8,128)(2,1)S(1)}, u32[]{:S(2)}, u32[]{:S(2)}) collective-permute-start(bf16[1,128,4,256]{3,1,2,0:T(8,128)(2,1)S(1)} %select_convert_fusion.6), channel_id=1, source_target_pairs={{0,64},{32,96},{64,0},{96,32},{1,65},{33,97},{65,1},{97,33},{2,66}... | collective-permute-start | bytes 786440 | tf_op jit(solution)/shard_map/ppermute | solution.py:448
  587.4 23.6 %collective-permute-start.6 = (bf16[4,256,384]{2,1,0:T(8,128)(2,1)S(1)}, bf16[4,256,384]{2,1,0:T(8,128)(2,1)S(1)}, u32[]{:S(2)}, u32[]{:S(2)}) collective-permute-start(bf16[4,256,384]{2,1,0:T(8,128)(2,1)S(1)} %bitcast.173), channel_id=1, source_target_pairs={{0,64},{32,96},{64,0},{96,32},{1,65},{33,97},{65,1},{97,33},{2,66}... | collective-permute-start | bytes 2359304 | tf_op jit(solution)/shard_map/ppermute | solution.py:448
  595.4 15.9 %collective-permute-start.10 = (bf16[1,128,2,256]{3,1,2,0:T(8,128)(2,1)S(1)}, bf16[1,128,2,256]{3,1,2,0:T(8,128)(2,1)S(1)}, u32[]{:S(2)}, u32[]{:S(2)}) collective-permute-start(bf16[1,128,2,256]{3,1,2,0:T(8,128)(2,1)S(1)} %select_convert_fusion.10), channel_id=1, source_target_pairs={{0,32},{32,0},{64,96},{96,64},{1,33},{33,1},{65,97},{97,65},{2,34}... | collective-permute-start | bytes 393224 | tf_op jit(solution)/shard_map/ppermute | solution.py:448
  611.4 6.1 collective-permute-start.11
  613.1 8.5 %collective-permute-start.8 = (bf16[1,256,384]{2,1,0:T(8,128)(2,1)S(1)}, bf16[1,256,384]{2,1,0:T(8,128)(2,1)S(1)}, u32[]{:S(2)}, u32[]{:S(2)}) collective-permute-start(bf16[1,256,384]{2,1,0:T(8,128)(2,1)S(1)} %select_convert_fusion.9), channel_id=1, source_target_pairs={{0,16},{16,0},{1,17},{17,1},{2,18},{18,2},{3,19},{19,3},{4,20},{20... | collective-permute-start | bytes 589832 | tf_op jit(solution)/shard_map/ppermute | solution.py:448
  663.0 5.5 collective-permute-start.19
  672.3 5.2 collective-permute-start.21
  (35 other events, 1078.4 us)
Sparse Core Ops, SparseCore 0:
  12.3 71.8 all-gather.4
  86.4 70.2 all-gather.6
  160.2 84.5 reduce-scatter.3
  247.7 70.0 all-gather.8
  337.7 84.9 reduce-scatter.5
  432.5 70.3 all-gather.10
  535.1 123.2 reduce-scatter.7

commit v8 on v7

--- a/solution.py
+++ b/solution.py
@@ -307,7 +307,11 @@
     feed_part = jnp.einsum(
         "rsf,fd->rsd", feed_input, w_out, preferred_element_type=jnp.float32
     ).astype(jnp.bfloat16)
-    feed_buffer = jnp.concatenate([jnp.zeros_like(feed_part), feed_part], 2)
+    feed_buffer = lax.dynamic_update_slice(
+        jnp.zeros(feed_part.shape[:2] + (2 * model_width,), feed_part.dtype),
+        feed_part,
+        (0, 0, model_width),
+    )
     feed_buffer, second_grad = lax.optimization_barrier((feed_buffer, second_grad))
     norm_two_back = jax.vjp(layer_norm, middle, ln2_gain, ln2_bias)[1]
     middle_part, grad_ln2_gain, grad_ln2_bias = norm_two_back(second_grad)
@@ -454,10 +458,12 @@
     shape = value.shape
     groups = lax.axis_size("group")
     dps = lax.axis_size("dp")
-    split = shape[:dim] + (groups * dps, shape[dim] // (groups * dps)) + shape[dim + 1 :]
-    value = value.reshape(split)
+    rest = shape[dim] // (groups * dps)
+    value = value.reshape(shape[:dim] + (groups // 2, 2, dps * rest) + shape[dim + 1 :])
+    value = jnp.swapaxes(value, dim, dim + 1)
+    value = value.reshape(shape[:dim] + (groups * dps, rest) + shape[dim + 1 :])
     value = halving_steps(
-        value, dim, [("group", groups, 2), ("group", groups, 1), ("dp", dps, 1)], jnp.bfloat16
+        value, dim, [("group", groups, 1), ("group", groups, 2), ("dp", dps, 1)], jnp.bfloat16
     )
     return value.reshape(shape[:dim] + (shape[dim] // (groups * dps),) + shape[dim + 1 :])
 

time: 713 us -> 711 us (level)
  waiting for transfers between devices: 451 us -> 420 us
  Pallas kernels: 31.1 us -> 52.5 us
  local copies, waits for them, and re-layouts: 25 us -> 43.6 us
  starting transfers between devices: 45.9 us -> 30.9 us
    ppermute x26, waiting for transfers between devices: 94.5 us -> 61.2 us  [halving_steps(): got = lax.ppermute(send, axis, [(i, i ^ bit) for i in range(size)])]
    reshape x0 -> x4, local copies, waits for them, and re-layouts: none -> 17.2 us  [halving_sum(): value.reshape(shape[:dim] + (groups // 2, 2, dps * rest) + shape[dim + 1:])]
    pallas_call x1, Pallas kernels: 12.4 us -> 28.1 us  [attention_backward(): pl.pallas_call(kernel, out_shape=tuple((jax.ShapeDtypeStruct((n, d), jnp....]
    ppermute x26, starting transfers between devices: 45.1 us -> 30 us  [halving_steps(): got = lax.ppermute(send, axis, [(i, i ^ bit) for i in range(size)])]
    reduce_scatter x1, waiting for transfers between devices: 35.6 us -> 44.1 us  [shards(): both = lax.psum_scatter(merged, 'tensor', scatter_dimension=0, tiled=True)]
  transfers between devices with their start and end apart: 33 -> 33, of which waited for: 25 -> 22; matrix products, arithmetic and copies ran while one was open for 14% -> 17% of each run, Pallas kernels for 3% -> 3%
where the time goes in v8:
time: 711 us; the launch traced here: 701 us
  waiting for transfers between devices  420 us (59%)
  matrix products  87.5 us (12%)
  Pallas kernels  52.5 us (7%)
  other arithmetic  49.9 us (7%)
  local copies, waits for them, and re-layouts  43.6 us (6%)
  starting transfers between devices  30.9 us (4%)
  between operations  16.5 us (2%)
    reduce_scatter x1, waiting for transfers between devices, shards(): lax.psum_scatter(attention_part, 'tensor', scatter_dimension=0, tiled=True)  77.5 us
    all_gather x1, waiting for transfers between devices, shards(): second_full = lax.all_gather(second_low, 'tensor', axis=0, tiled=True)  70 us
    all_gather x1, waiting for transfers between devices, shards(): piece = lax.all_gather(branch_low, 'tensor', axis=0, tiled=True)  69.9 us
    all_gather x1, waiting for transfers between devices, shards(): normed_full = lax.all_gather(normed_low, 'tensor', axis=0, tiled=True)  65.3 us
    ppermute x26, waiting for transfers between devices, halving_steps(): got = lax.ppermute(send, axis, [(i, i ^ bit) for i in range(size)])  61.2 us
    reduce_scatter x1, waiting for transfers between devices, shards(): both = lax.psum_scatter(merged, 'tensor', scatter_dimension=0, tiled=True)  44.1 us
    all_gather x1, waiting for transfers between devices, shards(): upstream_full = lax.all_gather(upstream, 'tensor', axis=0, tiled=True)  32.1 us
    ppermute x26, starting transfers between devices, halving_steps(): got = lax.ppermute(send, axis, [(i, i ^ bit) for i in range(size)])  30 us
  transfers between devices with their start and end apart: 33, of which 22 were waited for; matrix products, arithmetic and copies ran while one was open for 17% of the time, Pallas kernels for 3%

profile of v8, /device:TPU:96, one launch (start us, length us, event | category | flops | bytes accessed | tf_op | source)
XLA Modules:
  0.0 701.2 jit_solution(8267951499924752154)
XLA Ops:
  19.0 65.3 %all-gather.5.cloned.1.call-done = bf16[2048,1,2048]{2,0,1:T(8,128)(2,1)} async-done(((bf16[128,1,2048]{2,0,1:T(8,128)(2,1)}), bf16[2048,1,2048]{2,0,1:T(8,128)(2,1)}) %all-gather.5.cloned.1.call-update) | async-done | bytes 8388624 | tf_op jit(solution)/shard_map/all_gather | solution.py:232
  84.3 7.4 %fusion.38 = f32[2048,1,3,128]{3,0,2,1:T(8,128)S(1)} fusion(bf16[2048,1,2048]{2,0,1:T(8,128)(2,1)} %all-gather.5.cloned.1.call-done, bf16[2048,3,1,128]{0,3,1,2:T(8,128)(2,1)} %copy.29), kind=kOutput, calls=%fused_computation.41 | convolution fusion | flops 3221225472 | bytes 13107200 | tf_op jit(solution)/shard_map/dot_general | solution.py:234
  93.7 24.5 %shard_map.254 = (bf16[2048,128]{1,0:T(8,128)(2,1)}, f32[2048,1]{1,0:T(8,128)}) custom-call(s32[1]{0:T(128)} %dynamic_slice.7.len_ref, bf16[2048,128]{1,0:T(8,128)(2,1)} %get-tuple-element.105.q_ref, bf16[2048,128]{1,0:T(8,128)(2,1)} %fusion.67.k_ref, bf16[2048,128]{1,0:T(8,128)(2,1)} %get-tuple-element.104.v_ref), custom_call_target="tpu_custom_call" | custom-call | flops 1207959552 | bytes 2097152 | tf_op jit(solution)/shard_map/pallas_call | solution.py:79
  118.1 6.6 convert_bitcast_fusion.2
  124.7 32.1 %all-gather.7.cloned.1.call-done = bf16[2048,1,2048]{2,0,1:T(8,128)(2,1)} async-done(((bf16[128,1,2048]{2,0,1:T(8,128)(2,1)}), bf16[2048,1,2048]{2,0,1:T(8,128)(2,1)}) %all-gather.7.cloned.1.call-update) | async-done | bytes 8388624 | tf_op jit(solution)/shard_map/all_gather | solution.py:263
  156.9 10.5 %fusion.32 = f32[2048,1,512]{2,0,1:T(8,128)} fusion(bf16[512,2048]{1,0:T(8,128)(2,1)} %param.28, bf16[2048,1,2048]{2,0,1:T(8,128)(2,1)} %all-gather.7.cloned.1.call-done), kind=kOutput, calls=%fused_computation.38 | convolution fusion | flops 4294967296 | bytes 14680064 | tf_op jit(solution)/shard_map/rsd,fd->rsf/dot_general | solution.py:275
  167.4 77.5 %reduce-scatter.4.cloned.1.call-done = bf16[128,1,2048]{2,0,1:T(8,128)(2,1)} async-done(((bf16[2048,1,2048]{2,0,1:T(8,128)(2,1)}), bf16[128,1,2048]{2,0,1:T(8,128)(2,1)}) %reduce-scatter.4.cloned.1.call-update) | async-done | bytes 524304 | tf_op jit(solution)/shard_map/reduce_scatter | solution.py:269
  248.1 70.0 %all-gather.9.cloned.1.call-done = bf16[2048,1,2048]{2,0,1:T(8,128)(2,1)} async-done(((bf16[128,1,2048]{2,0,1:T(8,128)(2,1)}), bf16[2048,1,2048]{2,0,1:T(8,128)(2,1)}) %all-gather.9.cloned.1.call-update) | async-done | bytes 8388624 | tf_op jit(solution)/shard_map/all_gather | solution.py:278
  318.0 7.0 %fusion.6 = f32[2048,512]{1,0:T(8,128)S(1)} fusion(bf16[2048,512]{1,0:T(8,128)(2,1)S(1)} %copy-done, bf16[2048,1,2048]{2,0,1:T(8,128)(2,1)} %all-gather.9.cloned.1.call-done), kind=kOutput, calls=%fused_computation.7 | convolution fusion | flops 4294967296 | bytes 14680064 | tf_op jit(solution)/shard_map/dot_general | solution.py:280
  330.9 6.9 convert_bitcast_fusion.1
  341.2 7.1 %fusion.29 = f32[2048,512]{1,0:T(8,128)S(1)} fusion(bf16[2048,512]{1,0:T(8,128)(2,1)S(1)} %copy-done.13, bf16[2048,1,2048]{2,0,1:T(8,128)(2,1)} %all-gather.9.cloned.1.call-done, f32[]{:T(128)S(6)} %div.103), kind=kOutput, calls=%fused_computation.37 | convolution fusion | flops 4296015872 | bytes 14680068 | tf_op jit(solution)/shard_map/rd,rf->df/dot_general | solution.py:293
  350.5 10.0 %fusion.26 = f32[512,2048]{1,0:T(8,128)} fusion(bf16[2048,1,2048]{2,0,1:T(8,128)(2,1)} %all-gather.7.cloned.1.call-done, f32[]{:T(128)S(6)} %div.103, f32[2048,512]{1,0:T(8,128)S(1)} %copy-done.9, f32[512]{0:T(512)S(1)} %copy-done.21), kind=kOutput, calls=%fused_computation.36 | convolution fusion | flops 4306501632 | bytes 16779268 | tf_op jit(solution)/shard_map/rsf,rsd->fd/dot_general | solution.py:289
  360.6 6.6 reshape.425
  367.2 7.3 %copy.30 = f32[512,2,2,512]{0,3,1,2:T(8,128)} copy(f32[512,2,2,512]{3,2,1,0:T(2,128)} %reshape.425) | data formatting | bytes 8388608 | tf_op jit(solution)/shard_map/reshape | solution.py:462
  389.2 10.5 %collective-permute-done.1 = bf16[2,256,512]{2,1,0:T(8,128)(2,1)S(1)} collective-permute-done((bf16[2,256,512]{2,1,0:T(8,128)(2,1)S(1)}, bf16[2,256,512]{2,1,0:T(8,128)(2,1)S(1)}, u32[]{:S(2)}, u32[]{:S(2)}) %collective-permute-start.1) | collective-permute-done | bytes 524320 | tf_op jit(solution)/shard_map/ppermute | solution.py:452
  401.4 9.5 %collective-permute-done.4 = bf16[512,2,256]{0,2,1:T(8,128)(2,1)S(1)} collective-permute-done((bf16[512,2,256]{0,2,1:T(8,128)(2,1)S(1)}, bf16[512,2,256]{0,2,1:T(8,128)(2,1)S(1)}, u32[]{:S(2)}, u32[]{:S(2)}) %collective-permute-start.4) | collective-permute-done | bytes 524320 | tf_op jit(solution)/shard_map/ppermute | solution.py:452
  417.4 7.0 dynamic_update_slice.12
  431.1 69.9 %all-gather.11.cloned.1.call-done = bf16[2048,1,2048]{2,0,1:T(8,128)(2,1)} async-done(((bf16[128,1,2048]{2,0,1:T(8,128)(2,1)}), bf16[2048,1,2048]{2,0,1:T(8,128)(2,1)}) %all-gather.11.cloned.1.call-update) | async-done | bytes 8388624 | tf_op jit(solution)/shard_map/all_gather | solution.py:327
  507.6 28.1 %shard_map.255 = (bf16[2048,128]{1,0:T(8,128)(2,1)}, bf16[2048,128]{1,0:T(8,128)(2,1)}, bf16[2048,128]{1,0:T(8,128)(2,1)}) custom-call(s32[1]{0:T(128)} %dynamic_slice.7.len_ref, bf16[2048,128]{1,0:T(8,128)(2,1)} %get-tuple-element.105.q_ref, bf16[2048,128]{1,0:T(8,128)(2,1)} %fusion.67.k_ref, bf16[2048,128]{1,0:T(8,128)(2,1)} %get-tuple-element.104.v_ref, ...), custom_call_target="tpu_custom_call" | custom-call | flops 2415919104 | bytes 4194304 | tf_op jit(solution)/shard_map/pallas_call | solution.py:171
  539.1 9.6 %bitcast_dynamic-update-slice_fusion = bf16[2048,1,4096]{2,0,1:T(8,128)(2,1)} fusion(bf16[2048,1,4096]{2,0,1:T(8,128)(2,1)} %dynamic_update_slice.12, bf16[2048,384]{0,1:T(8,128)(2,1)} %bitcast.182, bf16[2048,384]{0,1:T(8,128)(2,1)} %bitcast.179), kind=kOutput, calls=%fused_computation | convolution fusion | flops 3225419776 | bytes 11534336 | tf_op jit(solution)/shard_map/rsc,dc->rsd/dot_general | solution.py:353
  566.4 7.6 %fusion.35 = f32[2048,384]{1,0:T(8,128)S(1)} fusion(bf16[2048,384]{0,1:T(8,128)(2,1)} %bitcast.183, bf16[2048,1,2048]{2,0,1:T(8,128)(2,1)} %all-gather.5.cloned.1.call-done, f32[]{:T(128)S(6)} %div.103), kind=kOutput, calls=%fused_computation.40 | convolution fusion | flops 3222011904 | bytes 13107204 | tf_op jit(solution)/shard_map/rd,rc->dc/dot_general | solution.py:347
  598.4 8.3 %collective-permute-done.7 = bf16[2,256,384]{2,1,0:T(8,128)(2,1)S(1)} collective-permute-done((bf16[2,256,384]{2,1,0:T(8,128)(2,1)S(1)}, bf16[2,256,384]{2,1,0:T(8,128)(2,1)S(1)}, u32[]{:S(2)}, u32[]{:S(2)}) %collective-permute-start.7) | collective-permute-done | bytes 393248 | tf_op jit(solution)/shard_map/ppermute | solution.py:452
  607.4 6.7 collective-permute-done.8
  615.3 44.1 %reduce-scatter.8.cloned.1.call-done = bf16[128,1,4096]{2,0,1:T(8,128)(2,1)} async-done(((bf16[2048,1,4096]{2,0,1:T(8,128)(2,1)}), bf16[128,1,4096]{2,0,1:T(8,128)(2,1)}) %reduce-scatter.8.cloned.1.call-update) | async-done | bytes 1048592 | tf_op jit(solution)/shard_map/reduce_scatter | solution.py:361
  (244 shorter events, 144.5 us)
Async XLA Ops:
  7.2 77.1 %all-gather.5.cloned.1.call-start = ((), (), s32[]{:S(2)}) async-start(), calls=%async_computation.3 | async-start | bytes 8912896 | tf_op jit(solution)/shard_map/all_gather | solution.py:232
  12.2 144.6 %all-gather.7.cloned.1.call-start = ((), (), s32[]{:S(2)}) async-start(), calls=%async_computation.4 | async-start | bytes 8912896 | tf_op jit(solution)/shard_map/all_gather | solution.py:263
  16.2 228.7 %reduce-scatter.4.cloned.1.call-start = ((), (), s32[]{:S(2)}) async-start(), calls=%async_computation.5 | async-start | bytes 8912896 | tf_op jit(solution)/shard_map/reduce_scatter | solution.py:269
  156.9 161.2 %all-gather.9.cloned.1.call-start = ((), (), s32[]{:S(2)}) async-start(), calls=%async_computation.6 | async-start | bytes 8912896 | tf_op jit(solution)/shard_map/all_gather | solution.py:278
  247.8 178.4 %reduce-scatter.6.cloned.1.call-start = ((), (), s32[]{:S(2)}) async-start(), calls=%async_computation.7 | async-start | bytes 8912896 | tf_op jit(solution)/shard_map/reduce_scatter | solution.py:304
  337.8 163.2 %all-gather.11.cloned.1.call-start = ((), (), s32[]{:S(2)}) async-start(), calls=%async_computation.8 | async-start | bytes 8912896 | tf_op jit(solution)/shard_map/all_gather | solution.py:327
  350.4 31.1 %collective-permute-start = (bf16[4,256,512]{2,1,0:T(8,128)(2,1)S(1)}, bf16[4,256,512]{2,1,0:T(8,128)(2,1)S(1)}, u32[]{:S(2)}, u32[]{:S(2)}) collective-permute-start(bf16[4,256,512]{2,1,0:T(8,128)(2,1)S(1)} %bitcast.184), channel_id=1, source_target_pairs={{0,32},{32,0},{64,96},{96,64},{1,33},{33,1},{65,97},{97,65},{2,34}... | collective-permute-start | bytes 3145736 | tf_op jit(solution)/shard_map/ppermute | solution.py:452
  378.2 7.5 %collective-permute-start.3 = (bf16[512,4,256]{0,2,1:T(8,128)(2,1)}, bf16[512,4,256]{0,2,1:T(8,128)(2,1)}, u32[]{:S(2)}, u32[]{:S(2)}) collective-permute-start(bf16[512,4,256]{0,2,1:T(8,128)(2,1)} %select_convert_fusion), channel_id=1, source_target_pairs={{0,32},{32,0},{64,96},{96,64},{1,33},{33,1},{65,97},{97,65},{2,34}... | collective-permute-start | bytes 3145736 | tf_op jit(solution)/shard_map/ppermute | solution.py:452
  384.9 14.8 %collective-permute-start.1 = (bf16[2,256,512]{2,1,0:T(8,128)(2,1)S(1)}, bf16[2,256,512]{2,1,0:T(8,128)(2,1)S(1)}, u32[]{:S(2)}, u32[]{:S(2)}) collective-permute-start(bf16[2,256,512]{2,1,0:T(8,128)(2,1)S(1)} %select_convert_fusion.4), channel_id=1, source_target_pairs={{0,64},{32,96},{64,0},{96,32},{1,65},{33,97},{65,1},{97,33},{2,66}... | collective-permute-start | bytes 1572872 | tf_op jit(solution)/shard_map/ppermute | solution.py:452
  387.8 23.2 %collective-permute-start.4 = (bf16[512,2,256]{0,2,1:T(8,128)(2,1)S(1)}, bf16[512,2,256]{0,2,1:T(8,128)(2,1)S(1)}, u32[]{:S(2)}, u32[]{:S(2)}) collective-permute-start(bf16[512,2,256]{0,2,1:T(8,128)(2,1)S(1)} %select_convert_fusion.3), channel_id=1, source_target_pairs={{0,64},{32,96},{64,0},{96,32},{1,65},{33,97},{65,1},{97,33},{2,66}... | collective-permute-start | bytes 1572872 | tf_op jit(solution)/shard_map/ppermute | solution.py:452
  400.1 24.2 %collective-permute-start.2 = (bf16[1,256,512]{2,1,0:T(8,128)(2,1)S(1)}, bf16[1,256,512]{2,1,0:T(8,128)(2,1)S(1)}, u32[]{:S(2)}, u32[]{:S(2)}) collective-permute-start(bf16[1,256,512]{2,1,0:T(8,128)(2,1)S(1)} %select_convert_fusion.8), channel_id=1, source_target_pairs={{0,16},{16,0},{1,17},{17,1},{2,18},{18,2},{3,19},{19,3},{4,20},{20... | collective-permute-start | bytes 786440 | tf_op jit(solution)/shard_map/ppermute | solution.py:452
  411.3 14.0 %collective-permute-start.5 = (bf16[512,1,256]{0,2,1:T(8,128)(2,1)S(1)}, bf16[512,1,256]{0,2,1:T(8,128)(2,1)S(1)}, u32[]{:S(2)}, u32[]{:S(2)}) collective-permute-start(bf16[512,1,256]{0,2,1:T(8,128)(2,1)S(1)} %select_convert_fusion.7), channel_id=1, source_target_pairs={{0,16},{16,0},{1,17},{17,1},{2,18},{18,2},{3,19},{19,3},{4,20},{20... | collective-permute-start | bytes 786440 | tf_op jit(solution)/shard_map/ppermute | solution.py:452
  430.7 228.7 %reduce-scatter.8.cloned.1.call-start = ((), (), s32[]{:S(2)}) async-start(), calls=%async_computation.9 | async-start | bytes 17825792 | tf_op jit(solution)/shard_map/reduce_scatter | solution.py:361
  552.5 5.8 collective-permute-start.12
  563.1 10.8 %collective-permute-start.14 = (f32[2,8,176]{2,0,1:T(2,128)S(1)}, f32[2,8,176]{2,0,1:T(2,128)S(1)}, u32[]{:S(2)}, u32[]{:S(2)}) collective-permute-start(f32[2,8,176]{2,0,1:T(2,128)S(1)} %broadcast_select_fusion.1), channel_id=1, source_target_pairs={{0,2},{1,3},{2,0},{3,1},{4,6},{5,7},{6,4},{7,5},{8,10},{9,11},{10,... | collective-permute-start | bytes 33800 | tf_op jit(solution)/shard_map/ppermute | solution.py:452
  586.0 5.2 collective-permute-start.18
  586.2 6.2 collective-permute-start.9
  586.7 6.6 collective-permute-start.6
  592.5 5.2 collective-permute-start.10
  595.2 11.5 %collective-permute-start.7 = (bf16[2,256,384]{2,1,0:T(8,128)(2,1)S(1)}, bf16[2,256,384]{2,1,0:T(8,128)(2,1)S(1)}, u32[]{:S(2)}, u32[]{:S(2)}) collective-permute-start(bf16[2,256,384]{2,1,0:T(8,128)(2,1)S(1)} %select_convert_fusion.5), channel_id=1, source_target_pairs={{0,64},{32,96},{64,0},{96,32},{1,65},{33,97},{65,1},{97,33},{2,66}... | collective-permute-start | bytes 1179656 | tf_op jit(solution)/shard_map/ppermute | solution.py:452
  597.8 9.6 %collective-permute-start.11 = (bf16[1,128,1,256]{1,3,2,0:T(8,128)(2,1)S(1)}, bf16[1,128,1,256]{1,3,2,0:T(8,128)(2,1)S(1)}, u32[]{:S(2)}, u32[]{:S(2)}) collective-permute-start(bf16[1,128,1,256]{1,3,2,0:T(8,128)(2,1)S(1)} %select_convert_fusion.11), channel_id=1, source_target_pairs={{0,16},{16,0},{1,17},{17,1},{2,18},{18,2},{3,19},{19,3},{4,20},{20... | collective-permute-start | bytes 196616 | tf_op jit(solution)/shard_map/ppermute | solution.py:452
  606.8 7.3 %collective-permute-start.8 = (bf16[1,256,384]{2,1,0:T(8,128)(2,1)S(1)}, bf16[1,256,384]{2,1,0:T(8,128)(2,1)S(1)}, u32[]{:S(2)}, u32[]{:S(2)}) collective-permute-start(bf16[1,256,384]{2,1,0:T(8,128)(2,1)S(1)} %select_convert_fusion.9), channel_id=1, source_target_pairs={{0,16},{16,0},{1,17},{17,1},{2,18},{18,2},{3,19},{19,3},{4,20},{20... | collective-permute-start | bytes 589832 | tf_op jit(solution)/shard_map/ppermute | solution.py:452
  664.0 5.5 collective-permute-start.19
  673.4 5.2 collective-permute-start.21
  (36 other events, 1139.0 us)
Sparse Core Ops, SparseCore 0:
  12.3 71.8 all-gather.4
  86.4 70.3 all-gather.6
  160.2 84.7 reduce-scatter.3
  248.0 70.0 all-gather.8
  337.9 84.6 reduce-scatter.5
  430.8 70.1 all-gather.10
  548.9 110.4 reduce-scatter.7

commit v9 on v8

--- a/solution.py
+++ b/solution.py
@@ -190,6 +190,48 @@
             bytes_accessed=8 * n * d * 2,
         ),
     )(length, q, k, v, do, lse)
+
+
+GRID = 4
+
+
+def grid_pairs(axis_of, delta):
+    out = []
+    for s in range(GRID * GRID):
+        x, y = divmod(s, GRID)
+        if axis_of == "x":
+            out.append((s, ((x + delta) % GRID) * GRID + y))
+        else:
+            out.append((s, x * GRID + (y + delta) % GRID))
+    return out
+
+
+def grid_position(axis_of):
+    t = lax.axis_index("tensor")
+    return t // GRID if axis_of == "x" else t % GRID
+
+
+def gather_line(block, axis_of):
+    pos = grid_position(axis_of)
+    from_left = lax.ppermute(block, "tensor", grid_pairs(axis_of, 1))
+    from_right = lax.ppermute(block, "tensor", grid_pairs(axis_of, -1))
+    half = block.shape[0] // 2
+    far_low = lax.ppermute(from_left[:half], "tensor", grid_pairs(axis_of, 1))
+    far_high = lax.ppermute(from_right[half:], "tensor", grid_pairs(axis_of, -1))
+    far = jnp.concatenate([far_low, far_high], 0)
+    ring = jnp.stack([block, from_right, far, from_left, block, from_right, far, from_left])
+    return lax.dynamic_slice_in_dim(ring, (GRID - pos) % GRID, GRID, 0)
+
+
+def gather_tensor(block):
+    rows, cols = block.shape
+    mid = cols // 2
+    first = gather_line(block[:, :mid], "y").reshape(GRID * rows, mid)
+    first = gather_line(first, "x").reshape(GRID * GRID * rows, mid)
+    second = gather_line(block[:, mid:], "x").reshape(GRID * rows, cols - mid)
+    second = gather_line(second, "y").reshape(GRID, GRID, rows, cols - mid)
+    second = jnp.transpose(second, (1, 0, 2, 3)).reshape(GRID * GRID * rows, cols - mid)
+    return jnp.concatenate([first, second], 1)
 
 
 def shards(
@@ -260,7 +302,9 @@
     positions = tensor_rank * row_count + jnp.arange(row_count, dtype=jnp.int32)
     live = positions[:, None] < seq_lengths[None, :]
     upstream = jnp.where(live[:, :, None], cotangent, jnp.zeros_like(cotangent))
-    upstream_full = lax.all_gather(upstream, "tensor", axis=0, tiled=True)
+    upstream_full = gather_tensor(upstream.reshape(row_count, seq_count * model_width)).reshape(
+        seq_total, seq_count, model_width
+    )
     attention_part = jnp.einsum(
         "rse,ed->rsd", attended, out_weight, preferred_element_type=jnp.float32
     ).astype(jnp.bfloat16)
@@ -319,7 +363,8 @@
     branch_low = middle_grad.astype(jnp.bfloat16)
     grad_b_o = jnp.sum(branch_low, axis=(0, 1), dtype=jnp.float32)
     grad_b_out = jnp.sum(upstream, axis=(0, 1), dtype=jnp.float32)
-    summed_in = halving_sum(grad_w_in * factor, 0)
+    feed_buffer, scaled_in = lax.optimization_barrier((feed_buffer, grad_w_in * factor))
+    summed_in = halving_sum(scaled_in, 0)
     summed_out = halving_sum(grad_w_out * factor, 1)
     summed_in, summed_out, branch_low = lax.optimization_barrier(
         (summed_in, summed_out, branch_low)

time: 711 us -> 748 us (1.052)
  starting transfers between devices: 30.9 us -> 83.9 us
  Pallas kernels: 52.5 us -> 25.9 us
  local copies, waits for them, and re-layouts: 43.6 us -> 69.7 us
  waiting for transfers between devices: 420 us -> 395 us
    all_gather x1, waiting for transfers between devices: 65.3 us -> 0.01 us  [shards(): normed_full = lax.all_gather(normed_low, 'tensor', axis=0, tiled=True)]
    ppermute x0 -> x16, waiting for transfers between devices: none -> 54.6 us  [the longest x4 35.9 us: gather_line(): from_left = lax.ppermute(block, 'tensor', grid_pairs(axis_of, 1))]
    all_gather x1 -> x0, waiting for transfers between devices: 32.1 us -> none  [shards(): upstream_full = lax.all_gather(upstream, 'tensor', axis=0, tiled=True)]
    ppermute x0 -> x16, starting transfers between devices: none -> 27.7 us  [the longest x4 14.6 us: gather_line(): lax.ppermute(from_right[half:], 'tensor', grid_pairs(axis_of, -1))]
    ppermute x26, starting transfers between devices: 30 us -> 55.3 us  [halving_steps(): got = lax.ppermute(send, axis, [(i, i ^ bit) for i in range(size)])]
    reduce_scatter x1, waiting for transfers between devices: 0.01 us -> 23.6 us  [shards(): lax.psum_scatter(second_part, 'tensor', scatter_dimension=0, tiled=True)]
    pallas_call x1, Pallas kernels: 28.1 us -> 10.3 us  [attention_backward(): pl.pallas_call(kernel, out_shape=tuple((jax.ShapeDtypeStruct((n, d), jnp....]
    unnamed x57 -> x88, local copies, waits for them, and re-layouts: 11.5 us -> 22 us
  transfers between devices with their start and end apart: 33 -> 48, of which waited for: 22 -> 34; matrix products, arithmetic and copies ran while one was open for 17% -> 19% of each run, Pallas kernels for 3% -> 0%
where the time goes in v9:
time: 748 us; the launch traced here: 736 us
  waiting for transfers between devices  395 us (53%)
  matrix products  92.2 us (12%)
  starting transfers between devices  83.9 us (11%)
  local copies, waits for them, and re-layouts  69.7 us (9%)
  other arithmetic  52.7 us (7%)
  Pallas kernels  25.9 us (3%)
  between operations  16.9 us (2%)
    reduce_scatter x1, waiting for transfers between devices, shards(): lax.psum_scatter(attention_part, 'tensor', scatter_dimension=0, tiled=True)  78.9 us
    all_gather x1, waiting for transfers between devices, shards(): second_full = lax.all_gather(second_low, 'tensor', axis=0, tiled=True)  70.1 us
    all_gather x1, waiting for transfers between devices, shards(): piece = lax.all_gather(branch_low, 'tensor', axis=0, tiled=True)  69.9 us
    ppermute x26, starting transfers between devices, halving_steps(): got = lax.ppermute(send, axis, [(i, i ^ bit) for i in range(size)])  55.3 us
    ppermute x26, waiting for transfers between devices, halving_steps(): got = lax.ppermute(send, axis, [(i, i ^ bit) for i in range(size)])  53.3 us
    reduce_scatter x1, waiting for transfers between devices, shards(): both = lax.psum_scatter(merged, 'tensor', scatter_dimension=0, tiled=True)  44.2 us
    ppermute x4, waiting for transfers between devices, gather_line(): from_left = lax.ppermute(block, 'tensor', grid_pairs(axis_of, 1))  35.9 us
    reduce_scatter x1, waiting for transfers between devices, shards(): lax.psum_scatter(second_part, 'tensor', scatter_dimension=0, tiled=True)  23.6 us
  transfers between devices with their start and end apart: 48, of which 34 were waited for; matrix products, arithmetic and copies ran while one was open for 19% of the time, Pallas kernels for 0%

profile of v9, /device:TPU:96, one launch (start us, length us, event | category | flops | bytes accessed | tf_op | source)
XLA Modules:
  0.0 736.1 jit_solution(14670949114852215721)
XLA Ops:
  55.6 35.2 %collective-permute-done.13 = bf16[512,1024]{1,0:T(8,128)(2,1)} collective-permute-done((bf16[512,1024]{1,0:T(8,128)(2,1)}, bf16[512,1024]{1,0:T(8,128)(2,1)}, u32[]{:S(2)}, u32[]{:S(2)}) %collective-permute-start.13) | collective-permute-done | bytes 1048608 | tf_op jit(solution)/shard_map/ppermute | solution.py:216
  105.7 8.3 %collective-permute-done.14 = bf16[256,1024]{1,0:T(8,128)(2,1)S(1)} collective-permute-done((bf16[256,1024]{1,0:T(8,128)(2,1)S(1)}, bf16[256,1024]{1,0:T(8,128)(2,1)S(1)}, u32[]{:S(2)}, u32[]{:S(2)}) %collective-permute-start.14) | collective-permute-done | bytes 524320 | tf_op jit(solution)/shard_map/ppermute | solution.py:219
  128.7 8.2 %maximum_bitcast_fusion = bf16[2048,1,2048]{2,0,1:T(8,128)(2,1)} fusion(bf16[2048,1024]{1,0:T(8,128)(2,1)} %bitcast.248, bf16[2048,1024]{1,0:T(8,128)(2,1)} %bitcast.249), kind=kLoop, calls=%fused_computation | loop fusion | flops 16777216 | bytes 16777216 | tf_op jit(solution)/shard_map/reshape | solution.py:305
  136.9 7.4 %fusion.38 = f32[2048,1,3,128]{3,0,2,1:T(8,128)S(1)} fusion(bf16[2048,1,2048]{2,0,1:T(8,128)(2,1)} %all-gather.4.cloned.1.call-done, bf16[2048,3,1,128]{0,3,1,2:T(8,128)(2,1)} %copy.35), kind=kOutput, calls=%fused_computation.42 | convolution fusion | flops 3221225472 | bytes 13107200 | tf_op jit(solution)/shard_map/dot_general | solution.py:276
  146.3 15.7 %shard_map.254 = (bf16[2048,128]{1,0:T(8,128)(2,1)}, f32[2048,1]{1,0:T(8,128)}) custom-call(s32[1]{0:T(128)} %dynamic_slice.19.len_ref, bf16[2048,128]{1,0:T(8,128)(2,1)} %get-tuple-element.121.q_ref, bf16[2048,128]{1,0:T(8,128)(2,1)} %fusion.71.k_ref, bf16[2048,128]{1,0:T(8,128)(2,1)} %get-tuple-element.120.v_ref), custom_call_target="tpu_custom_call" | custom-call | flops 1207959552 | bytes 2097152 | tf_op jit(solution)/shard_map/pallas_call | solution.py:79
  162.0 6.6 convert_bitcast_fusion.2
  168.9 10.6 %fusion.32 = f32[2048,1,512]{2,0,1:T(8,128)} fusion(bf16[512,2048]{1,0:T(8,128)(2,1)} %param.28, bf16[2048,1,2048]{2,0,1:T(8,128)(2,1)} %maximum_bitcast_fusion), kind=kOutput, calls=%fused_computation.39 | convolution fusion | flops 4294967296 | bytes 14680064 | tf_op jit(solution)/shard_map/rsd,fd->rsf/dot_general | solution.py:319
  179.5 78.9 %reduce-scatter.4.cloned.1.call-done = bf16[128,1,2048]{2,0,1:T(8,128)(2,1)} async-done(((bf16[2048,1,2048]{2,0,1:T(8,128)(2,1)}), bf16[128,1,2048]{2,0,1:T(8,128)(2,1)}) %reduce-scatter.4.cloned.1.call-update) | async-done | bytes 524304 | tf_op jit(solution)/shard_map/reduce_scatter | solution.py:313
  261.3 70.1 %all-gather.6.cloned.1.call-done = bf16[2048,1,2048]{2,0,1:T(8,128)(2,1)} async-done(((bf16[128,1,2048]{2,0,1:T(8,128)(2,1)}), bf16[2048,1,2048]{2,0,1:T(8,128)(2,1)}) %all-gather.6.cloned.1.call-update) | async-done | bytes 8388624 | tf_op jit(solution)/shard_map/all_gather | solution.py:322
  331.4 7.0 fusion.6
  344.1 6.9 convert_bitcast_fusion.1
  354.5 11.7 %fusion.26 = f32[512,2048]{1,0:T(8,128)} fusion(bf16[2048,1,2048]{2,0,1:T(8,128)(2,1)} %maximum_bitcast_fusion, f32[]{:T(128)S(6)} %div.105, f32[2048,512]{1,0:T(8,128)} %copy-done.11, f32[512]{0:T(512)S(1)} %copy-done.26), kind=kOutput, calls=%fused_computation.37 | convolution fusion | flops 4306501632 | bytes 16779268 | tf_op jit(solution)/shard_map/rsf,rsd->fd/dot_general | solution.py:333
  366.2 6.7 reshape.453
  372.9 7.5 %copy.37 = f32[512,2,2,512]{0,3,1,2:T(8,128)} copy(f32[512,2,2,512]{3,2,1,0:T(2,128)} %reshape.453) | data formatting | bytes 8388608 | tf_op jit(solution)/shard_map/reshape | solution.py:507
  383.0 10.0 %fusion.29 = f32[2048,512]{1,0:T(8,128)} fusion(bf16[2048,512]{1,0:T(8,128)(2,1)S(1)} %copy-done.15, bf16[2048,1,2048]{2,0,1:T(8,128)(2,1)} %all-gather.6.cloned.1.call-done, f32[]{:T(128)S(6)} %div.105), kind=kOutput, calls=%fused_computation.38 | convolution fusion | flops 4296015872 | bytes 14680068 | tf_op jit(solution)/shard_map/rd,rf->df/dot_general | solution.py:337
  400.0 7.0 dynamic_update_slice.12
  412.4 23.6 %reduce-scatter.6.cloned.1.call-done = bf16[128,1,2048]{2,0,1:T(8,128)(2,1)} async-done(((bf16[2048,1,2048]{2,0,1:T(8,128)(2,1)}), bf16[128,1,2048]{2,0,1:T(8,128)(2,1)}) %reduce-scatter.6.cloned.1.call-update) | async-done | bytes 524304 | tf_op jit(solution)/shard_map/reduce_scatter | solution.py:348
  444.2 12.8 %collective-permute-done.17 = bf16[2,256,512]{2,1,0:T(8,128)(2,1)S(1)} collective-permute-done((bf16[2,256,512]{2,1,0:T(8,128)(2,1)S(1)}, bf16[2,256,512]{2,1,0:T(8,128)(2,1)S(1)}, u32[]{:S(2)}, u32[]{:S(2)}) %collective-permute-start.17) | collective-permute-done | bytes 524320 | tf_op jit(solution)/shard_map/ppermute | solution.py:497
  467.7 69.9 %all-gather.8.cloned.1.call-done = bf16[2048,1,2048]{2,0,1:T(8,128)(2,1)} async-done(((bf16[128,1,2048]{2,0,1:T(8,128)(2,1)}), bf16[2048,1,2048]{2,0,1:T(8,128)(2,1)}) %all-gather.8.cloned.1.call-update) | async-done | bytes 8388624 | tf_op jit(solution)/shard_map/all_gather | solution.py:372
  544.2 10.3 %shard_map.255 = (bf16[2048,128]{1,0:T(8,128)(2,1)}, bf16[2048,128]{1,0:T(8,128)(2,1)}, bf16[2048,128]{1,0:T(8,128)(2,1)}) custom-call(s32[1]{0:T(128)} %dynamic_slice.19.len_ref, bf16[2048,128]{1,0:T(8,128)(2,1)} %get-tuple-element.121.q_ref, bf16[2048,128]{1,0:T(8,128)(2,1)} %fusion.71.k_ref, bf16[2048,128]{1,0:T(8,128)(2,1)} %get-tuple-element.120.v_ref, ...), custom_call_target="tpu_custom_call" | custom-call | flops 2415919104 | bytes 4194304 | tf_op jit(solution)/shard_map/pallas_call | solution.py:171
  557.8 9.8 %bitcast_dynamic-update-slice_fusion = bf16[2048,1,4096]{2,0,1:T(8,128)(2,1)} fusion(bf16[2048,1,4096]{2,0,1:T(8,128)(2,1)} %dynamic_update_slice.12, bf16[2048,384]{0,1:T(8,128)(2,1)} %bitcast.264, bf16[2048,384]{0,1:T(8,128)(2,1)} %bitcast.261), kind=kOutput, calls=%fused_computation.1 | convolution fusion | flops 3225419776 | bytes 11534336 | tf_op jit(solution)/shard_map/rsc,dc->rsd/dot_general | solution.py:398
  585.0 7.5 %fusion.35 = f32[2048,384]{1,0:T(8,128)S(1)} fusion(bf16[2048,384]{0,1:T(8,128)(2,1)} %bitcast.265, bf16[2048,1,2048]{2,0,1:T(8,128)(2,1)} %all-gather.4.cloned.1.call-done, f32[]{:T(128)S(6)} %div.105), kind=kOutput, calls=%fused_computation.41 | convolution fusion | flops 3222011904 | bytes 13107204 | tf_op jit(solution)/shard_map/rd,rc->dc/dot_general | solution.py:392
  604.5 19.6 %collective-permute-start.34 = (f32[1,1,176]{2,0,1:T(1,128)S(1)}, f32[1,1,176]{2,0,1:T(1,128)S(1)}, u32[]{:S(2)}, u32[]{:S(2)}) collective-permute-start(f32[1,1,176]{2,0,1:T(1,128)S(1)} %broadcast_select_fusion.15), channel_id=1, source_target_pairs={{0,16},{16,0},{1,17},{17,1},{2,18},{18,2},{3,19},{19,3},{4,20},{20... | collective-permute-start | bytes 2120 | tf_op jit(solution)/shard_map/ppermute | solution.py:497
  650.0 44.2 %reduce-scatter.8.cloned.1.call-done = bf16[128,1,4096]{2,0,1:T(8,128)(2,1)} async-done(((bf16[2048,1,4096]{2,0,1:T(8,128)(2,1)}), bf16[128,1,4096]{2,0,1:T(8,128)(2,1)}) %reduce-scatter.8.cloned.1.call-update) | async-done | bytes 1048592 | tf_op jit(solution)/shard_map/reduce_scatter | solution.py:406
  (333 shorter events, 223.7 us)
Async XLA Ops:
  7.2 129.7 %all-gather.4.cloned.1.call-start = ((), (), s32[]{:S(2)}) async-start(), calls=%async_computation.3 | async-start | bytes 8912896 | tf_op jit(solution)/shard_map/all_gather | solution.py:274
  12.2 246.1 %reduce-scatter.4.cloned.1.call-start = ((), (), s32[]{:S(2)}) async-start(), calls=%async_computation.4 | async-start | bytes 8912896 | tf_op jit(solution)/shard_map/reduce_scatter | solution.py:313
  19.2 11.8 %collective-permute-start.8 = (bf16[128,1024]{1,0:T(8,128)(2,1)}, bf16[128,1024]{1,0:T(8,128)(2,1)}, u32[]{:S(2)}, u32[]{:S(2)}) collective-permute-start(bf16[128,1024]{1,0:T(8,128)(2,1)} %get-tuple-element.128), channel_id=1, source_target_pairs={{0,12},{1,13},{2,14},{3,15},{4,0},{5,1},{6,2},{7,3},{8,4},{9,5},{1... | collective-permute-start | bytes 786440 | tf_op jit(solution)/shard_map/ppermute | solution.py:217
  22.0 14.0 %collective-permute-start.9 = (bf16[128,1024]{1,0:T(8,128)(2,1)}, bf16[128,1024]{1,0:T(8,128)(2,1)S(1)}, u32[]{:S(2)}, u32[]{:S(2)}) collective-permute-start(bf16[128,1024]{1,0:T(8,128)(2,1)} %get-tuple-element.128), channel_id=1, source_target_pairs={{0,4},{1,5},{2,6},{3,7},{4,8},{5,9},{6,10},{7,11},{8,12},{9,13},{1... | collective-permute-start | bytes 786440 | tf_op jit(solution)/shard_map/ppermute | solution.py:216
  25.1 11.9 %collective-permute-start.3 = (bf16[64,1024]{1,0:T(8,128)(2,1)S(1)}, bf16[64,1024]{1,0:T(8,128)(2,1)S(1)}, u32[]{:S(2)}, u32[]{:S(2)}) collective-permute-start(bf16[64,1024]{1,0:T(8,128)(2,1)S(1)} %slice.362), channel_id=1, source_target_pairs={{0,3},{1,0},{2,1},{3,2},{4,7},{5,4},{6,5},{7,6},{8,11},{9,8},{10,9... | collective-permute-start | bytes 393224 | tf_op jit(solution)/shard_map/ppermute | solution.py:220
  44.5 46.4 %collective-permute-start.13 = (bf16[512,1024]{1,0:T(8,128)(2,1)}, bf16[512,1024]{1,0:T(8,128)(2,1)}, u32[]{:S(2)}, u32[]{:S(2)}) collective-permute-start(bf16[512,1024]{1,0:T(8,128)(2,1)} %bitcast.30), channel_id=1, source_target_pairs={{0,1},{1,2},{2,3},{3,0},{4,5},{5,6},{6,7},{7,4},{8,9},{9,10},{10,1... | collective-permute-start | bytes 3145736 | tf_op jit(solution)/shard_map/ppermute | solution.py:216
  44.7 47.8 %collective-permute-start.12 = (bf16[512,1024]{1,0:T(8,128)(2,1)}, bf16[512,1024]{1,0:T(8,128)(2,1)}, u32[]{:S(2)}, u32[]{:S(2)}) collective-permute-start(bf16[512,1024]{1,0:T(8,128)(2,1)} %bitcast.30), channel_id=1, source_target_pairs={{0,3},{1,0},{2,1},{3,2},{4,7},{5,4},{6,5},{7,6},{8,11},{9,8},{10,9... | collective-permute-start | bytes 3145736 | tf_op jit(solution)/shard_map/ppermute | solution.py:217
  48.3 49.1 %collective-permute-start.5 = (bf16[512,1024]{1,0:T(8,128)(2,1)S(1)}, bf16[512,1024]{1,0:T(8,128)(2,1)}, u32[]{:S(2)}, u32[]{:S(2)}) collective-permute-start(bf16[512,1024]{1,0:T(8,128)(2,1)S(1)} %bitcast.252), channel_id=1, source_target_pairs={{0,4},{1,5},{2,6},{3,7},{4,8},{5,9},{6,10},{7,11},{8,12},{9,13},{1... | collective-permute-start | bytes 3145736 | tf_op jit(solution)/shard_map/ppermute | solution.py:216
  48.4 50.1 %collective-permute-start.4 = (bf16[512,1024]{1,0:T(8,128)(2,1)S(1)}, bf16[512,1024]{1,0:T(8,128)(2,1)}, u32[]{:S(2)}, u32[]{:S(2)}) collective-permute-start(bf16[512,1024]{1,0:T(8,128)(2,1)S(1)} %bitcast.253), channel_id=1, source_target_pairs={{0,12},{1,13},{2,14},{3,15},{4,0},{5,1},{6,2},{7,3},{8,4},{9,5},{1... | collective-permute-start | bytes 3145736 | tf_op jit(solution)/shard_map/ppermute | solution.py:217
  91.9 22.0 %collective-permute-start.14 = (bf16[256,1024]{1,0:T(8,128)(2,1)S(1)}, bf16[256,1024]{1,0:T(8,128)(2,1)S(1)}, u32[]{:S(2)}, u32[]{:S(2)}) collective-permute-start(bf16[256,1024]{1,0:T(8,128)(2,1)S(1)} %slice.368), channel_id=1, source_target_pairs={{0,1},{1,2},{2,3},{3,0},{4,5},{5,6},{6,7},{7,4},{8,9},{9,10},{10,1... | collective-permute-start | bytes 1572872 | tf_op jit(solution)/shard_map/ppermute | solution.py:219
  93.6 20.3 %collective-permute-start.15 = (bf16[256,1024]{1,0:T(8,128)(2,1)S(1)}, bf16[256,1024]{1,0:T(8,128)(2,1)S(1)}, u32[]{:S(2)}, u32[]{:S(2)}) collective-permute-start(bf16[256,1024]{1,0:T(8,128)(2,1)S(1)} %slice.369), channel_id=1, source_target_pairs={{0,3},{1,0},{2,1},{3,2},{4,7},{5,4},{6,5},{7,6},{8,11},{9,8},{10,9... | collective-permute-start | bytes 1572872 | tf_op jit(solution)/shard_map/ppermute | solution.py:220
  98.4 23.8 %collective-permute-start.6 = (bf16[256,1024]{1,0:T(8,128)(2,1)S(1)}, bf16[256,1024]{1,0:T(8,128)(2,1)S(1)}, u32[]{:S(2)}, u32[]{:S(2)}) collective-permute-start(bf16[256,1024]{1,0:T(8,128)(2,1)S(1)} %slice.363), channel_id=1, source_target_pairs={{0,4},{1,5},{2,6},{3,7},{4,8},{5,9},{6,10},{7,11},{8,12},{9,13},{1... | collective-permute-start | bytes 1572872 | tf_op jit(solution)/shard_map/ppermute | solution.py:219
  99.6 22.6 %collective-permute-start.7 = (bf16[256,1024]{1,0:T(8,128)(2,1)S(1)}, bf16[256,1024]{1,0:T(8,128)(2,1)S(1)}, u32[]{:S(2)}, u32[]{:S(2)}) collective-permute-start(bf16[256,1024]{1,0:T(8,128)(2,1)S(1)} %slice.364), channel_id=1, source_target_pairs={{0,12},{1,13},{2,14},{3,15},{4,0},{5,1},{6,2},{7,3},{8,4},{9,5},{1... | collective-permute-start | bytes 1572872 | tf_op jit(solution)/shard_map/ppermute | solution.py:220
  168.6 162.7 %all-gather.6.cloned.1.call-start = ((), (), s32[]{:S(2)}) async-start(), calls=%async_computation.5 | async-start | bytes 8912896 | tf_op jit(solution)/shard_map/all_gather | solution.py:322
  261.2 174.8 %reduce-scatter.6.cloned.1.call-start = ((), (), s32[]{:S(2)}) async-start(), calls=%async_computation.6 | async-start | bytes 8912896 | tf_op jit(solution)/shard_map/reduce_scatter | solution.py:348
  351.1 186.5 %all-gather.8.cloned.1.call-start = ((), (), s32[]{:S(2)}) async-start(), calls=%async_computation.7 | async-start | bytes 8912896 | tf_op jit(solution)/shard_map/all_gather | solution.py:372
  393.8 15.3 %collective-permute-start.20 = (bf16[512,2,256]{0,2,1:T(8,128)(2,1)S(1)}, bf16[512,2,256]{0,2,1:T(8,128)(2,1)S(1)}, u32[]{:S(2)}, u32[]{:S(2)}) collective-permute-start(bf16[512,2,256]{0,2,1:T(8,128)(2,1)S(1)} %select_convert_fusion.3), channel_id=1, source_target_pairs={{0,64},{32,96},{64,0},{96,32},{1,65},{33,97},{65,1},{97,33},{2,66}... | collective-permute-start | bytes 1572872 | tf_op jit(solution)/shard_map/ppermute | solution.py:497
  411.1 28.8 %collective-permute-start.21 = (bf16[512,1,256]{0,2,1:T(8,128)(2,1)}, bf16[512,1,256]{0,2,1:T(8,128)(2,1)S(1)}, u32[]{:S(2)}, u32[]{:S(2)}) collective-permute-start(bf16[512,1,256]{0,2,1:T(8,128)(2,1)} %select_convert_fusion.7), channel_id=1, source_target_pairs={{0,16},{16,0},{1,17},{17,1},{2,18},{18,2},{3,19},{19,3},{4,20},{20... | collective-permute-start | bytes 786440 | tf_op jit(solution)/shard_map/ppermute | solution.py:497
  443.0 14.0 %collective-permute-start.17 = (bf16[2,256,512]{2,1,0:T(8,128)(2,1)S(1)}, bf16[2,256,512]{2,1,0:T(8,128)(2,1)S(1)}, u32[]{:S(2)}, u32[]{:S(2)}) collective-permute-start(bf16[2,256,512]{2,1,0:T(8,128)(2,1)S(1)} %select_convert_fusion.4), channel_id=1, source_target_pairs={{0,64},{32,96},{64,0},{96,32},{1,65},{33,97},{65,1},{97,33},{2,66}... | collective-permute-start | bytes 1572872 | tf_op jit(solution)/shard_map/ppermute | solution.py:497
  467.5 226.8 %reduce-scatter.8.cloned.1.call-start = ((), (), s32[]{:S(2)}) async-start(), calls=%async_computation.8 | async-start | bytes 17825792 | tf_op jit(solution)/shard_map/reduce_scatter | solution.py:406
  581.4 11.1 %collective-permute-start.30 = (f32[2,8,176]{2,0,1:T(2,128)S(1)}, f32[2,8,176]{2,0,1:T(2,128)S(1)}, u32[]{:S(2)}, u32[]{:S(2)}) collective-permute-start(f32[2,8,176]{2,0,1:T(2,128)S(1)} %broadcast_select_fusion.1), channel_id=1, source_target_pairs={{0,2},{1,3},{2,0},{3,1},{4,6},{5,7},{6,4},{7,5},{8,10},{9,11},{10,... | collective-permute-start | bytes 33800 | tf_op jit(solution)/shard_map/ppermute | solution.py:497
  604.5 21.1 %collective-permute-start.34 = (f32[1,1,176]{2,0,1:T(1,128)S(1)}, f32[1,1,176]{2,0,1:T(1,128)S(1)}, u32[]{:S(2)}, u32[]{:S(2)}) collective-permute-start(f32[1,1,176]{2,0,1:T(1,128)S(1)} %broadcast_select_fusion.15), channel_id=1, source_target_pairs={{0,16},{16,0},{1,17},{17,1},{2,18},{18,2},{3,19},{19,3},{4,20},{20... | collective-permute-start | bytes 2120 | tf_op jit(solution)/shard_map/ppermute | solution.py:497
  629.0 12.0 %collective-permute-start.23 = (bf16[2,256,384]{2,1,0:T(8,128)(2,1)S(1)}, bf16[2,256,384]{2,1,0:T(8,128)(2,1)S(1)}, u32[]{:S(2)}, u32[]{:S(2)}) collective-permute-start(bf16[2,256,384]{2,1,0:T(8,128)(2,1)S(1)} %select_convert_fusion.5), channel_id=1, source_target_pairs={{0,64},{32,96},{64,0},{96,32},{1,65},{33,97},{65,1},{97,33},{2,66}... | collective-permute-start | bytes 1179656 | tf_op jit(solution)/shard_map/ppermute | solution.py:497
  632.4 12.7 %collective-permute-start.27 = (bf16[1,128,1,256]{1,3,2,0:T(8,128)(2,1)S(1)}, bf16[1,128,1,256]{1,3,2,0:T(8,128)(2,1)S(1)}, u32[]{:S(2)}, u32[]{:S(2)}) collective-permute-start(bf16[1,128,1,256]{1,3,2,0:T(8,128)(2,1)S(1)} %select_convert_fusion.11), channel_id=1, source_target_pairs={{0,16},{16,0},{1,17},{17,1},{2,18},{18,2},{3,19},{19,3},{4,20},{20... | collective-permute-start | bytes 196616 | tf_op jit(solution)/shard_map/ppermute | solution.py:497
  (58 other events, 1376.6 us)
Sparse Core Ops, SparseCore 0:
  12.4 102.0 all-gather.3
  168.7 89.5 reduce-scatter.3
  261.3 70.0 all-gather.5
  351.2 84.7 reduce-scatter.5
  467.6 69.9 all-gather.7
  567.8 126.4 reduce-scatter.7

commit v10 on v8

--- a/solution.py
+++ b/solution.py
@@ -44,8 +44,14 @@
     def scores(j, m):
         first = pl.multiple_of(j * block_k, block_k)
         k = k_ref[pl.ds(first, block_k), :]
-        s = lax.dot_general(q, k, (((1,), (1,)), ((), ())), preferred_element_type=jnp.float32)
-        s = jnp.where(_valid(i * block_q, first, block_q, block_k, length), s * scale, NEGATIVE)
+        s = lax.dot_general(q, k, (((1,), (1,)), ((), ())), preferred_element_type=jnp.float32) * scale
+        edge = (first + block_k > i * block_q) | (first + block_k > length)
+        s = lax.cond(
+            edge,
+            lambda v: jnp.where(_valid(i * block_q, first, block_q, block_k, length), v, NEGATIVE),
+            lambda v: v,
+            s,
+        )
         s_buf[:, pl.ds(first, block_k)] = s
         return jnp.maximum(m, jnp.max(s, axis=1, keepdims=True))
 
@@ -126,9 +132,17 @@
             k = k_ref[pl.ds(first, block_k), :]
             v = v_ref[pl.ds(first, block_k), :]
             s = lax.dot_general(q, k, (((1,), (1,)), ((), ())), preferred_element_type=jnp.float32)
-            valid = _valid(i * block_q, first, block_q, block_k, length)
-            s = jnp.where(valid, s * scale, NEGATIVE)
-            p = jnp.where(valid, jnp.exp(s - lse), 0.0)
+            edge = (first + block_k > i * block_q) | (first + block_k > length)
+            p = lax.cond(
+                edge,
+                lambda v: jnp.where(
+                    _valid(i * block_q, first, block_q, block_k, length),
+                    jnp.exp(jnp.where(_valid(i * block_q, first, block_q, block_k, length), v, NEGATIVE) - lse),
+                    0.0,
+                ),
+                lambda v: jnp.exp(v - lse),
+                s * scale,
+            )
             dp = lax.dot_general(do, v, (((1,), (1,)), ((), ())), preferred_element_type=jnp.float32)
             p_buf[:, pl.ds(first, block_k)] = p
             dp_buf[:, pl.ds(first, block_k)] = dp
@@ -319,7 +333,8 @@
     branch_low = middle_grad.astype(jnp.bfloat16)
     grad_b_o = jnp.sum(branch_low, axis=(0, 1), dtype=jnp.float32)
     grad_b_out = jnp.sum(upstream, axis=(0, 1), dtype=jnp.float32)
-    summed_in = halving_sum(grad_w_in * factor, 0)
+    feed_buffer, scaled_in = lax.optimization_barrier((feed_buffer, grad_w_in * factor))
+    summed_in = halving_sum(scaled_in, 0)
     summed_out = halving_sum(grad_w_out * factor, 1)
     summed_in, summed_out, branch_low = lax.optimization_barrier(
         (summed_in, summed_out, branch_low)
@@ -415,22 +430,12 @@
 
 
 def reduce_vectors(vectors, factor):
-    tensor_count = lax.axis_size("tensor")
-    group_count = lax.axis_size("group")
-    dp_count = lax.axis_size("dp")
-    pieces = [
-        jnp.transpose((item * factor).reshape(group_count * dp_count, tensor_count, -1), (1, 0, 2))
-        for item in vectors
-    ]
-    widths = [piece.shape[2] for piece in pieces]
-    packed = jnp.concatenate(pieces, 2)
-    packed = halving_steps(
-        packed, 0, [("tensor", tensor_count, bit) for bit in (8, 4, 2, 1)]
-    )
-    packed = halving_steps(
-        packed, 1, [("group", group_count, 2), ("group", group_count, 1), ("dp", dp_count, 1)]
-    )
-    flat = packed.reshape(-1)
+    devices = lax.axis_size("group") * lax.axis_size("dp") * lax.axis_size("tensor")
+    pieces = [(item * factor).reshape(devices, -1) for item in vectors]
+    widths = [piece.shape[1] for piece in pieces]
+    packed = jnp.concatenate(pieces, 1)
+    packed = lax.all_to_all(packed, ("group", "dp", "tensor"), 0, 0, tiled=True)
+    flat = jnp.sum(packed, axis=0)
     parts = []
     offset = 0
     for width in widths:

time: 711 us -> 737 us (1.037)
  Pallas kernels: 52.5 us -> 23.1 us
  starting transfers between devices: 30.9 us -> 56.6 us
  waiting for transfers between devices: 420 us -> 438 us
  matrix products: 87.5 us -> 96.9 us
    all_to_all x0 -> x2, starting transfers between devices: none -> 46.1 us  [reduce_vectors(): packed = lax.all_to_all(packed, ('group', 'dp', 'tensor'), 0, 0, tiled=True)]
    ppermute x26 -> x12, waiting for transfers between devices: 61.2 us -> 37.6 us  [halving_steps(): got = lax.ppermute(send, axis, [(i, i ^ bit) for i in range(size)])]
    reduce_scatter x1, waiting for transfers between devices: 0.01 us -> 23.6 us  [shards(): lax.psum_scatter(second_part, 'tensor', scatter_dimension=0, tiled=True)]
    ppermute x26 -> x12, starting transfers between devices: 30 us -> 9.76 us  [halving_steps(): got = lax.ppermute(send, axis, [(i, i ^ bit) for i in range(size)])]
    pallas_call x1, Pallas kernels: 28.1 us -> 9.9 us  [attention_backward(): pl.pallas_call(kernel, out_shape=tuple((jax.ShapeDtypeStruct((n, d), jnp....]
    pallas_call x1, Pallas kernels: 24.5 us -> 13.2 us  [attention_forward(): pl.pallas_call(kernel, out_shape=(jax.ShapeDtypeStruct((n, d), jnp.bfloat...]
    all_gather x1, waiting for transfers between devices: 32.1 us -> 43.3 us  [shards(): upstream_full = lax.all_gather(upstream, 'tensor', axis=0, tiled=True)]
  transfers between devices with their start and end apart: 33 -> 21, of which waited for: 22 -> 15; matrix products, arithmetic and copies ran while one was open for 17% -> 18% of each run, Pallas kernels for 3% -> 2%
where the time goes in v10:
time: 737 us; the launch traced here: 723 us
  waiting for transfers between devices  438 us (59%)
  matrix products  96.9 us (13%)
  starting transfers between devices  56.6 us (8%)
  local copies, waits for them, and re-layouts  46.1 us (6%)
  other arithmetic  45.9 us (6%)
  Pallas kernels  23.1 us (3%)
  between operations  16.6 us (2%)
    reduce_scatter x1, waiting for transfers between devices, shards(): lax.psum_scatter(attention_part, 'tensor', scatter_dimension=0, tiled=True)  77.6 us
    all_gather x1, waiting for transfers between devices, shards(): piece = lax.all_gather(branch_low, 'tensor', axis=0, tiled=True)  70.2 us
    all_gather x1, waiting for transfers between devices, shards(): second_full = lax.all_gather(second_low, 'tensor', axis=0, tiled=True)  69.7 us
    all_gather x1, waiting for transfers between devices, shards(): normed_full = lax.all_gather(normed_low, 'tensor', axis=0, tiled=True)  65.3 us
    reduce_scatter x1, waiting for transfers between devices, shards(): both = lax.psum_scatter(merged, 'tensor', scatter_dimension=0, tiled=True)  50.5 us
    all_to_all x2, starting transfers between devices, reduce_vectors(): packed = lax.all_to_all(packed, ('group', 'dp', 'tensor'), 0, 0, tiled=True)  46.1 us
    all_gather x1, waiting for transfers between devices, shards(): upstream_full = lax.all_gather(upstream, 'tensor', axis=0, tiled=True)  43.3 us
    ppermute x12, waiting for transfers between devices, halving_steps(): got = lax.ppermute(send, axis, [(i, i ^ bit) for i in range(size)])  37.6 us
  transfers between devices with their start and end apart: 21, of which 15 were waited for; matrix products, arithmetic and copies ran while one was open for 18% of the time, Pallas kernels for 2%

profile of v10, /device:TPU:96, one launch (start us, length us, event | category | flops | bytes accessed | tf_op | source)
XLA Modules:
  0.0 723.3 jit_solution(3431816188248457981)
XLA Ops:
  18.9 65.3 %all-gather.5.cloned.1.call-done = bf16[2048,1,2048]{2,0,1:T(8,128)(2,1)} async-done(((bf16[128,1,2048]{2,0,1:T(8,128)(2,1)}), bf16[2048,1,2048]{2,0,1:T(8,128)(2,1)}) %all-gather.5.cloned.1.call-update) | async-done | bytes 8388624 | tf_op jit(solution)/shard_map/all_gather | solution.py:246
  84.3 7.4 %fusion.38 = f32[2048,1,3,128]{3,0,2,1:T(8,128)S(1)} fusion(bf16[2048,1,2048]{2,0,1:T(8,128)(2,1)} %all-gather.5.cloned.1.call-done, bf16[2048,3,1,128]{0,3,1,2:T(8,128)(2,1)} %copy.35), kind=kOutput, calls=%fused_computation.41 | convolution fusion | flops 3221225472 | bytes 13107200 | tf_op jit(solution)/shard_map/dot_general | solution.py:248
  93.7 13.2 %shard_map.254 = (bf16[2048,128]{1,0:T(8,128)(2,1)}, f32[2048,1]{1,0:T(8,128)}) custom-call(s32[1]{0:T(128)} %dynamic_slice.7.len_ref, bf16[2048,128]{1,0:T(8,128)(2,1)} %get-tuple-element.123.q_ref, bf16[2048,128]{1,0:T(8,128)(2,1)} %fusion.67.k_ref, bf16[2048,128]{1,0:T(8,128)(2,1)} %get-tuple-element.122.v_ref), custom_call_target="tpu_custom_call" | custom-call | flops 1207959552 | bytes 2097152 | tf_op jit(solution)/shard_map/pallas_call | solution.py:85
  113.5 43.3 %all-gather.7.cloned.1.call-done = bf16[2048,1,2048]{2,0,1:T(8,128)(2,1)} async-done(((bf16[128,1,2048]{2,0,1:T(8,128)(2,1)}), bf16[2048,1,2048]{2,0,1:T(8,128)(2,1)}) %all-gather.7.cloned.1.call-update) | async-done | bytes 8388624 | tf_op jit(solution)/shard_map/all_gather | solution.py:277
  156.9 10.5 %fusion.32 = f32[2048,1,512]{2,0,1:T(8,128)} fusion(bf16[512,2048]{1,0:T(8,128)(2,1)} %param.28, bf16[2048,1,2048]{2,0,1:T(8,128)(2,1)} %all-gather.7.cloned.1.call-done), kind=kOutput, calls=%fused_computation.38 | convolution fusion | flops 4294967296 | bytes 14680064 | tf_op jit(solution)/shard_map/rsd,fd->rsf/dot_general | solution.py:289
  167.4 77.6 %reduce-scatter.4.cloned.1.call-done = bf16[128,1,2048]{2,0,1:T(8,128)(2,1)} async-done(((bf16[2048,1,2048]{2,0,1:T(8,128)(2,1)}), bf16[128,1,2048]{2,0,1:T(8,128)(2,1)}) %reduce-scatter.4.cloned.1.call-update) | async-done | bytes 524304 | tf_op jit(solution)/shard_map/reduce_scatter | solution.py:283
  248.3 69.7 %all-gather.9.cloned.1.call-done = bf16[2048,1,2048]{2,0,1:T(8,128)(2,1)} async-done(((bf16[128,1,2048]{2,0,1:T(8,128)(2,1)}), bf16[2048,1,2048]{2,0,1:T(8,128)(2,1)}) %all-gather.9.cloned.1.call-update) | async-done | bytes 8388624 | tf_op jit(solution)/shard_map/all_gather | solution.py:292
  318.0 7.0 fusion.6
  330.7 6.9 convert_bitcast_fusion.1
  341.0 11.7 %fusion.26 = f32[512,2048]{1,0:T(8,128)} fusion(bf16[2048,1,2048]{2,0,1:T(8,128)(2,1)} %all-gather.7.cloned.1.call-done, f32[]{:T(128)S(6)} %div.68, f32[2048,512]{1,0:T(8,128)} %copy-done.12, f32[512]{0:T(512)S(1)} %copy-done.23), kind=kOutput, calls=%fused_computation.36 | convolution fusion | flops 4306501632 | bytes 16779268 | tf_op jit(solution)/shard_map/rsf,rsd->fd/dot_general | solution.py:303
  359.3 7.5 %copy.36 = f32[512,2,2,512]{0,3,1,2:T(8,128)} copy(f32[512,2,2,512]{3,2,1,0:T(2,128)} %reshape.427) | data formatting | bytes 8388608 | tf_op jit(solution)/shard_map/reshape | solution.py:467
  369.6 10.0 %fusion.29 = f32[2048,512]{1,0:T(8,128)} fusion(bf16[2048,512]{1,0:T(8,128)(2,1)S(1)} %copy-done.16, bf16[2048,1,2048]{2,0,1:T(8,128)(2,1)} %all-gather.9.cloned.1.call-done, f32[]{:T(128)S(6)} %div.68), kind=kOutput, calls=%fused_computation.37 | convolution fusion | flops 4296015872 | bytes 14680068 | tf_op jit(solution)/shard_map/rd,rf->df/dot_general | solution.py:307
  386.6 6.9 dynamic_update_slice.12
  398.5 23.6 %reduce-scatter.6.cloned.1.call-done = bf16[128,1,2048]{2,0,1:T(8,128)(2,1)} async-done(((bf16[2048,1,2048]{2,0,1:T(8,128)(2,1)}), bf16[128,1,2048]{2,0,1:T(8,128)(2,1)}) %reduce-scatter.6.cloned.1.call-update) | async-done | bytes 524304 | tf_op jit(solution)/shard_map/reduce_scatter | solution.py:318
  430.5 12.7 %collective-permute-done.1 = bf16[2,256,512]{2,1,0:T(8,128)(2,1)S(1)} collective-permute-done((bf16[2,256,512]{2,1,0:T(8,128)(2,1)S(1)}, bf16[2,256,512]{2,1,0:T(8,128)(2,1)S(1)}, u32[]{:S(2)}, u32[]{:S(2)}) %collective-permute-start.1) | collective-permute-done | bytes 524320 | tf_op jit(solution)/shard_map/ppermute | solution.py:457
  446.0 6.7 collective-permute-done.2
  453.7 70.2 %all-gather.11.cloned.1.call-done = bf16[2048,1,2048]{2,0,1:T(8,128)(2,1)} async-done(((bf16[128,1,2048]{2,0,1:T(8,128)(2,1)}), bf16[2048,1,2048]{2,0,1:T(8,128)(2,1)}) %all-gather.11.cloned.1.call-update) | async-done | bytes 8388624 | tf_op jit(solution)/shard_map/all_gather | solution.py:342
  530.4 9.9 %shard_map.255 = (bf16[2048,128]{1,0:T(8,128)(2,1)}, bf16[2048,128]{1,0:T(8,128)(2,1)}, bf16[2048,128]{1,0:T(8,128)(2,1)}) custom-call(s32[1]{0:T(128)} %dynamic_slice.7.len_ref, bf16[2048,128]{1,0:T(8,128)(2,1)} %get-tuple-element.123.q_ref, bf16[2048,128]{1,0:T(8,128)(2,1)} %fusion.67.k_ref, bf16[2048,128]{1,0:T(8,128)(2,1)} %get-tuple-element.122.v_ref, ...), custom_call_target="tpu_custom_call" | custom-call | flops 2415919104 | bytes 4194304 | tf_op jit(solution)/shard_map/pallas_call | solution.py:185
  543.7 9.6 %bitcast_dynamic-update-slice_fusion = bf16[2048,1,4096]{2,0,1:T(8,128)(2,1)} fusion(bf16[2048,1,4096]{2,0,1:T(8,128)(2,1)} %dynamic_update_slice.12, bf16[2048,384]{0,1:T(8,128)(2,1)} %bitcast.155, bf16[2048,384]{0,1:T(8,128)(2,1)} %bitcast.152), kind=kOutput, calls=%fused_computation | convolution fusion | flops 3225419776 | bytes 11534336 | tf_op jit(solution)/shard_map/rsc,dc->rsd/dot_general | solution.py:368
  569.3 37.9 %all-to-all-start = ((f32[128,1,176]{2,1,0:T(1,128)}), f32[128,1,176]{2,1,0:T(1,128)S(1)}, u32[]{:S(2)}, u32[]{:S(2)}) async-start(f32[128,1,176]{2,1,0:T(1,128)} %copy.39), calls=%async_computation.3 | async-start | bytes 262144 | tf_op jit(solution)/shard_map/all_to_all | solution.py:437
  609.3 8.1 %fusion.35 = f32[2048,384]{1,0:T(8,128)S(1)} fusion(bf16[2048,384]{0,1:T(8,128)(2,1)} %bitcast.156, bf16[2048,1,2048]{2,0,1:T(8,128)(2,1)} %all-gather.5.cloned.1.call-done, f32[]{:T(128)S(6)} %div.68), kind=kOutput, calls=%fused_computation.40 | convolution fusion | flops 3222011904 | bytes 13107204 | tf_op jit(solution)/shard_map/rd,rc->dc/dot_general | solution.py:362
  627.9 7.5 %collective-permute-done.7 = bf16[2,256,384]{2,1,0:T(8,128)(2,1)S(1)} collective-permute-done((bf16[2,256,384]{2,1,0:T(8,128)(2,1)S(1)}, bf16[2,256,384]{2,1,0:T(8,128)(2,1)S(1)}, u32[]{:S(2)}, u32[]{:S(2)}) %collective-permute-start.7) | collective-permute-done | bytes 393248 | tf_op jit(solution)/shard_map/ppermute | solution.py:457
  644.2 50.5 %reduce-scatter.8.cloned.1.call-done = bf16[128,1,4096]{2,0,1:T(8,128)(2,1)} async-done(((bf16[2048,1,4096]{2,0,1:T(8,128)(2,1)}), bf16[128,1,4096]{2,0,1:T(8,128)(2,1)}) %reduce-scatter.8.cloned.1.call-update) | async-done | bytes 1048592 | tf_op jit(solution)/shard_map/reduce_scatter | solution.py:376
  699.9 8.2 %all-to-all-start.1 = ((f32[128,1,16]{2,1,0:T(1,128)}), f32[128,1,16]{2,1,0:T(1,128)S(1)}, u32[]{:S(2)}, u32[]{:S(2)}) async-start(f32[128,1,16]{2,1,0:T(1,128)} %bitcast.51), calls=%async_computation.4 | async-start | bytes 131072 | tf_op jit(solution)/shard_map/all_to_all | solution.py:437
  (194 shorter events, 124.8 us)
Async XLA Ops:
  7.2 310.8 %copy-start = (bf16[2048,512]{1,0:T(8,128)(2,1)S(1)}, bf16[2048,512]{1,0:T(8,128)(2,1)}, u32[]{:S(2)}) copy-start(bf16[2048,512]{1,0:T(8,128)(2,1)} %param.26) | copy-start | bytes 6291460
  7.2 77.1 %all-gather.5.cloned.1.call-start = ((), (), s32[]{:S(2)}) async-start(), calls=%async_computation.5 | async-start | bytes 8912896 | tf_op jit(solution)/shard_map/all_gather | solution.py:246
  12.2 144.6 %all-gather.7.cloned.1.call-start = ((), (), s32[]{:S(2)}) async-start(), calls=%async_computation.6 | async-start | bytes 8912896 | tf_op jit(solution)/shard_map/all_gather | solution.py:277
  16.2 228.7 %reduce-scatter.4.cloned.1.call-start = ((), (), s32[]{:S(2)}) async-start(), calls=%async_computation.7 | async-start | bytes 8912896 | tf_op jit(solution)/shard_map/reduce_scatter | solution.py:283
  156.8 88.1 %copy-start.20 = (f32[2048]{0:T(1024)S(1)}, f32[2048]{0:T(1024)}, u32[]{:S(2)}) copy-start(f32[2048]{0:T(1024)} %param.23) | copy-start | bytes 24580
  156.8 161.2 %all-gather.9.cloned.1.call-start = ((), (), s32[]{:S(2)}) async-start(), calls=%async_computation.8 | async-start | bytes 8912896 | tf_op jit(solution)/shard_map/all_gather | solution.py:292
  167.4 79.4 %copy-start.21 = (f32[2048]{0:T(1024)S(1)}, f32[2048]{0:T(1024)}, u32[]{:S(2)}) copy-start(f32[2048]{0:T(1024)} %param.25) | copy-start | bytes 24580
  247.8 174.3 %reduce-scatter.6.cloned.1.call-start = ((), (), s32[]{:S(2)}) async-start(), calls=%async_computation.9 | async-start | bytes 8912896 | tf_op jit(solution)/shard_map/reduce_scatter | solution.py:318
  337.6 186.2 %all-gather.11.cloned.1.call-start = ((), (), s32[]{:S(2)}) async-start(), calls=%async_computation.10 | async-start | bytes 8912896 | tf_op jit(solution)/shard_map/all_gather | solution.py:342
  369.3 10.3 %collective-permute-start.3 = (bf16[512,4,256]{0,2,1:T(8,128)(2,1)S(1)}, bf16[512,4,256]{0,2,1:T(8,128)(2,1)S(1)}, u32[]{:S(2)}, u32[]{:S(2)}) collective-permute-start(bf16[512,4,256]{0,2,1:T(8,128)(2,1)S(1)} %select_convert_fusion), channel_id=1, source_target_pairs={{0,32},{32,0},{64,96},{96,64},{1,33},{33,1},{65,97},{97,65},{2,34}... | collective-permute-start | bytes 3145736 | tf_op jit(solution)/shard_map/ppermute | solution.py:457
  380.4 14.9 %collective-permute-start.4 = (bf16[512,2,256]{0,2,1:T(8,128)(2,1)S(1)}, bf16[512,2,256]{0,2,1:T(8,128)(2,1)S(1)}, u32[]{:S(2)}, u32[]{:S(2)}) collective-permute-start(bf16[512,2,256]{0,2,1:T(8,128)(2,1)S(1)} %select_convert_fusion.3), channel_id=1, source_target_pairs={{0,64},{32,96},{64,0},{96,32},{1,65},{33,97},{65,1},{97,33},{2,66}... | collective-permute-start | bytes 1572872 | tf_op jit(solution)/shard_map/ppermute | solution.py:457
  397.2 28.8 %collective-permute-start.5 = (bf16[512,1,256]{0,2,1:T(8,128)(2,1)}, bf16[512,1,256]{0,2,1:T(8,128)(2,1)S(1)}, u32[]{:S(2)}, u32[]{:S(2)}) collective-permute-start(bf16[512,1,256]{0,2,1:T(8,128)(2,1)} %select_convert_fusion.7), channel_id=1, source_target_pairs={{0,16},{16,0},{1,17},{17,1},{2,18},{18,2},{3,19},{19,3},{4,20},{20... | collective-permute-start | bytes 786440 | tf_op jit(solution)/shard_map/ppermute | solution.py:457
  426.0 2.7 collective-permute-start
  429.2 14.0 %collective-permute-start.1 = (bf16[2,256,512]{2,1,0:T(8,128)(2,1)S(1)}, bf16[2,256,512]{2,1,0:T(8,128)(2,1)S(1)}, u32[]{:S(2)}, u32[]{:S(2)}) collective-permute-start(bf16[2,256,512]{2,1,0:T(8,128)(2,1)S(1)} %select_convert_fusion.4), channel_id=1, source_target_pairs={{0,64},{32,96},{64,0},{96,32},{1,65},{33,97},{65,1},{97,33},{2,66}... | collective-permute-start | bytes 1572872 | tf_op jit(solution)/shard_map/ppermute | solution.py:457
  443.6 9.1 %collective-permute-start.2 = (bf16[1,256,512]{2,1,0:T(8,128)(2,1)S(1)}, bf16[1,256,512]{2,1,0:T(8,128)(2,1)S(1)}, u32[]{:S(2)}, u32[]{:S(2)}) collective-permute-start(bf16[1,256,512]{2,1,0:T(8,128)(2,1)S(1)} %select_convert_fusion.8), channel_id=1, source_target_pairs={{0,16},{16,0},{1,17},{17,1},{2,18},{18,2},{3,19},{19,3},{4,20},{20... | collective-permute-start | bytes 786440 | tf_op jit(solution)/shard_map/ppermute | solution.py:457
  453.6 241.1 %reduce-scatter.8.cloned.1.call-start = ((), (), s32[]{:S(2)}) async-start(), calls=%async_computation.11 | async-start | bytes 17825792 | tf_op jit(solution)/shard_map/reduce_scatter | solution.py:376
  569.3 50.0 %all-to-all-start = ((f32[128,1,176]{2,1,0:T(1,128)}), f32[128,1,176]{2,1,0:T(1,128)S(1)}, u32[]{:S(2)}, u32[]{:S(2)}) async-start(f32[128,1,176]{2,1,0:T(1,128)} %copy.39), calls=%async_computation.3 | async-start | bytes 262144 | tf_op jit(solution)/shard_map/all_to_all | solution.py:437
  609.1 11.5 %collective-permute-start.9 = (bf16[1,128,4,256]{1,3,2,0:T(8,128)(2,1)}, bf16[1,128,4,256]{1,3,2,0:T(8,128)(2,1)S(1)}, u32[]{:S(2)}, u32[]{:S(2)}) collective-permute-start(bf16[1,128,4,256]{1,3,2,0:T(8,128)(2,1)} %select_convert_fusion.6), channel_id=1, source_target_pairs={{0,32},{32,0},{64,96},{96,64},{1,33},{33,1},{65,97},{97,65},{2,34}... | collective-permute-start | bytes 786440 | tf_op jit(solution)/shard_map/ppermute | solution.py:457
  617.5 3.9 collective-permute-start.6
  620.8 6.1 collective-permute-start.10
  623.3 12.1 %collective-permute-start.7 = (bf16[2,256,384]{2,1,0:T(8,128)(2,1)S(1)}, bf16[2,256,384]{2,1,0:T(8,128)(2,1)S(1)}, u32[]{:S(2)}, u32[]{:S(2)}) collective-permute-start(bf16[2,256,384]{2,1,0:T(8,128)(2,1)S(1)} %select_convert_fusion.5), channel_id=1, source_target_pairs={{0,64},{32,96},{64,0},{96,32},{1,65},{33,97},{65,1},{97,33},{2,66}... | collective-permute-start | bytes 1179656 | tf_op jit(solution)/shard_map/ppermute | solution.py:457
  627.0 9.8 %collective-permute-start.11 = (bf16[1,128,1,256]{1,3,2,0:T(8,128)(2,1)S(1)}, bf16[1,128,1,256]{1,3,2,0:T(8,128)(2,1)S(1)}, u32[]{:S(2)}, u32[]{:S(2)}) collective-permute-start(bf16[1,128,1,256]{1,3,2,0:T(8,128)(2,1)S(1)} %select_convert_fusion.11), channel_id=1, source_target_pairs={{0,16},{16,0},{1,17},{17,1},{2,18},{18,2},{3,19},{19,3},{4,20},{20... | collective-permute-start | bytes 196616 | tf_op jit(solution)/shard_map/ppermute | solution.py:457
  635.6 7.4 %collective-permute-start.8 = (bf16[1,256,384]{2,1,0:T(8,128)(2,1)S(1)}, bf16[1,256,384]{2,1,0:T(8,128)(2,1)S(1)}, u32[]{:S(2)}, u32[]{:S(2)}) collective-permute-start(bf16[1,256,384]{2,1,0:T(8,128)(2,1)S(1)} %select_convert_fusion.9), channel_id=1, source_target_pairs={{0,16},{16,0},{1,17},{17,1},{2,18},{18,2},{3,19},{19,3},{4,20},{20... | collective-permute-start | bytes 589832 | tf_op jit(solution)/shard_map/ppermute | solution.py:457
  699.9 15.4 %all-to-all-start.1 = ((f32[128,1,16]{2,1,0:T(1,128)}), f32[128,1,16]{2,1,0:T(1,128)S(1)}, u32[]{:S(2)}, u32[]{:S(2)}) async-start(f32[128,1,16]{2,1,0:T(1,128)} %bitcast.51), calls=%async_computation.4 | async-start | bytes 131072 | tf_op jit(solution)/shard_map/all_to_all | solution.py:437
  (24 other events, 529.3 us)
Sparse Core Ops, SparseCore 0:
  12.3 71.8 all-gather.4
  86.4 70.3 all-gather.6
  160.2 84.6 reduce-scatter.3
  247.9 70.0 all-gather.8
  337.7 84.3 reduce-scatter.5
  453.8 70.0 all-gather.10
  553.5 141.1 reduce-scatter.7

commit v11 on v10

--- a/solution.py
+++ b/solution.py
@@ -333,8 +333,7 @@
     branch_low = middle_grad.astype(jnp.bfloat16)
     grad_b_o = jnp.sum(branch_low, axis=(0, 1), dtype=jnp.float32)
     grad_b_out = jnp.sum(upstream, axis=(0, 1), dtype=jnp.float32)
-    feed_buffer, scaled_in = lax.optimization_barrier((feed_buffer, grad_w_in * factor))
-    summed_in = halving_sum(scaled_in, 0)
+    summed_in = halving_sum(grad_w_in * factor, 0)
     summed_out = halving_sum(grad_w_out * factor, 1)
     summed_in, summed_out, branch_low = lax.optimization_barrier(
         (summed_in, summed_out, branch_low)

time: 737 us -> 713 us (0.967)
  waiting for transfers between devices: 438 us -> 412 us
    reduce_scatter x1, waiting for transfers between devices: 23.6 us -> 0.01 us  [shards(): lax.psum_scatter(second_part, 'tensor', scatter_dimension=0, tiled=True)]
  transfers between devices with their start and end apart: 21 -> 21, of which waited for: 15 -> 12; matrix products, arithmetic and copies ran while one was open for 18% -> 18% of each run, Pallas kernels for 2% -> 2%
where the time goes in v11:
time: 713 us; the launch traced here: 700 us
  waiting for transfers between devices  412 us (58%)
  matrix products  92.3 us (13%)
  starting transfers between devices  57.4 us (8%)
  other arithmetic  51 us (7%)
  local copies, waits for them, and re-layouts  47.2 us (7%)
  Pallas kernels  23.1 us (3%)
  between operations  16.6 us (2%)
    reduce_scatter x1, waiting for transfers between devices, shards(): lax.psum_scatter(attention_part, 'tensor', scatter_dimension=0, tiled=True)  77.3 us
    all_gather x1, waiting for transfers between devices, shards(): piece = lax.all_gather(branch_low, 'tensor', axis=0, tiled=True)  70.2 us
    all_gather x1, waiting for transfers between devices, shards(): second_full = lax.all_gather(second_low, 'tensor', axis=0, tiled=True)  69.6 us
    all_gather x1, waiting for transfers between devices, shards(): normed_full = lax.all_gather(normed_low, 'tensor', axis=0, tiled=True)  65.4 us
    reduce_scatter x1, waiting for transfers between devices, shards(): both = lax.psum_scatter(merged, 'tensor', scatter_dimension=0, tiled=True)  50.6 us
    all_to_all x2, starting transfers between devices, reduce_vectors(): packed = lax.all_to_all(packed, ('group', 'dp', 'tensor'), 0, 0, tiled=True)  46.1 us
    all_gather x1, waiting for transfers between devices, shards(): upstream_full = lax.all_gather(upstream, 'tensor', axis=0, tiled=True)  43.3 us
    ppermute x12, waiting for transfers between devices, halving_steps(): got = lax.ppermute(send, axis, [(i, i ^ bit) for i in range(size)])  35.6 us
  transfers between devices with their start and end apart: 21, of which 12 were waited for; matrix products, arithmetic and copies ran while one was open for 18% of the time, Pallas kernels for 2%

profile of v11, /device:TPU:96, one launch (start us, length us, event | category | flops | bytes accessed | tf_op | source)
XLA Modules:
  0.0 699.9 jit_solution(3255084776874233470)
XLA Ops:
  18.9 65.4 %all-gather.5.cloned.1.call-done = bf16[2048,1,2048]{2,0,1:T(8,128)(2,1)} async-done(((bf16[128,1,2048]{2,0,1:T(8,128)(2,1)}), bf16[2048,1,2048]{2,0,1:T(8,128)(2,1)}) %all-gather.5.cloned.1.call-update) | async-done | bytes 8388624 | tf_op jit(solution)/shard_map/all_gather | solution.py:246
  84.3 7.4 %fusion.38 = f32[2048,1,3,128]{3,0,2,1:T(8,128)S(1)} fusion(bf16[2048,1,2048]{2,0,1:T(8,128)(2,1)} %all-gather.5.cloned.1.call-done, bf16[2048,3,1,128]{0,3,1,2:T(8,128)(2,1)} %copy.35), kind=kOutput, calls=%fused_computation.41 | convolution fusion | flops 3221225472 | bytes 13107200 | tf_op jit(solution)/shard_map/dot_general | solution.py:248
  93.7 13.2 %shard_map.254 = (bf16[2048,128]{1,0:T(8,128)(2,1)}, f32[2048,1]{1,0:T(8,128)}) custom-call(s32[1]{0:T(128)} %dynamic_slice.7.len_ref, bf16[2048,128]{1,0:T(8,128)(2,1)} %get-tuple-element.119.q_ref, bf16[2048,128]{1,0:T(8,128)(2,1)} %fusion.67.k_ref, bf16[2048,128]{1,0:T(8,128)(2,1)} %get-tuple-element.118.v_ref), custom_call_target="tpu_custom_call" | custom-call | flops 1207959552 | bytes 2097152 | tf_op jit(solution)/shard_map/pallas_call | solution.py:85
  113.5 43.3 %all-gather.7.cloned.1.call-done = bf16[2048,1,2048]{2,0,1:T(8,128)(2,1)} async-done(((bf16[128,1,2048]{2,0,1:T(8,128)(2,1)}), bf16[2048,1,2048]{2,0,1:T(8,128)(2,1)}) %all-gather.7.cloned.1.call-update) | async-done | bytes 8388624 | tf_op jit(solution)/shard_map/all_gather | solution.py:277
  156.9 10.5 %fusion.32 = f32[2048,1,512]{2,0,1:T(8,128)} fusion(bf16[512,2048]{1,0:T(8,128)(2,1)} %param.28, bf16[2048,1,2048]{2,0,1:T(8,128)(2,1)} %all-gather.7.cloned.1.call-done), kind=kOutput, calls=%fused_computation.38 | convolution fusion | flops 4294967296 | bytes 14680064 | tf_op jit(solution)/shard_map/rsd,fd->rsf/dot_general | solution.py:289
  167.4 77.3 %reduce-scatter.4.cloned.1.call-done = bf16[128,1,2048]{2,0,1:T(8,128)(2,1)} async-done(((bf16[2048,1,2048]{2,0,1:T(8,128)(2,1)}), bf16[128,1,2048]{2,0,1:T(8,128)(2,1)}) %reduce-scatter.4.cloned.1.call-update) | async-done | bytes 524304 | tf_op jit(solution)/shard_map/reduce_scatter | solution.py:283
  248.1 69.6 %all-gather.9.cloned.1.call-done = bf16[2048,1,2048]{2,0,1:T(8,128)(2,1)} async-done(((bf16[128,1,2048]{2,0,1:T(8,128)(2,1)}), bf16[2048,1,2048]{2,0,1:T(8,128)(2,1)}) %all-gather.9.cloned.1.call-update) | async-done | bytes 8388624 | tf_op jit(solution)/shard_map/all_gather | solution.py:292
  317.7 7.0 %fusion.6 = f32[2048,512]{1,0:T(8,128)S(1)} fusion(bf16[2048,512]{1,0:T(8,128)(2,1)S(1)} %copy-done, bf16[2048,1,2048]{2,0,1:T(8,128)(2,1)} %all-gather.9.cloned.1.call-done), kind=kOutput, calls=%fused_computation.7 | convolution fusion | flops 4294967296 | bytes 14680064 | tf_op jit(solution)/shard_map/dot_general | solution.py:294
  330.4 6.9 convert_bitcast_fusion.1
  340.8 7.1 %fusion.29 = f32[2048,512]{1,0:T(8,128)S(1)} fusion(bf16[2048,512]{1,0:T(8,128)(2,1)S(1)} %copy-done.14, bf16[2048,1,2048]{2,0,1:T(8,128)(2,1)} %all-gather.9.cloned.1.call-done, f32[]{:T(128)S(6)} %div.71), kind=kOutput, calls=%fused_computation.37 | convolution fusion | flops 4296015872 | bytes 14680068 | tf_op jit(solution)/shard_map/rd,rf->df/dot_general | solution.py:307
  350.1 10.0 %fusion.26 = f32[512,2048]{1,0:T(8,128)} fusion(bf16[2048,1,2048]{2,0,1:T(8,128)(2,1)} %all-gather.7.cloned.1.call-done, f32[]{:T(128)S(6)} %div.71, f32[2048,512]{1,0:T(8,128)S(1)} %copy-done.10, f32[512]{0:T(512)S(1)} %copy-done.22), kind=kOutput, calls=%fused_computation.36 | convolution fusion | flops 4306501632 | bytes 16779268 | tf_op jit(solution)/shard_map/rsf,rsd->fd/dot_general | solution.py:303
  360.1 6.7 reshape.427
  366.8 7.3 %copy.36 = f32[512,2,2,512]{0,3,1,2:T(8,128)} copy(f32[512,2,2,512]{3,2,1,0:T(2,128)} %reshape.427) | data formatting | bytes 8388608 | tf_op jit(solution)/shard_map/reshape | solution.py:466
  388.7 10.6 %collective-permute-done.1 = bf16[2,256,512]{2,1,0:T(8,128)(2,1)S(1)} collective-permute-done((bf16[2,256,512]{2,1,0:T(8,128)(2,1)S(1)}, bf16[2,256,512]{2,1,0:T(8,128)(2,1)S(1)}, u32[]{:S(2)}, u32[]{:S(2)}) %collective-permute-start.1) | collective-permute-done | bytes 524320 | tf_op jit(solution)/shard_map/ppermute | solution.py:456
  401.0 9.5 %collective-permute-done.4 = bf16[512,2,256]{0,2,1:T(8,128)(2,1)S(1)} collective-permute-done((bf16[512,2,256]{0,2,1:T(8,128)(2,1)S(1)}, bf16[512,2,256]{0,2,1:T(8,128)(2,1)S(1)}, u32[]{:S(2)}, u32[]{:S(2)}) %collective-permute-start.4) | collective-permute-done | bytes 524320 | tf_op jit(solution)/shard_map/ppermute | solution.py:456
  416.9 6.9 dynamic_update_slice.12
  430.1 70.2 %all-gather.11.cloned.1.call-done = bf16[2048,1,2048]{2,0,1:T(8,128)(2,1)} async-done(((bf16[128,1,2048]{2,0,1:T(8,128)(2,1)}), bf16[2048,1,2048]{2,0,1:T(8,128)(2,1)}) %all-gather.11.cloned.1.call-update) | async-done | bytes 8388624 | tf_op jit(solution)/shard_map/all_gather | solution.py:341
  507.0 9.9 %shard_map.255 = (bf16[2048,128]{1,0:T(8,128)(2,1)}, bf16[2048,128]{1,0:T(8,128)(2,1)}, bf16[2048,128]{1,0:T(8,128)(2,1)}) custom-call(s32[1]{0:T(128)} %dynamic_slice.7.len_ref, bf16[2048,128]{1,0:T(8,128)(2,1)} %get-tuple-element.119.q_ref, bf16[2048,128]{1,0:T(8,128)(2,1)} %fusion.67.k_ref, bf16[2048,128]{1,0:T(8,128)(2,1)} %get-tuple-element.118.v_ref, ...), custom_call_target="tpu_custom_call" | custom-call | flops 2415919104 | bytes 4194304 | tf_op jit(solution)/shard_map/pallas_call | solution.py:185
  520.3 9.8 %bitcast_dynamic-update-slice_fusion = bf16[2048,1,4096]{2,0,1:T(8,128)(2,1)} fusion(bf16[2048,1,4096]{2,0,1:T(8,128)(2,1)} %dynamic_update_slice.12, bf16[2048,384]{0,1:T(8,128)(2,1)} %bitcast.155, bf16[2048,384]{0,1:T(8,128)(2,1)} %bitcast.152), kind=kOutput, calls=%fused_computation | convolution fusion | flops 3225419776 | bytes 11534336 | tf_op jit(solution)/shard_map/rsc,dc->rsd/dot_general | solution.py:367
  545.9 38.0 %all-to-all-start = ((f32[128,1,176]{2,1,0:T(1,128)}), f32[128,1,176]{2,1,0:T(1,128)S(1)}, u32[]{:S(2)}, u32[]{:S(2)}) async-start(f32[128,1,176]{2,1,0:T(1,128)} %copy.39), calls=%async_computation.3 | async-start | bytes 262144 | tf_op jit(solution)/shard_map/all_to_all | solution.py:436
  586.0 8.0 %fusion.35 = f32[2048,384]{1,0:T(8,128)S(1)} fusion(bf16[2048,384]{0,1:T(8,128)(2,1)} %bitcast.156, bf16[2048,1,2048]{2,0,1:T(8,128)(2,1)} %all-gather.5.cloned.1.call-done, f32[]{:T(128)S(6)} %div.71), kind=kOutput, calls=%fused_computation.40 | convolution fusion | flops 3222011904 | bytes 13107204 | tf_op jit(solution)/shard_map/rd,rc->dc/dot_general | solution.py:361
  604.6 7.5 %collective-permute-done.7 = bf16[2,256,384]{2,1,0:T(8,128)(2,1)S(1)} collective-permute-done((bf16[2,256,384]{2,1,0:T(8,128)(2,1)S(1)}, bf16[2,256,384]{2,1,0:T(8,128)(2,1)S(1)}, u32[]{:S(2)}, u32[]{:S(2)}) %collective-permute-start.7) | collective-permute-done | bytes 393248 | tf_op jit(solution)/shard_map/ppermute | solution.py:456
  620.8 50.6 %reduce-scatter.8.cloned.1.call-done = bf16[128,1,4096]{2,0,1:T(8,128)(2,1)} async-done(((bf16[2048,1,4096]{2,0,1:T(8,128)(2,1)}), bf16[128,1,4096]{2,0,1:T(8,128)(2,1)}) %reduce-scatter.8.cloned.1.call-update) | async-done | bytes 1048592 | tf_op jit(solution)/shard_map/reduce_scatter | solution.py:375
  676.6 8.2 %all-to-all-start.1 = ((f32[128,1,16]{2,1,0:T(1,128)}), f32[128,1,16]{2,1,0:T(1,128)S(1)}, u32[]{:S(2)}, u32[]{:S(2)}) async-start(f32[128,1,16]{2,1,0:T(1,128)} %bitcast.51), calls=%async_computation.4 | async-start | bytes 131072 | tf_op jit(solution)/shard_map/all_to_all | solution.py:436
  (192 shorter events, 122.5 us)
Async XLA Ops:
  7.2 310.5 %copy-start = (bf16[2048,512]{1,0:T(8,128)(2,1)S(1)}, bf16[2048,512]{1,0:T(8,128)(2,1)}, u32[]{:S(2)}) copy-start(bf16[2048,512]{1,0:T(8,128)(2,1)} %param.26) | copy-start | bytes 6291460
  7.2 77.1 %all-gather.5.cloned.1.call-start = ((), (), s32[]{:S(2)}) async-start(), calls=%async_computation.5 | async-start | bytes 8912896 | tf_op jit(solution)/shard_map/all_gather | solution.py:246
  12.2 144.6 %all-gather.7.cloned.1.call-start = ((), (), s32[]{:S(2)}) async-start(), calls=%async_computation.6 | async-start | bytes 8912896 | tf_op jit(solution)/shard_map/all_gather | solution.py:277
  16.2 228.5 %reduce-scatter.4.cloned.1.call-start = ((), (), s32[]{:S(2)}) async-start(), calls=%async_computation.7 | async-start | bytes 8912896 | tf_op jit(solution)/shard_map/reduce_scatter | solution.py:283
  156.8 87.9 %copy-start.19 = (f32[2048]{0:T(1024)S(1)}, f32[2048]{0:T(1024)}, u32[]{:S(2)}) copy-start(f32[2048]{0:T(1024)} %param.23) | copy-start | bytes 24580
  156.8 160.8 %all-gather.9.cloned.1.call-start = ((), (), s32[]{:S(2)}) async-start(), calls=%async_computation.8 | async-start | bytes 8912896 | tf_op jit(solution)/shard_map/all_gather | solution.py:292
  247.6 178.1 %reduce-scatter.6.cloned.1.call-start = ((), (), s32[]{:S(2)}) async-start(), calls=%async_computation.9 | async-start | bytes 8912896 | tf_op jit(solution)/shard_map/reduce_scatter | solution.py:318
  337.4 163.0 %all-gather.11.cloned.1.call-start = ((), (), s32[]{:S(2)}) async-start(), calls=%async_computation.10 | async-start | bytes 8912896 | tf_op jit(solution)/shard_map/all_gather | solution.py:341
  350.0 31.1 %collective-permute-start = (bf16[4,256,512]{2,1,0:T(8,128)(2,1)S(1)}, bf16[4,256,512]{2,1,0:T(8,128)(2,1)S(1)}, u32[]{:S(2)}, u32[]{:S(2)}) collective-permute-start(bf16[4,256,512]{2,1,0:T(8,128)(2,1)S(1)} %bitcast.157), channel_id=1, source_target_pairs={{0,32},{32,0},{64,96},{96,64},{1,33},{33,1},{65,97},{97,65},{2,34}... | collective-permute-start | bytes 3145736 | tf_op jit(solution)/shard_map/ppermute | solution.py:456
  377.8 7.5 %collective-permute-start.3 = (bf16[512,4,256]{0,2,1:T(8,128)(2,1)}, bf16[512,4,256]{0,2,1:T(8,128)(2,1)}, u32[]{:S(2)}, u32[]{:S(2)}) collective-permute-start(bf16[512,4,256]{0,2,1:T(8,128)(2,1)} %select_convert_fusion), channel_id=1, source_target_pairs={{0,32},{32,0},{64,96},{96,64},{1,33},{33,1},{65,97},{97,65},{2,34}... | collective-permute-start | bytes 3145736 | tf_op jit(solution)/shard_map/ppermute | solution.py:456
  384.4 14.8 %collective-permute-start.1 = (bf16[2,256,512]{2,1,0:T(8,128)(2,1)S(1)}, bf16[2,256,512]{2,1,0:T(8,128)(2,1)S(1)}, u32[]{:S(2)}, u32[]{:S(2)}) collective-permute-start(bf16[2,256,512]{2,1,0:T(8,128)(2,1)S(1)} %select_convert_fusion.4), channel_id=1, source_target_pairs={{0,64},{32,96},{64,0},{96,32},{1,65},{33,97},{65,1},{97,33},{2,66}... | collective-permute-start | bytes 1572872 | tf_op jit(solution)/shard_map/ppermute | solution.py:456
  387.4 23.1 %collective-permute-start.4 = (bf16[512,2,256]{0,2,1:T(8,128)(2,1)S(1)}, bf16[512,2,256]{0,2,1:T(8,128)(2,1)S(1)}, u32[]{:S(2)}, u32[]{:S(2)}) collective-permute-start(bf16[512,2,256]{0,2,1:T(8,128)(2,1)S(1)} %select_convert_fusion.3), channel_id=1, source_target_pairs={{0,64},{32,96},{64,0},{96,32},{1,65},{33,97},{65,1},{97,33},{2,66}... | collective-permute-start | bytes 1572872 | tf_op jit(solution)/shard_map/ppermute | solution.py:456
  399.6 24.2 %collective-permute-start.2 = (bf16[1,256,512]{2,1,0:T(8,128)(2,1)S(1)}, bf16[1,256,512]{2,1,0:T(8,128)(2,1)S(1)}, u32[]{:S(2)}, u32[]{:S(2)}) collective-permute-start(bf16[1,256,512]{2,1,0:T(8,128)(2,1)S(1)} %select_convert_fusion.8), channel_id=1, source_target_pairs={{0,16},{16,0},{1,17},{17,1},{2,18},{18,2},{3,19},{19,3},{4,20},{20... | collective-permute-start | bytes 786440 | tf_op jit(solution)/shard_map/ppermute | solution.py:456
  410.8 13.9 %collective-permute-start.5 = (bf16[512,1,256]{0,2,1:T(8,128)(2,1)S(1)}, bf16[512,1,256]{0,2,1:T(8,128)(2,1)S(1)}, u32[]{:S(2)}, u32[]{:S(2)}) collective-permute-start(bf16[512,1,256]{0,2,1:T(8,128)(2,1)S(1)} %select_convert_fusion.7), channel_id=1, source_target_pairs={{0,16},{16,0},{1,17},{17,1},{2,18},{18,2},{3,19},{19,3},{4,20},{20... | collective-permute-start | bytes 786440 | tf_op jit(solution)/shard_map/ppermute | solution.py:456
  427.6 79.4 %copy-start.6 = (f32[128,1,2048]{2,0,1:T(8,128)}, f32[128,1,2048]{2,0,1:T(8,128)S(1)}, u32[]{:S(2)}) copy-start(f32[128,1,2048]{2,0,1:T(8,128)S(1)} %get-tuple-element.116) | copy-start | bytes 3145732
  430.1 241.3 %reduce-scatter.8.cloned.1.call-start = ((), (), s32[]{:S(2)}) async-start(), calls=%async_computation.11 | async-start | bytes 17825792 | tf_op jit(solution)/shard_map/reduce_scatter | solution.py:375
  545.9 50.1 %all-to-all-start = ((f32[128,1,176]{2,1,0:T(1,128)}), f32[128,1,176]{2,1,0:T(1,128)S(1)}, u32[]{:S(2)}, u32[]{:S(2)}) async-start(f32[128,1,176]{2,1,0:T(1,128)} %copy.39), calls=%async_computation.3 | async-start | bytes 262144 | tf_op jit(solution)/shard_map/all_to_all | solution.py:436
  585.8 11.5 %collective-permute-start.9 = (bf16[1,128,4,256]{1,3,2,0:T(8,128)(2,1)}, bf16[1,128,4,256]{1,3,2,0:T(8,128)(2,1)S(1)}, u32[]{:S(2)}, u32[]{:S(2)}) collective-permute-start(bf16[1,128,4,256]{1,3,2,0:T(8,128)(2,1)} %select_convert_fusion.6), channel_id=1, source_target_pairs={{0,32},{32,0},{64,96},{96,64},{1,33},{33,1},{65,97},{97,65},{2,34}... | collective-permute-start | bytes 786440 | tf_op jit(solution)/shard_map/ppermute | solution.py:456
  594.2 4.0 collective-permute-start.6
  597.4 6.0 collective-permute-start.10
  600.0 12.1 %collective-permute-start.7 = (bf16[2,256,384]{2,1,0:T(8,128)(2,1)S(1)}, bf16[2,256,384]{2,1,0:T(8,128)(2,1)S(1)}, u32[]{:S(2)}, u32[]{:S(2)}) collective-permute-start(bf16[2,256,384]{2,1,0:T(8,128)(2,1)S(1)} %select_convert_fusion.5), channel_id=1, source_target_pairs={{0,64},{32,96},{64,0},{96,32},{1,65},{33,97},{65,1},{97,33},{2,66}... | collective-permute-start | bytes 1179656 | tf_op jit(solution)/shard_map/ppermute | solution.py:456
  603.6 9.9 %collective-permute-start.11 = (bf16[1,128,1,256]{1,3,2,0:T(8,128)(2,1)S(1)}, bf16[1,128,1,256]{1,3,2,0:T(8,128)(2,1)S(1)}, u32[]{:S(2)}, u32[]{:S(2)}) collective-permute-start(bf16[1,128,1,256]{1,3,2,0:T(8,128)(2,1)S(1)} %select_convert_fusion.11), channel_id=1, source_target_pairs={{0,16},{16,0},{1,17},{17,1},{2,18},{18,2},{3,19},{19,3},{4,20},{20... | collective-permute-start | bytes 196616 | tf_op jit(solution)/shard_map/ppermute | solution.py:456
  612.3 7.3 %collective-permute-start.8 = (bf16[1,256,384]{2,1,0:T(8,128)(2,1)S(1)}, bf16[1,256,384]{2,1,0:T(8,128)(2,1)S(1)}, u32[]{:S(2)}, u32[]{:S(2)}) collective-permute-start(bf16[1,256,384]{2,1,0:T(8,128)(2,1)S(1)} %select_convert_fusion.9), channel_id=1, source_target_pairs={{0,16},{16,0},{1,17},{17,1},{2,18},{18,2},{3,19},{19,3},{4,20},{20... | collective-permute-start | bytes 589832 | tf_op jit(solution)/shard_map/ppermute | solution.py:456
  676.6 15.4 %all-to-all-start.1 = ((f32[128,1,16]{2,1,0:T(1,128)}), f32[128,1,16]{2,1,0:T(1,128)S(1)}, u32[]{:S(2)}, u32[]{:S(2)}) async-start(f32[128,1,16]{2,1,0:T(1,128)} %bitcast.51), calls=%async_computation.4 | async-start | bytes 131072 | tf_op jit(solution)/shard_map/all_to_all | solution.py:436
  (23 other events, 579.2 us)
Sparse Core Ops, SparseCore 0:
  12.3 71.8 all-gather.4
  86.4 70.3 all-gather.6
  160.2 84.4 reduce-scatter.3
  247.7 69.9 all-gather.8
  337.5 84.7 reduce-scatter.5
  430.2 70.1 all-gather.10
  530.2 141.1 reduce-scatter.7

commit v12 on v11

--- a/solution.py
+++ b/solution.py
@@ -77,7 +77,7 @@
     lse_ref[...] = peak + jnp.log(total)
 
 
-def attention_forward(q, k, v, length, *, block_q=256, block_k=256):
+def attention_forward(q, k, v, length, *, block_q=512, block_k=512):
     n, d = q.shape
     scale = 1.0 / math.sqrt(d)
     kernel = partial(_attn_fwd_kernel, block_q=block_q, block_k=block_k, scale=scale)
@@ -175,7 +175,7 @@
         dv_ref[...] = dv_acc[...].astype(dv_ref.dtype)
 
 
-def attention_backward(q, k, v, do, lse, length, *, block_q=256, block_k=256):
+def attention_backward(q, k, v, do, lse, length, *, block_q=512, block_k=512):
     n, d = q.shape
     scale = 1.0 / math.sqrt(d)
     kernel = partial(_attn_bwd_kernel, block_q=block_q, block_k=block_k, scale=scale)

time: 713 us -> 696 us (0.976)
  starting transfers between devices: 57.4 us -> 27.5 us
  Pallas kernels: 23.1 us -> 41.7 us
    all_to_all x2, starting transfers between devices: 46.1 us -> 16.5 us  [reduce_vectors(): packed = lax.all_to_all(packed, ('group', 'dp', 'tensor'), 0, 0, tiled=True)]
    pallas_call x1, Pallas kernels: 9.9 us -> 24.8 us  [attention_backward(): pl.pallas_call(kernel, out_shape=tuple((jax.ShapeDtypeStruct((n, d), jnp....]
  transfers between devices with their start and end apart: 21 -> 21, of which waited for: 12 -> 12; matrix products, arithmetic and copies ran while one was open for 18% -> 19% of each run, Pallas kernels for 2% -> 2%
where the time goes in v12:
time: 696 us; the launch traced here: 685 us
  waiting for transfers between devices  409 us (59%)
  matrix products  92.2 us (13%)
  other arithmetic  50.9 us (7%)
  local copies, waits for them, and re-layouts  46.9 us (7%)
  Pallas kernels  41.7 us (6%)
  starting transfers between devices  27.5 us (4%)
  between operations  16.3 us (2%)
    reduce_scatter x1, waiting for transfers between devices, shards(): lax.psum_scatter(attention_part, 'tensor', scatter_dimension=0, tiled=True)  77.4 us
    all_gather x1, waiting for transfers between devices, shards(): piece = lax.all_gather(branch_low, 'tensor', axis=0, tiled=True)  70.2 us
    all_gather x1, waiting for transfers between devices, shards(): second_full = lax.all_gather(second_low, 'tensor', axis=0, tiled=True)  70.1 us
    all_gather x1, waiting for transfers between devices, shards(): normed_full = lax.all_gather(normed_low, 'tensor', axis=0, tiled=True)  65.4 us
    reduce_scatter x1, waiting for transfers between devices, shards(): both = lax.psum_scatter(merged, 'tensor', scatter_dimension=0, tiled=True)  50.6 us
    all_gather x1, waiting for transfers between devices, shards(): upstream_full = lax.all_gather(upstream, 'tensor', axis=0, tiled=True)  39.7 us
    ppermute x12, waiting for transfers between devices, halving_steps(): got = lax.ppermute(send, axis, [(i, i ^ bit) for i in range(size)])  35.7 us
    pallas_call x1, Pallas kernels, attention_backward(): pl.pallas_call(kernel, out_shape=tuple((jax.ShapeDtypeStruct((n, d), jnp....  24.8 us
  transfers between devices with their start and end apart: 21, of which 12 were waited for; matrix products, arithmetic and copies ran while one was open for 19% of the time, Pallas kernels for 2%

profile of v12, /device:TPU:96, one launch (start us, length us, event | category | flops | bytes accessed | tf_op | source)
XLA Modules:
  0.0 684.9 jit_solution(13205418407284794175)
XLA Ops:
  18.9 65.4 %all-gather.5.cloned.1.call-done = bf16[2048,1,2048]{2,0,1:T(8,128)(2,1)} async-done(((bf16[128,1,2048]{2,0,1:T(8,128)(2,1)}), bf16[2048,1,2048]{2,0,1:T(8,128)(2,1)}) %all-gather.5.cloned.1.call-update) | async-done | bytes 8388624 | tf_op jit(solution)/shard_map/all_gather | solution.py:246
  84.3 7.4 %fusion.38 = f32[2048,1,3,128]{3,0,2,1:T(8,128)S(1)} fusion(bf16[2048,1,2048]{2,0,1:T(8,128)(2,1)} %all-gather.5.cloned.1.call-done, bf16[2048,3,1,128]{0,3,1,2:T(8,128)(2,1)} %copy.35), kind=kOutput, calls=%fused_computation.41 | convolution fusion | flops 3221225472 | bytes 13107200 | tf_op jit(solution)/shard_map/dot_general | solution.py:248
  93.7 16.9 %shard_map.254 = (bf16[2048,128]{1,0:T(8,128)(2,1)}, f32[2048,1]{1,0:T(8,128)}) custom-call(s32[1]{0:T(128)} %dynamic_slice.7.len_ref, bf16[2048,128]{1,0:T(8,128)(2,1)} %get-tuple-element.119.q_ref, bf16[2048,128]{1,0:T(8,128)(2,1)} %fusion.67.k_ref, bf16[2048,128]{1,0:T(8,128)(2,1)} %get-tuple-element.118.v_ref), custom_call_target="tpu_custom_call" | custom-call | flops 1342177280 | bytes 2097152 | tf_op jit(solution)/shard_map/pallas_call | solution.py:85
  117.1 39.7 %all-gather.7.cloned.1.call-done = bf16[2048,1,2048]{2,0,1:T(8,128)(2,1)} async-done(((bf16[128,1,2048]{2,0,1:T(8,128)(2,1)}), bf16[2048,1,2048]{2,0,1:T(8,128)(2,1)}) %all-gather.7.cloned.1.call-update) | async-done | bytes 8388624 | tf_op jit(solution)/shard_map/all_gather | solution.py:277
  157.0 10.5 %fusion.32 = f32[2048,1,512]{2,0,1:T(8,128)} fusion(bf16[512,2048]{1,0:T(8,128)(2,1)} %param.28, bf16[2048,1,2048]{2,0,1:T(8,128)(2,1)} %all-gather.7.cloned.1.call-done), kind=kOutput, calls=%fused_computation.38 | convolution fusion | flops 4294967296 | bytes 14680064 | tf_op jit(solution)/shard_map/rsd,fd->rsf/dot_general | solution.py:289
  167.5 77.4 %reduce-scatter.4.cloned.1.call-done = bf16[128,1,2048]{2,0,1:T(8,128)(2,1)} async-done(((bf16[2048,1,2048]{2,0,1:T(8,128)(2,1)}), bf16[128,1,2048]{2,0,1:T(8,128)(2,1)}) %reduce-scatter.4.cloned.1.call-update) | async-done | bytes 524304 | tf_op jit(solution)/shard_map/reduce_scatter | solution.py:283
  247.9 70.1 %all-gather.9.cloned.1.call-done = bf16[2048,1,2048]{2,0,1:T(8,128)(2,1)} async-done(((bf16[128,1,2048]{2,0,1:T(8,128)(2,1)}), bf16[2048,1,2048]{2,0,1:T(8,128)(2,1)}) %all-gather.9.cloned.1.call-update) | async-done | bytes 8388624 | tf_op jit(solution)/shard_map/all_gather | solution.py:292
  318.0 7.0 %fusion.6 = f32[2048,512]{1,0:T(8,128)S(1)} fusion(bf16[2048,512]{1,0:T(8,128)(2,1)S(1)} %copy-done, bf16[2048,1,2048]{2,0,1:T(8,128)(2,1)} %all-gather.9.cloned.1.call-done), kind=kOutput, calls=%fused_computation.7 | convolution fusion | flops 4294967296 | bytes 14680064 | tf_op jit(solution)/shard_map/dot_general | solution.py:294
  330.8 6.9 %convert_bitcast_fusion.1 = bf16[2048,1,2048]{2,0,1:T(8,128)(2,1)} fusion(bf16[2048,512]{1,0:T(8,128)(2,1)S(1)} %get-tuple-element.108, bf16[2048,512]{1,0:T(8,128)(2,1)S(1)} %copy-done), kind=kOutput, calls=%fused_computation.18 | convolution fusion | flops 4299161600 | bytes 12582912 | tf_op jit(solution)/shard_map/rsf,df->rsd/dot_general | solution.py:315
  341.1 7.1 %fusion.29 = f32[2048,512]{1,0:T(8,128)S(1)} fusion(bf16[2048,512]{1,0:T(8,128)(2,1)S(1)} %copy-done.14, bf16[2048,1,2048]{2,0,1:T(8,128)(2,1)} %all-gather.9.cloned.1.call-done, f32[]{:T(128)S(6)} %div.71), kind=kOutput, calls=%fused_computation.37 | convolution fusion | flops 4296015872 | bytes 14680068 | tf_op jit(solution)/shard_map/rd,rf->df/dot_general | solution.py:307
  350.4 10.0 %fusion.26 = f32[512,2048]{1,0:T(8,128)} fusion(bf16[2048,1,2048]{2,0,1:T(8,128)(2,1)} %all-gather.7.cloned.1.call-done, f32[]{:T(128)S(6)} %div.71, f32[2048,512]{1,0:T(8,128)S(1)} %copy-done.10, f32[512]{0:T(512)S(1)} %copy-done.22), kind=kOutput, calls=%fused_computation.36 | convolution fusion | flops 4306501632 | bytes 16779268 | tf_op jit(solution)/shard_map/rsf,rsd->fd/dot_general | solution.py:303
  360.4 6.7 reshape.427
  367.1 7.4 %copy.36 = f32[512,2,2,512]{0,3,1,2:T(8,128)} copy(f32[512,2,2,512]{3,2,1,0:T(2,128)} %reshape.427) | data formatting | bytes 8388608 | tf_op jit(solution)/shard_map/reshape | solution.py:466
  388.8 10.6 %collective-permute-done.1 = bf16[2,256,512]{2,1,0:T(8,128)(2,1)S(1)} collective-permute-done((bf16[2,256,512]{2,1,0:T(8,128)(2,1)S(1)}, bf16[2,256,512]{2,1,0:T(8,128)(2,1)S(1)}, u32[]{:S(2)}, u32[]{:S(2)}) %collective-permute-start.1) | collective-permute-done | bytes 524320 | tf_op jit(solution)/shard_map/ppermute | solution.py:456
  401.1 9.5 %collective-permute-done.4 = bf16[512,2,256]{0,2,1:T(8,128)(2,1)S(1)} collective-permute-done((bf16[512,2,256]{0,2,1:T(8,128)(2,1)S(1)}, bf16[512,2,256]{0,2,1:T(8,128)(2,1)S(1)}, u32[]{:S(2)}, u32[]{:S(2)}) %collective-permute-start.4) | collective-permute-done | bytes 524320 | tf_op jit(solution)/shard_map/ppermute | solution.py:456
  417.0 6.9 %dynamic_update_slice.12 = bf16[2048,1,4096]{2,0,1:T(8,128)(2,1)} pad(bf16[2048,1,2048]{2,0,1:T(8,128)(2,1)S(1)} %convert_bitcast_fusion, bf16[]{:T(256)} %constant.136.clone.1), padding=0_0x0_0x2048_0 | pad | bytes 25165826 | tf_op jit(solution)/shard_map/dynamic_update_slice | solution.py:324
  430.3 70.2 %all-gather.11.cloned.1.call-done = bf16[2048,1,2048]{2,0,1:T(8,128)(2,1)} async-done(((bf16[128,1,2048]{2,0,1:T(8,128)(2,1)}), bf16[2048,1,2048]{2,0,1:T(8,128)(2,1)}) %all-gather.11.cloned.1.call-update) | async-done | bytes 8388624 | tf_op jit(solution)/shard_map/all_gather | solution.py:341
  507.1 24.8 %shard_map.255 = (bf16[2048,128]{1,0:T(8,128)(2,1)}, bf16[2048,128]{1,0:T(8,128)(2,1)}, bf16[2048,128]{1,0:T(8,128)(2,1)}) custom-call(s32[1]{0:T(128)} %dynamic_slice.7.len_ref, bf16[2048,128]{1,0:T(8,128)(2,1)} %get-tuple-element.119.q_ref, bf16[2048,128]{1,0:T(8,128)(2,1)} %fusion.67.k_ref, bf16[2048,128]{1,0:T(8,128)(2,1)} %get-tuple-element.118.v_ref, ...), custom_call_target="tpu_custom_call" | custom-call | flops 2684354560 | bytes 4194304 | tf_op jit(solution)/shard_map/pallas_call | solution.py:185
  535.2 9.7 %bitcast_dynamic-update-slice_fusion = bf16[2048,1,4096]{2,0,1:T(8,128)(2,1)} fusion(bf16[2048,1,4096]{2,0,1:T(8,128)(2,1)} %dynamic_update_slice.12, bf16[2048,384]{0,1:T(8,128)(2,1)} %bitcast.155, bf16[2048,384]{0,1:T(8,128)(2,1)} %bitcast.152), kind=kOutput, calls=%fused_computation | convolution fusion | flops 3225419776 | bytes 11534336 | tf_op jit(solution)/shard_map/rsc,dc->rsd/dot_general | solution.py:367
  560.9 8.3 %all-to-all-start = ((f32[128,1,176]{2,1,0:T(1,128)}), f32[128,1,176]{2,1,0:T(1,128)S(1)}, u32[]{:S(2)}, u32[]{:S(2)}) async-start(f32[128,1,176]{2,1,0:T(1,128)} %copy.39), calls=%async_computation.3 | async-start | bytes 262144 | tf_op jit(solution)/shard_map/all_to_all | solution.py:436
  571.3 7.8 %fusion.35 = f32[2048,384]{1,0:T(8,128)S(1)} fusion(bf16[2048,384]{0,1:T(8,128)(2,1)} %bitcast.156, bf16[2048,1,2048]{2,0,1:T(8,128)(2,1)} %all-gather.5.cloned.1.call-done, f32[]{:T(128)S(6)} %div.71), kind=kOutput, calls=%fused_computation.40 | convolution fusion | flops 3222011904 | bytes 13107204 | tf_op jit(solution)/shard_map/rd,rc->dc/dot_general | solution.py:361
  589.7 7.5 %collective-permute-done.7 = bf16[2,256,384]{2,1,0:T(8,128)(2,1)S(1)} collective-permute-done((bf16[2,256,384]{2,1,0:T(8,128)(2,1)S(1)}, bf16[2,256,384]{2,1,0:T(8,128)(2,1)S(1)}, u32[]{:S(2)}, u32[]{:S(2)}) %collective-permute-start.7) | collective-permute-done | bytes 393248 | tf_op jit(solution)/shard_map/ppermute | solution.py:456
  605.9 50.6 %reduce-scatter.8.cloned.1.call-done = bf16[128,1,4096]{2,0,1:T(8,128)(2,1)} async-done(((bf16[2048,1,4096]{2,0,1:T(8,128)(2,1)}), bf16[128,1,4096]{2,0,1:T(8,128)(2,1)}) %reduce-scatter.8.cloned.1.call-update) | async-done | bytes 1048592 | tf_op jit(solution)/shard_map/reduce_scatter | solution.py:375
  661.8 8.2 %all-to-all-start.1 = ((f32[128,1,16]{2,1,0:T(1,128)}), f32[128,1,16]{2,1,0:T(1,128)S(1)}, u32[]{:S(2)}, u32[]{:S(2)}) async-start(f32[128,1,16]{2,1,0:T(1,128)} %bitcast.51), calls=%async_computation.4 | async-start | bytes 131072 | tf_op jit(solution)/shard_map/all_to_all | solution.py:436
  (192 shorter events, 122.0 us)
Async XLA Ops:
  7.2 310.8 %copy-start = (bf16[2048,512]{1,0:T(8,128)(2,1)S(1)}, bf16[2048,512]{1,0:T(8,128)(2,1)}, u32[]{:S(2)}) copy-start(bf16[2048,512]{1,0:T(8,128)(2,1)} %param.26) | copy-start | bytes 6291460
  7.2 77.1 %all-gather.5.cloned.1.call-start = ((), (), s32[]{:S(2)}) async-start(), calls=%async_computation.5 | async-start | bytes 8912896 | tf_op jit(solution)/shard_map/all_gather | solution.py:246
  12.2 144.6 %all-gather.7.cloned.1.call-start = ((), (), s32[]{:S(2)}) async-start(), calls=%async_computation.6 | async-start | bytes 8912896 | tf_op jit(solution)/shard_map/all_gather | solution.py:277
  16.2 228.7 %reduce-scatter.4.cloned.1.call-start = ((), (), s32[]{:S(2)}) async-start(), calls=%async_computation.7 | async-start | bytes 8912896 | tf_op jit(solution)/shard_map/reduce_scatter | solution.py:283
  156.8 88.1 %copy-start.19 = (f32[2048]{0:T(1024)S(1)}, f32[2048]{0:T(1024)}, u32[]{:S(2)}) copy-start(f32[2048]{0:T(1024)} %param.23) | copy-start | bytes 24580
  156.8 161.2 %all-gather.9.cloned.1.call-start = ((), (), s32[]{:S(2)}) async-start(), calls=%async_computation.8 | async-start | bytes 8912896 | tf_op jit(solution)/shard_map/all_gather | solution.py:292
  247.8 178.0 %reduce-scatter.6.cloned.1.call-start = ((), (), s32[]{:S(2)}) async-start(), calls=%async_computation.9 | async-start | bytes 8912896 | tf_op jit(solution)/shard_map/reduce_scatter | solution.py:318
  337.7 162.8 %all-gather.11.cloned.1.call-start = ((), (), s32[]{:S(2)}) async-start(), calls=%async_computation.10 | async-start | bytes 8912896 | tf_op jit(solution)/shard_map/all_gather | solution.py:341
  350.3 30.9 %collective-permute-start = (bf16[4,256,512]{2,1,0:T(8,128)(2,1)S(1)}, bf16[4,256,512]{2,1,0:T(8,128)(2,1)S(1)}, u32[]{:S(2)}, u32[]{:S(2)}) collective-permute-start(bf16[4,256,512]{2,1,0:T(8,128)(2,1)S(1)} %bitcast.157), channel_id=1, source_target_pairs={{0,32},{32,0},{64,96},{96,64},{1,33},{33,1},{65,97},{97,65},{2,34}... | collective-permute-start | bytes 3145736 | tf_op jit(solution)/shard_map/ppermute | solution.py:456
  378.2 7.3 %collective-permute-start.3 = (bf16[512,4,256]{0,2,1:T(8,128)(2,1)}, bf16[512,4,256]{0,2,1:T(8,128)(2,1)}, u32[]{:S(2)}, u32[]{:S(2)}) collective-permute-start(bf16[512,4,256]{0,2,1:T(8,128)(2,1)} %select_convert_fusion), channel_id=1, source_target_pairs={{0,32},{32,0},{64,96},{96,64},{1,33},{33,1},{65,97},{97,65},{2,34}... | collective-permute-start | bytes 3145736 | tf_op jit(solution)/shard_map/ppermute | solution.py:456
  384.6 14.8 %collective-permute-start.1 = (bf16[2,256,512]{2,1,0:T(8,128)(2,1)S(1)}, bf16[2,256,512]{2,1,0:T(8,128)(2,1)S(1)}, u32[]{:S(2)}, u32[]{:S(2)}) collective-permute-start(bf16[2,256,512]{2,1,0:T(8,128)(2,1)S(1)} %select_convert_fusion.4), channel_id=1, source_target_pairs={{0,64},{32,96},{64,0},{96,32},{1,65},{33,97},{65,1},{97,33},{2,66}... | collective-permute-start | bytes 1572872 | tf_op jit(solution)/shard_map/ppermute | solution.py:456
  387.5 23.1 %collective-permute-start.4 = (bf16[512,2,256]{0,2,1:T(8,128)(2,1)S(1)}, bf16[512,2,256]{0,2,1:T(8,128)(2,1)S(1)}, u32[]{:S(2)}, u32[]{:S(2)}) collective-permute-start(bf16[512,2,256]{0,2,1:T(8,128)(2,1)S(1)} %select_convert_fusion.3), channel_id=1, source_target_pairs={{0,64},{32,96},{64,0},{96,32},{1,65},{33,97},{65,1},{97,33},{2,66}... | collective-permute-start | bytes 1572872 | tf_op jit(solution)/shard_map/ppermute | solution.py:456
  399.7 24.2 %collective-permute-start.2 = (bf16[1,256,512]{2,1,0:T(8,128)(2,1)S(1)}, bf16[1,256,512]{2,1,0:T(8,128)(2,1)S(1)}, u32[]{:S(2)}, u32[]{:S(2)}) collective-permute-start(bf16[1,256,512]{2,1,0:T(8,128)(2,1)S(1)} %select_convert_fusion.8), channel_id=1, source_target_pairs={{0,16},{16,0},{1,17},{17,1},{2,18},{18,2},{3,19},{19,3},{4,20},{20... | collective-permute-start | bytes 786440 | tf_op jit(solution)/shard_map/ppermute | solution.py:456
  410.9 13.9 %collective-permute-start.5 = (bf16[512,1,256]{0,2,1:T(8,128)(2,1)S(1)}, bf16[512,1,256]{0,2,1:T(8,128)(2,1)S(1)}, u32[]{:S(2)}, u32[]{:S(2)}) collective-permute-start(bf16[512,1,256]{0,2,1:T(8,128)(2,1)S(1)} %select_convert_fusion.7), channel_id=1, source_target_pairs={{0,16},{16,0},{1,17},{17,1},{2,18},{18,2},{3,19},{19,3},{4,20},{20... | collective-permute-start | bytes 786440 | tf_op jit(solution)/shard_map/ppermute | solution.py:456
  427.7 79.3 %copy-start.6 = (f32[128,1,2048]{2,0,1:T(8,128)}, f32[128,1,2048]{2,0,1:T(8,128)S(1)}, u32[]{:S(2)}) copy-start(f32[128,1,2048]{2,0,1:T(8,128)S(1)} %get-tuple-element.116) | copy-start | bytes 3145732
  430.2 226.3 %reduce-scatter.8.cloned.1.call-start = ((), (), s32[]{:S(2)}) async-start(), calls=%async_computation.11 | async-start | bytes 17825792 | tf_op jit(solution)/shard_map/reduce_scatter | solution.py:375
  560.9 20.2 %all-to-all-start = ((f32[128,1,176]{2,1,0:T(1,128)}), f32[128,1,176]{2,1,0:T(1,128)S(1)}, u32[]{:S(2)}, u32[]{:S(2)}) async-start(f32[128,1,176]{2,1,0:T(1,128)} %copy.39), calls=%async_computation.3 | async-start | bytes 262144 | tf_op jit(solution)/shard_map/all_to_all | solution.py:436
  571.1 11.3 %collective-permute-start.9 = (bf16[1,128,4,256]{1,3,2,0:T(8,128)(2,1)}, bf16[1,128,4,256]{1,3,2,0:T(8,128)(2,1)S(1)}, u32[]{:S(2)}, u32[]{:S(2)}) collective-permute-start(bf16[1,128,4,256]{1,3,2,0:T(8,128)(2,1)} %select_convert_fusion.6), channel_id=1, source_target_pairs={{0,32},{32,0},{64,96},{96,64},{1,33},{33,1},{65,97},{97,65},{2,34}... | collective-permute-start | bytes 786440 | tf_op jit(solution)/shard_map/ppermute | solution.py:456
  579.3 4.0 collective-permute-start.6
  582.6 6.0 collective-permute-start.10
  585.1 12.1 %collective-permute-start.7 = (bf16[2,256,384]{2,1,0:T(8,128)(2,1)S(1)}, bf16[2,256,384]{2,1,0:T(8,128)(2,1)S(1)}, u32[]{:S(2)}, u32[]{:S(2)}) collective-permute-start(bf16[2,256,384]{2,1,0:T(8,128)(2,1)S(1)} %select_convert_fusion.5), channel_id=1, source_target_pairs={{0,64},{32,96},{64,0},{96,32},{1,65},{33,97},{65,1},{97,33},{2,66}... | collective-permute-start | bytes 1179656 | tf_op jit(solution)/shard_map/ppermute | solution.py:456
  588.7 9.9 %collective-permute-start.11 = (bf16[1,128,1,256]{1,3,2,0:T(8,128)(2,1)S(1)}, bf16[1,128,1,256]{1,3,2,0:T(8,128)(2,1)S(1)}, u32[]{:S(2)}, u32[]{:S(2)}) collective-permute-start(bf16[1,128,1,256]{1,3,2,0:T(8,128)(2,1)S(1)} %select_convert_fusion.11), channel_id=1, source_target_pairs={{0,16},{16,0},{1,17},{17,1},{2,18},{18,2},{3,19},{19,3},{4,20},{20... | collective-permute-start | bytes 196616 | tf_op jit(solution)/shard_map/ppermute | solution.py:456
  597.4 7.4 %collective-permute-start.8 = (bf16[1,256,384]{2,1,0:T(8,128)(2,1)S(1)}, bf16[1,256,384]{2,1,0:T(8,128)(2,1)S(1)}, u32[]{:S(2)}, u32[]{:S(2)}) collective-permute-start(bf16[1,256,384]{2,1,0:T(8,128)(2,1)S(1)} %select_convert_fusion.9), channel_id=1, source_target_pairs={{0,16},{16,0},{1,17},{17,1},{2,18},{18,2},{3,19},{19,3},{4,20},{20... | collective-permute-start | bytes 589832 | tf_op jit(solution)/shard_map/ppermute | solution.py:456
  661.8 15.4 %all-to-all-start.1 = ((f32[128,1,16]{2,1,0:T(1,128)}), f32[128,1,16]{2,1,0:T(1,128)S(1)}, u32[]{:S(2)}, u32[]{:S(2)}) async-start(f32[128,1,16]{2,1,0:T(1,128)} %bitcast.51), calls=%async_computation.4 | async-start | bytes 131072 | tf_op jit(solution)/shard_map/all_to_all | solution.py:436
  (23 other events, 582.5 us)
Sparse Core Ops, SparseCore 0:
  12.3 71.8 all-gather.4
  86.4 70.3 all-gather.6
  160.2 84.6 reduce-scatter.3
  247.9 70.0 all-gather.8
  337.8 84.6 reduce-scatter.5
  430.3 70.0 all-gather.10
  545.1 111.3 reduce-scatter.7

commit v13 on v12

--- a/solution.py
+++ b/solution.py
@@ -243,7 +243,22 @@
     )
     inputs = tokens.astype(jnp.float32)
     normed_low = layer_norm(inputs, ln1_gain, ln1_bias).astype(jnp.bfloat16)
-    normed_full = lax.all_gather(normed_low, "tensor", axis=0, tiled=True)
+    positions = tensor_rank * row_count + jnp.arange(row_count, dtype=jnp.int32)
+    live = positions[:, None] < seq_lengths[None, :]
+    upstream = jnp.where(live[:, :, None], cotangent, jnp.zeros_like(cotangent))
+    front = jnp.concatenate(
+        [
+            normed_low.reshape(row_count, seq_count * model_width),
+            upstream.reshape(row_count, seq_count * model_width),
+            w_o.reshape(row_count, -1),
+        ],
+        1,
+    )
+    front = lax.all_gather(front, "tensor", axis=0, tiled=True)
+    wide = seq_count * model_width
+    normed_full = front[:, :wide].reshape(seq_total, seq_count, model_width)
+    upstream_full = front[:, wide : 2 * wide].reshape(seq_total, seq_count, model_width)
+    out_full = front[:, 2 * wide :].reshape(-1, model_width)
     joint_weight = w_qkv.reshape(model_width, 3 * local_width)
     projected = jnp.dot(
         normed_full.reshape(seq_total * seq_count, model_width),
@@ -271,25 +286,24 @@
     ]
     attended = per_row([o for o, _ in forward_items])
     out_weight = w_o.reshape(local_width, model_width)
-    positions = tensor_rank * row_count + jnp.arange(row_count, dtype=jnp.int32)
-    live = positions[:, None] < seq_lengths[None, :]
-    upstream = jnp.where(live[:, :, None], cotangent, jnp.zeros_like(cotangent))
-    upstream_full = lax.all_gather(upstream, "tensor", axis=0, tiled=True)
-    attention_part = jnp.einsum(
-        "rse,ed->rsd", attended, out_weight, preferred_element_type=jnp.float32
-    ).astype(jnp.bfloat16)
-    attention_part, upstream_full = lax.optimization_barrier((attention_part, upstream_full))
+    own_rows = lax.all_to_all(
+        jnp.transpose(attended, (1, 0, 2)).reshape(seq_count * seq_total, local_width),
+        "tensor",
+        0,
+        1,
+        tiled=True,
+    )
     attention = (
-        lax.psum_scatter(attention_part, "tensor", scatter_dimension=0, tiled=True).astype(
-            jnp.float32
+        jnp.dot(own_rows, out_full, preferred_element_type=jnp.float32).reshape(
+            seq_count, row_count, model_width
         )
-        + b_o
-    )
+    )
+    attention = jnp.transpose(attention, (1, 0, 2)) + b_o
     middle = inputs + attention
     act_grad = jnp.einsum("rsd,fd->rsf", upstream_full, w_out, preferred_element_type=jnp.float32)
-    middle, act_grad = lax.optimization_barrier((middle, act_grad))
     second_low = layer_norm(middle, ln2_gain, ln2_bias).astype(jnp.bfloat16)
     second_full = lax.all_gather(second_low, "tensor", axis=0, tiled=True)
+    second_full, act_grad = lax.optimization_barrier((second_full, act_grad))
     pre_act = (
         jnp.dot(
             second_full.reshape(seq_total * seq_count, model_width),

time: 696 us -> 670 us (0.963)
  waiting for transfers between devices: 409 us -> 372 us
  Pallas kernels: 41.7 us -> 24.5 us
  blocking collectives: 0 us -> 16.6 us
  starting transfers between devices: 27.5 us -> 41.2 us
    reduce_scatter x1 -> x0, waiting for transfers between devices: 77.4 us -> none  [shards(): lax.psum_scatter(attention_part, 'tensor', scatter_dimension=0, tiled=True)]
    all_gather x2 -> x1, waiting for transfers between devices: 105 us -> 153 us  [shards(): front = lax.all_gather(front, 'tensor', axis=0, tiled=True)]
    all_to_all x0 -> x1, blocking collectives: none -> 16.6 us  [shards(): lax.all_to_all(jnp.transpose(attended, (1, 0, 2)).reshape(seq_count * seq...]
    all_to_all x2, starting transfers between devices: 16.5 us -> 29.9 us  [reduce_vectors(): packed = lax.all_to_all(packed, ('group', 'dp', 'tensor'), 0, 0, tiled=True)]
    pallas_call x1, Pallas kernels: 24.8 us -> 11.4 us  [attention_backward(): pl.pallas_call(kernel, out_shape=tuple((jax.ShapeDtypeStruct((n, d), jnp....]
    all_gather x1, waiting for transfers between devices: 70.1 us -> 61.7 us  [shards(): second_full = lax.all_gather(second_low, 'tensor', axis=0, tiled=True)]
  transfers between devices with their start and end apart: 21 -> 19, of which waited for: 12 -> 10; matrix products, arithmetic and copies ran while one was open for 19% -> 17% of each run, Pallas kernels for 2% -> 0%
where the time goes in v13:
time: 670 us; the launch traced here: 660 us
  waiting for transfers between devices  372 us (56%)
  matrix products  91.4 us (14%)
  other arithmetic  50 us (7%)
  local copies, waits for them, and re-layouts  48.8 us (7%)
  starting transfers between devices  41.2 us (6%)
  Pallas kernels  24.5 us (4%)
  blocking collectives  16.6 us (2%)
  between operations  16 us (2%)
    all_gather x1, waiting for transfers between devices, shards(): front = lax.all_gather(front, 'tensor', axis=0, tiled=True)  153 us
    all_gather x1, waiting for transfers between devices, shards(): piece = lax.all_gather(branch_low, 'tensor', axis=0, tiled=True)  70.3 us
    all_gather x1, waiting for transfers between devices, shards(): second_full = lax.all_gather(second_low, 'tensor', axis=0, tiled=True)  61.7 us
    reduce_scatter x1, waiting for transfers between devices, shards(): both = lax.psum_scatter(merged, 'tensor', scatter_dimension=0, tiled=True)  50.8 us
    ppermute x12, waiting for transfers between devices, halving_steps(): got = lax.ppermute(send, axis, [(i, i ^ bit) for i in range(size)])  35.8 us
    all_to_all x2, starting transfers between devices, reduce_vectors(): packed = lax.all_to_all(packed, ('group', 'dp', 'tensor'), 0, 0, tiled=True)  29.9 us
    reshape x4, local copies, waits for them, and re-layouts, halving_sum(): value.reshape(shape[:dim] + (groups // 2, 2, dps * rest) + shape[dim + 1:])  19.5 us
    all_to_all x1, blocking collectives, shards(): lax.all_to_all(jnp.transpose(attended, (1, 0, 2)).reshape(seq_count * seq...  16.6 us
  transfers between devices with their start and end apart: 19, of which 10 were waited for; matrix products, arithmetic and copies ran while one was open for 17% of the time, Pallas kernels for 0%

profile of v13, /device:TPU:96, one launch (start us, length us, event | category | flops | bytes accessed | tf_op | source)
XLA Modules:
  0.0 660.1 jit_solution(15684835156344036544)
XLA Ops:
  19.6 152.8 %all-gather.4.cloned.1.call-done = bf16[2048,6144]{1,0:T(8,128)(2,1)} async-done(((bf16[128,6144]{1,0:T(8,128)(2,1)}), bf16[2048,6144]{1,0:T(8,128)(2,1)}) %all-gather.4.cloned.1.call-update) | async-done | bytes 25165840 | tf_op jit(solution)/shard_map/all_gather | solution.py:257
  172.4 7.4 %fusion.41 = f32[2048,1,3,128]{3,0,2,1:T(8,128)S(1)} fusion(bf16[2048,6144]{1,0:T(8,128)(2,1)} %all-gather.4.cloned.1.call-done, bf16[2048,3,1,128]{0,3,1,2:T(8,128)(2,1)} %copy.36), kind=kOutput, calls=%fused_computation.43 | convolution fusion | flops 3221225472 | bytes 13107200 | tf_op jit(solution)/shard_map/dot_general | solution.py:263
  181.8 13.1 %shard_map.254 = (bf16[2048,128]{1,0:T(8,128)(2,1)}, f32[2048,1]{1,0:T(8,128)}) custom-call(s32[1]{0:T(128)} %dynamic_slice.7.len_ref, bf16[2048,128]{1,0:T(8,128)(2,1)} %get-tuple-element.113.q_ref, bf16[2048,128]{1,0:T(8,128)(2,1)} %fusion.79.k_ref, bf16[2048,128]{1,0:T(8,128)(2,1)} %get-tuple-element.112.v_ref), custom_call_target="tpu_custom_call" | custom-call | flops 1342177280 | bytes 2097152 | tf_op jit(solution)/shard_map/pallas_call | solution.py:85
  196.2 16.6 %all_to_all.34 = bf16[16,128,128]{1,2,0:T(8,128)(2,1)S(1)} all-to-all(bf16[16,128,128]{1,2,0:T(8,128)(2,1)S(1)} %copy.37), channel_id=1, replica_groups=mesh['group'=4,'dp'=2,'tensor'=16] {'tensor'}, dimensions={0} | all-to-all | bytes 1048576 | tf_op jit(solution)/shard_map/all_to_all | solution.py:289
  219.3 10.6 %fusion.35 = f32[2048,1,512]{2,0,1:T(8,128)} fusion(bf16[512,2048]{1,0:T(8,128)(2,1)} %param.28, bf16[2048,6144]{1,0:T(8,128)(2,1)} %all-gather.4.cloned.1.call-done), kind=kOutput, calls=%fused_computation.40 | convolution fusion | flops 4294967296 | bytes 14680064 | tf_op jit(solution)/shard_map/rsd,fd->rsf/dot_general | solution.py:303
  229.9 61.7 %all-gather.6.cloned.1.call-done = bf16[2048,1,2048]{2,0,1:T(8,128)(2,1)} async-done(((bf16[128,1,2048]{2,0,1:T(8,128)(2,1)}), bf16[2048,1,2048]{2,0,1:T(8,128)(2,1)}) %all-gather.6.cloned.1.call-update) | async-done | bytes 8388624 | tf_op jit(solution)/shard_map/all_gather | solution.py:305
  291.5 7.0 %fusion.8 = f32[2048,512]{1,0:T(8,128)S(1)} fusion(bf16[2048,512]{1,0:T(8,128)(2,1)S(1)} %copy-done, bf16[2048,1,2048]{2,0,1:T(8,128)(2,1)} %all-gather.6.cloned.1.call-done), kind=kOutput, calls=%fused_computation.9 | convolution fusion | flops 4294967296 | bytes 14680064 | tf_op jit(solution)/shard_map/dot_general | solution.py:308
  304.2 6.9 %convert_bitcast_fusion.1 = bf16[2048,1,2048]{2,0,1:T(8,128)(2,1)} fusion(bf16[2048,512]{1,0:T(8,128)(2,1)S(1)} %get-tuple-element.104, bf16[2048,512]{1,0:T(8,128)(2,1)S(1)} %copy-done), kind=kOutput, calls=%fused_computation.14 | convolution fusion | flops 4299161600 | bytes 12582912 | tf_op jit(solution)/shard_map/rsf,df->rsd/dot_general | solution.py:329
  314.6 7.1 %fusion.32 = f32[2048,512]{1,0:T(8,128)S(1)} fusion(bf16[2048,512]{1,0:T(8,128)(2,1)S(1)} %copy-done.14, bf16[2048,1,2048]{2,0,1:T(8,128)(2,1)} %all-gather.6.cloned.1.call-done, f32[]{:T(128)S(6)} %div.71), kind=kOutput, calls=%fused_computation.39 | convolution fusion | flops 4296015872 | bytes 14680068 | tf_op jit(solution)/shard_map/rd,rf->df/dot_general | solution.py:321
  324.2 10.7 %fusion.29 = f32[512,2048]{1,0:T(8,128)} fusion(bf16[2048,6144]{1,0:T(8,128)(2,1)} %all-gather.4.cloned.1.call-done, f32[]{:T(128)S(6)} %div.71, f32[2048,512]{1,0:T(8,128)S(1)} %copy-done.9, f32[512]{0:T(512)S(1)} %copy-done.20), kind=kOutput, calls=%fused_computation.38 | convolution fusion | flops 4306501632 | bytes 16779268 | tf_op jit(solution)/shard_map/rsf,rsd->fd/dot_general | solution.py:317
  334.8 6.7 %reshape.431 = f32[512,2,2,512]{3,2,1,0:T(2,128)} reshape(f32[512,2048]{1,0:T(8,128)} %fusion.29) | data formatting | bytes 8388608 | tf_op jit(solution)/shard_map/reshape | solution.py:480
  341.6 7.3 %copy.38 = f32[512,2,2,512]{0,3,1,2:T(8,128)} copy(f32[512,2,2,512]{3,2,1,0:T(2,128)} %reshape.431) | data formatting | bytes 8388608 | tf_op jit(solution)/shard_map/reshape | solution.py:480
  363.3 10.5 %collective-permute-done.1 = bf16[2,256,512]{2,1,0:T(8,128)(2,1)S(1)} collective-permute-done((bf16[2,256,512]{2,1,0:T(8,128)(2,1)S(1)}, bf16[2,256,512]{2,1,0:T(8,128)(2,1)S(1)}, u32[]{:S(2)}, u32[]{:S(2)}) %collective-permute-start.1) | collective-permute-done | bytes 524320 | tf_op jit(solution)/shard_map/ppermute | solution.py:470
  375.5 9.5 %collective-permute-done.4 = bf16[512,2,256]{0,2,1:T(8,128)(2,1)S(1)} collective-permute-done((bf16[512,2,256]{0,2,1:T(8,128)(2,1)S(1)}, bf16[512,2,256]{0,2,1:T(8,128)(2,1)S(1)}, u32[]{:S(2)}, u32[]{:S(2)}) %collective-permute-start.4) | collective-permute-done | bytes 524320 | tf_op jit(solution)/shard_map/ppermute | solution.py:470
  391.8 7.0 %dynamic_update_slice.12 = bf16[2048,1,4096]{2,0,1:T(8,128)(2,1)} pad(bf16[2048,1,2048]{2,0,1:T(8,128)(2,1)S(1)} %convert_bitcast_fusion, bf16[]{:T(256)} %constant.136.clone.1), padding=0_0x0_0x2048_0 | pad | bytes 25165826 | tf_op jit(solution)/shard_map/dynamic_update_slice | solution.py:338
  405.3 70.3 %all-gather.8.cloned.1.call-done = bf16[2048,1,2048]{2,0,1:T(8,128)(2,1)} async-done(((bf16[128,1,2048]{2,0,1:T(8,128)(2,1)}), bf16[2048,1,2048]{2,0,1:T(8,128)(2,1)}) %all-gather.8.cloned.1.call-update) | async-done | bytes 8388624 | tf_op jit(solution)/shard_map/all_gather | solution.py:355
  475.6 6.6 fusion.56.do_ref
  482.2 11.4 %shard_map.255 = (bf16[2048,128]{1,0:T(8,128)(2,1)}, bf16[2048,128]{1,0:T(8,128)(2,1)}, bf16[2048,128]{1,0:T(8,128)(2,1)}) custom-call(s32[1]{0:T(128)} %dynamic_slice.7.len_ref, bf16[2048,128]{1,0:T(8,128)(2,1)} %get-tuple-element.113.q_ref, bf16[2048,128]{1,0:T(8,128)(2,1)} %fusion.79.k_ref, bf16[2048,128]{1,0:T(8,128)(2,1)} %get-tuple-element.112.v_ref, ...), custom_call_target="tpu_custom_call" | custom-call | flops 2684354560 | bytes 4194304 | tf_op jit(solution)/shard_map/pallas_call | solution.py:185
  497.0 9.9 %bitcast_dynamic-update-slice_fusion = bf16[2048,1,4096]{2,0,1:T(8,128)(2,1)} fusion(bf16[2048,1,4096]{2,0,1:T(8,128)(2,1)} %dynamic_update_slice.12, bf16[2048,384]{0,1:T(8,128)(2,1)} %bitcast.150, bf16[2048,384]{0,1:T(8,128)(2,1)} %bitcast.146), kind=kOutput, calls=%fused_computation.2 | convolution fusion | flops 3225419776 | bytes 11534336 | tf_op jit(solution)/shard_map/rsc,dc->rsd/dot_general | solution.py:381
  522.8 21.7 %all-to-all-start.1 = ((f32[128,1,176]{2,1,0:T(1,128)}), f32[128,1,176]{2,1,0:T(1,128)S(1)}, u32[]{:S(2)}, u32[]{:S(2)}) async-start(f32[128,1,176]{2,1,0:T(1,128)} %copy.41), calls=%async_computation.3 | async-start | bytes 262144 | tf_op jit(solution)/shard_map/all_to_all | solution.py:450
  546.6 7.9 %fusion.38 = f32[2048,384]{1,0:T(8,128)S(1)} fusion(bf16[2048,384]{0,1:T(8,128)(2,1)} %bitcast.151, bf16[2048,6144]{1,0:T(8,128)(2,1)} %all-gather.4.cloned.1.call-done, f32[]{:T(128)S(6)} %div.71), kind=kOutput, calls=%fused_computation.42 | convolution fusion | flops 3222011904 | bytes 13107204 | tf_op jit(solution)/shard_map/rd,rc->dc/dot_general | solution.py:375
  565.0 7.6 %collective-permute-done.7 = bf16[2,256,384]{2,1,0:T(8,128)(2,1)S(1)} collective-permute-done((bf16[2,256,384]{2,1,0:T(8,128)(2,1)S(1)}, bf16[2,256,384]{2,1,0:T(8,128)(2,1)S(1)}, u32[]{:S(2)}, u32[]{:S(2)}) %collective-permute-start.7) | collective-permute-done | bytes 393248 | tf_op jit(solution)/shard_map/ppermute | solution.py:470
  581.3 50.8 %reduce-scatter.5.cloned.1.call-done = bf16[128,1,4096]{2,0,1:T(8,128)(2,1)} async-done(((bf16[2048,1,4096]{2,0,1:T(8,128)(2,1)}), bf16[128,1,4096]{2,0,1:T(8,128)(2,1)}) %reduce-scatter.5.cloned.1.call-update) | async-done | bytes 1048592 | tf_op jit(solution)/shard_map/reduce_scatter | solution.py:389
  637.3 8.2 %all-to-all-start.2 = ((f32[128,1,16]{2,1,0:T(1,128)}), f32[128,1,16]{2,1,0:T(1,128)S(1)}, u32[]{:S(2)}, u32[]{:S(2)}) async-start(f32[128,1,16]{2,1,0:T(1,128)} %bitcast.54), calls=%async_computation.4 | async-start | bytes 131072 | tf_op jit(solution)/shard_map/all_to_all | solution.py:450
  (185 shorter events, 114.7 us)
Async XLA Ops:
  7.2 284.3 %copy-start = (bf16[2048,512]{1,0:T(8,128)(2,1)S(1)}, bf16[2048,512]{1,0:T(8,128)(2,1)}, u32[]{:S(2)}) copy-start(bf16[2048,512]{1,0:T(8,128)(2,1)} %param.26) | copy-start | bytes 6291460
  7.2 165.2 %all-gather.4.cloned.1.call-start = ((), (), s32[]{:S(2)}) async-start(), calls=%async_computation.5 | async-start | bytes 26738688 | tf_op jit(solution)/shard_map/all_gather | solution.py:257
  16.9 274.6 %all-gather.6.cloned.1.call-start = ((), (), s32[]{:S(2)}) async-start(), calls=%async_computation.6 | async-start | bytes 8912896 | tf_op jit(solution)/shard_map/all_gather | solution.py:305
  219.0 181.7 %reduce-scatter.3.cloned.1.call-start = ((), (), s32[]{:S(2)}) async-start(), calls=%async_computation.7 | async-start | bytes 8912896 | tf_op jit(solution)/shard_map/reduce_scatter | solution.py:332
  311.2 164.5 %all-gather.8.cloned.1.call-start = ((), (), s32[]{:S(2)}) async-start(), calls=%async_computation.8 | async-start | bytes 8912896 | tf_op jit(solution)/shard_map/all_gather | solution.py:355
  323.8 31.8 %collective-permute-start = (bf16[4,256,512]{2,1,0:T(8,128)(2,1)S(1)}, bf16[4,256,512]{2,1,0:T(8,128)(2,1)S(1)}, u32[]{:S(2)}, u32[]{:S(2)}) collective-permute-start(bf16[4,256,512]{2,1,0:T(8,128)(2,1)S(1)} %bitcast.152), channel_id=1, source_target_pairs={{0,32},{32,0},{64,96},{96,64},{1,33},{33,1},{65,97},{97,65},{2,34}... | collective-permute-start | bytes 3145736 | tf_op jit(solution)/shard_map/ppermute | solution.py:470
  352.4 7.4 %collective-permute-start.3 = (bf16[512,4,256]{0,2,1:T(8,128)(2,1)}, bf16[512,4,256]{0,2,1:T(8,128)(2,1)}, u32[]{:S(2)}, u32[]{:S(2)}) collective-permute-start(bf16[512,4,256]{0,2,1:T(8,128)(2,1)} %select_convert_fusion), channel_id=1, source_target_pairs={{0,32},{32,0},{64,96},{96,64},{1,33},{33,1},{65,97},{97,65},{2,34}... | collective-permute-start | bytes 3145736 | tf_op jit(solution)/shard_map/ppermute | solution.py:470
  359.0 14.8 %collective-permute-start.1 = (bf16[2,256,512]{2,1,0:T(8,128)(2,1)S(1)}, bf16[2,256,512]{2,1,0:T(8,128)(2,1)S(1)}, u32[]{:S(2)}, u32[]{:S(2)}) collective-permute-start(bf16[2,256,512]{2,1,0:T(8,128)(2,1)S(1)} %select_convert_fusion.4), channel_id=1, source_target_pairs={{0,64},{32,96},{64,0},{96,32},{1,65},{33,97},{65,1},{97,33},{2,66}... | collective-permute-start | bytes 1572872 | tf_op jit(solution)/shard_map/ppermute | solution.py:470
  361.9 23.1 %collective-permute-start.4 = (bf16[512,2,256]{0,2,1:T(8,128)(2,1)S(1)}, bf16[512,2,256]{0,2,1:T(8,128)(2,1)S(1)}, u32[]{:S(2)}, u32[]{:S(2)}) collective-permute-start(bf16[512,2,256]{0,2,1:T(8,128)(2,1)S(1)} %select_convert_fusion.3), channel_id=1, source_target_pairs={{0,64},{32,96},{64,0},{96,32},{1,65},{33,97},{65,1},{97,33},{2,66}... | collective-permute-start | bytes 1572872 | tf_op jit(solution)/shard_map/ppermute | solution.py:470
  374.2 24.7 %collective-permute-start.2 = (bf16[1,256,512]{2,1,0:T(8,128)(2,1)S(1)}, bf16[1,256,512]{2,1,0:T(8,128)(2,1)S(1)}, u32[]{:S(2)}, u32[]{:S(2)}) collective-permute-start(bf16[1,256,512]{2,1,0:T(8,128)(2,1)S(1)} %select_convert_fusion.8), channel_id=1, source_target_pairs={{0,16},{16,0},{1,17},{17,1},{2,18},{18,2},{3,19},{19,3},{4,20},{20... | collective-permute-start | bytes 786440 | tf_op jit(solution)/shard_map/ppermute | solution.py:470
  385.4 14.4 %collective-permute-start.5 = (bf16[512,1,256]{0,2,1:T(8,128)(2,1)S(1)}, bf16[512,1,256]{0,2,1:T(8,128)(2,1)S(1)}, u32[]{:S(2)}, u32[]{:S(2)}) collective-permute-start(bf16[512,1,256]{0,2,1:T(8,128)(2,1)S(1)} %select_convert_fusion.7), channel_id=1, source_target_pairs={{0,16},{16,0},{1,17},{17,1},{2,18},{18,2},{3,19},{19,3},{4,20},{20... | collective-permute-start | bytes 786440 | tf_op jit(solution)/shard_map/ppermute | solution.py:470
  402.7 79.5 %copy-start.6 = (f32[128,1,2048]{2,0,1:T(8,128)}, f32[128,1,2048]{2,0,1:T(8,128)S(1)}, u32[]{:S(2)}) copy-start(f32[128,1,2048]{2,0,1:T(8,128)S(1)} %get-tuple-element.110) | copy-start | bytes 3145732
  405.3 226.8 %reduce-scatter.5.cloned.1.call-start = ((), (), s32[]{:S(2)}) async-start(), calls=%async_computation.9 | async-start | bytes 17825792 | tf_op jit(solution)/shard_map/reduce_scatter | solution.py:389
  522.8 33.7 %all-to-all-start.1 = ((f32[128,1,176]{2,1,0:T(1,128)}), f32[128,1,176]{2,1,0:T(1,128)S(1)}, u32[]{:S(2)}, u32[]{:S(2)}) async-start(f32[128,1,176]{2,1,0:T(1,128)} %copy.41), calls=%async_computation.3 | async-start | bytes 262144 | tf_op jit(solution)/shard_map/all_to_all | solution.py:450
  546.5 11.4 %collective-permute-start.9 = (bf16[1,128,4,256]{1,3,2,0:T(8,128)(2,1)}, bf16[1,128,4,256]{1,3,2,0:T(8,128)(2,1)S(1)}, u32[]{:S(2)}, u32[]{:S(2)}) collective-permute-start(bf16[1,128,4,256]{1,3,2,0:T(8,128)(2,1)} %select_convert_fusion.6), channel_id=1, source_target_pairs={{0,32},{32,0},{64,96},{96,64},{1,33},{33,1},{65,97},{97,65},{2,34}... | collective-permute-start | bytes 786440 | tf_op jit(solution)/shard_map/ppermute | solution.py:470
  554.7 3.9 collective-permute-start.6
  558.0 6.0 collective-permute-start.10
  560.5 12.1 %collective-permute-start.7 = (bf16[2,256,384]{2,1,0:T(8,128)(2,1)S(1)}, bf16[2,256,384]{2,1,0:T(8,128)(2,1)S(1)}, u32[]{:S(2)}, u32[]{:S(2)}) collective-permute-start(bf16[2,256,384]{2,1,0:T(8,128)(2,1)S(1)} %select_convert_fusion.5), channel_id=1, source_target_pairs={{0,64},{32,96},{64,0},{96,32},{1,65},{33,97},{65,1},{97,33},{2,66}... | collective-permute-start | bytes 1179656 | tf_op jit(solution)/shard_map/ppermute | solution.py:470
  564.1 69.4 %copy-start.4 = (bf16[128,1,2048]{2,0,1:T(8,128)(2,1)S(1)}, bf16[128,1,2048]{2,0,1:T(8,128)(2,1)}, u32[]{:S(2)}) copy-start(bf16[128,1,2048]{2,0,1:T(8,128)(2,1)} %param.15) | copy-start | bytes 1572868
  564.1 69.4 %copy-start.16 = (f32[2048]{0:T(1024)S(1)}, f32[2048]{0:T(1024)}, u32[]{:S(2)}) copy-start(f32[2048]{0:T(1024)} %param.18) | copy-start | bytes 24580
  564.1 9.8 %collective-permute-start.11 = (bf16[1,128,1,256]{1,3,2,0:T(8,128)(2,1)S(1)}, bf16[1,128,1,256]{1,3,2,0:T(8,128)(2,1)S(1)}, u32[]{:S(2)}, u32[]{:S(2)}) collective-permute-start(bf16[1,128,1,256]{1,3,2,0:T(8,128)(2,1)S(1)} %select_convert_fusion.11), channel_id=1, source_target_pairs={{0,16},{16,0},{1,17},{17,1},{2,18},{18,2},{3,19},{19,3},{4,20},{20... | collective-permute-start | bytes 196616 | tf_op jit(solution)/shard_map/ppermute | solution.py:470
  572.8 7.3 %collective-permute-start.8 = (bf16[1,256,384]{2,1,0:T(8,128)(2,1)S(1)}, bf16[1,256,384]{2,1,0:T(8,128)(2,1)S(1)}, u32[]{:S(2)}, u32[]{:S(2)}) collective-permute-start(bf16[1,256,384]{2,1,0:T(8,128)(2,1)S(1)} %select_convert_fusion.9), channel_id=1, source_target_pairs={{0,16},{16,0},{1,17},{17,1},{2,18},{18,2},{3,19},{19,3},{4,20},{20... | collective-permute-start | bytes 589832 | tf_op jit(solution)/shard_map/ppermute | solution.py:470
  574.0 71.6 %copy-start.19 = (f32[2048]{0:T(1024)S(1)}, f32[2048]{0:T(1024)}, u32[]{:S(2)}) copy-start(f32[2048]{0:T(1024)} %param.29) | copy-start | bytes 24580
  637.3 15.4 %all-to-all-start.2 = ((f32[128,1,16]{2,1,0:T(1,128)}), f32[128,1,16]{2,1,0:T(1,128)S(1)}, u32[]{:S(2)}, u32[]{:S(2)}) async-start(f32[128,1,16]{2,1,0:T(1,128)} %bitcast.54), calls=%async_computation.4 | async-start | bytes 131072 | tf_op jit(solution)/shard_map/all_to_all | solution.py:450
  (20 other events, 223.4 us)
Sparse Core Ops, SparseCore 0:
  17.0 155.3 all-gather.3
  219.2 72.3 all-gather.5
  311.3 84.8 reduce-scatter.2
  405.4 70.2 all-gather.7
  507.1 124.9 reduce-scatter.4

commit v14 on v13

--- a/solution.py
+++ b/solution.py
@@ -247,18 +247,14 @@
     live = positions[:, None] < seq_lengths[None, :]
     upstream = jnp.where(live[:, :, None], cotangent, jnp.zeros_like(cotangent))
     front = jnp.concatenate(
-        [
-            normed_low.reshape(row_count, seq_count * model_width),
-            upstream.reshape(row_count, seq_count * model_width),
-            w_o.reshape(row_count, -1),
-        ],
-        1,
+        [normed_low.reshape(row_count, seq_count * model_width), w_o.reshape(row_count, -1)], 1
     )
     front = lax.all_gather(front, "tensor", axis=0, tiled=True)
     wide = seq_count * model_width
     normed_full = front[:, :wide].reshape(seq_total, seq_count, model_width)
-    upstream_full = front[:, wide : 2 * wide].reshape(seq_total, seq_count, model_width)
-    out_full = front[:, 2 * wide :].reshape(-1, model_width)
+    out_full = front[:, wide:].reshape(-1, model_width)
+    upstream, front = lax.optimization_barrier((upstream, front))
+    upstream_full = lax.all_gather(upstream, "tensor", axis=0, tiled=True)
     joint_weight = w_qkv.reshape(model_width, 3 * local_width)
     projected = jnp.dot(
         normed_full.reshape(seq_total * seq_count, model_width),
@@ -302,6 +298,7 @@
     middle = inputs + attention
     act_grad = jnp.einsum("rsd,fd->rsf", upstream_full, w_out, preferred_element_type=jnp.float32)
     second_low = layer_norm(middle, ln2_gain, ln2_bias).astype(jnp.bfloat16)
+    second_low, upstream_full = lax.optimization_barrier((second_low, upstream_full))
     second_full = lax.all_gather(second_low, "tensor", axis=0, tiled=True)
     second_full, act_grad = lax.optimization_barrier((second_full, act_grad))
     pre_act = (

time: 670 us -> 652 us (0.973)
  waiting for transfers between devices: 372 us -> 361 us
  Pallas kernels: 24.5 us -> 17 us
    all_gather x1, waiting for transfers between devices: 153 us -> 110 us  [shards(): front = lax.all_gather(front, 'tensor', axis=0, tiled=True)]
    all_gather x0 -> x1, waiting for transfers between devices: none -> 31.2 us  [shards(): upstream_full = lax.all_gather(upstream, 'tensor', axis=0, tiled=True)]
  transfers between devices with their start and end apart: 19 -> 20, of which waited for: 10 -> 11; matrix products, arithmetic and copies ran while one was open for 17% -> 20% of each run, Pallas kernels for 0% -> 1%
where the time goes in v14:
time: 652 us; the launch traced here: 641 us
  waiting for transfers between devices  361 us (55%)
  matrix products  90.5 us (14%)
  other arithmetic  49.7 us (8%)
  local copies, waits for them, and re-layouts  47.2 us (7%)
  starting transfers between devices  44.2 us (7%)
  Pallas kernels  17 us (3%)
  between operations  16.3 us (2%)
  blocking collectives  15.2 us (2%)
    all_gather x1, waiting for transfers between devices, shards(): front = lax.all_gather(front, 'tensor', axis=0, tiled=True)  110 us
    all_gather x1, waiting for transfers between devices, shards(): piece = lax.all_gather(branch_low, 'tensor', axis=0, tiled=True)  70.1 us
    all_gather x1, waiting for transfers between devices, shards(): second_full = lax.all_gather(second_low, 'tensor', axis=0, tiled=True)  62.2 us
    reduce_scatter x1, waiting for transfers between devices, shards(): both = lax.psum_scatter(merged, 'tensor', scatter_dimension=0, tiled=True)  50.7 us
    ppermute x12, waiting for transfers between devices, halving_steps(): got = lax.ppermute(send, axis, [(i, i ^ bit) for i in range(size)])  36 us
    all_to_all x2, starting transfers between devices, reduce_vectors(): packed = lax.all_to_all(packed, ('group', 'dp', 'tensor'), 0, 0, tiled=True)  33.3 us
    all_gather x1, waiting for transfers between devices, shards(): upstream_full = lax.all_gather(upstream, 'tensor', axis=0, tiled=True)  31.2 us
    reshape x4, local copies, waits for them, and re-layouts, halving_sum(): value.reshape(shape[:dim] + (groups // 2, 2, dps * rest) + shape[dim + 1:])  19.4 us
  transfers between devices with their start and end apart: 20, of which 11 were waited for; matrix products, arithmetic and copies ran while one was open for 20% of the time, Pallas kernels for 1%

profile of v14, /device:TPU:96, one launch (start us, length us, event | category | flops | bytes accessed | tf_op | source)
XLA Modules:
  0.0 641.0 jit_solution(15434311158437853773)
XLA Ops:
  15.8 110.4 %all-gather.5.cloned.1.call-done = bf16[2048,4096]{1,0:T(8,128)(2,1)} async-done(((bf16[128,4096]{1,0:T(8,128)(2,1)}), bf16[2048,4096]{1,0:T(8,128)(2,1)}) %all-gather.5.cloned.1.call-update) | async-done | bytes 16777232 | tf_op jit(solution)/shard_map/all_gather | solution.py:252
  128.9 7.4 %fusion.41 = f32[2048,1,3,128]{3,0,2,1:T(8,128)S(1)} fusion(bf16[2048,4096]{1,0:T(8,128)(2,1)} %all-gather.5.cloned.1.call-done, bf16[2048,3,1,128]{0,3,1,2:T(8,128)(2,1)} %copy.36), kind=kOutput, calls=%fused_computation.43 | convolution fusion | flops 3221225472 | bytes 13107200 | tf_op jit(solution)/shard_map/dot_general | solution.py:259
  138.3 9.4 %shard_map.254 = (bf16[2048,128]{1,0:T(8,128)(2,1)}, f32[2048,1]{1,0:T(8,128)}) custom-call(s32[1]{0:T(128)} %dynamic_slice.7.len_ref, bf16[2048,128]{1,0:T(8,128)(2,1)} %get-tuple-element.119.q_ref, bf16[2048,128]{1,0:T(8,128)(2,1)} %fusion.79.k_ref, bf16[2048,128]{1,0:T(8,128)(2,1)} %get-tuple-element.118.v_ref), custom_call_target="tpu_custom_call" | custom-call | flops 1342177280 | bytes 2097152 | tf_op jit(solution)/shard_map/pallas_call | solution.py:85
  149.0 15.2 %all_to_all.34 = bf16[16,128,128]{1,2,0:T(8,128)(2,1)S(1)} all-to-all(bf16[16,128,128]{1,2,0:T(8,128)(2,1)S(1)} %copy.37), channel_id=1, replica_groups=mesh['group'=4,'dp'=2,'tensor'=16] {'tensor'}, dimensions={0} | all-to-all | bytes 1048576 | tf_op jit(solution)/shard_map/all_to_all | solution.py:285
  170.3 31.2 %all-gather.7.cloned.1.call-done = bf16[2048,1,2048]{2,0,1:T(8,128)(2,1)} async-done(((bf16[128,1,2048]{2,0,1:T(8,128)(2,1)}), bf16[2048,1,2048]{2,0,1:T(8,128)(2,1)}) %all-gather.7.cloned.1.call-update) | async-done | bytes 8388624 | tf_op jit(solution)/shard_map/all_gather | solution.py:257
  201.8 10.6 %fusion.35 = f32[2048,1,512]{2,0,1:T(8,128)} fusion(bf16[512,2048]{1,0:T(8,128)(2,1)} %param.28, bf16[2048,1,2048]{2,0,1:T(8,128)(2,1)} %all-gather.7.cloned.1.call-done), kind=kOutput, calls=%fused_computation.40 | convolution fusion | flops 4294967296 | bytes 14680064 | tf_op jit(solution)/shard_map/rsd,fd->rsf/dot_general | solution.py:299
  212.4 62.2 %all-gather.9.cloned.1.call-done = bf16[2048,1,2048]{2,0,1:T(8,128)(2,1)} async-done(((bf16[128,1,2048]{2,0,1:T(8,128)(2,1)}), bf16[2048,1,2048]{2,0,1:T(8,128)(2,1)}) %all-gather.9.cloned.1.call-update) | async-done | bytes 8388624 | tf_op jit(solution)/shard_map/all_gather | solution.py:302
  274.6 7.0 %fusion.10 = f32[2048,512]{1,0:T(8,128)S(1)} fusion(bf16[2048,512]{1,0:T(8,128)(2,1)S(1)} %copy-done, bf16[2048,1,2048]{2,0,1:T(8,128)(2,1)} %all-gather.9.cloned.1.call-done), kind=kOutput, calls=%fused_computation.11 | convolution fusion | flops 4294967296 | bytes 14680064 | tf_op jit(solution)/shard_map/dot_general | solution.py:305
  287.4 6.9 %convert_bitcast_fusion.1 = bf16[2048,1,2048]{2,0,1:T(8,128)(2,1)} fusion(bf16[2048,512]{1,0:T(8,128)(2,1)S(1)} %get-tuple-element.110, bf16[2048,512]{1,0:T(8,128)(2,1)S(1)} %copy-done), kind=kOutput, calls=%fused_computation.18 | convolution fusion | flops 4299161600 | bytes 12582912 | tf_op jit(solution)/shard_map/rsf,df->rsd/dot_general | solution.py:326
  297.1 7.1 %fusion.32 = f32[2048,512]{1,0:T(8,128)S(1)} fusion(bf16[2048,512]{1,0:T(8,128)(2,1)S(1)} %copy-done.14, bf16[2048,1,2048]{2,0,1:T(8,128)(2,1)} %all-gather.9.cloned.1.call-done, f32[]{:T(128)S(6)} %div.71), kind=kOutput, calls=%fused_computation.39 | convolution fusion | flops 4296015872 | bytes 14680068 | tf_op jit(solution)/shard_map/rd,rf->df/dot_general | solution.py:318
  306.8 10.0 %fusion.29 = f32[512,2048]{1,0:T(8,128)} fusion(bf16[2048,1,2048]{2,0,1:T(8,128)(2,1)} %all-gather.7.cloned.1.call-done, f32[]{:T(128)S(6)} %div.71, f32[2048,512]{1,0:T(8,128)S(1)} %copy-done.9, f32[512]{0:T(512)S(1)} %copy-done.21), kind=kOutput, calls=%fused_computation.38 | convolution fusion | flops 4306501632 | bytes 16779268 | tf_op jit(solution)/shard_map/rsf,rsd->fd/dot_general | solution.py:314
  316.8 6.7 %reshape.430 = f32[512,2,2,512]{3,2,1,0:T(2,128)} reshape(f32[512,2048]{1,0:T(8,128)} %fusion.29) | data formatting | bytes 8388608 | tf_op jit(solution)/shard_map/reshape | solution.py:477
  323.5 7.3 %copy.38 = f32[512,2,2,512]{0,3,1,2:T(8,128)} copy(f32[512,2,2,512]{3,2,1,0:T(2,128)} %reshape.430) | data formatting | bytes 8388608 | tf_op jit(solution)/shard_map/reshape | solution.py:477
  345.3 10.6 %collective-permute-done.1 = bf16[2,256,512]{2,1,0:T(8,128)(2,1)S(1)} collective-permute-done((bf16[2,256,512]{2,1,0:T(8,128)(2,1)S(1)}, bf16[2,256,512]{2,1,0:T(8,128)(2,1)S(1)}, u32[]{:S(2)}, u32[]{:S(2)}) %collective-permute-start.1) | collective-permute-done | bytes 524320 | tf_op jit(solution)/shard_map/ppermute | solution.py:467
  357.5 9.6 %collective-permute-done.4 = bf16[512,2,256]{0,2,1:T(8,128)(2,1)S(1)} collective-permute-done((bf16[512,2,256]{0,2,1:T(8,128)(2,1)S(1)}, bf16[512,2,256]{0,2,1:T(8,128)(2,1)S(1)}, u32[]{:S(2)}, u32[]{:S(2)}) %collective-permute-start.4) | collective-permute-done | bytes 524320 | tf_op jit(solution)/shard_map/ppermute | solution.py:467
  373.5 6.9 %dynamic_update_slice.12 = bf16[2048,1,4096]{2,0,1:T(8,128)(2,1)} pad(bf16[2048,1,2048]{2,0,1:T(8,128)(2,1)S(1)} %convert_bitcast_fusion, bf16[]{:T(256)} %constant.136.clone.1), padding=0_0x0_0x2048_0 | pad | bytes 25165826 | tf_op jit(solution)/shard_map/dynamic_update_slice | solution.py:335
  386.7 70.1 %all-gather.11.cloned.1.call-done = bf16[2048,1,2048]{2,0,1:T(8,128)(2,1)} async-done(((bf16[128,1,2048]{2,0,1:T(8,128)(2,1)}), bf16[2048,1,2048]{2,0,1:T(8,128)(2,1)}) %all-gather.11.cloned.1.call-update) | async-done | bytes 8388624 | tf_op jit(solution)/shard_map/all_gather | solution.py:352
  463.4 7.6 %shard_map.255 = (bf16[2048,128]{1,0:T(8,128)(2,1)}, bf16[2048,128]{1,0:T(8,128)(2,1)}, bf16[2048,128]{1,0:T(8,128)(2,1)}) custom-call(s32[1]{0:T(128)} %dynamic_slice.7.len_ref, bf16[2048,128]{1,0:T(8,128)(2,1)} %get-tuple-element.119.q_ref, bf16[2048,128]{1,0:T(8,128)(2,1)} %fusion.79.k_ref, bf16[2048,128]{1,0:T(8,128)(2,1)} %get-tuple-element.118.v_ref, ...), custom_call_target="tpu_custom_call" | custom-call | flops 2684354560 | bytes 4194304 | tf_op jit(solution)/shard_map/pallas_call | solution.py:185
  474.4 9.8 %bitcast_dynamic-update-slice_fusion = bf16[2048,1,4096]{2,0,1:T(8,128)(2,1)} fusion(bf16[2048,1,4096]{2,0,1:T(8,128)(2,1)} %dynamic_update_slice.12, bf16[2048,384]{0,1:T(8,128)(2,1)} %bitcast.158, bf16[2048,384]{0,1:T(8,128)(2,1)} %bitcast.154), kind=kOutput, calls=%fused_computation.2 | convolution fusion | flops 3225419776 | bytes 11534336 | tf_op jit(solution)/shard_map/rsc,dc->rsd/dot_general | solution.py:378
  500.0 25.1 %all-to-all-start.1 = ((f32[128,1,176]{2,1,0:T(1,128)}), f32[128,1,176]{2,1,0:T(1,128)S(1)}, u32[]{:S(2)}, u32[]{:S(2)}) async-start(f32[128,1,176]{2,1,0:T(1,128)} %copy.41), calls=%async_computation.3 | async-start | bytes 262144 | tf_op jit(solution)/shard_map/all_to_all | solution.py:447
  527.3 7.9 %fusion.38 = f32[2048,384]{1,0:T(8,128)S(1)} fusion(bf16[2048,384]{0,1:T(8,128)(2,1)} %bitcast.159, bf16[2048,4096]{1,0:T(8,128)(2,1)} %all-gather.5.cloned.1.call-done, f32[]{:T(128)S(6)} %div.71), kind=kOutput, calls=%fused_computation.42 | convolution fusion | flops 3222011904 | bytes 13107204 | tf_op jit(solution)/shard_map/rd,rc->dc/dot_general | solution.py:372
  545.6 7.7 %collective-permute-done.7 = bf16[2,256,384]{2,1,0:T(8,128)(2,1)S(1)} collective-permute-done((bf16[2,256,384]{2,1,0:T(8,128)(2,1)S(1)}, bf16[2,256,384]{2,1,0:T(8,128)(2,1)S(1)}, u32[]{:S(2)}, u32[]{:S(2)}) %collective-permute-start.7) | collective-permute-done | bytes 393248 | tf_op jit(solution)/shard_map/ppermute | solution.py:467
  561.9 50.7 %reduce-scatter.5.cloned.1.call-done = bf16[128,1,4096]{2,0,1:T(8,128)(2,1)} async-done(((bf16[2048,1,4096]{2,0,1:T(8,128)(2,1)}), bf16[128,1,4096]{2,0,1:T(8,128)(2,1)}) %reduce-scatter.5.cloned.1.call-update) | async-done | bytes 1048592 | tf_op jit(solution)/shard_map/reduce_scatter | solution.py:386
  617.8 8.2 %all-to-all-start.2 = ((f32[128,1,16]{2,1,0:T(1,128)}), f32[128,1,16]{2,1,0:T(1,128)S(1)}, u32[]{:S(2)}, u32[]{:S(2)}) async-start(f32[128,1,16]{2,1,0:T(1,128)} %bitcast.55), calls=%async_computation.4 | async-start | bytes 131072 | tf_op jit(solution)/shard_map/all_to_all | solution.py:447
  (190 shorter events, 119.2 us)
Async XLA Ops:
  7.2 267.4 %copy-start = (bf16[2048,512]{1,0:T(8,128)(2,1)S(1)}, bf16[2048,512]{1,0:T(8,128)(2,1)}, u32[]{:S(2)}) copy-start(bf16[2048,512]{1,0:T(8,128)(2,1)} %param.26) | copy-start | bytes 6291460
  7.2 119.0 %all-gather.5.cloned.1.call-start = ((), (), s32[]{:S(2)}) async-start(), calls=%async_computation.5 | async-start | bytes 17825792 | tf_op jit(solution)/shard_map/all_gather | solution.py:252
  11.4 117.5 %copy-start.22 = (f32[2,128]{1,0:T(2,128)S(1)}, f32[2,128]{1,0:T(2,128)}, u32[]{:S(2)}) copy-start(f32[2,128]{1,0:T(2,128)} %param.21) | copy-start | bytes 3076
  13.6 188.0 %all-gather.7.cloned.1.call-start = ((), (), s32[]{:S(2)}) async-start(), calls=%async_computation.6 | async-start | bytes 8912896 | tf_op jit(solution)/shard_map/all_gather | solution.py:257
  126.2 148.4 %all-gather.9.cloned.1.call-start = ((), (), s32[]{:S(2)}) async-start(), calls=%async_computation.7 | async-start | bytes 8912896 | tf_op jit(solution)/shard_map/all_gather | solution.py:302
  201.5 180.7 %reduce-scatter.3.cloned.1.call-start = ((), (), s32[]{:S(2)}) async-start(), calls=%async_computation.8 | async-start | bytes 8912896 | tf_op jit(solution)/shard_map/reduce_scatter | solution.py:329
  294.3 162.6 %all-gather.11.cloned.1.call-start = ((), (), s32[]{:S(2)}) async-start(), calls=%async_computation.9 | async-start | bytes 8912896 | tf_op jit(solution)/shard_map/all_gather | solution.py:352
  306.3 31.3 %collective-permute-start = (bf16[4,256,512]{2,1,0:T(8,128)(2,1)S(1)}, bf16[4,256,512]{2,1,0:T(8,128)(2,1)S(1)}, u32[]{:S(2)}, u32[]{:S(2)}) collective-permute-start(bf16[4,256,512]{2,1,0:T(8,128)(2,1)S(1)} %bitcast.160), channel_id=1, source_target_pairs={{0,32},{32,0},{64,96},{96,64},{1,33},{33,1},{65,97},{97,65},{2,34}... | collective-permute-start | bytes 3145736 | tf_op jit(solution)/shard_map/ppermute | solution.py:467
  334.4 7.4 %collective-permute-start.3 = (bf16[512,4,256]{0,2,1:T(8,128)(2,1)}, bf16[512,4,256]{0,2,1:T(8,128)(2,1)}, u32[]{:S(2)}, u32[]{:S(2)}) collective-permute-start(bf16[512,4,256]{0,2,1:T(8,128)(2,1)} %select_convert_fusion), channel_id=1, source_target_pairs={{0,32},{32,0},{64,96},{96,64},{1,33},{33,1},{65,97},{97,65},{2,34}... | collective-permute-start | bytes 3145736 | tf_op jit(solution)/shard_map/ppermute | solution.py:467
  341.0 14.8 %collective-permute-start.1 = (bf16[2,256,512]{2,1,0:T(8,128)(2,1)S(1)}, bf16[2,256,512]{2,1,0:T(8,128)(2,1)S(1)}, u32[]{:S(2)}, u32[]{:S(2)}) collective-permute-start(bf16[2,256,512]{2,1,0:T(8,128)(2,1)S(1)} %select_convert_fusion.4), channel_id=1, source_target_pairs={{0,64},{32,96},{64,0},{96,32},{1,65},{33,97},{65,1},{97,33},{2,66}... | collective-permute-start | bytes 1572872 | tf_op jit(solution)/shard_map/ppermute | solution.py:467
  344.0 23.2 %collective-permute-start.4 = (bf16[512,2,256]{0,2,1:T(8,128)(2,1)S(1)}, bf16[512,2,256]{0,2,1:T(8,128)(2,1)S(1)}, u32[]{:S(2)}, u32[]{:S(2)}) collective-permute-start(bf16[512,2,256]{0,2,1:T(8,128)(2,1)S(1)} %select_convert_fusion.3), channel_id=1, source_target_pairs={{0,64},{32,96},{64,0},{96,32},{1,65},{33,97},{65,1},{97,33},{2,66}... | collective-permute-start | bytes 1572872 | tf_op jit(solution)/shard_map/ppermute | solution.py:467
  356.2 24.1 %collective-permute-start.2 = (bf16[1,256,512]{2,1,0:T(8,128)(2,1)S(1)}, bf16[1,256,512]{2,1,0:T(8,128)(2,1)S(1)}, u32[]{:S(2)}, u32[]{:S(2)}) collective-permute-start(bf16[1,256,512]{2,1,0:T(8,128)(2,1)S(1)} %select_convert_fusion.8), channel_id=1, source_target_pairs={{0,16},{16,0},{1,17},{17,1},{2,18},{18,2},{3,19},{19,3},{4,20},{20... | collective-permute-start | bytes 786440 | tf_op jit(solution)/shard_map/ppermute | solution.py:467
  367.4 13.9 %collective-permute-start.5 = (bf16[512,1,256]{0,2,1:T(8,128)(2,1)S(1)}, bf16[512,1,256]{0,2,1:T(8,128)(2,1)S(1)}, u32[]{:S(2)}, u32[]{:S(2)}) collective-permute-start(bf16[512,1,256]{0,2,1:T(8,128)(2,1)S(1)} %select_convert_fusion.7), channel_id=1, source_target_pairs={{0,16},{16,0},{1,17},{17,1},{2,18},{18,2},{3,19},{19,3},{4,20},{20... | collective-permute-start | bytes 786440 | tf_op jit(solution)/shard_map/ppermute | solution.py:467
  384.2 79.3 %copy-start.6 = (f32[128,1,2048]{2,0,1:T(8,128)}, f32[128,1,2048]{2,0,1:T(8,128)S(1)}, u32[]{:S(2)}) copy-start(f32[128,1,2048]{2,0,1:T(8,128)S(1)} %get-tuple-element.116) | copy-start | bytes 3145732
  386.7 225.9 %reduce-scatter.5.cloned.1.call-start = ((), (), s32[]{:S(2)}) async-start(), calls=%async_computation.10 | async-start | bytes 17825792 | tf_op jit(solution)/shard_map/reduce_scatter | solution.py:386
  500.0 37.1 %all-to-all-start.1 = ((f32[128,1,176]{2,1,0:T(1,128)}), f32[128,1,176]{2,1,0:T(1,128)S(1)}, u32[]{:S(2)}, u32[]{:S(2)}) async-start(f32[128,1,176]{2,1,0:T(1,128)} %copy.41), calls=%async_computation.3 | async-start | bytes 262144 | tf_op jit(solution)/shard_map/all_to_all | solution.py:447
  527.1 11.4 %collective-permute-start.9 = (bf16[1,128,4,256]{1,3,2,0:T(8,128)(2,1)}, bf16[1,128,4,256]{1,3,2,0:T(8,128)(2,1)S(1)}, u32[]{:S(2)}, u32[]{:S(2)}) collective-permute-start(bf16[1,128,4,256]{1,3,2,0:T(8,128)(2,1)} %select_convert_fusion.6), channel_id=1, source_target_pairs={{0,32},{32,0},{64,96},{96,64},{1,33},{33,1},{65,97},{97,65},{2,34}... | collective-permute-start | bytes 786440 | tf_op jit(solution)/shard_map/ppermute | solution.py:467
  535.3 4.0 collective-permute-start.6
  538.6 6.0 collective-permute-start.10
  541.2 12.1 %collective-permute-start.7 = (bf16[2,256,384]{2,1,0:T(8,128)(2,1)S(1)}, bf16[2,256,384]{2,1,0:T(8,128)(2,1)S(1)}, u32[]{:S(2)}, u32[]{:S(2)}) collective-permute-start(bf16[2,256,384]{2,1,0:T(8,128)(2,1)S(1)} %select_convert_fusion.5), channel_id=1, source_target_pairs={{0,64},{32,96},{64,0},{96,32},{1,65},{33,97},{65,1},{97,33},{2,66}... | collective-permute-start | bytes 1179656 | tf_op jit(solution)/shard_map/ppermute | solution.py:467
  544.7 9.8 %collective-permute-start.11 = (bf16[1,128,1,256]{1,3,2,0:T(8,128)(2,1)S(1)}, bf16[1,128,1,256]{1,3,2,0:T(8,128)(2,1)S(1)}, u32[]{:S(2)}, u32[]{:S(2)}) collective-permute-start(bf16[1,128,1,256]{1,3,2,0:T(8,128)(2,1)S(1)} %select_convert_fusion.11), channel_id=1, source_target_pairs={{0,16},{16,0},{1,17},{17,1},{2,18},{18,2},{3,19},{19,3},{4,20},{20... | collective-permute-start | bytes 196616 | tf_op jit(solution)/shard_map/ppermute | solution.py:467
  553.5 7.3 %collective-permute-start.8 = (bf16[1,256,384]{2,1,0:T(8,128)(2,1)S(1)}, bf16[1,256,384]{2,1,0:T(8,128)(2,1)S(1)}, u32[]{:S(2)}, u32[]{:S(2)}) collective-permute-start(bf16[1,256,384]{2,1,0:T(8,128)(2,1)S(1)} %select_convert_fusion.9), channel_id=1, source_target_pairs={{0,16},{16,0},{1,17},{17,1},{2,18},{18,2},{3,19},{19,3},{4,20},{20... | collective-permute-start | bytes 589832 | tf_op jit(solution)/shard_map/ppermute | solution.py:467
  554.6 71.5 %copy-start.20 = (f32[2048]{0:T(1024)S(1)}, f32[2048]{0:T(1024)}, u32[]{:S(2)}) copy-start(f32[2048]{0:T(1024)} %param.29) | copy-start | bytes 24580
  617.8 15.5 %all-to-all-start.2 = ((f32[128,1,16]{2,1,0:T(1,128)}), f32[128,1,16]{2,1,0:T(1,128)S(1)}, u32[]{:S(2)}, u32[]{:S(2)}) async-start(f32[128,1,16]{2,1,0:T(1,128)} %bitcast.55), calls=%async_computation.4 | async-start | bytes 131072 | tf_op jit(solution)/shard_map/all_to_all | solution.py:447
  (22 other events, 364.5 us)
Sparse Core Ops, SparseCore 0:
  13.7 112.4 all-gather.4
  128.3 73.1 all-gather.6
  204.2 70.3 all-gather.8
  294.4 84.3 reduce-scatter.2
  386.8 69.9 all-gather.10
  484.4 128.1 reduce-scatter.4

commit v15 on v14

--- a/solution.py
+++ b/solution.py
@@ -351,8 +351,14 @@
     )
     piece = lax.all_gather(branch_low, "tensor", axis=0, tiled=True)
     weight_grad = jnp.einsum("rse,rsd->ed", attended, piece, preferred_element_type=jnp.float32)
-    part = jnp.einsum("rsd,ed->rse", piece, out_weight, preferred_element_type=jnp.float32)
-    attended_grad = part.astype(jnp.bfloat16)
+    heads_grad = jnp.dot(
+        branch_low.reshape(row_count * seq_count, model_width),
+        out_full.T,
+        preferred_element_type=jnp.float32,
+    ).astype(jnp.bfloat16)
+    attended_grad = lax.all_to_all(heads_grad, "tensor", 1, 0, tiled=True).reshape(
+        seq_total, seq_count, local_width
+    )
     backward_items = [
         attention_backward(
             item(query, s, h),

time: 652 us -> 616 us (0.945)
  waiting for transfers between devices: 361 us -> 295 us
  blocking collectives: 15.2 us -> 36 us
  Pallas kernels: 17 us -> 24.6 us
    all_gather x1, waiting for transfers between devices: 70.1 us -> 0.01 us  [shards(): piece = lax.all_gather(branch_low, 'tensor', axis=0, tiled=True)]
    all_to_all x0 -> x1, blocking collectives: none -> 20.4 us  [shards(): lax.all_to_all(heads_grad, 'tensor', 1, 0, tiled=True)]
    all_to_all x2, starting transfers between devices: 33.3 us -> 19.1 us  [reduce_vectors(): packed = lax.all_to_all(packed, ('group', 'dp', 'tensor'), 0, 0, tiled=True)]
    ppermute x12, starting transfers between devices: 10.4 us -> 22.9 us  [halving_steps(): got = lax.ppermute(send, axis, [(i, i ^ bit) for i in range(size)])]
    reduce_scatter x1, waiting for transfers between devices: 50.7 us -> 63.2 us  [shards(): both = lax.psum_scatter(merged, 'tensor', scatter_dimension=0, tiled=True)]
    ppermute x12, waiting for transfers between devices: 36 us -> 26.5 us  [halving_steps(): got = lax.ppermute(send, axis, [(i, i ^ bit) for i in range(size)])]
  transfers between devices with their start and end apart: 20 -> 20, of which waited for: 11 -> 11; matrix products, arithmetic and copies ran while one was open for 20% -> 25% of each run, Pallas kernels for 1% -> 4%
where the time goes in v15:
time: 616 us; the launch traced here: 604 us
  waiting for transfers between devices  295 us (48%)
  matrix products  88.9 us (14%)
  other arithmetic  53.4 us (9%)
  local copies, waits for them, and re-layouts  47.2 us (8%)
  starting transfers between devices  42.6 us (7%)
  blocking collectives  36 us (6%)
  Pallas kernels  24.6 us (4%)
  between operations  16.5 us (3%)
    all_gather x1, waiting for transfers between devices, shards(): front = lax.all_gather(front, 'tensor', axis=0, tiled=True)  110 us
    reduce_scatter x1, waiting for transfers between devices, shards(): both = lax.psum_scatter(merged, 'tensor', scatter_dimension=0, tiled=True)  63.2 us
    all_gather x1, waiting for transfers between devices, shards(): second_full = lax.all_gather(second_low, 'tensor', axis=0, tiled=True)  61.3 us
    all_gather x1, waiting for transfers between devices, shards(): upstream_full = lax.all_gather(upstream, 'tensor', axis=0, tiled=True)  29.1 us
    ppermute x12, waiting for transfers between devices, halving_steps(): got = lax.ppermute(send, axis, [(i, i ^ bit) for i in range(size)])  26.5 us
    ppermute x12, starting transfers between devices, halving_steps(): got = lax.ppermute(send, axis, [(i, i ^ bit) for i in range(size)])  22.9 us
    all_to_all x1, blocking collectives, shards(): lax.all_to_all(heads_grad, 'tensor', 1, 0, tiled=True)  20.4 us
    reshape x4, local copies, waits for them, and re-layouts, halving_sum(): value.reshape(shape[:dim] + (groups // 2, 2, dps * rest) + shape[dim + 1:])  19.4 us
  transfers between devices with their start and end apart: 20, of which 11 were waited for; matrix products, arithmetic and copies ran while one was open for 25% of the time, Pallas kernels for 4%

profile of v15, /device:TPU:96, one launch (start us, length us, event | category | flops | bytes accessed | tf_op | source)
XLA Modules:
  0.0 604.0 jit_solution(2181112442097068316)
XLA Ops:
  15.8 110.5 %all-gather.5.cloned.1.call-done = bf16[2048,4096]{1,0:T(8,128)(2,1)} async-done(((bf16[128,4096]{1,0:T(8,128)(2,1)}), bf16[2048,4096]{1,0:T(8,128)(2,1)}) %all-gather.5.cloned.1.call-update) | async-done | bytes 16777232 | tf_op jit(solution)/shard_map/all_gather | solution.py:252
  128.9 7.4 %fusion.41 = f32[2048,1,3,128]{3,0,2,1:T(8,128)S(1)} fusion(bf16[2048,4096]{1,0:T(8,128)(2,1)} %all-gather.5.cloned.1.call-done, bf16[2048,3,1,128]{0,3,1,2:T(8,128)(2,1)} %copy.38), kind=kOutput, calls=%fused_computation.43 | convolution fusion | flops 3221225472 | bytes 13107200 | tf_op jit(solution)/shard_map/dot_general | solution.py:259
  138.3 13.2 %shard_map.254 = (bf16[2048,128]{1,0:T(8,128)(2,1)}, f32[2048,1]{1,0:T(8,128)}) custom-call(s32[1]{0:T(128)} %dynamic_slice.7.len_ref, bf16[2048,128]{1,0:T(8,128)(2,1)} %get-tuple-element.119.q_ref, bf16[2048,128]{1,0:T(8,128)(2,1)} %fusion.82.k_ref, bf16[2048,128]{1,0:T(8,128)(2,1)} %get-tuple-element.118.v_ref), custom_call_target="tpu_custom_call" | custom-call | flops 1342177280 | bytes 2097152 | tf_op jit(solution)/shard_map/pallas_call | solution.py:85
  152.8 15.6 %all_to_all.53 = bf16[16,128,128]{1,2,0:T(8,128)(2,1)S(1)} all-to-all(bf16[16,128,128]{1,2,0:T(8,128)(2,1)S(1)} %copy.39), channel_id=1, replica_groups=mesh['group'=4,'dp'=2,'tensor'=16] {'tensor'}, dimensions={0} | all-to-all | bytes 1048576 | tf_op jit(solution)/shard_map/all_to_all | solution.py:285
  174.6 29.1 %all-gather.7.cloned.1.call-done = bf16[2048,1,2048]{2,0,1:T(8,128)(2,1)} async-done(((bf16[128,1,2048]{2,0,1:T(8,128)(2,1)}), bf16[2048,1,2048]{2,0,1:T(8,128)(2,1)}) %all-gather.7.cloned.1.call-update) | async-done | bytes 8388624 | tf_op jit(solution)/shard_map/all_gather | solution.py:257
  203.9 10.6 %fusion.35 = f32[2048,1,512]{2,0,1:T(8,128)} fusion(bf16[512,2048]{1,0:T(8,128)(2,1)} %param.28, bf16[2048,1,2048]{2,0,1:T(8,128)(2,1)} %all-gather.7.cloned.1.call-done), kind=kOutput, calls=%fused_computation.40 | convolution fusion | flops 4294967296 | bytes 14680064 | tf_op jit(solution)/shard_map/rsd,fd->rsf/dot_general | solution.py:299
  214.5 61.3 %all-gather.9.cloned.1.call-done = bf16[2048,1,2048]{2,0,1:T(8,128)(2,1)} async-done(((bf16[128,1,2048]{2,0,1:T(8,128)(2,1)}), bf16[2048,1,2048]{2,0,1:T(8,128)(2,1)}) %all-gather.9.cloned.1.call-update) | async-done | bytes 8388624 | tf_op jit(solution)/shard_map/all_gather | solution.py:302
  275.8 7.0 %fusion.6 = f32[2048,512]{1,0:T(8,128)S(1)} fusion(bf16[2048,512]{1,0:T(8,128)(2,1)S(1)} %copy-done, bf16[2048,1,2048]{2,0,1:T(8,128)(2,1)} %all-gather.9.cloned.1.call-done), kind=kOutput, calls=%fused_computation.7 | convolution fusion | flops 4294967296 | bytes 14680064 | tf_op jit(solution)/shard_map/dot_general | solution.py:305
  288.6 6.9 %convert_bitcast_fusion.1 = bf16[2048,1,2048]{2,0,1:T(8,128)(2,1)} fusion(bf16[2048,512]{1,0:T(8,128)(2,1)S(1)} %get-tuple-element.110, bf16[2048,512]{1,0:T(8,128)(2,1)S(1)} %copy-done), kind=kOutput, calls=%fused_computation.14 | convolution fusion | flops 4299161600 | bytes 12582912 | tf_op jit(solution)/shard_map/rsf,df->rsd/dot_general | solution.py:326
  298.3 7.1 %fusion.32 = f32[2048,512]{1,0:T(8,128)S(1)} fusion(bf16[2048,512]{1,0:T(8,128)(2,1)S(1)} %copy-done.16, bf16[2048,1,2048]{2,0,1:T(8,128)(2,1)} %all-gather.9.cloned.1.call-done, f32[]{:T(128)S(6)} %div.71), kind=kOutput, calls=%fused_computation.39 | convolution fusion | flops 4296015872 | bytes 14680068 | tf_op jit(solution)/shard_map/rd,rf->df/dot_general | solution.py:318
  308.1 10.0 %fusion.29 = f32[512,2048]{1,0:T(8,128)} fusion(bf16[2048,1,2048]{2,0,1:T(8,128)(2,1)} %all-gather.7.cloned.1.call-done, f32[]{:T(128)S(6)} %div.71, f32[2048,512]{1,0:T(8,128)S(1)} %copy-done.11, f32[512]{0:T(512)S(1)} %copy-done.23), kind=kOutput, calls=%fused_computation.38 | convolution fusion | flops 4306501632 | bytes 16779268 | tf_op jit(solution)/shard_map/rsf,rsd->fd/dot_general | solution.py:314
  318.1 6.7 %reshape.431 = f32[512,2,2,512]{3,2,1,0:T(2,128)} reshape(f32[512,2048]{1,0:T(8,128)} %fusion.29) | data formatting | bytes 8388608 | tf_op jit(solution)/shard_map/reshape | solution.py:483
  324.8 7.3 %copy.40 = f32[512,2,2,512]{0,3,1,2:T(8,128)} copy(f32[512,2,2,512]{3,2,1,0:T(2,128)} %reshape.431) | data formatting | bytes 8388608 | tf_op jit(solution)/shard_map/reshape | solution.py:483
  346.4 10.6 %collective-permute-done.1 = bf16[2,256,512]{2,1,0:T(8,128)(2,1)S(1)} collective-permute-done((bf16[2,256,512]{2,1,0:T(8,128)(2,1)S(1)}, bf16[2,256,512]{2,1,0:T(8,128)(2,1)S(1)}, u32[]{:S(2)}, u32[]{:S(2)}) %collective-permute-start.1) | collective-permute-done | bytes 524320 | tf_op jit(solution)/shard_map/ppermute | solution.py:473
  358.8 9.5 %collective-permute-done.4 = bf16[512,2,256]{0,2,1:T(8,128)(2,1)S(1)} collective-permute-done((bf16[512,2,256]{0,2,1:T(8,128)(2,1)S(1)}, bf16[512,2,256]{0,2,1:T(8,128)(2,1)S(1)}, u32[]{:S(2)}, u32[]{:S(2)}) %collective-permute-start.4) | collective-permute-done | bytes 524320 | tf_op jit(solution)/shard_map/ppermute | solution.py:473
  374.7 6.9 %dynamic_update_slice.12 = bf16[2048,1,4096]{2,0,1:T(8,128)(2,1)} pad(bf16[2048,1,2048]{2,0,1:T(8,128)(2,1)S(1)} %convert_bitcast_fusion, bf16[]{:T(256)} %constant.136.clone.1), padding=0_0x0_0x2048_0 | pad | bytes 25165826 | tf_op jit(solution)/shard_map/dynamic_update_slice | solution.py:335
  394.8 20.4 %all_to_all.54 = bf16[128,16,128]{2,0,1:T(8,128)(2,1)} all-to-all(bf16[128,16,128]{2,0,1:T(8,128)(2,1)S(1)} %bitcast.163), channel_id=1, replica_groups=mesh['group'=4,'dp'=2,'tensor'=16] {'tensor'}, dimensions={1} | all-to-all | bytes 1048576 | tf_op jit(solution)/shard_map/all_to_all | solution.py:359
  415.1 11.4 %shard_map.255 = (bf16[2048,128]{1,0:T(8,128)(2,1)}, bf16[2048,128]{1,0:T(8,128)(2,1)}, bf16[2048,128]{1,0:T(8,128)(2,1)}) custom-call(s32[1]{0:T(128)} %dynamic_slice.7.len_ref, bf16[2048,128]{1,0:T(8,128)(2,1)} %get-tuple-element.119.q_ref, bf16[2048,128]{1,0:T(8,128)(2,1)} %fusion.82.k_ref, bf16[2048,128]{1,0:T(8,128)(2,1)} %get-tuple-element.118.v_ref, ...), custom_call_target="tpu_custom_call" | custom-call | flops 2684354560 | bytes 4194304 | tf_op jit(solution)/shard_map/pallas_call | solution.py:185
  430.0 9.7 %bitcast_dynamic-update-slice_fusion = bf16[2048,1,4096]{2,0,1:T(8,128)(2,1)} fusion(bf16[2048,1,4096]{2,0,1:T(8,128)(2,1)} %dynamic_update_slice.12, bf16[2048,384]{0,1:T(8,128)(2,1)} %bitcast.164, bf16[2048,384]{0,1:T(8,128)(2,1)} %bitcast.159), kind=kOutput, calls=%fused_computation.2 | convolution fusion | flops 3225419776 | bytes 11534336 | tf_op jit(solution)/shard_map/rsc,dc->rsd/dot_general | solution.py:384
  440.4 7.7 %fusion.38 = f32[2048,384]{1,0:T(8,128)S(1)} fusion(bf16[2048,384]{0,1:T(8,128)(2,1)} %bitcast.165, bf16[2048,4096]{1,0:T(8,128)(2,1)} %all-gather.5.cloned.1.call-done, f32[]{:T(128)S(6)} %div.71), kind=kOutput, calls=%fused_computation.42 | convolution fusion | flops 3222011904 | bytes 13107204 | tf_op jit(solution)/shard_map/rd,rc->dc/dot_general | solution.py:378
  449.3 10.3 %collective-permute-start.6 = (bf16[4,256,384]{2,1,0:T(8,128)(2,1)}, bf16[4,256,384]{2,1,0:T(8,128)(2,1)}, u32[]{:S(2)}, u32[]{:S(2)}) collective-permute-start(bf16[4,256,384]{2,1,0:T(8,128)(2,1)} %bitcast.49), channel_id=1, source_target_pairs={{0,32},{32,0},{64,96},{96,64},{1,33},{33,1},{65,97},{97,65},{2,34}... | collective-permute-start | bytes 2359304 | tf_op jit(solution)/shard_map/ppermute | solution.py:473
  462.0 11.0 %all-to-all-start.2 = ((f32[128,1,176]{2,1,0:T(1,128)}), f32[128,1,176]{2,1,0:T(1,128)S(1)}, u32[]{:S(2)}, u32[]{:S(2)}) async-start(f32[128,1,176]{2,1,0:T(1,128)} %copy.44), calls=%async_computation.4 | async-start | bytes 262144 | tf_op jit(solution)/shard_map/all_to_all | solution.py:453
  512.5 63.2 %reduce-scatter.5.cloned.1.call-done = bf16[128,1,4096]{2,0,1:T(8,128)(2,1)} async-done(((bf16[2048,1,4096]{2,0,1:T(8,128)(2,1)}), bf16[128,1,4096]{2,0,1:T(8,128)(2,1)}) %reduce-scatter.5.cloned.1.call-update) | async-done | bytes 1048592 | tf_op jit(solution)/shard_map/reduce_scatter | solution.py:392
  580.9 8.1 %all-to-all-start.3 = ((f32[128,1,16]{2,1,0:T(1,128)}), f32[128,1,16]{2,1,0:T(1,128)S(1)}, u32[]{:S(2)}, u32[]{:S(2)}) async-start(f32[128,1,16]{2,1,0:T(1,128)} %bitcast.58), calls=%async_computation.5 | async-start | bytes 131072 | tf_op jit(solution)/shard_map/all_to_all | solution.py:453
  (202 shorter events, 126.2 us)
Async XLA Ops:
  7.2 268.6 %copy-start = (bf16[2048,512]{1,0:T(8,128)(2,1)S(1)}, bf16[2048,512]{1,0:T(8,128)(2,1)}, u32[]{:S(2)}) copy-start(bf16[2048,512]{1,0:T(8,128)(2,1)} %param.26) | copy-start | bytes 6291460
  7.2 119.0 %all-gather.5.cloned.1.call-start = ((), (), s32[]{:S(2)}) async-start(), calls=%async_computation.6 | async-start | bytes 17825792 | tf_op jit(solution)/shard_map/all_gather | solution.py:252
  9.9 119.0 %copy-start.27 = (f32[128]{0:T(128)}, f32[128]{0:T(128)S(1)}, u32[]{:S(2)}) copy-start(f32[128]{0:T(128)S(1)} %fusion.73) | copy-start | bytes 1540
  11.4 117.5 %copy-start.25 = (f32[2,128]{1,0:T(2,128)S(1)}, f32[2,128]{1,0:T(2,128)}, u32[]{:S(2)}) copy-start(f32[2,128]{1,0:T(2,128)} %param.21) | copy-start | bytes 3076
  13.6 190.1 %all-gather.7.cloned.1.call-start = ((), (), s32[]{:S(2)}) async-start(), calls=%async_computation.7 | async-start | bytes 8912896 | tf_op jit(solution)/shard_map/all_gather | solution.py:257
  126.2 149.6 %all-gather.9.cloned.1.call-start = ((), (), s32[]{:S(2)}) async-start(), calls=%async_computation.8 | async-start | bytes 8912896 | tf_op jit(solution)/shard_map/all_gather | solution.py:302
  203.7 179.8 %reduce-scatter.3.cloned.1.call-start = ((), (), s32[]{:S(2)}) async-start(), calls=%async_computation.9 | async-start | bytes 8912896 | tf_op jit(solution)/shard_map/reduce_scatter | solution.py:329
  295.5 189.9 %all-gather.11.cloned.1.call-start = ((), (), s32[]{:S(2)}) async-start(), calls=%async_computation.11 | async-start | bytes 8912896 | tf_op jit(solution)/shard_map/all_gather | solution.py:352
  307.6 31.3 %collective-permute-start = (bf16[4,256,512]{2,1,0:T(8,128)(2,1)S(1)}, bf16[4,256,512]{2,1,0:T(8,128)(2,1)S(1)}, u32[]{:S(2)}, u32[]{:S(2)}) collective-permute-start(bf16[4,256,512]{2,1,0:T(8,128)(2,1)S(1)} %bitcast.166), channel_id=1, source_target_pairs={{0,32},{32,0},{64,96},{96,64},{1,33},{33,1},{65,97},{97,65},{2,34}... | collective-permute-start | bytes 3145736 | tf_op jit(solution)/shard_map/ppermute | solution.py:473
  335.6 7.4 %collective-permute-start.3 = (bf16[512,4,256]{0,2,1:T(8,128)(2,1)}, bf16[512,4,256]{0,2,1:T(8,128)(2,1)}, u32[]{:S(2)}, u32[]{:S(2)}) collective-permute-start(bf16[512,4,256]{0,2,1:T(8,128)(2,1)} %select_convert_fusion), channel_id=1, source_target_pairs={{0,32},{32,0},{64,96},{96,64},{1,33},{33,1},{65,97},{97,65},{2,34}... | collective-permute-start | bytes 3145736 | tf_op jit(solution)/shard_map/ppermute | solution.py:473
  342.2 14.8 %collective-permute-start.1 = (bf16[2,256,512]{2,1,0:T(8,128)(2,1)S(1)}, bf16[2,256,512]{2,1,0:T(8,128)(2,1)S(1)}, u32[]{:S(2)}, u32[]{:S(2)}) collective-permute-start(bf16[2,256,512]{2,1,0:T(8,128)(2,1)S(1)} %select_convert_fusion.4), channel_id=1, source_target_pairs={{0,64},{32,96},{64,0},{96,32},{1,65},{33,97},{65,1},{97,33},{2,66}... | collective-permute-start | bytes 1572872 | tf_op jit(solution)/shard_map/ppermute | solution.py:473
  345.2 23.1 %collective-permute-start.4 = (bf16[512,2,256]{0,2,1:T(8,128)(2,1)S(1)}, bf16[512,2,256]{0,2,1:T(8,128)(2,1)S(1)}, u32[]{:S(2)}, u32[]{:S(2)}) collective-permute-start(bf16[512,2,256]{0,2,1:T(8,128)(2,1)S(1)} %select_convert_fusion.3), channel_id=1, source_target_pairs={{0,64},{32,96},{64,0},{96,32},{1,65},{33,97},{65,1},{97,33},{2,66}... | collective-permute-start | bytes 1572872 | tf_op jit(solution)/shard_map/ppermute | solution.py:473
  357.4 24.2 %collective-permute-start.2 = (bf16[1,256,512]{2,1,0:T(8,128)(2,1)S(1)}, bf16[1,256,512]{2,1,0:T(8,128)(2,1)S(1)}, u32[]{:S(2)}, u32[]{:S(2)}) collective-permute-start(bf16[1,256,512]{2,1,0:T(8,128)(2,1)S(1)} %select_convert_fusion.8), channel_id=1, source_target_pairs={{0,16},{16,0},{1,17},{17,1},{2,18},{18,2},{3,19},{19,3},{4,20},{20... | collective-permute-start | bytes 786440 | tf_op jit(solution)/shard_map/ppermute | solution.py:473
  368.6 13.9 %collective-permute-start.5 = (bf16[512,1,256]{0,2,1:T(8,128)(2,1)S(1)}, bf16[512,1,256]{0,2,1:T(8,128)(2,1)S(1)}, u32[]{:S(2)}, u32[]{:S(2)}) collective-permute-start(bf16[512,1,256]{0,2,1:T(8,128)(2,1)S(1)} %select_convert_fusion.7), channel_id=1, source_target_pairs={{0,16},{16,0},{1,17},{17,1},{2,18},{18,2},{3,19},{19,3},{4,20},{20... | collective-permute-start | bytes 786440 | tf_op jit(solution)/shard_map/ppermute | solution.py:473
  387.9 187.8 %reduce-scatter.5.cloned.1.call-start = ((), (), s32[]{:S(2)}) async-start(), calls=%async_computation.10 | async-start | bytes 17825792 | tf_op jit(solution)/shard_map/reduce_scatter | solution.py:392
  449.3 32.8 %collective-permute-start.6 = (bf16[4,256,384]{2,1,0:T(8,128)(2,1)}, bf16[4,256,384]{2,1,0:T(8,128)(2,1)}, u32[]{:S(2)}, u32[]{:S(2)}) collective-permute-start(bf16[4,256,384]{2,1,0:T(8,128)(2,1)} %bitcast.49), channel_id=1, source_target_pairs={{0,32},{32,0},{64,96},{96,64},{1,33},{33,1},{65,97},{97,65},{2,34}... | collective-permute-start | bytes 2359304 | tf_op jit(solution)/shard_map/ppermute | solution.py:473
  462.0 18.8 %all-to-all-start.2 = ((f32[128,1,176]{2,1,0:T(1,128)}), f32[128,1,176]{2,1,0:T(1,128)S(1)}, u32[]{:S(2)}, u32[]{:S(2)}) async-start(f32[128,1,176]{2,1,0:T(1,128)} %copy.44), calls=%async_computation.4 | async-start | bytes 262144 | tf_op jit(solution)/shard_map/all_to_all | solution.py:453
  484.0 14.1 %collective-permute-start.7 = (bf16[2,256,384]{2,1,0:T(8,128)(2,1)S(1)}, bf16[2,256,384]{2,1,0:T(8,128)(2,1)}, u32[]{:S(2)}, u32[]{:S(2)}) collective-permute-start(bf16[2,256,384]{2,1,0:T(8,128)(2,1)S(1)} %select_convert_fusion.5), channel_id=1, source_target_pairs={{0,64},{32,96},{64,0},{96,32},{1,65},{33,97},{65,1},{97,33},{2,66}... | collective-permute-start | bytes 1179656 | tf_op jit(solution)/shard_map/ppermute | solution.py:473
  498.1 1.6 collective-permute-start.9
  499.8 6.4 %collective-permute-start.10 = (bf16[1,128,2,256]{1,3,2,0:T(8,128)(2,1)S(1)}, bf16[1,128,2,256]{1,3,2,0:T(8,128)(2,1)S(1)}, u32[]{:S(2)}, u32[]{:S(2)}) collective-permute-start(bf16[1,128,2,256]{1,3,2,0:T(8,128)(2,1)S(1)} %select_convert_fusion.10), channel_id=1, source_target_pairs={{0,64},{32,96},{64,0},{96,32},{1,65},{33,97},{65,1},{97,33},{2,66}... | collective-permute-start | bytes 393224 | tf_op jit(solution)/shard_map/ppermute | solution.py:473
  500.7 10.6 %collective-permute-start.8 = (bf16[1,256,384]{2,1,0:T(8,128)(2,1)S(1)}, bf16[1,256,384]{2,1,0:T(8,128)(2,1)S(1)}, u32[]{:S(2)}, u32[]{:S(2)}) collective-permute-start(bf16[1,256,384]{2,1,0:T(8,128)(2,1)S(1)} %select_convert_fusion.9), channel_id=1, source_target_pairs={{0,16},{16,0},{1,17},{17,1},{2,18},{18,2},{3,19},{19,3},{4,20},{20... | collective-permute-start | bytes 589832 | tf_op jit(solution)/shard_map/ppermute | solution.py:473
  506.3 6.2 %collective-permute-start.11 = (bf16[1,128,1,256]{1,3,2,0:T(8,128)(2,1)S(1)}, bf16[1,128,1,256]{1,3,2,0:T(8,128)(2,1)S(1)}, u32[]{:S(2)}, u32[]{:S(2)}) collective-permute-start(bf16[1,128,1,256]{1,3,2,0:T(8,128)(2,1)S(1)} %select_convert_fusion.11), channel_id=1, source_target_pairs={{0,16},{16,0},{1,17},{17,1},{2,18},{18,2},{3,19},{19,3},{4,20},{20... | collective-permute-start | bytes 196616 | tf_op jit(solution)/shard_map/ppermute | solution.py:473
  511.4 77.7 %copy-start.22 = (f32[2048]{0:T(1024)S(1)}, f32[2048]{0:T(1024)}, u32[]{:S(2)}) copy-start(f32[2048]{0:T(1024)} %param.29) | copy-start | bytes 24580
  580.9 15.3 %all-to-all-start.3 = ((f32[128,1,16]{2,1,0:T(1,128)}), f32[128,1,16]{2,1,0:T(1,128)S(1)}, u32[]{:S(2)}, u32[]{:S(2)}) async-start(f32[128,1,16]{2,1,0:T(1,128)} %bitcast.58), calls=%async_computation.5 | async-start | bytes 131072 | tf_op jit(solution)/shard_map/all_to_all | solution.py:453
  (27 other events, 527.6 us)
Sparse Core Ops, SparseCore 0:
  13.7 112.4 all-gather.4
  128.4 75.2 all-gather.6
  206.4 69.4 all-gather.8
  295.6 84.7 reduce-scatter.2
  388.0 73.9 all-gather.10
  465.3 110.4 reduce-scatter.4

commit v16 on v15

--- a/solution.py
+++ b/solution.py
@@ -246,13 +246,20 @@
     positions = tensor_rank * row_count + jnp.arange(row_count, dtype=jnp.int32)
     live = positions[:, None] < seq_lengths[None, :]
     upstream = jnp.where(live[:, :, None], cotangent, jnp.zeros_like(cotangent))
+    core = group_rank % 2
+    half_width = model_width // 2
     front = jnp.concatenate(
-        [normed_low.reshape(row_count, seq_count * model_width), w_o.reshape(row_count, -1)], 1
+        [
+            normed_low.reshape(row_count, seq_count * model_width),
+            lax.dynamic_slice_in_dim(w_o.reshape(row_count, -1), core * half_width, half_width, 1),
+        ],
+        1,
     )
     front = lax.all_gather(front, "tensor", axis=0, tiled=True)
     wide = seq_count * model_width
     normed_full = front[:, :wide].reshape(seq_total, seq_count, model_width)
-    out_full = front[:, wide:].reshape(-1, model_width)
+    out_mine = front[:, wide:]
+    out_other = lax.ppermute(out_mine, "group", [(g, g ^ 1) for g in range(group_count)])
     upstream, front = lax.optimization_barrier((upstream, front))
     upstream_full = lax.all_gather(upstream, "tensor", axis=0, tiled=True)
     joint_weight = w_qkv.reshape(model_width, 3 * local_width)
@@ -290,7 +297,11 @@
         tiled=True,
     )
     attention = (
-        jnp.dot(own_rows, out_full, preferred_element_type=jnp.float32).reshape(
+        half_columns(
+            jnp.dot(own_rows, out_mine, preferred_element_type=jnp.float32),
+            jnp.dot(own_rows, out_other, preferred_element_type=jnp.float32),
+            core,
+        ).reshape(
             seq_count, row_count, model_width
         )
     )
@@ -351,10 +362,18 @@
     )
     piece = lax.all_gather(branch_low, "tensor", axis=0, tiled=True)
     weight_grad = jnp.einsum("rse,rsd->ed", attended, piece, preferred_element_type=jnp.float32)
-    heads_grad = jnp.dot(
-        branch_low.reshape(row_count * seq_count, model_width),
-        out_full.T,
-        preferred_element_type=jnp.float32,
+    branch_rows = branch_low.reshape(row_count * seq_count, model_width)
+    heads_grad = (
+        jnp.dot(
+            lax.dynamic_slice_in_dim(branch_rows, core * half_width, half_width, 1),
+            out_mine.T,
+            preferred_element_type=jnp.float32,
+        )
+        + jnp.dot(
+            lax.dynamic_slice_in_dim(branch_rows, (1 - core) * half_width, half_width, 1),
+            out_other.T,
+            preferred_element_type=jnp.float32,
+        )
     ).astype(jnp.bfloat16)
     attended_grad = lax.all_to_all(heads_grad, "tensor", 1, 0, tiled=True).reshape(
         seq_total, seq_count, local_width
@@ -460,6 +479,12 @@
     return tuple(parts)
 
 
+def half_columns(mine, other, core):
+    return jnp.where(
+        core == 0, jnp.concatenate([mine, other], 1), jnp.concatenate([other, mine], 1)
+    )
+
+
 def halving_steps(value, dim, steps, send_type=None):
     for axis, size, bit in steps:
         half = value.shape[dim] // 2

time: 616 us -> 597 us (0.969)
  waiting for transfers between devices: 295 us -> 274 us
  Pallas kernels: 24.6 us -> 41.5 us
  blocking collectives: 36 us -> 20.2 us
  starting transfers between devices: 42.6 us -> 35.2 us
  local copies, waits for them, and re-layouts: 47.2 us -> 53.7 us
    all_gather x1, waiting for transfers between devices: 110 us -> 88.1 us  [shards(): front = lax.all_gather(front, 'tensor', axis=0, tiled=True)]
    all_to_all x1 -> x0, blocking collectives: 15.6 us -> none  [shards(): lax.all_to_all(jnp.transpose(attended, (1, 0, 2)).reshape(seq_count * seq...]
    all_to_all x0 -> x1, waiting for transfers between devices: none -> 14.8 us  [shards(): lax.all_to_all(jnp.transpose(attended, (1, 0, 2)).reshape(seq_count * seq...]
    all_gather x1, waiting for transfers between devices: 29.1 us -> 14.6 us  [shards(): upstream_full = lax.all_gather(upstream, 'tensor', axis=0, tiled=True)]
    pallas_call x1, Pallas kernels: 11.4 us -> 24.6 us  [attention_backward(): pl.pallas_call(kernel, out_shape=tuple((jax.ShapeDtypeStruct((n, d), jnp....]
    ppermute x12, starting transfers between devices: 22.9 us -> 13 us  [halving_steps(): got = lax.ppermute(send, axis, [(i, i ^ bit) for i in range(size)])]
    dot_general x2 -> x4, matrix products: 11.3 us -> 13.8 us  [the longest x1 3.81 us: shards(): jnp.dot(lax.dynamic_slice_in_dim(branch_rows, core * half_width, half_wid...]
  transfers between devices with their start and end apart: 20 -> 22, of which waited for: 11 -> 12; matrix products, arithmetic and copies ran while one was open for 25% -> 27% of each run, Pallas kernels for 4% -> 7%
where the time goes in v16:
time: 597 us; the launch traced here: 586 us
  waiting for transfers between devices  274 us (46%)
  matrix products  91.1 us (15%)
  local copies, waits for them, and re-layouts  53.7 us (9%)
  other arithmetic  53.7 us (9%)
  Pallas kernels  41.5 us (7%)
  starting transfers between devices  35.2 us (6%)
  blocking collectives  20.2 us (3%)
  between operations  16.6 us (3%)
    all_gather x1, waiting for transfers between devices, shards(): front = lax.all_gather(front, 'tensor', axis=0, tiled=True)  88.1 us
    all_gather x1, waiting for transfers between devices, shards(): second_full = lax.all_gather(second_low, 'tensor', axis=0, tiled=True)  62.4 us
    reduce_scatter x1, waiting for transfers between devices, shards(): both = lax.psum_scatter(merged, 'tensor', scatter_dimension=0, tiled=True)  62.1 us
    ppermute x12, waiting for transfers between devices, halving_steps(): got = lax.ppermute(send, axis, [(i, i ^ bit) for i in range(size)])  26.4 us
    pallas_call x1, Pallas kernels, attention_backward(): pl.pallas_call(kernel, out_shape=tuple((jax.ShapeDtypeStruct((n, d), jnp....  24.6 us
    all_to_all x1, blocking collectives, shards(): lax.all_to_all(heads_grad, 'tensor', 1, 0, tiled=True)  20.2 us
    reshape x4, local copies, waits for them, and re-layouts, halving_sum(): value.reshape(shape[:dim] + (groups // 2, 2, dps * rest) + shape[dim + 1:])  19.4 us
    pallas_call x1, Pallas kernels, attention_forward(): pl.pallas_call(kernel, out_shape=(jax.ShapeDtypeStruct((n, d), jnp.bfloat...  16.9 us
  transfers between devices with their start and end apart: 22, of which 12 were waited for; matrix products, arithmetic and copies ran while one was open for 27% of the time, Pallas kernels for 7%

profile of v16, /device:TPU:96, one launch (start us, length us, event | category | flops | bytes accessed | tf_op | source)
XLA Modules:
  0.0 585.6 jit_solution(16155327791323908222)
XLA Ops:
  16.6 88.1 %all-gather.5.cloned.1.call-done = bf16[2048,3072]{1,0:T(8,128)(2,1)} async-done(((bf16[128,3072]{1,0:T(8,128)(2,1)}), bf16[2048,3072]{1,0:T(8,128)(2,1)}) %all-gather.5.cloned.1.call-update) | async-done | bytes 12582928 | tf_op jit(solution)/shard_map/all_gather | solution.py:258
  112.0 7.4 %fusion.37 = f32[2048,1,3,128]{3,0,2,1:T(8,128)S(1)} fusion(bf16[2048,3072]{1,0:T(8,128)(2,1)} %all-gather.5.cloned.1.call-done, bf16[2048,3,1,128]{0,3,1,2:T(8,128)(2,1)} %copy.38), kind=kOutput, calls=%fused_computation.39 | convolution fusion | flops 3221225472 | bytes 13107200 | tf_op jit(solution)/shard_map/dot_general | solution.py:266
  121.4 16.9 %shard_map.254 = (bf16[2048,128]{1,0:T(8,128)(2,1)}, f32[2048,1]{1,0:T(8,128)}) custom-call(s32[1]{0:T(128)} %dynamic_slice.22.len_ref, bf16[2048,128]{1,0:T(8,128)(2,1)} %get-tuple-element.121.q_ref, bf16[2048,128]{1,0:T(8,128)(2,1)} %fusion.66.k_ref, bf16[2048,128]{1,0:T(8,128)(2,1)} %get-tuple-element.120.v_ref), custom_call_target="tpu_custom_call" | custom-call | flops 1342177280 | bytes 2097152 | tf_op jit(solution)/shard_map/pallas_call | solution.py:85
  145.7 14.8 %all-to-all-done = bf16[16,128,128]{1,2,0:T(8,128)(2,1)S(1)} async-done(((bf16[16,128,128]{1,2,0:T(8,128)(2,1)}), bf16[16,128,128]{1,2,0:T(8,128)(2,1)S(1)}, u32[]{:S(2)}, u32[]{:S(2)}) %all-to-all-start) | async-done | bytes 524320 | tf_op jit(solution)/shard_map/all_to_all | solution.py:292
  168.4 14.6 %all-gather.7.cloned.1.call-done = bf16[2048,1,2048]{2,0,1:T(8,128)(2,1)} async-done(((bf16[128,1,2048]{2,0,1:T(8,128)(2,1)}), bf16[2048,1,2048]{2,0,1:T(8,128)(2,1)}) %all-gather.7.cloned.1.call-update) | async-done | bytes 8388624 | tf_op jit(solution)/shard_map/all_gather | solution.py:264
  183.2 10.5 %fusion.31 = f32[2048,1,512]{2,0,1:T(8,128)} fusion(bf16[512,2048]{1,0:T(8,128)(2,1)} %param.28, bf16[2048,1,2048]{2,0,1:T(8,128)(2,1)} %all-gather.7.cloned.1.call-done), kind=kOutput, calls=%fused_computation.36 | convolution fusion | flops 4294967296 | bytes 14680064 | tf_op jit(solution)/shard_map/rsd,fd->rsf/dot_general | solution.py:310
  193.7 62.4 %all-gather.9.cloned.1.call-done = bf16[2048,1,2048]{2,0,1:T(8,128)(2,1)} async-done(((bf16[128,1,2048]{2,0,1:T(8,128)(2,1)}), bf16[2048,1,2048]{2,0,1:T(8,128)(2,1)}) %all-gather.9.cloned.1.call-update) | async-done | bytes 8388624 | tf_op jit(solution)/shard_map/all_gather | solution.py:313
  256.1 7.0 %fusion.6 = f32[2048,512]{1,0:T(8,128)S(1)} fusion(bf16[2048,512]{1,0:T(8,128)(2,1)S(1)} %copy-done, bf16[2048,1,2048]{2,0,1:T(8,128)(2,1)} %all-gather.9.cloned.1.call-done), kind=kOutput, calls=%fused_computation.7 | convolution fusion | flops 4294967296 | bytes 14680064 | tf_op jit(solution)/shard_map/dot_general | solution.py:316
  268.8 6.9 %convert_bitcast_fusion.1 = bf16[2048,1,2048]{2,0,1:T(8,128)(2,1)} fusion(bf16[2048,512]{1,0:T(8,128)(2,1)S(1)} %get-tuple-element.110, bf16[2048,512]{1,0:T(8,128)(2,1)S(1)} %copy-done), kind=kOutput, calls=%fused_computation.14 | convolution fusion | flops 4299161600 | bytes 12582912 | tf_op jit(solution)/shard_map/rsf,df->rsd/dot_general | solution.py:337
  278.6 7.1 %fusion.28 = f32[2048,512]{1,0:T(8,128)S(1)} fusion(bf16[2048,512]{1,0:T(8,128)(2,1)S(1)} %copy-done.18, bf16[2048,1,2048]{2,0,1:T(8,128)(2,1)} %all-gather.9.cloned.1.call-done, f32[]{:T(128)S(6)} %div.71), kind=kOutput, calls=%fused_computation.35 | convolution fusion | flops 4296015872 | bytes 14680068 | tf_op jit(solution)/shard_map/rd,rf->df/dot_general | solution.py:329
  288.3 10.0 %fusion.25 = f32[512,2048]{1,0:T(8,128)} fusion(bf16[2048,1,2048]{2,0,1:T(8,128)(2,1)} %all-gather.7.cloned.1.call-done, f32[]{:T(128)S(6)} %div.71, f32[2048,512]{1,0:T(8,128)S(1)} %copy-done.12, f32[512]{0:T(512)S(1)} %copy-done.25), kind=kOutput, calls=%fused_computation.34 | convolution fusion | flops 4306501632 | bytes 16779268 | tf_op jit(solution)/shard_map/rsf,rsd->fd/dot_general | solution.py:325
  298.3 6.7 %reshape.504 = f32[512,2,2,512]{3,2,1,0:T(2,128)} reshape(f32[512,2048]{1,0:T(8,128)} %fusion.25) | data formatting | bytes 8388608 | tf_op jit(solution)/shard_map/reshape | solution.py:508
  305.0 7.3 %copy.40 = f32[512,2,2,512]{0,3,1,2:T(8,128)} copy(f32[512,2,2,512]{3,2,1,0:T(2,128)} %reshape.504) | data formatting | bytes 8388608 | tf_op jit(solution)/shard_map/reshape | solution.py:508
  326.8 10.6 %collective-permute-done.2 = bf16[2,256,512]{2,1,0:T(8,128)(2,1)S(1)} collective-permute-done((bf16[2,256,512]{2,1,0:T(8,128)(2,1)S(1)}, bf16[2,256,512]{2,1,0:T(8,128)(2,1)S(1)}, u32[]{:S(2)}, u32[]{:S(2)}) %collective-permute-start.2) | collective-permute-done | bytes 524320 | tf_op jit(solution)/shard_map/ppermute | solution.py:498
  339.1 9.5 %collective-permute-done.5 = bf16[512,2,256]{0,2,1:T(8,128)(2,1)S(1)} collective-permute-done((bf16[512,2,256]{0,2,1:T(8,128)(2,1)S(1)}, bf16[512,2,256]{0,2,1:T(8,128)(2,1)S(1)}, u32[]{:S(2)}, u32[]{:S(2)}) %collective-permute-start.5) | collective-permute-done | bytes 524320 | tf_op jit(solution)/shard_map/ppermute | solution.py:498
  355.0 6.9 %dynamic_update_slice.12 = bf16[2048,1,4096]{2,0,1:T(8,128)(2,1)} pad(bf16[2048,1,2048]{2,0,1:T(8,128)(2,1)S(1)} %convert_bitcast_fusion, bf16[]{:T(256)} %constant.147.clone.1), padding=0_0x0_0x2048_0 | pad | bytes 25165826 | tf_op jit(solution)/shard_map/dynamic_update_slice | solution.py:346
  376.3 20.2 %all_to_all.53 = bf16[128,16,128]{2,0,1:T(8,128)(2,1)} all-to-all(bf16[128,16,128]{2,0,1:T(8,128)(2,1)S(1)} %bitcast.172), channel_id=1, replica_groups=mesh['group'=4,'dp'=2,'tensor'=16] {'tensor'}, dimensions={1} | all-to-all | bytes 1048576 | tf_op jit(solution)/shard_map/all_to_all | solution.py:378
  396.5 24.6 %shard_map.255 = (bf16[2048,128]{1,0:T(8,128)(2,1)}, bf16[2048,128]{1,0:T(8,128)(2,1)}, bf16[2048,128]{1,0:T(8,128)(2,1)}) custom-call(s32[1]{0:T(128)} %dynamic_slice.22.len_ref, bf16[2048,128]{1,0:T(8,128)(2,1)} %get-tuple-element.121.q_ref, bf16[2048,128]{1,0:T(8,128)(2,1)} %fusion.66.k_ref, bf16[2048,128]{1,0:T(8,128)(2,1)} %get-tuple-element.120.v_ref, ...), custom_call_target="tpu_custom_call" | custom-call | flops 2684354560 | bytes 4194304 | tf_op jit(solution)/shard_map/pallas_call | solution.py:185
  424.5 9.7 %bitcast_dynamic-update-slice_fusion = bf16[2048,1,4096]{2,0,1:T(8,128)(2,1)} fusion(bf16[2048,1,4096]{2,0,1:T(8,128)(2,1)} %dynamic_update_slice.12, bf16[2048,384]{0,1:T(8,128)(2,1)} %bitcast.173, bf16[2048,384]{0,1:T(8,128)(2,1)} %bitcast.166), kind=kOutput, calls=%fused_computation.2 | convolution fusion | flops 3225419776 | bytes 11534336 | tf_op jit(solution)/shard_map/rsc,dc->rsd/dot_general | solution.py:403
  435.0 7.6 %fusion.34 = f32[2048,384]{1,0:T(8,128)S(1)} fusion(bf16[2048,384]{0,1:T(8,128)(2,1)} %bitcast.174, bf16[2048,3072]{1,0:T(8,128)(2,1)} %all-gather.5.cloned.1.call-done, f32[]{:T(128)S(6)} %div.71), kind=kOutput, calls=%fused_computation.38 | convolution fusion | flops 3222011904 | bytes 13107204 | tf_op jit(solution)/shard_map/rd,rc->dc/dot_general | solution.py:397
  446.5 8.1 %all-to-all-start.2 = ((f32[128,1,176]{2,1,0:T(1,128)}), f32[128,1,176]{2,1,0:T(1,128)S(1)}, u32[]{:S(2)}, u32[]{:S(2)}) async-start(f32[128,1,176]{2,1,0:T(1,128)} %copy.44), calls=%async_computation.4 | async-start | bytes 262144 | tf_op jit(solution)/shard_map/all_to_all | solution.py:472
  468.0 5.8 fusion.40
  495.1 62.1 %reduce-scatter.5.cloned.1.call-done = bf16[128,1,4096]{2,0,1:T(8,128)(2,1)} async-done(((bf16[2048,1,4096]{2,0,1:T(8,128)(2,1)}), bf16[128,1,4096]{2,0,1:T(8,128)(2,1)}) %reduce-scatter.5.cloned.1.call-update) | async-done | bytes 1048592 | tf_op jit(solution)/shard_map/reduce_scatter | solution.py:411
  562.5 8.2 %all-to-all-start.3 = ((f32[128,1,16]{2,1,0:T(1,128)}), f32[128,1,16]{2,1,0:T(1,128)S(1)}, u32[]{:S(2)}, u32[]{:S(2)}) async-start(f32[128,1,16]{2,1,0:T(1,128)} %bitcast.61), calls=%async_computation.5 | async-start | bytes 131072 | tf_op jit(solution)/shard_map/all_to_all | solution.py:472
  (212 shorter events, 136.1 us)
Async XLA Ops:
  7.2 248.9 %copy-start = (bf16[2048,512]{1,0:T(8,128)(2,1)S(1)}, bf16[2048,512]{1,0:T(8,128)(2,1)}, u32[]{:S(2)}) copy-start(bf16[2048,512]{1,0:T(8,128)(2,1)} %param.26) | copy-start | bytes 6291460
  7.2 97.5 %all-gather.5.cloned.1.call-start = ((), (), s32[]{:S(2)}) async-start(), calls=%async_computation.6 | async-start | bytes 13369344 | tf_op jit(solution)/shard_map/all_gather | solution.py:258
  9.9 99.5 %copy-start.29 = (f32[128]{0:T(128)}, f32[128]{0:T(128)S(1)}, u32[]{:S(2)}) copy-start(f32[128]{0:T(128)S(1)} %fusion.56) | copy-start | bytes 1540
  13.4 169.6 %all-gather.7.cloned.1.call-start = ((), (), s32[]{:S(2)}) async-start(), calls=%async_computation.7 | async-start | bytes 8912896 | tf_op jit(solution)/shard_map/all_gather | solution.py:264
  109.4 54.3 %collective-permute-start = (bf16[2048,1024]{1,0:T(8,128)(2,1)}, bf16[2048,1024]{1,0:T(8,128)(2,1)}, u32[]{:S(2)}, u32[]{:S(2)}) collective-permute-start(bf16[2048,1024]{1,0:T(8,128)(2,1)} %slice.185), channel_id=1, source_target_pairs={{0,32},{32,0},{64,96},{96,64},{1,33},{33,1},{65,97},{97,65},{2,34}... | collective-permute-start | bytes 12582920 | tf_op jit(solution)/shard_map/ppermute | solution.py:262
  140.4 20.1 %all-to-all-start = ((bf16[16,128,128]{1,2,0:T(8,128)(2,1)}), bf16[16,128,128]{1,2,0:T(8,128)(2,1)S(1)}, u32[]{:S(2)}, u32[]{:S(2)}) async-start(bf16[16,128,128]{1,2,0:T(8,128)(2,1)} %copy.39), calls=%async_computation | async-start | bytes 1048576 | tf_op jit(solution)/shard_map/all_to_all | solution.py:292
  145.6 110.5 %all-gather.9.cloned.1.call-start = ((), (), s32[]{:S(2)}) async-start(), calls=%async_computation.8 | async-start | bytes 8912896 | tf_op jit(solution)/shard_map/all_gather | solution.py:313
  183.0 180.8 %reduce-scatter.3.cloned.1.call-start = ((), (), s32[]{:S(2)}) async-start(), calls=%async_computation.9 | async-start | bytes 8912896 | tf_op jit(solution)/shard_map/reduce_scatter | solution.py:340
  275.8 192.2 %all-gather.11.cloned.1.call-start = ((), (), s32[]{:S(2)}) async-start(), calls=%async_computation.11 | async-start | bytes 8912896 | tf_op jit(solution)/shard_map/all_gather | solution.py:363
  287.8 31.3 %collective-permute-start.1 = (bf16[4,256,512]{2,1,0:T(8,128)(2,1)S(1)}, bf16[4,256,512]{2,1,0:T(8,128)(2,1)S(1)}, u32[]{:S(2)}, u32[]{:S(2)}) collective-permute-start(bf16[4,256,512]{2,1,0:T(8,128)(2,1)S(1)} %bitcast.175), channel_id=1, source_target_pairs={{0,32},{32,0},{64,96},{96,64},{1,33},{33,1},{65,97},{97,65},{2,34}... | collective-permute-start | bytes 3145736 | tf_op jit(solution)/shard_map/ppermute | solution.py:498
  315.9 7.5 %collective-permute-start.4 = (bf16[512,4,256]{0,2,1:T(8,128)(2,1)}, bf16[512,4,256]{0,2,1:T(8,128)(2,1)}, u32[]{:S(2)}, u32[]{:S(2)}) collective-permute-start(bf16[512,4,256]{0,2,1:T(8,128)(2,1)} %select_convert_fusion), channel_id=1, source_target_pairs={{0,32},{32,0},{64,96},{96,64},{1,33},{33,1},{65,97},{97,65},{2,34}... | collective-permute-start | bytes 3145736 | tf_op jit(solution)/shard_map/ppermute | solution.py:498
  322.6 14.8 %collective-permute-start.2 = (bf16[2,256,512]{2,1,0:T(8,128)(2,1)S(1)}, bf16[2,256,512]{2,1,0:T(8,128)(2,1)S(1)}, u32[]{:S(2)}, u32[]{:S(2)}) collective-permute-start(bf16[2,256,512]{2,1,0:T(8,128)(2,1)S(1)} %select_convert_fusion.4), channel_id=1, source_target_pairs={{0,64},{32,96},{64,0},{96,32},{1,65},{33,97},{65,1},{97,33},{2,66}... | collective-permute-start | bytes 1572872 | tf_op jit(solution)/shard_map/ppermute | solution.py:498
  325.5 23.2 %collective-permute-start.5 = (bf16[512,2,256]{0,2,1:T(8,128)(2,1)S(1)}, bf16[512,2,256]{0,2,1:T(8,128)(2,1)S(1)}, u32[]{:S(2)}, u32[]{:S(2)}) collective-permute-start(bf16[512,2,256]{0,2,1:T(8,128)(2,1)S(1)} %select_convert_fusion.3), channel_id=1, source_target_pairs={{0,64},{32,96},{64,0},{96,32},{1,65},{33,97},{65,1},{97,33},{2,66}... | collective-permute-start | bytes 1572872 | tf_op jit(solution)/shard_map/ppermute | solution.py:498
  337.8 24.2 %collective-permute-start.3 = (bf16[1,256,512]{2,1,0:T(8,128)(2,1)S(1)}, bf16[1,256,512]{2,1,0:T(8,128)(2,1)S(1)}, u32[]{:S(2)}, u32[]{:S(2)}) collective-permute-start(bf16[1,256,512]{2,1,0:T(8,128)(2,1)S(1)} %select_convert_fusion.8), channel_id=1, source_target_pairs={{0,16},{16,0},{1,17},{17,1},{2,18},{18,2},{3,19},{19,3},{4,20},{20... | collective-permute-start | bytes 786440 | tf_op jit(solution)/shard_map/ppermute | solution.py:498
  349.0 13.9 %collective-permute-start.6 = (bf16[512,1,256]{0,2,1:T(8,128)(2,1)S(1)}, bf16[512,1,256]{0,2,1:T(8,128)(2,1)S(1)}, u32[]{:S(2)}, u32[]{:S(2)}) collective-permute-start(bf16[512,1,256]{0,2,1:T(8,128)(2,1)S(1)} %select_convert_fusion.7), channel_id=1, source_target_pairs={{0,16},{16,0},{1,17},{17,1},{2,18},{18,2},{3,19},{19,3},{4,20},{20... | collective-permute-start | bytes 786440 | tf_op jit(solution)/shard_map/ppermute | solution.py:498
  368.3 188.9 %reduce-scatter.5.cloned.1.call-start = ((), (), s32[]{:S(2)}) async-start(), calls=%async_computation.10 | async-start | bytes 17825792 | tf_op jit(solution)/shard_map/reduce_scatter | solution.py:411
  443.7 20.9 %collective-permute-start.7 = (bf16[4,256,384]{2,1,0:T(8,128)(2,1)}, bf16[4,256,384]{2,1,0:T(8,128)(2,1)}, u32[]{:S(2)}, u32[]{:S(2)}) collective-permute-start(bf16[4,256,384]{2,1,0:T(8,128)(2,1)} %bitcast.52), channel_id=1, source_target_pairs={{0,32},{32,0},{64,96},{96,64},{1,33},{33,1},{65,97},{97,65},{2,34}... | collective-permute-start | bytes 2359304 | tf_op jit(solution)/shard_map/ppermute | solution.py:498
  446.5 16.8 %all-to-all-start.2 = ((f32[128,1,176]{2,1,0:T(1,128)}), f32[128,1,176]{2,1,0:T(1,128)S(1)}, u32[]{:S(2)}, u32[]{:S(2)}) async-start(f32[128,1,176]{2,1,0:T(1,128)} %copy.44), calls=%async_computation.4 | async-start | bytes 262144 | tf_op jit(solution)/shard_map/all_to_all | solution.py:472
  466.6 14.1 %collective-permute-start.8 = (bf16[2,256,384]{2,1,0:T(8,128)(2,1)S(1)}, bf16[2,256,384]{2,1,0:T(8,128)(2,1)}, u32[]{:S(2)}, u32[]{:S(2)}) collective-permute-start(bf16[2,256,384]{2,1,0:T(8,128)(2,1)S(1)} %select_convert_fusion.5), channel_id=1, source_target_pairs={{0,64},{32,96},{64,0},{96,32},{1,65},{33,97},{65,1},{97,33},{2,66}... | collective-permute-start | bytes 1179656 | tf_op jit(solution)/shard_map/ppermute | solution.py:498
  480.6 1.6 collective-permute-start.10
  482.3 6.4 %collective-permute-start.11 = (bf16[1,128,2,256]{1,3,2,0:T(8,128)(2,1)S(1)}, bf16[1,128,2,256]{1,3,2,0:T(8,128)(2,1)S(1)}, u32[]{:S(2)}, u32[]{:S(2)}) collective-permute-start(bf16[1,128,2,256]{1,3,2,0:T(8,128)(2,1)S(1)} %select_convert_fusion.10), channel_id=1, source_target_pairs={{0,64},{32,96},{64,0},{96,32},{1,65},{33,97},{65,1},{97,33},{2,66}... | collective-permute-start | bytes 393224 | tf_op jit(solution)/shard_map/ppermute | solution.py:498
  483.2 10.7 %collective-permute-start.9 = (bf16[1,256,384]{2,1,0:T(8,128)(2,1)S(1)}, bf16[1,256,384]{2,1,0:T(8,128)(2,1)S(1)}, u32[]{:S(2)}, u32[]{:S(2)}) collective-permute-start(bf16[1,256,384]{2,1,0:T(8,128)(2,1)S(1)} %select_convert_fusion.9), channel_id=1, source_target_pairs={{0,16},{16,0},{1,17},{17,1},{2,18},{18,2},{3,19},{19,3},{4,20},{20... | collective-permute-start | bytes 589832 | tf_op jit(solution)/shard_map/ppermute | solution.py:498
  488.8 6.3 %collective-permute-start.12 = (bf16[1,128,1,256]{1,3,2,0:T(8,128)(2,1)S(1)}, bf16[1,128,1,256]{1,3,2,0:T(8,128)(2,1)S(1)}, u32[]{:S(2)}, u32[]{:S(2)}) collective-permute-start(bf16[1,128,1,256]{1,3,2,0:T(8,128)(2,1)S(1)} %select_convert_fusion.11), channel_id=1, source_target_pairs={{0,16},{16,0},{1,17},{17,1},{2,18},{18,2},{3,19},{19,3},{4,20},{20... | collective-permute-start | bytes 196616 | tf_op jit(solution)/shard_map/ppermute | solution.py:498
  562.5 15.4 %all-to-all-start.3 = ((f32[128,1,16]{2,1,0:T(1,128)}), f32[128,1,16]{2,1,0:T(1,128)S(1)}, u32[]{:S(2)}, u32[]{:S(2)}) async-start(f32[128,1,16]{2,1,0:T(1,128)} %bitcast.61), calls=%async_computation.5 | async-start | bytes 131072 | tf_op jit(solution)/shard_map/all_to_all | solution.py:472
  (30 other events, 563.9 us)
Sparse Core Ops, SparseCore 0:
  13.5 91.1 all-gather.4
  106.8 76.0 all-gather.6
  185.7 70.3 all-gather.8
  275.9 84.6 reduce-scatter.2
  368.4 74.2 all-gather.10
  446.0 111.2 reduce-scatter.4

commit v17 on v16

--- a/solution.py
+++ b/solution.py
@@ -505,11 +505,9 @@
     groups = lax.axis_size("group")
     dps = lax.axis_size("dp")
     rest = shape[dim] // (groups * dps)
-    value = value.reshape(shape[:dim] + (groups // 2, 2, dps * rest) + shape[dim + 1 :])
-    value = jnp.swapaxes(value, dim, dim + 1)
     value = value.reshape(shape[:dim] + (groups * dps, rest) + shape[dim + 1 :])
     value = halving_steps(
-        value, dim, [("group", groups, 1), ("group", groups, 2), ("dp", dps, 1)], jnp.bfloat16
+        value, dim, [("group", groups, 2), ("group", groups, 1), ("dp", dps, 1)], jnp.bfloat16
     )
     return value.reshape(shape[:dim] + (shape[dim] // (groups * dps),) + shape[dim + 1 :])
 

time: 597 us -> 600 us (level)
  waiting for transfers between devices: 274 us -> 310 us
  Pallas kernels: 41.5 us -> 16.8 us
  local copies, waits for them, and re-layouts: 53.7 us -> 32 us
  starting transfers between devices: 35.2 us -> 51.3 us
    ppermute x12, waiting for transfers between devices: 26.4 us -> 49.3 us  [halving_steps(): got = lax.ppermute(send, axis, [(i, i ^ bit) for i in range(size)])]
    reshape x4 -> x0, local copies, waits for them, and re-layouts: 19.4 us -> none  [halving_sum(): value.reshape(shape[:dim] + (groups // 2, 2, dps * rest) + shape[dim + 1:])]
    pallas_call x1, Pallas kernels: 24.6 us -> 7.42 us  [attention_backward(): pl.pallas_call(kernel, out_shape=tuple((jax.ShapeDtypeStruct((n, d), jnp....]
    ppermute x12, starting transfers between devices: 13 us -> 29.1 us  [halving_steps(): got = lax.ppermute(send, axis, [(i, i ^ bit) for i in range(size)])]
    all_gather x1, waiting for transfers between devices: 14.6 us -> 22.3 us  [shards(): upstream_full = lax.all_gather(upstream, 'tensor', axis=0, tiled=True)]
    pallas_call x1, Pallas kernels: 16.9 us -> 9.37 us  [attention_forward(): pl.pallas_call(kernel, out_shape=(jax.ShapeDtypeStruct((n, d), jnp.bfloat...]
  transfers between devices with their start and end apart: 22 -> 22, of which waited for: 12 -> 12; matrix products, arithmetic and copies ran while one was open for 27% -> 23% of each run, Pallas kernels for 7% -> 3%
where the time goes in v17:
time: 600 us; the launch traced here: 588 us
  waiting for transfers between devices  310 us (52%)
  matrix products  88.7 us (15%)
  other arithmetic  52.5 us (9%)
  starting transfers between devices  51.3 us (9%)
  local copies, waits for them, and re-layouts  32 us (5%)
  blocking collectives  20.9 us (3%)
  Pallas kernels  16.8 us (3%)
  between operations  16.6 us (3%)
    all_gather x1, waiting for transfers between devices, shards(): front = lax.all_gather(front, 'tensor', axis=0, tiled=True)  88.1 us
    reduce_scatter x1, waiting for transfers between devices, shards(): both = lax.psum_scatter(merged, 'tensor', scatter_dimension=0, tiled=True)  64.4 us
    all_gather x1, waiting for transfers between devices, shards(): second_full = lax.all_gather(second_low, 'tensor', axis=0, tiled=True)  62.4 us
    ppermute x12, waiting for transfers between devices, halving_steps(): got = lax.ppermute(send, axis, [(i, i ^ bit) for i in range(size)])  49.3 us
    ppermute x12, starting transfers between devices, halving_steps(): got = lax.ppermute(send, axis, [(i, i ^ bit) for i in range(size)])  29.1 us
    all_gather x1, waiting for transfers between devices, shards(): upstream_full = lax.all_gather(upstream, 'tensor', axis=0, tiled=True)  22.3 us
    all_to_all x1, blocking collectives, shards(): lax.all_to_all(heads_grad, 'tensor', 1, 0, tiled=True)  20.9 us
    all_to_all x2, starting transfers between devices, reduce_vectors(): packed = lax.all_to_all(packed, ('group', 'dp', 'tensor'), 0, 0, tiled=True)  16.1 us
  transfers between devices with their start and end apart: 22, of which 12 were waited for; matrix products, arithmetic and copies ran while one was open for 23% of the time, Pallas kernels for 3%

profile of v17, /device:TPU:96, one launch (start us, length us, event | category | flops | bytes accessed | tf_op | source)
XLA Modules:
  0.0 588.4 jit_solution(797999224754808945)
XLA Ops:
  16.6 88.1 %all-gather.5.cloned.1.call-done = bf16[2048,3072]{1,0:T(8,128)(2,1)} async-done(((bf16[128,3072]{1,0:T(8,128)(2,1)}), bf16[2048,3072]{1,0:T(8,128)(2,1)}) %all-gather.5.cloned.1.call-update) | async-done | bytes 12582928 | tf_op jit(solution)/shard_map/all_gather | solution.py:258
  112.0 7.4 %fusion.37 = f32[2048,1,3,128]{3,0,2,1:T(8,128)S(1)} fusion(bf16[2048,3072]{1,0:T(8,128)(2,1)} %all-gather.5.cloned.1.call-done, bf16[2048,3,1,128]{0,3,1,2:T(8,128)(2,1)} %copy.42), kind=kOutput, calls=%fused_computation.39 | convolution fusion | flops 3221225472 | bytes 13107200 | tf_op jit(solution)/shard_map/dot_general | solution.py:266
  121.4 9.4 %shard_map.254 = (bf16[2048,128]{1,0:T(8,128)(2,1)}, f32[2048,1]{1,0:T(8,128)}) custom-call(s32[1]{0:T(128)} %dynamic_slice.22.len_ref, bf16[2048,128]{1,0:T(8,128)(2,1)} %get-tuple-element.95.q_ref, bf16[2048,128]{1,0:T(8,128)(2,1)} %fusion.66.k_ref, bf16[2048,128]{1,0:T(8,128)(2,1)} %get-tuple-element.94.v_ref), custom_call_target="tpu_custom_call" | custom-call | flops 1342177280 | bytes 2097152 | tf_op jit(solution)/shard_map/pallas_call | solution.py:85
  138.1 14.7 %all-to-all-done = bf16[16,128,128]{1,2,0:T(8,128)(2,1)S(1)} async-done(((bf16[16,128,128]{1,2,0:T(8,128)(2,1)}), bf16[16,128,128]{1,2,0:T(8,128)(2,1)S(1)}, u32[]{:S(2)}, u32[]{:S(2)}) %all-to-all-start) | async-done | bytes 524320 | tf_op jit(solution)/shard_map/all_to_all | solution.py:292
  160.4 22.3 %all-gather.7.cloned.1.call-done = bf16[2048,1,2048]{2,0,1:T(8,128)(2,1)} async-done(((bf16[128,1,2048]{2,0,1:T(8,128)(2,1)}), bf16[2048,1,2048]{2,0,1:T(8,128)(2,1)}) %all-gather.7.cloned.1.call-update) | async-done | bytes 8388624 | tf_op jit(solution)/shard_map/all_gather | solution.py:264
  183.0 10.5 %fusion.31 = f32[2048,1,512]{2,0,1:T(8,128)} fusion(bf16[512,2048]{1,0:T(8,128)(2,1)} %param.28, bf16[2048,1,2048]{2,0,1:T(8,128)(2,1)} %all-gather.7.cloned.1.call-done), kind=kOutput, calls=%fused_computation.36 | convolution fusion | flops 4294967296 | bytes 14680064 | tf_op jit(solution)/shard_map/rsd,fd->rsf/dot_general | solution.py:310
  193.5 62.4 %all-gather.9.cloned.1.call-done = bf16[2048,1,2048]{2,0,1:T(8,128)(2,1)} async-done(((bf16[128,1,2048]{2,0,1:T(8,128)(2,1)}), bf16[2048,1,2048]{2,0,1:T(8,128)(2,1)}) %all-gather.9.cloned.1.call-update) | async-done | bytes 8388624 | tf_op jit(solution)/shard_map/all_gather | solution.py:313
  255.9 7.0 %fusion.6 = f32[2048,512]{1,0:T(8,128)S(1)} fusion(bf16[2048,512]{1,0:T(8,128)(2,1)S(1)} %copy-done, bf16[2048,1,2048]{2,0,1:T(8,128)(2,1)} %all-gather.9.cloned.1.call-done), kind=kOutput, calls=%fused_computation.7 | convolution fusion | flops 4294967296 | bytes 14680064 | tf_op jit(solution)/shard_map/dot_general | solution.py:316
  268.6 7.0 %convert_bitcast_fusion.1 = bf16[2048,1,2048]{2,0,1:T(8,128)(2,1)} fusion(bf16[2048,512]{1,0:T(8,128)(2,1)S(1)} %get-tuple-element.82, bf16[2048,512]{1,0:T(8,128)(2,1)S(1)} %copy-done), kind=kOutput, calls=%fused_computation.14 | convolution fusion | flops 4299161600 | bytes 12582912 | tf_op jit(solution)/shard_map/rsf,df->rsd/dot_general | solution.py:337
  278.9 8.5 %fusion.25 = f32[512,2048]{1,0:T(8,128)S(1)} fusion(bf16[2048,1,2048]{2,0,1:T(8,128)(2,1)} %all-gather.7.cloned.1.call-done, f32[]{:T(128)S(6)} %div.71, f32[2048,512]{1,0:T(8,128)} %copy-done.10, f32[512]{0:T(512)S(1)} %copy-done.22), kind=kOutput, calls=%fused_computation.34 | convolution fusion | flops 4306501632 | bytes 16779268 | tf_op jit(solution)/shard_map/rsf,rsd->fd/dot_general | solution.py:325
  289.4 7.1 %fusion.28 = f32[2048,512]{1,0:T(8,128)S(1)} fusion(bf16[2048,512]{1,0:T(8,128)(2,1)S(1)} %copy-done.16, bf16[2048,1,2048]{2,0,1:T(8,128)(2,1)} %all-gather.9.cloned.1.call-done, f32[]{:T(128)S(6)} %div.71), kind=kOutput, calls=%fused_computation.35 | convolution fusion | flops 4296015872 | bytes 14680068 | tf_op jit(solution)/shard_map/rd,rf->df/dot_general | solution.py:329
  306.3 17.9 %collective-permute-done.1 = bf16[4,256,512]{2,1,0:T(8,128)(2,1)} collective-permute-done((bf16[4,256,512]{2,1,0:T(8,128)(2,1)}, bf16[4,256,512]{2,1,0:T(8,128)(2,1)}, u32[]{:S(2)}, u32[]{:S(2)}) %collective-permute-start.1) | collective-permute-done | bytes 1048608 | tf_op jit(solution)/shard_map/ppermute | solution.py:498
  326.1 19.4 %collective-permute-done.4 = bf16[512,4,256]{2,0,1:T(8,128)(2,1)} collective-permute-done((bf16[512,4,256]{2,0,1:T(8,128)(2,1)}, bf16[512,4,256]{2,0,1:T(8,128)(2,1)}, u32[]{:S(2)}, u32[]{:S(2)}) %collective-permute-start.4) | collective-permute-done | bytes 1048608 | tf_op jit(solution)/shard_map/ppermute | solution.py:498
  356.9 6.9 %dynamic_update_slice.12 = bf16[2048,1,4096]{2,0,1:T(8,128)(2,1)} pad(bf16[2048,1,2048]{2,0,1:T(8,128)(2,1)S(1)} %convert_bitcast_fusion, bf16[]{:T(256)} %constant.147.clone.1), padding=0_0x0_0x2048_0 | pad | bytes 25165826 | tf_op jit(solution)/shard_map/dynamic_update_slice | solution.py:346
  377.9 20.9 %all_to_all.53 = bf16[128,16,128]{2,0,1:T(8,128)(2,1)} all-to-all(bf16[128,16,128]{2,0,1:T(8,128)(2,1)S(1)} %bitcast.161), channel_id=1, replica_groups=mesh['group'=4,'dp'=2,'tensor'=16] {'tensor'}, dimensions={1} | all-to-all | bytes 1048576 | tf_op jit(solution)/shard_map/all_to_all | solution.py:378
  398.7 7.4 %shard_map.255 = (bf16[2048,128]{1,0:T(8,128)(2,1)}, bf16[2048,128]{1,0:T(8,128)(2,1)}, bf16[2048,128]{1,0:T(8,128)(2,1)}) custom-call(s32[1]{0:T(128)} %dynamic_slice.22.len_ref, bf16[2048,128]{1,0:T(8,128)(2,1)} %get-tuple-element.95.q_ref, bf16[2048,128]{1,0:T(8,128)(2,1)} %fusion.66.k_ref, bf16[2048,128]{1,0:T(8,128)(2,1)} %get-tuple-element.94.v_ref, ...), custom_call_target="tpu_custom_call" | custom-call | flops 2684354560 | bytes 4194304 | tf_op jit(solution)/shard_map/pallas_call | solution.py:185
  409.6 9.7 %bitcast_dynamic-update-slice_fusion = bf16[2048,1,4096]{2,0,1:T(8,128)(2,1)} fusion(bf16[2048,1,4096]{2,0,1:T(8,128)(2,1)} %dynamic_update_slice.12, bf16[2048,384]{0,1:T(8,128)(2,1)} %bitcast.162, bf16[2048,384]{0,1:T(8,128)(2,1)} %bitcast.152), kind=kOutput, calls=%fused_computation.2 | convolution fusion | flops 3225419776 | bytes 11534336 | tf_op jit(solution)/shard_map/rsc,dc->rsd/dot_general | solution.py:403
  420.1 7.7 %fusion.34 = f32[2048,384]{1,0:T(8,128)S(1)} fusion(bf16[2048,384]{0,1:T(8,128)(2,1)} %bitcast.163, bf16[2048,3072]{1,0:T(8,128)(2,1)} %all-gather.5.cloned.1.call-done, f32[]{:T(128)S(6)} %div.71), kind=kOutput, calls=%fused_computation.38 | convolution fusion | flops 3222011904 | bytes 13107204 | tf_op jit(solution)/shard_map/rd,rc->dc/dot_general | solution.py:397
  429.0 18.1 %collective-permute-start.7 = (bf16[4,256,384]{2,1,0:T(8,128)(2,1)}, bf16[4,256,384]{2,1,0:T(8,128)(2,1)}, u32[]{:S(2)}, u32[]{:S(2)}) collective-permute-start(bf16[4,256,384]{2,1,0:T(8,128)(2,1)} %bitcast.43), channel_id=1, source_target_pairs={{0,64},{32,96},{64,0},{96,32},{1,65},{33,97},{65,1},{97,33},{2,66}... | collective-permute-start | bytes 2359304 | tf_op jit(solution)/shard_map/ppermute | solution.py:498
  449.4 7.9 %all-to-all-start.2 = ((f32[128,1,176]{2,1,0:T(1,128)}), f32[128,1,176]{2,1,0:T(1,128)S(1)}, u32[]{:S(2)}, u32[]{:S(2)}) async-start(f32[128,1,176]{2,1,0:T(1,128)} %copy.50), calls=%async_computation.4 | async-start | bytes 262144 | tf_op jit(solution)/shard_map/all_to_all | solution.py:472
  477.4 6.2 %collective-permute-done.10 = bf16[1,128,4,256]{3,1,2,0:T(8,128)(2,1)S(1)} collective-permute-done((bf16[1,128,4,256]{3,1,2,0:T(8,128)(2,1)S(1)}, bf16[1,128,4,256]{3,1,2,0:T(8,128)(2,1)S(1)}, u32[]{:S(2)}, u32[]{:S(2)}) %collective-permute-start.10) | collective-permute-done | bytes 262176 | tf_op jit(solution)/shard_map/ppermute | solution.py:498
  487.7 5.5 collective-permute-done.9
  495.1 64.4 %reduce-scatter.5.cloned.1.call-done = bf16[128,1,4096]{2,0,1:T(8,128)(2,1)} async-done(((bf16[2048,1,4096]{2,0,1:T(8,128)(2,1)}), bf16[128,1,4096]{2,0,1:T(8,128)(2,1)}) %reduce-scatter.5.cloned.1.call-update) | async-done | bytes 1048592 | tf_op jit(solution)/shard_map/reduce_scatter | solution.py:411
  565.3 8.2 %all-to-all-start.3 = ((f32[128,1,16]{2,1,0:T(1,128)}), f32[128,1,16]{2,1,0:T(1,128)S(1)}, u32[]{:S(2)}, u32[]{:S(2)}) async-start(f32[128,1,16]{2,1,0:T(1,128)} %bitcast.49), calls=%async_computation.5 | async-start | bytes 131072 | tf_op jit(solution)/shard_map/all_to_all | solution.py:472
  (204 shorter events, 127.1 us)
Async XLA Ops:
  7.2 248.7 %copy-start = (bf16[2048,512]{1,0:T(8,128)(2,1)S(1)}, bf16[2048,512]{1,0:T(8,128)(2,1)}, u32[]{:S(2)}) copy-start(bf16[2048,512]{1,0:T(8,128)(2,1)} %param.26) | copy-start | bytes 6291460
  7.2 97.5 %all-gather.5.cloned.1.call-start = ((), (), s32[]{:S(2)}) async-start(), calls=%async_computation.6 | async-start | bytes 13369344 | tf_op jit(solution)/shard_map/all_gather | solution.py:258
  9.9 99.4 %copy-start.26 = (f32[128]{0:T(128)}, f32[128]{0:T(128)S(1)}, u32[]{:S(2)}) copy-start(f32[128]{0:T(128)S(1)} %fusion.56) | copy-start | bytes 1540
  13.4 169.4 %all-gather.7.cloned.1.call-start = ((), (), s32[]{:S(2)}) async-start(), calls=%async_computation.7 | async-start | bytes 8912896 | tf_op jit(solution)/shard_map/all_gather | solution.py:264
  109.3 46.5 %collective-permute-start = (bf16[2048,1024]{1,0:T(8,128)(2,1)}, bf16[2048,1024]{1,0:T(8,128)(2,1)}, u32[]{:S(2)}, u32[]{:S(2)}) collective-permute-start(bf16[2048,1024]{1,0:T(8,128)(2,1)} %slice.185), channel_id=1, source_target_pairs={{0,32},{32,0},{64,96},{96,64},{1,33},{33,1},{65,97},{97,65},{2,34}... | collective-permute-start | bytes 12582920 | tf_op jit(solution)/shard_map/ppermute | solution.py:262
  132.8 20.0 %all-to-all-start = ((bf16[16,128,128]{1,2,0:T(8,128)(2,1)}), bf16[16,128,128]{1,2,0:T(8,128)(2,1)S(1)}, u32[]{:S(2)}, u32[]{:S(2)}) async-start(bf16[16,128,128]{1,2,0:T(8,128)(2,1)} %copy.43), calls=%async_computation | async-start | bytes 1048576 | tf_op jit(solution)/shard_map/all_to_all | solution.py:292
  138.0 117.9 %all-gather.9.cloned.1.call-start = ((), (), s32[]{:S(2)}) async-start(), calls=%async_computation.8 | async-start | bytes 8912896 | tf_op jit(solution)/shard_map/all_gather | solution.py:313
  182.8 182.9 %reduce-scatter.3.cloned.1.call-start = ((), (), s32[]{:S(2)}) async-start(), calls=%async_computation.9 | async-start | bytes 8912896 | tf_op jit(solution)/shard_map/reduce_scatter | solution.py:340
  275.6 193.6 %all-gather.11.cloned.1.call-start = ((), (), s32[]{:S(2)}) async-start(), calls=%async_computation.11 | async-start | bytes 8912896 | tf_op jit(solution)/shard_map/all_gather | solution.py:363
  297.8 26.4 %collective-permute-start.1 = (bf16[4,256,512]{2,1,0:T(8,128)(2,1)}, bf16[4,256,512]{2,1,0:T(8,128)(2,1)}, u32[]{:S(2)}, u32[]{:S(2)}) collective-permute-start(bf16[4,256,512]{2,1,0:T(8,128)(2,1)} %bitcast.29), channel_id=1, source_target_pairs={{0,64},{32,96},{64,0},{96,32},{1,65},{33,97},{65,1},{97,33},{2,66}... | collective-permute-start | bytes 3145736 | tf_op jit(solution)/shard_map/ppermute | solution.py:498
  302.4 43.1 %collective-permute-start.4 = (bf16[512,4,256]{2,0,1:T(8,128)(2,1)}, bf16[512,4,256]{2,0,1:T(8,128)(2,1)}, u32[]{:S(2)}, u32[]{:S(2)}) collective-permute-start(bf16[512,4,256]{2,0,1:T(8,128)(2,1)} %select_convert_fusion), channel_id=1, source_target_pairs={{0,64},{32,96},{64,0},{96,32},{1,65},{33,97},{65,1},{97,33},{2,66}... | collective-permute-start | bytes 3145736 | tf_op jit(solution)/shard_map/ppermute | solution.py:498
  326.0 21.7 %collective-permute-start.2 = (bf16[2,256,512]{2,1,0:T(8,128)(2,1)S(1)}, bf16[2,256,512]{2,1,0:T(8,128)(2,1)S(1)}, u32[]{:S(2)}, u32[]{:S(2)}) collective-permute-start(bf16[2,256,512]{2,1,0:T(8,128)(2,1)S(1)} %select_convert_fusion.4), channel_id=1, source_target_pairs={{0,32},{32,0},{64,96},{96,64},{1,33},{33,1},{65,97},{97,65},{2,34}... | collective-permute-start | bytes 1572872 | tf_op jit(solution)/shard_map/ppermute | solution.py:498
  347.6 2.0 collective-permute-start.5
  348.0 15.8 %collective-permute-start.3 = (bf16[1,256,512]{2,1,0:T(8,128)(2,1)S(1)}, bf16[1,256,512]{2,1,0:T(8,128)(2,1)S(1)}, u32[]{:S(2)}, u32[]{:S(2)}) collective-permute-start(bf16[1,256,512]{2,1,0:T(8,128)(2,1)S(1)} %select_convert_fusion.8), channel_id=1, source_target_pairs={{0,16},{16,0},{1,17},{17,1},{2,18},{18,2},{3,19},{19,3},{4,20},{20... | collective-permute-start | bytes 786440 | tf_op jit(solution)/shard_map/ppermute | solution.py:498
  349.9 14.9 %collective-permute-start.6 = (bf16[512,1,256]{2,0,1:T(8,128)(2,1)S(1)}, bf16[512,1,256]{2,0,1:T(8,128)(2,1)S(1)}, u32[]{:S(2)}, u32[]{:S(2)}) collective-permute-start(bf16[512,1,256]{2,0,1:T(8,128)(2,1)S(1)} %select_convert_fusion.7), channel_id=1, source_target_pairs={{0,16},{16,0},{1,17},{17,1},{2,18},{18,2},{3,19},{19,3},{4,20},{20... | collective-permute-start | bytes 786440 | tf_op jit(solution)/shard_map/ppermute | solution.py:498
  370.1 189.5 %reduce-scatter.5.cloned.1.call-start = ((), (), s32[]{:S(2)}) async-start(), calls=%async_computation.10 | async-start | bytes 17825792 | tf_op jit(solution)/shard_map/reduce_scatter | solution.py:411
  429.0 38.3 %collective-permute-start.7 = (bf16[4,256,384]{2,1,0:T(8,128)(2,1)}, bf16[4,256,384]{2,1,0:T(8,128)(2,1)}, u32[]{:S(2)}, u32[]{:S(2)}) collective-permute-start(bf16[4,256,384]{2,1,0:T(8,128)(2,1)} %bitcast.43), channel_id=1, source_target_pairs={{0,64},{32,96},{64,0},{96,32},{1,65},{33,97},{65,1},{97,33},{2,66}... | collective-permute-start | bytes 2359304 | tf_op jit(solution)/shard_map/ppermute | solution.py:498
  449.4 16.6 %all-to-all-start.2 = ((f32[128,1,176]{2,1,0:T(1,128)}), f32[128,1,176]{2,1,0:T(1,128)S(1)}, u32[]{:S(2)}, u32[]{:S(2)}) async-start(f32[128,1,176]{2,1,0:T(1,128)} %copy.50), calls=%async_computation.4 | async-start | bytes 262144 | tf_op jit(solution)/shard_map/all_to_all | solution.py:472
  469.2 7.1 %collective-permute-start.8 = (bf16[2,256,384]{2,1,0:T(8,128)(2,1)S(1)}, bf16[2,256,384]{2,1,0:T(8,128)(2,1)}, u32[]{:S(2)}, u32[]{:S(2)}) collective-permute-start(bf16[2,256,384]{2,1,0:T(8,128)(2,1)S(1)} %select_convert_fusion.5), channel_id=1, source_target_pairs={{0,32},{32,0},{64,96},{96,64},{1,33},{33,1},{65,97},{97,65},{2,34}... | collective-permute-start | bytes 1179656 | tf_op jit(solution)/shard_map/ppermute | solution.py:498
  474.8 8.8 %collective-permute-start.10 = (bf16[1,128,4,256]{3,1,2,0:T(8,128)(2,1)S(1)}, bf16[1,128,4,256]{3,1,2,0:T(8,128)(2,1)S(1)}, u32[]{:S(2)}, u32[]{:S(2)}) collective-permute-start(bf16[1,128,4,256]{3,1,2,0:T(8,128)(2,1)S(1)} %select_convert_fusion.6), channel_id=1, source_target_pairs={{0,64},{32,96},{64,0},{96,32},{1,65},{33,97},{65,1},{97,33},{2,66}... | collective-permute-start | bytes 786440 | tf_op jit(solution)/shard_map/ppermute | solution.py:498
  483.8 2.5 collective-permute-start.11
  484.0 9.3 %collective-permute-start.9 = (bf16[1,256,384]{2,1,0:T(8,128)(2,1)S(1)}, bf16[1,256,384]{2,1,0:T(8,128)(2,1)S(1)}, u32[]{:S(2)}, u32[]{:S(2)}) collective-permute-start(bf16[1,256,384]{2,1,0:T(8,128)(2,1)S(1)} %select_convert_fusion.9), channel_id=1, source_target_pairs={{0,16},{16,0},{1,17},{17,1},{2,18},{18,2},{3,19},{19,3},{4,20},{20... | collective-permute-start | bytes 589832 | tf_op jit(solution)/shard_map/ppermute | solution.py:498
  486.4 8.1 %collective-permute-start.12 = (bf16[1,128,1,256]{3,1,2,0:T(8,128)(2,1)S(1)}, bf16[1,128,1,256]{3,1,2,0:T(8,128)(2,1)S(1)}, u32[]{:S(2)}, u32[]{:S(2)}) collective-permute-start(bf16[1,128,1,256]{3,1,2,0:T(8,128)(2,1)S(1)} %select_convert_fusion.11), channel_id=1, source_target_pairs={{0,16},{16,0},{1,17},{17,1},{2,18},{18,2},{3,19},{19,3},{4,20},{20... | collective-permute-start | bytes 196616 | tf_op jit(solution)/shard_map/ppermute | solution.py:498
  565.3 15.4 %all-to-all-start.3 = ((f32[128,1,16]{2,1,0:T(1,128)}), f32[128,1,16]{2,1,0:T(1,128)S(1)}, u32[]{:S(2)}, u32[]{:S(2)}) async-start(f32[128,1,16]{2,1,0:T(1,128)} %bitcast.49), calls=%async_computation.5 | async-start | bytes 131072 | tf_op jit(solution)/shard_map/all_to_all | solution.py:472
  (27 other events, 510.8 us)
Sparse Core Ops, SparseCore 0:
  13.5 91.1 all-gather.4
  106.8 75.8 all-gather.6
  185.5 70.3 all-gather.8
  275.8 84.4 reduce-scatter.2
  370.2 74.4 all-gather.10
  448.0 111.5 reduce-scatter.4

commit v18 on v16

--- a/solution.py
+++ b/solution.py
@@ -340,14 +340,10 @@
     second_grad = lax.psum_scatter(
         second_part, "tensor", scatter_dimension=0, tiled=True
     ).astype(jnp.float32)
-    feed_part = jnp.einsum(
-        "rsf,fd->rsd", feed_input, w_out, preferred_element_type=jnp.float32
+    padded_out = jnp.concatenate([jnp.zeros_like(w_out), w_out], 1)
+    feed_buffer = jnp.einsum(
+        "rsf,fd->rsd", feed_input, padded_out, preferred_element_type=jnp.float32
     ).astype(jnp.bfloat16)
-    feed_buffer = lax.dynamic_update_slice(
-        jnp.zeros(feed_part.shape[:2] + (2 * model_width,), feed_part.dtype),
-        feed_part,
-        (0, 0, model_width),
-    )
     feed_buffer, second_grad = lax.optimization_barrier((feed_buffer, second_grad))
     norm_two_back = jax.vjp(layer_norm, middle, ln2_gain, ln2_bias)[1]
     middle_part, grad_ln2_gain, grad_ln2_bias = norm_two_back(second_grad)

time: 597 us -> 597 us (level)
  local copies, waits for them, and re-layouts: 53.7 us -> 46.8 us
  matrix products: 91.1 us -> 97.8 us
    dynamic_update_slice x1 -> x0, local copies, waits for them, and re-layouts: 6.94 us -> none  [shards(): lax.dynamic_update_slice(jnp.zeros(feed_part.shape[:2] + (2 * model_width...]
    dot_general x1, matrix products: 4.71 us -> 11.6 us  [shards(): jnp.einsum('rsf,fd->rsd', feed_input, padded_out, preferred_element_type=...]
where the time goes in v18:
time: 597 us; the launch traced here: 586 us
  waiting for transfers between devices  274 us (46%)
  matrix products  97.8 us (16%)
  other arithmetic  53.6 us (9%)
  local copies, waits for them, and re-layouts  46.8 us (8%)
  Pallas kernels  41.4 us (7%)
  starting transfers between devices  34.9 us (6%)
  blocking collectives  20.3 us (3%)
  between operations  16.5 us (3%)
    all_gather x1, waiting for transfers between devices, shards(): front = lax.all_gather(front, 'tensor', axis=0, tiled=True)  88.1 us
    all_gather x1, waiting for transfers between devices, shards(): second_full = lax.all_gather(second_low, 'tensor', axis=0, tiled=True)  63.1 us
    reduce_scatter x1, waiting for transfers between devices, shards(): both = lax.psum_scatter(merged, 'tensor', scatter_dimension=0, tiled=True)  62.2 us
    ppermute x12, waiting for transfers between devices, halving_steps(): got = lax.ppermute(send, axis, [(i, i ^ bit) for i in range(size)])  26.6 us
    pallas_call x1, Pallas kernels, attention_backward(): pl.pallas_call(kernel, out_shape=tuple((jax.ShapeDtypeStruct((n, d), jnp....  24.6 us
    all_to_all x1, blocking collectives, shards(): lax.all_to_all(heads_grad, 'tensor', 1, 0, tiled=True)  20.3 us
    reshape x4, local copies, waits for them, and re-layouts, halving_sum(): value.reshape(shape[:dim] + (groups // 2, 2, dps * rest) + shape[dim + 1:])  19.4 us
    pallas_call x1, Pallas kernels, attention_forward(): pl.pallas_call(kernel, out_shape=(jax.ShapeDtypeStruct((n, d), jnp.bfloat...  16.9 us
  transfers between devices with their start and end apart: 22, of which 12 were waited for; matrix products, arithmetic and copies ran while one was open for 27% of the time, Pallas kernels for 7%

profile of v18, /device:TPU:96, one launch (start us, length us, event | category | flops | bytes accessed | tf_op | source)
XLA Modules:
  0.0 585.6 jit_solution(16300874041935548301)
XLA Ops:
  16.6 88.1 %all-gather.5.cloned.1.call-done = bf16[2048,3072]{1,0:T(8,128)(2,1)} async-done(((bf16[128,3072]{1,0:T(8,128)(2,1)}), bf16[2048,3072]{1,0:T(8,128)(2,1)}) %all-gather.5.cloned.1.call-update) | async-done | bytes 12582928 | tf_op jit(solution)/shard_map/all_gather | solution.py:258
  112.0 7.4 %fusion.38 = f32[2048,1,3,128]{3,0,2,1:T(8,128)S(1)} fusion(bf16[2048,3072]{1,0:T(8,128)(2,1)} %all-gather.5.cloned.1.call-done, bf16[2048,3,1,128]{0,3,1,2:T(8,128)(2,1)} %copy.38), kind=kOutput, calls=%fused_computation.40 | convolution fusion | flops 3221225472 | bytes 13107200 | tf_op jit(solution)/shard_map/dot_general | solution.py:266
  121.4 16.9 %shard_map.254 = (bf16[2048,128]{1,0:T(8,128)(2,1)}, f32[2048,1]{1,0:T(8,128)}) custom-call(s32[1]{0:T(128)} %dynamic_slice.22.len_ref, bf16[2048,128]{1,0:T(8,128)(2,1)} %get-tuple-element.121.q_ref, bf16[2048,128]{1,0:T(8,128)(2,1)} %fusion.67.k_ref, bf16[2048,128]{1,0:T(8,128)(2,1)} %get-tuple-element.120.v_ref), custom_call_target="tpu_custom_call" | custom-call | flops 1342177280 | bytes 2097152 | tf_op jit(solution)/shard_map/pallas_call | solution.py:85
  145.7 13.5 %all-to-all-done = bf16[16,128,128]{1,2,0:T(8,128)(2,1)S(1)} async-done(((bf16[16,128,128]{1,2,0:T(8,128)(2,1)}), bf16[16,128,128]{1,2,0:T(8,128)(2,1)S(1)}, u32[]{:S(2)}, u32[]{:S(2)}) %all-to-all-start) | async-done | bytes 524320 | tf_op jit(solution)/shard_map/all_to_all | solution.py:292
  167.0 15.3 %all-gather.7.cloned.1.call-done = bf16[2048,1,2048]{2,0,1:T(8,128)(2,1)} async-done(((bf16[128,1,2048]{2,0,1:T(8,128)(2,1)}), bf16[2048,1,2048]{2,0,1:T(8,128)(2,1)}) %all-gather.7.cloned.1.call-update) | async-done | bytes 8388624 | tf_op jit(solution)/shard_map/all_gather | solution.py:264
  182.5 10.5 %fusion.32 = f32[2048,1,512]{2,0,1:T(8,128)} fusion(bf16[512,2048]{1,0:T(8,128)(2,1)} %param.28, bf16[2048,1,2048]{2,0,1:T(8,128)(2,1)} %all-gather.7.cloned.1.call-done), kind=kOutput, calls=%fused_computation.37 | convolution fusion | flops 4294967296 | bytes 14680064 | tf_op jit(solution)/shard_map/rsd,fd->rsf/dot_general | solution.py:310
  193.0 63.1 %all-gather.9.cloned.1.call-done = bf16[2048,1,2048]{2,0,1:T(8,128)(2,1)} async-done(((bf16[128,1,2048]{2,0,1:T(8,128)(2,1)}), bf16[2048,1,2048]{2,0,1:T(8,128)(2,1)}) %all-gather.9.cloned.1.call-update) | async-done | bytes 8388624 | tf_op jit(solution)/shard_map/all_gather | solution.py:313
  256.1 7.0 %fusion.6 = f32[2048,512]{1,0:T(8,128)S(1)} fusion(bf16[2048,512]{1,0:T(8,128)(2,1)S(1)} %copy-done, bf16[2048,1,2048]{2,0,1:T(8,128)(2,1)} %all-gather.9.cloned.1.call-done), kind=kOutput, calls=%fused_computation.8 | convolution fusion | flops 4294967296 | bytes 14680064 | tf_op jit(solution)/shard_map/dot_general | solution.py:316
  268.8 6.9 %convert_bitcast_fusion.1 = bf16[2048,1,2048]{2,0,1:T(8,128)(2,1)} fusion(bf16[2048,512]{1,0:T(8,128)(2,1)S(1)} %get-tuple-element.110, bf16[2048,512]{1,0:T(8,128)(2,1)S(1)} %copy-done), kind=kOutput, calls=%fused_computation.14 | convolution fusion | flops 4299161600 | bytes 12582912 | tf_op jit(solution)/shard_map/rsf,df->rsd/dot_general | solution.py:337
  278.6 7.1 %fusion.29 = f32[2048,512]{1,0:T(8,128)S(1)} fusion(bf16[2048,512]{1,0:T(8,128)(2,1)S(1)} %copy-done.18, bf16[2048,1,2048]{2,0,1:T(8,128)(2,1)} %all-gather.9.cloned.1.call-done, f32[]{:T(128)S(6)} %div.71), kind=kOutput, calls=%fused_computation.36 | convolution fusion | flops 4296015872 | bytes 14680068 | tf_op jit(solution)/shard_map/rd,rf->df/dot_general | solution.py:329
  288.4 10.0 %fusion.26 = f32[512,2048]{1,0:T(8,128)} fusion(bf16[2048,1,2048]{2,0,1:T(8,128)(2,1)} %all-gather.7.cloned.1.call-done, f32[]{:T(128)S(6)} %div.71, f32[2048,512]{1,0:T(8,128)S(1)} %copy-done.12, f32[512]{0:T(512)S(1)} %copy-done.25), kind=kOutput, calls=%fused_computation.35 | convolution fusion | flops 4306501632 | bytes 16779268 | tf_op jit(solution)/shard_map/rsf,rsd->fd/dot_general | solution.py:325
  298.3 6.7 %reshape.504 = f32[512,2,2,512]{3,2,1,0:T(2,128)} reshape(f32[512,2048]{1,0:T(8,128)} %fusion.26) | data formatting | bytes 8388608 | tf_op jit(solution)/shard_map/reshape | solution.py:504
  305.0 7.3 %copy.40 = f32[512,2,2,512]{0,3,1,2:T(8,128)} copy(f32[512,2,2,512]{3,2,1,0:T(2,128)} %reshape.504) | data formatting | bytes 8388608 | tf_op jit(solution)/shard_map/reshape | solution.py:504
  326.7 10.6 %collective-permute-done.2 = bf16[2,256,512]{2,1,0:T(8,128)(2,1)S(1)} collective-permute-done((bf16[2,256,512]{2,1,0:T(8,128)(2,1)S(1)}, bf16[2,256,512]{2,1,0:T(8,128)(2,1)S(1)}, u32[]{:S(2)}, u32[]{:S(2)}) %collective-permute-start.2) | collective-permute-done | bytes 524320 | tf_op jit(solution)/shard_map/ppermute | solution.py:494
  339.1 9.5 %collective-permute-done.5 = bf16[512,2,256]{0,2,1:T(8,128)(2,1)S(1)} collective-permute-done((bf16[512,2,256]{0,2,1:T(8,128)(2,1)S(1)}, bf16[512,2,256]{0,2,1:T(8,128)(2,1)S(1)}, u32[]{:S(2)}, u32[]{:S(2)}) %collective-permute-start.5) | collective-permute-done | bytes 524320 | tf_op jit(solution)/shard_map/ppermute | solution.py:494
  350.3 11.6 %convert_bitcast_fusion = bf16[2048,1,4096]{2,0,1:T(8,128)(2,1)} fusion(bf16[512,2048]{1,0:T(8,128)(2,1)S(1)} %copy-done.31, bf16[2048,1,512]{2,0,1:T(8,128)(2,1)S(1)} %copy-done.16), kind=kOutput, calls=%fused_computation | convolution fusion | flops 8598323200 | bytes 20971520 | tf_op jit(solution)/shard_map/rsf,fd->rsd/dot_general | solution.py:344
  376.1 20.3 %all_to_all.53 = bf16[128,16,128]{2,0,1:T(8,128)(2,1)} all-to-all(bf16[128,16,128]{2,0,1:T(8,128)(2,1)S(1)} %bitcast.171), channel_id=1, replica_groups=mesh['group'=4,'dp'=2,'tensor'=16] {'tensor'}, dimensions={1} | all-to-all | bytes 1048576 | tf_op jit(solution)/shard_map/all_to_all | solution.py:374
  396.5 24.6 %shard_map.255 = (bf16[2048,128]{1,0:T(8,128)(2,1)}, bf16[2048,128]{1,0:T(8,128)(2,1)}, bf16[2048,128]{1,0:T(8,128)(2,1)}) custom-call(s32[1]{0:T(128)} %dynamic_slice.22.len_ref, bf16[2048,128]{1,0:T(8,128)(2,1)} %get-tuple-element.121.q_ref, bf16[2048,128]{1,0:T(8,128)(2,1)} %fusion.67.k_ref, bf16[2048,128]{1,0:T(8,128)(2,1)} %get-tuple-element.120.v_ref, ...), custom_call_target="tpu_custom_call" | custom-call | flops 2684354560 | bytes 4194304 | tf_op jit(solution)/shard_map/pallas_call | solution.py:185
  424.5 9.7 %bitcast_dynamic-update-slice_fusion = bf16[2048,1,4096]{2,0,1:T(8,128)(2,1)} fusion(bf16[2048,1,4096]{2,0,1:T(8,128)(2,1)} %convert_bitcast_fusion, bf16[2048,384]{0,1:T(8,128)(2,1)} %bitcast.172, bf16[2048,384]{0,1:T(8,128)(2,1)} %bitcast.165), kind=kOutput, calls=%fused_computation.3 | convolution fusion | flops 3225419776 | bytes 11534336 | tf_op jit(solution)/shard_map/rsc,dc->rsd/dot_general | solution.py:399
  434.9 7.6 %fusion.35 = f32[2048,384]{1,0:T(8,128)S(1)} fusion(bf16[2048,384]{0,1:T(8,128)(2,1)} %bitcast.173, bf16[2048,3072]{1,0:T(8,128)(2,1)} %all-gather.5.cloned.1.call-done, f32[]{:T(128)S(6)} %div.71), kind=kOutput, calls=%fused_computation.39 | convolution fusion | flops 3222011904 | bytes 13107204 | tf_op jit(solution)/shard_map/rd,rc->dc/dot_general | solution.py:393
  446.5 8.2 %all-to-all-start.2 = ((f32[128,1,176]{2,1,0:T(1,128)}), f32[128,1,176]{2,1,0:T(1,128)S(1)}, u32[]{:S(2)}, u32[]{:S(2)}) async-start(f32[128,1,176]{2,1,0:T(1,128)} %copy.44), calls=%async_computation.4 | async-start | bytes 262144 | tf_op jit(solution)/shard_map/all_to_all | solution.py:468
  468.0 5.8 fusion.41
  495.0 62.2 %reduce-scatter.5.cloned.1.call-done = bf16[128,1,4096]{2,0,1:T(8,128)(2,1)} async-done(((bf16[2048,1,4096]{2,0,1:T(8,128)(2,1)}), bf16[128,1,4096]{2,0,1:T(8,128)(2,1)}) %reduce-scatter.5.cloned.1.call-update) | async-done | bytes 1048592 | tf_op jit(solution)/shard_map/reduce_scatter | solution.py:407
  562.5 8.1 %all-to-all-start.3 = ((f32[128,1,16]{2,1,0:T(1,128)}), f32[128,1,16]{2,1,0:T(1,128)S(1)}, u32[]{:S(2)}, u32[]{:S(2)}) async-start(f32[128,1,16]{2,1,0:T(1,128)} %bitcast.61), calls=%async_computation.5 | async-start | bytes 131072 | tf_op jit(solution)/shard_map/all_to_all | solution.py:468
  (211 shorter events, 131.2 us)
Async XLA Ops:
  7.2 248.9 %copy-start = (bf16[2048,512]{1,0:T(8,128)(2,1)S(1)}, bf16[2048,512]{1,0:T(8,128)(2,1)}, u32[]{:S(2)}) copy-start(bf16[2048,512]{1,0:T(8,128)(2,1)} %param.26) | copy-start | bytes 6291460
  7.2 97.5 %all-gather.5.cloned.1.call-start = ((), (), s32[]{:S(2)}) async-start(), calls=%async_computation.6 | async-start | bytes 13369344 | tf_op jit(solution)/shard_map/all_gather | solution.py:258
  9.9 99.5 %copy-start.29 = (f32[128]{0:T(128)}, f32[128]{0:T(128)S(1)}, u32[]{:S(2)}) copy-start(f32[128]{0:T(128)S(1)} %fusion.57) | copy-start | bytes 1540
  13.4 168.9 %all-gather.7.cloned.1.call-start = ((), (), s32[]{:S(2)}) async-start(), calls=%async_computation.7 | async-start | bytes 8912896 | tf_op jit(solution)/shard_map/all_gather | solution.py:264
  109.4 52.9 %collective-permute-start = (bf16[2048,1024]{1,0:T(8,128)(2,1)}, bf16[2048,1024]{1,0:T(8,128)(2,1)}, u32[]{:S(2)}, u32[]{:S(2)}) collective-permute-start(bf16[2048,1024]{1,0:T(8,128)(2,1)} %slice.185), channel_id=1, source_target_pairs={{0,32},{32,0},{64,96},{96,64},{1,33},{33,1},{65,97},{97,65},{2,34}... | collective-permute-start | bytes 12582920 | tf_op jit(solution)/shard_map/ppermute | solution.py:262
  140.4 18.8 %all-to-all-start = ((bf16[16,128,128]{1,2,0:T(8,128)(2,1)}), bf16[16,128,128]{1,2,0:T(8,128)(2,1)S(1)}, u32[]{:S(2)}, u32[]{:S(2)}) async-start(bf16[16,128,128]{1,2,0:T(8,128)(2,1)} %copy.39), calls=%async_computation | async-start | bytes 1048576 | tf_op jit(solution)/shard_map/all_to_all | solution.py:292
  145.6 110.5 %all-gather.9.cloned.1.call-start = ((), (), s32[]{:S(2)}) async-start(), calls=%async_computation.8 | async-start | bytes 8912896 | tf_op jit(solution)/shard_map/all_gather | solution.py:313
  182.3 181.4 %reduce-scatter.3.cloned.1.call-start = ((), (), s32[]{:S(2)}) async-start(), calls=%async_computation.9 | async-start | bytes 8912896 | tf_op jit(solution)/shard_map/reduce_scatter | solution.py:340
  275.8 192.2 %all-gather.11.cloned.1.call-start = ((), (), s32[]{:S(2)}) async-start(), calls=%async_computation.11 | async-start | bytes 8912896 | tf_op jit(solution)/shard_map/all_gather | solution.py:359
  287.9 31.3 %collective-permute-start.1 = (bf16[4,256,512]{2,1,0:T(8,128)(2,1)S(1)}, bf16[4,256,512]{2,1,0:T(8,128)(2,1)S(1)}, u32[]{:S(2)}, u32[]{:S(2)}) collective-permute-start(bf16[4,256,512]{2,1,0:T(8,128)(2,1)S(1)} %bitcast.174), channel_id=1, source_target_pairs={{0,32},{32,0},{64,96},{96,64},{1,33},{33,1},{65,97},{97,65},{2,34}... | collective-permute-start | bytes 3145736 | tf_op jit(solution)/shard_map/ppermute | solution.py:494
  315.9 7.5 %collective-permute-start.4 = (bf16[512,4,256]{0,2,1:T(8,128)(2,1)}, bf16[512,4,256]{0,2,1:T(8,128)(2,1)}, u32[]{:S(2)}, u32[]{:S(2)}) collective-permute-start(bf16[512,4,256]{0,2,1:T(8,128)(2,1)} %select_convert_fusion), channel_id=1, source_target_pairs={{0,32},{32,0},{64,96},{96,64},{1,33},{33,1},{65,97},{97,65},{2,34}... | collective-permute-start | bytes 3145736 | tf_op jit(solution)/shard_map/ppermute | solution.py:494
  322.5 14.8 %collective-permute-start.2 = (bf16[2,256,512]{2,1,0:T(8,128)(2,1)S(1)}, bf16[2,256,512]{2,1,0:T(8,128)(2,1)S(1)}, u32[]{:S(2)}, u32[]{:S(2)}) collective-permute-start(bf16[2,256,512]{2,1,0:T(8,128)(2,1)S(1)} %select_convert_fusion.4), channel_id=1, source_target_pairs={{0,64},{32,96},{64,0},{96,32},{1,65},{33,97},{65,1},{97,33},{2,66}... | collective-permute-start | bytes 1572872 | tf_op jit(solution)/shard_map/ppermute | solution.py:494
  325.5 23.1 %collective-permute-start.5 = (bf16[512,2,256]{0,2,1:T(8,128)(2,1)S(1)}, bf16[512,2,256]{0,2,1:T(8,128)(2,1)S(1)}, u32[]{:S(2)}, u32[]{:S(2)}) collective-permute-start(bf16[512,2,256]{0,2,1:T(8,128)(2,1)S(1)} %select_convert_fusion.3), channel_id=1, source_target_pairs={{0,64},{32,96},{64,0},{96,32},{1,65},{33,97},{65,1},{97,33},{2,66}... | collective-permute-start | bytes 1572872 | tf_op jit(solution)/shard_map/ppermute | solution.py:494
  337.7 24.1 %collective-permute-start.3 = (bf16[1,256,512]{2,1,0:T(8,128)(2,1)S(1)}, bf16[1,256,512]{2,1,0:T(8,128)(2,1)S(1)}, u32[]{:S(2)}, u32[]{:S(2)}) collective-permute-start(bf16[1,256,512]{2,1,0:T(8,128)(2,1)S(1)} %select_convert_fusion.8), channel_id=1, source_target_pairs={{0,16},{16,0},{1,17},{17,1},{2,18},{18,2},{3,19},{19,3},{4,20},{20... | collective-permute-start | bytes 786440 | tf_op jit(solution)/shard_map/ppermute | solution.py:494
  348.9 13.8 %collective-permute-start.6 = (bf16[512,1,256]{0,2,1:T(8,128)(2,1)S(1)}, bf16[512,1,256]{0,2,1:T(8,128)(2,1)S(1)}, u32[]{:S(2)}, u32[]{:S(2)}) collective-permute-start(bf16[512,1,256]{0,2,1:T(8,128)(2,1)S(1)} %select_convert_fusion.7), channel_id=1, source_target_pairs={{0,16},{16,0},{1,17},{17,1},{2,18},{18,2},{3,19},{19,3},{4,20},{20... | collective-permute-start | bytes 786440 | tf_op jit(solution)/shard_map/ppermute | solution.py:494
  368.2 189.1 %reduce-scatter.5.cloned.1.call-start = ((), (), s32[]{:S(2)}) async-start(), calls=%async_computation.10 | async-start | bytes 17825792 | tf_op jit(solution)/shard_map/reduce_scatter | solution.py:407
  443.7 21.0 %collective-permute-start.7 = (bf16[4,256,384]{2,1,0:T(8,128)(2,1)}, bf16[4,256,384]{2,1,0:T(8,128)(2,1)}, u32[]{:S(2)}, u32[]{:S(2)}) collective-permute-start(bf16[4,256,384]{2,1,0:T(8,128)(2,1)} %bitcast.52), channel_id=1, source_target_pairs={{0,32},{32,0},{64,96},{96,64},{1,33},{33,1},{65,97},{97,65},{2,34}... | collective-permute-start | bytes 2359304 | tf_op jit(solution)/shard_map/ppermute | solution.py:494
  446.5 16.8 %all-to-all-start.2 = ((f32[128,1,176]{2,1,0:T(1,128)}), f32[128,1,176]{2,1,0:T(1,128)S(1)}, u32[]{:S(2)}, u32[]{:S(2)}) async-start(f32[128,1,176]{2,1,0:T(1,128)} %copy.44), calls=%async_computation.4 | async-start | bytes 262144 | tf_op jit(solution)/shard_map/all_to_all | solution.py:468
  466.6 14.2 %collective-permute-start.8 = (bf16[2,256,384]{2,1,0:T(8,128)(2,1)S(1)}, bf16[2,256,384]{2,1,0:T(8,128)(2,1)}, u32[]{:S(2)}, u32[]{:S(2)}) collective-permute-start(bf16[2,256,384]{2,1,0:T(8,128)(2,1)S(1)} %select_convert_fusion.5), channel_id=1, source_target_pairs={{0,64},{32,96},{64,0},{96,32},{1,65},{33,97},{65,1},{97,33},{2,66}... | collective-permute-start | bytes 1179656 | tf_op jit(solution)/shard_map/ppermute | solution.py:494
  480.6 1.6 collective-permute-start.10
  482.4 6.4 %collective-permute-start.11 = (bf16[1,128,2,256]{1,3,2,0:T(8,128)(2,1)S(1)}, bf16[1,128,2,256]{1,3,2,0:T(8,128)(2,1)S(1)}, u32[]{:S(2)}, u32[]{:S(2)}) collective-permute-start(bf16[1,128,2,256]{1,3,2,0:T(8,128)(2,1)S(1)} %select_convert_fusion.10), channel_id=1, source_target_pairs={{0,64},{32,96},{64,0},{96,32},{1,65},{33,97},{65,1},{97,33},{2,66}... | collective-permute-start | bytes 393224 | tf_op jit(solution)/shard_map/ppermute | solution.py:494
  483.2 10.6 %collective-permute-start.9 = (bf16[1,256,384]{2,1,0:T(8,128)(2,1)S(1)}, bf16[1,256,384]{2,1,0:T(8,128)(2,1)S(1)}, u32[]{:S(2)}, u32[]{:S(2)}) collective-permute-start(bf16[1,256,384]{2,1,0:T(8,128)(2,1)S(1)} %select_convert_fusion.9), channel_id=1, source_target_pairs={{0,16},{16,0},{1,17},{17,1},{2,18},{18,2},{3,19},{19,3},{4,20},{20... | collective-permute-start | bytes 589832 | tf_op jit(solution)/shard_map/ppermute | solution.py:494
  488.9 6.1 %collective-permute-start.12 = (bf16[1,128,1,256]{1,3,2,0:T(8,128)(2,1)S(1)}, bf16[1,128,1,256]{1,3,2,0:T(8,128)(2,1)S(1)}, u32[]{:S(2)}, u32[]{:S(2)}) collective-permute-start(bf16[1,128,1,256]{1,3,2,0:T(8,128)(2,1)S(1)} %select_convert_fusion.11), channel_id=1, source_target_pairs={{0,16},{16,0},{1,17},{17,1},{2,18},{18,2},{3,19},{19,3},{4,20},{20... | collective-permute-start | bytes 196616 | tf_op jit(solution)/shard_map/ppermute | solution.py:494
  562.5 15.4 %all-to-all-start.3 = ((f32[128,1,16]{2,1,0:T(1,128)}), f32[128,1,16]{2,1,0:T(1,128)S(1)}, u32[]{:S(2)}, u32[]{:S(2)}) async-start(f32[128,1,16]{2,1,0:T(1,128)} %bitcast.61), calls=%async_computation.5 | async-start | bytes 131072 | tf_op jit(solution)/shard_map/all_to_all | solution.py:468
  (30 other events, 564.2 us)
Sparse Core Ops, SparseCore 0:
  13.5 91.1 all-gather.4
  106.8 75.3 all-gather.6
  185.0 71.0 all-gather.8
  275.9 84.4 reduce-scatter.2
  368.3 74.2 all-gather.10
  445.9 111.3 reduce-scatter.4

commit v19 on v16

--- a/solution.py
+++ b/solution.py
@@ -246,12 +246,11 @@
     positions = tensor_rank * row_count + jnp.arange(row_count, dtype=jnp.int32)
     live = positions[:, None] < seq_lengths[None, :]
     upstream = jnp.where(live[:, :, None], cotangent, jnp.zeros_like(cotangent))
-    core = group_rank % 2
-    half_width = model_width // 2
+    quarter = model_width // group_count
     front = jnp.concatenate(
         [
             normed_low.reshape(row_count, seq_count * model_width),
-            lax.dynamic_slice_in_dim(w_o.reshape(row_count, -1), core * half_width, half_width, 1),
+            lax.dynamic_slice_in_dim(w_o.reshape(row_count, -1), group_rank * quarter, quarter, 1),
         ],
         1,
     )
@@ -259,7 +258,16 @@
     wide = seq_count * model_width
     normed_full = front[:, :wide].reshape(seq_total, seq_count, model_width)
     out_mine = front[:, wide:]
-    out_other = lax.ppermute(out_mine, "group", [(g, g ^ 1) for g in range(group_count)])
+    out_pair = lax.ppermute(out_mine, "group", [(g, g ^ 2) for g in range(group_count)])
+    out_both = jnp.concatenate([out_mine, out_pair], 1)
+    out_rest = lax.ppermute(out_both, "group", [(g, g ^ 1) for g in range(group_count)])
+    quarter_ids = (group_rank, group_rank ^ 2, group_rank ^ 1, group_rank ^ 3)
+    quarter_cols = (
+        out_mine,
+        out_pair,
+        out_rest[:, :quarter],
+        out_rest[:, quarter:],
+    )
     upstream, front = lax.optimization_barrier((upstream, front))
     upstream_full = lax.all_gather(upstream, "tensor", axis=0, tiled=True)
     joint_weight = w_qkv.reshape(model_width, 3 * local_width)
@@ -297,10 +305,10 @@
         tiled=True,
     )
     attention = (
-        half_columns(
-            jnp.dot(own_rows, out_mine, preferred_element_type=jnp.float32),
-            jnp.dot(own_rows, out_other, preferred_element_type=jnp.float32),
-            core,
+        place_columns(
+            [jnp.dot(own_rows, cols, preferred_element_type=jnp.float32) for cols in quarter_cols],
+            quarter_ids,
+            quarter,
         ).reshape(
             seq_count, row_count, model_width
         )
@@ -363,17 +371,13 @@
     piece = lax.all_gather(branch_low, "tensor", axis=0, tiled=True)
     weight_grad = jnp.einsum("rse,rsd->ed", attended, piece, preferred_element_type=jnp.float32)
     branch_rows = branch_low.reshape(row_count * seq_count, model_width)
-    heads_grad = (
+    heads_grad = sum(
         jnp.dot(
-            lax.dynamic_slice_in_dim(branch_rows, core * half_width, half_width, 1),
-            out_mine.T,
+            lax.dynamic_slice_in_dim(branch_rows, qid * quarter, quarter, 1),
+            cols.T,
             preferred_element_type=jnp.float32,
         )
-        + jnp.dot(
-            lax.dynamic_slice_in_dim(branch_rows, (1 - core) * half_width, half_width, 1),
-            out_other.T,
-            preferred_element_type=jnp.float32,
-        )
+        for qid, cols in zip(quarter_ids, quarter_cols)
     ).astype(jnp.bfloat16)
     attended_grad = lax.all_to_all(heads_grad, "tensor", 1, 0, tiled=True).reshape(
         seq_total, seq_count, local_width
@@ -479,6 +483,13 @@
     return tuple(parts)
 
 
+def place_columns(blocks, ids, width):
+    out = jnp.zeros(blocks[0].shape[:-1] + (width * len(blocks),), blocks[0].dtype)
+    for block, index in zip(blocks, ids):
+        out = lax.dynamic_update_slice_in_dim(out, block, index * width, out.ndim - 1)
+    return out
+
+
 def half_columns(mine, other, core):
     return jnp.where(
         core == 0, jnp.concatenate([mine, other], 1), jnp.concatenate([other, mine], 1)

time: 597 us -> 613 us (1.027)
  waiting for transfers between devices: 274 us -> 287 us
    ppermute x1 -> x2, waiting for transfers between devices: 0.01 us -> 46.6 us  [the longest x1 46.6 us: shards(): lax.ppermute(out_mine, 'group', [(g, g ^ 2) for g in range(group_count)])]
    all_gather x1, waiting for transfers between devices: 14.6 us -> 0.01 us  [shards(): upstream_full = lax.all_gather(upstream, 'tensor', axis=0, tiled=True)]
    all_gather x1, waiting for transfers between devices: 88.1 us -> 78.5 us  [shards(): front = lax.all_gather(front, 'tensor', axis=0, tiled=True)]
    dot_general x4 -> x8, matrix products: 13.8 us -> 15 us  [the longest x4 8.25 us: shards(): jnp.dot(lax.dynamic_slice_in_dim(branch_rows, qid * quarter, quarter, 1),...]
  transfers between devices with their start and end apart: 22 -> 23, of which waited for: 12 -> 12; matrix products, arithmetic and copies ran while one was open for 27% -> 27% of each run, Pallas kernels for 7% -> 7%
where the time goes in v19:
time: 613 us; the launch traced here: 602 us
  waiting for transfers between devices  287 us (47%)
  matrix products  92.6 us (15%)
  other arithmetic  56 us (9%)
  local copies, waits for them, and re-layouts  51.9 us (8%)
  Pallas kernels  41.5 us (7%)
  starting transfers between devices  35.5 us (6%)
  blocking collectives  20.4 us (3%)
  between operations  16.6 us (3%)
    all_gather x1, waiting for transfers between devices, shards(): front = lax.all_gather(front, 'tensor', axis=0, tiled=True)  78.5 us
    reduce_scatter x1, waiting for transfers between devices, shards(): both = lax.psum_scatter(merged, 'tensor', scatter_dimension=0, tiled=True)  62.2 us
    all_gather x1, waiting for transfers between devices, shards(): second_full = lax.all_gather(second_low, 'tensor', axis=0, tiled=True)  57.6 us
    ppermute x1, waiting for transfers between devices, shards(): lax.ppermute(out_mine, 'group', [(g, g ^ 2) for g in range(group_count)])  46.6 us
    ppermute x12, waiting for transfers between devices, halving_steps(): got = lax.ppermute(send, axis, [(i, i ^ bit) for i in range(size)])  26.3 us
    pallas_call x1, Pallas kernels, attention_backward(): pl.pallas_call(kernel, out_shape=tuple((jax.ShapeDtypeStruct((n, d), jnp....  24.7 us
    all_to_all x1, blocking collectives, shards(): lax.all_to_all(heads_grad, 'tensor', 1, 0, tiled=True)  20.4 us
    reshape x4, local copies, waits for them, and re-layouts, halving_sum(): value.reshape(shape[:dim] + (groups // 2, 2, dps * rest) + shape[dim + 1:])  19.4 us
  transfers between devices with their start and end apart: 23, of which 12 were waited for; matrix products, arithmetic and copies ran while one was open for 27% of the time, Pallas kernels for 7%

profile of v19, /device:TPU:96, one launch (start us, length us, event | category | flops | bytes accessed | tf_op | source)
XLA Modules:
  0.0 601.8 jit_solution(16839838955881733589)
XLA Ops:
  16.5 78.5 %all-gather.5.cloned.1.call-done = bf16[2048,2560]{1,0:T(8,128)(2,1)} async-done(((bf16[128,2560]{1,0:T(8,128)(2,1)}), bf16[2048,2560]{1,0:T(8,128)(2,1)}) %all-gather.5.cloned.1.call-update) | async-done | bytes 10485776 | tf_op jit(solution)/shard_map/all_gather | solution.py:257
  97.6 46.6 %collective-permute-done = bf16[2048,512]{1,0:T(8,128)(2,1)S(1)} collective-permute-done((bf16[2048,512]{1,0:T(8,128)(2,1)S(1)}, bf16[2048,512]{1,0:T(8,128)(2,1)S(1)}, u32[]{:S(2)}, u32[]{:S(2)}) %collective-permute-start) | collective-permute-done | bytes 2097184 | tf_op jit(solution)/shard_map/ppermute | solution.py:261
  149.5 7.5 %fusion.37 = f32[2048,1,3,128]{3,0,2,1:T(8,128)S(1)} fusion(bf16[2048,2560]{1,0:T(8,128)(2,1)} %all-gather.5.cloned.1.call-done, bf16[2048,3,1,128]{0,3,1,2:T(8,128)(2,1)} %copy.38), kind=kOutput, calls=%fused_computation.40 | convolution fusion | flops 3221225472 | bytes 13107200 | tf_op jit(solution)/shard_map/dot_general | solution.py:274
  159.0 16.8 %shard_map.254 = (bf16[2048,128]{1,0:T(8,128)(2,1)}, f32[2048,1]{1,0:T(8,128)}) custom-call(s32[1]{0:T(128)} %dynamic_slice.32.len_ref, bf16[2048,128]{1,0:T(8,128)(2,1)} %get-tuple-element.121.q_ref, bf16[2048,128]{1,0:T(8,128)(2,1)} %fusion.89.k_ref, bf16[2048,128]{1,0:T(8,128)(2,1)} %get-tuple-element.120.v_ref), custom_call_target="tpu_custom_call" | custom-call | flops 1342177280 | bytes 2097152 | tf_op jit(solution)/shard_map/pallas_call | solution.py:85
  183.2 10.9 %all-to-all-done = bf16[16,128,128]{1,2,0:T(8,128)(2,1)S(1)} async-done(((bf16[16,128,128]{1,2,0:T(8,128)(2,1)}), bf16[16,128,128]{1,2,0:T(8,128)(2,1)S(1)}, u32[]{:S(2)}, u32[]{:S(2)}) %all-to-all-start) | async-done | bytes 524320 | tf_op jit(solution)/shard_map/all_to_all | solution.py:300
  202.9 10.6 %fusion.31 = f32[2048,1,512]{2,0,1:T(8,128)} fusion(bf16[512,2048]{1,0:T(8,128)(2,1)} %param.28, bf16[2048,1,2048]{2,0,1:T(8,128)(2,1)} %all-gather.7.cloned.1.call-done), kind=kOutput, calls=%fused_computation.37 | convolution fusion | flops 4294967296 | bytes 14680064 | tf_op jit(solution)/shard_map/rsd,fd->rsf/dot_general | solution.py:318
  213.5 57.6 %all-gather.9.cloned.1.call-done = bf16[2048,1,2048]{2,0,1:T(8,128)(2,1)} async-done(((bf16[128,1,2048]{2,0,1:T(8,128)(2,1)}), bf16[2048,1,2048]{2,0,1:T(8,128)(2,1)}) %all-gather.9.cloned.1.call-update) | async-done | bytes 8388624 | tf_op jit(solution)/shard_map/all_gather | solution.py:321
  271.2 7.0 %fusion.6 = f32[2048,512]{1,0:T(8,128)S(1)} fusion(bf16[2048,512]{1,0:T(8,128)(2,1)S(1)} %copy-done, bf16[2048,1,2048]{2,0,1:T(8,128)(2,1)} %all-gather.9.cloned.1.call-done), kind=kOutput, calls=%fused_computation.7 | convolution fusion | flops 4294967296 | bytes 14680064 | tf_op jit(solution)/shard_map/dot_general | solution.py:324
  283.9 6.9 %convert_bitcast_fusion.1 = bf16[2048,1,2048]{2,0,1:T(8,128)(2,1)} fusion(bf16[2048,512]{1,0:T(8,128)(2,1)S(1)} %get-tuple-element.110, bf16[2048,512]{1,0:T(8,128)(2,1)S(1)} %copy-done), kind=kOutput, calls=%fused_computation.14 | convolution fusion | flops 4299161600 | bytes 12582912 | tf_op jit(solution)/shard_map/rsf,df->rsd/dot_general | solution.py:345
  293.7 7.1 %fusion.28 = f32[2048,512]{1,0:T(8,128)S(1)} fusion(bf16[2048,512]{1,0:T(8,128)(2,1)S(1)} %copy-done.21, bf16[2048,1,2048]{2,0,1:T(8,128)(2,1)} %all-gather.9.cloned.1.call-done, f32[]{:T(128)S(6)} %div.71), kind=kOutput, calls=%fused_computation.36 | convolution fusion | flops 4296015872 | bytes 14680068 | tf_op jit(solution)/shard_map/rd,rf->df/dot_general | solution.py:337
  303.5 10.0 %fusion.25 = f32[512,2048]{1,0:T(8,128)} fusion(bf16[2048,1,2048]{2,0,1:T(8,128)(2,1)} %all-gather.7.cloned.1.call-done, f32[]{:T(128)S(6)} %div.71, f32[2048,512]{1,0:T(8,128)S(1)} %copy-done.16, f32[512]{0:T(512)S(1)} %copy-done.28), kind=kOutput, calls=%fused_computation.35 | convolution fusion | flops 4306501632 | bytes 16779268 | tf_op jit(solution)/shard_map/rsf,rsd->fd/dot_general | solution.py:333
  313.4 6.7 %reshape.438 = f32[512,2,2,512]{3,2,1,0:T(2,128)} reshape(f32[512,2048]{1,0:T(8,128)} %fusion.25) | data formatting | bytes 8388608 | tf_op jit(solution)/shard_map/reshape | solution.py:519
  320.1 7.3 %copy.40 = f32[512,2,2,512]{0,3,1,2:T(8,128)} copy(f32[512,2,2,512]{3,2,1,0:T(2,128)} %reshape.438) | data formatting | bytes 8388608 | tf_op jit(solution)/shard_map/reshape | solution.py:519
  341.8 10.6 %collective-permute-done.3 = bf16[2,256,512]{2,1,0:T(8,128)(2,1)S(1)} collective-permute-done((bf16[2,256,512]{2,1,0:T(8,128)(2,1)S(1)}, bf16[2,256,512]{2,1,0:T(8,128)(2,1)S(1)}, u32[]{:S(2)}, u32[]{:S(2)}) %collective-permute-start.3) | collective-permute-done | bytes 524320 | tf_op jit(solution)/shard_map/ppermute | solution.py:509
  354.2 9.5 %collective-permute-done.6 = bf16[512,2,256]{0,2,1:T(8,128)(2,1)S(1)} collective-permute-done((bf16[512,2,256]{0,2,1:T(8,128)(2,1)S(1)}, bf16[512,2,256]{0,2,1:T(8,128)(2,1)S(1)}, u32[]{:S(2)}, u32[]{:S(2)}) %collective-permute-start.6) | collective-permute-done | bytes 524320 | tf_op jit(solution)/shard_map/ppermute | solution.py:509
  370.1 7.0 %dynamic_update_slice.32 = bf16[2048,1,4096]{2,0,1:T(8,128)(2,1)} pad(bf16[2048,1,2048]{2,0,1:T(8,128)(2,1)S(1)} %convert_bitcast_fusion, bf16[]{:T(256)} %constant.151.clone.1), padding=0_0x0_0x2048_0 | pad | bytes 25165826 | tf_op jit(solution)/shard_map/dynamic_update_slice | solution.py:354
  392.8 20.4 %all_to_all.53 = bf16[128,16,128]{2,0,1:T(8,128)(2,1)} all-to-all(bf16[128,16,128]{2,0,1:T(8,128)(2,1)S(1)} %bitcast.194), channel_id=1, replica_groups=mesh['group'=4,'dp'=2,'tensor'=16] {'tensor'}, dimensions={1} | all-to-all | bytes 1048576 | tf_op jit(solution)/shard_map/all_to_all | solution.py:382
  413.2 24.7 %shard_map.255 = (bf16[2048,128]{1,0:T(8,128)(2,1)}, bf16[2048,128]{1,0:T(8,128)(2,1)}, bf16[2048,128]{1,0:T(8,128)(2,1)}) custom-call(s32[1]{0:T(128)} %dynamic_slice.32.len_ref, bf16[2048,128]{1,0:T(8,128)(2,1)} %get-tuple-element.121.q_ref, bf16[2048,128]{1,0:T(8,128)(2,1)} %fusion.89.k_ref, bf16[2048,128]{1,0:T(8,128)(2,1)} %get-tuple-element.120.v_ref, ...), custom_call_target="tpu_custom_call" | custom-call | flops 2684354560 | bytes 4194304 | tf_op jit(solution)/shard_map/pallas_call | solution.py:185
  441.3 9.7 %bitcast_dynamic-update-slice_fusion = bf16[2048,1,4096]{2,0,1:T(8,128)(2,1)} fusion(bf16[2048,1,4096]{2,0,1:T(8,128)(2,1)} %dynamic_update_slice.32, bf16[2048,384]{0,1:T(8,128)(2,1)} %bitcast.195, bf16[2048,384]{0,1:T(8,128)(2,1)} %bitcast.190), kind=kOutput, calls=%fused_computation.2 | convolution fusion | flops 3225419776 | bytes 11534336 | tf_op jit(solution)/shard_map/rsc,dc->rsd/dot_general | solution.py:407
  451.7 7.6 %fusion.34 = f32[2048,384]{1,0:T(8,128)S(1)} fusion(bf16[2048,384]{0,1:T(8,128)(2,1)} %bitcast.196, bf16[2048,2560]{1,0:T(8,128)(2,1)} %all-gather.5.cloned.1.call-done, f32[]{:T(128)S(6)} %div.71), kind=kOutput, calls=%fused_computation.39 | convolution fusion | flops 3222011904 | bytes 13107204 | tf_op jit(solution)/shard_map/rd,rc->dc/dot_general | solution.py:401
  463.3 7.5 %all-to-all-start.2 = ((f32[128,1,176]{2,1,0:T(1,128)}), f32[128,1,176]{2,1,0:T(1,128)S(1)}, u32[]{:S(2)}, u32[]{:S(2)}) async-start(f32[128,1,176]{2,1,0:T(1,128)} %copy.44), calls=%async_computation.4 | async-start | bytes 262144 | tf_op jit(solution)/shard_map/all_to_all | solution.py:476
  484.1 5.8 fusion.41
  511.3 62.2 %reduce-scatter.5.cloned.1.call-done = bf16[128,1,4096]{2,0,1:T(8,128)(2,1)} async-done(((bf16[2048,1,4096]{2,0,1:T(8,128)(2,1)}), bf16[128,1,4096]{2,0,1:T(8,128)(2,1)}) %reduce-scatter.5.cloned.1.call-update) | async-done | bytes 1048592 | tf_op jit(solution)/shard_map/reduce_scatter | solution.py:415
  578.6 8.2 %all-to-all-start.3 = ((f32[128,1,16]{2,1,0:T(1,128)}), f32[128,1,16]{2,1,0:T(1,128)S(1)}, u32[]{:S(2)}, u32[]{:S(2)}) async-start(f32[128,1,16]{2,1,0:T(1,128)} %bitcast.65), calls=%async_computation.5 | async-start | bytes 131072 | tf_op jit(solution)/shard_map/all_to_all | solution.py:476
  (226 shorter events, 138.7 us)
Async XLA Ops:
  7.2 264.0 %copy-start = (bf16[2048,512]{1,0:T(8,128)(2,1)S(1)}, bf16[2048,512]{1,0:T(8,128)(2,1)}, u32[]{:S(2)}) copy-start(bf16[2048,512]{1,0:T(8,128)(2,1)} %param.26) | copy-start | bytes 6291460
  7.2 87.8 %all-gather.5.cloned.1.call-start = ((), (), s32[]{:S(2)}) async-start(), calls=%async_computation.6 | async-start | bytes 11141120 | tf_op jit(solution)/shard_map/all_gather | solution.py:257
  13.2 189.4 %all-gather.7.cloned.1.call-start = ((), (), s32[]{:S(2)}) async-start(), calls=%async_computation.7 | async-start | bytes 8912896 | tf_op jit(solution)/shard_map/all_gather | solution.py:272
  96.7 47.4 %collective-permute-start = (bf16[2048,512]{1,0:T(8,128)(2,1)S(1)}, bf16[2048,512]{1,0:T(8,128)(2,1)S(1)}, u32[]{:S(2)}, u32[]{:S(2)}) collective-permute-start(bf16[2048,512]{1,0:T(8,128)(2,1)S(1)} %slice.193), channel_id=1, source_target_pairs={{0,64},{32,96},{64,0},{96,32},{1,65},{33,97},{65,1},{97,33},{2,66}... | collective-permute-start | bytes 6291464 | tf_op jit(solution)/shard_map/ppermute | solution.py:261
  146.8 50.1 %collective-permute-start.1 = (bf16[2048,1024]{1,0:T(8,128)(2,1)}, bf16[2048,1024]{1,0:T(8,128)(2,1)}, u32[]{:S(2)}, u32[]{:S(2)}) collective-permute-start(bf16[2048,1024]{1,0:T(8,128)(2,1)} %pad_maximum_fusion), channel_id=1, source_target_pairs={{0,32},{32,0},{64,96},{96,64},{1,33},{33,1},{65,97},{97,65},{2,34}... | collective-permute-start | bytes 12582920 | tf_op jit(solution)/shard_map/ppermute | solution.py:263
  177.8 16.3 %all-to-all-start = ((bf16[16,128,128]{1,2,0:T(8,128)(2,1)}), bf16[16,128,128]{1,2,0:T(8,128)(2,1)S(1)}, u32[]{:S(2)}, u32[]{:S(2)}) async-start(bf16[16,128,128]{1,2,0:T(8,128)(2,1)} %copy.39), calls=%async_computation | async-start | bytes 1048576 | tf_op jit(solution)/shard_map/all_to_all | solution.py:300
  183.1 88.0 %all-gather.9.cloned.1.call-start = ((), (), s32[]{:S(2)}) async-start(), calls=%async_computation.8 | async-start | bytes 8912896 | tf_op jit(solution)/shard_map/all_gather | solution.py:321
  202.7 176.3 %reduce-scatter.3.cloned.1.call-start = ((), (), s32[]{:S(2)}) async-start(), calls=%async_computation.9 | async-start | bytes 8912896 | tf_op jit(solution)/shard_map/reduce_scatter | solution.py:348
  290.9 193.3 %all-gather.11.cloned.1.call-start = ((), (), s32[]{:S(2)}) async-start(), calls=%async_computation.11 | async-start | bytes 8912896 | tf_op jit(solution)/shard_map/all_gather | solution.py:371
  303.0 31.3 %collective-permute-start.2 = (bf16[4,256,512]{2,1,0:T(8,128)(2,1)S(1)}, bf16[4,256,512]{2,1,0:T(8,128)(2,1)S(1)}, u32[]{:S(2)}, u32[]{:S(2)}) collective-permute-start(bf16[4,256,512]{2,1,0:T(8,128)(2,1)S(1)} %bitcast.197), channel_id=1, source_target_pairs={{0,32},{32,0},{64,96},{96,64},{1,33},{33,1},{65,97},{97,65},{2,34}... | collective-permute-start | bytes 3145736 | tf_op jit(solution)/shard_map/ppermute | solution.py:509
  331.1 7.4 %collective-permute-start.5 = (bf16[512,4,256]{0,2,1:T(8,128)(2,1)}, bf16[512,4,256]{0,2,1:T(8,128)(2,1)}, u32[]{:S(2)}, u32[]{:S(2)}) collective-permute-start(bf16[512,4,256]{0,2,1:T(8,128)(2,1)} %select_convert_fusion), channel_id=1, source_target_pairs={{0,32},{32,0},{64,96},{96,64},{1,33},{33,1},{65,97},{97,65},{2,34}... | collective-permute-start | bytes 3145736 | tf_op jit(solution)/shard_map/ppermute | solution.py:509
  337.6 14.8 %collective-permute-start.3 = (bf16[2,256,512]{2,1,0:T(8,128)(2,1)S(1)}, bf16[2,256,512]{2,1,0:T(8,128)(2,1)S(1)}, u32[]{:S(2)}, u32[]{:S(2)}) collective-permute-start(bf16[2,256,512]{2,1,0:T(8,128)(2,1)S(1)} %select_convert_fusion.4), channel_id=1, source_target_pairs={{0,64},{32,96},{64,0},{96,32},{1,65},{33,97},{65,1},{97,33},{2,66}... | collective-permute-start | bytes 1572872 | tf_op jit(solution)/shard_map/ppermute | solution.py:509
  340.6 23.1 %collective-permute-start.6 = (bf16[512,2,256]{0,2,1:T(8,128)(2,1)S(1)}, bf16[512,2,256]{0,2,1:T(8,128)(2,1)S(1)}, u32[]{:S(2)}, u32[]{:S(2)}) collective-permute-start(bf16[512,2,256]{0,2,1:T(8,128)(2,1)S(1)} %select_convert_fusion.3), channel_id=1, source_target_pairs={{0,64},{32,96},{64,0},{96,32},{1,65},{33,97},{65,1},{97,33},{2,66}... | collective-permute-start | bytes 1572872 | tf_op jit(solution)/shard_map/ppermute | solution.py:509
  352.8 24.3 %collective-permute-start.4 = (bf16[1,256,512]{2,1,0:T(8,128)(2,1)S(1)}, bf16[1,256,512]{2,1,0:T(8,128)(2,1)S(1)}, u32[]{:S(2)}, u32[]{:S(2)}) collective-permute-start(bf16[1,256,512]{2,1,0:T(8,128)(2,1)S(1)} %select_convert_fusion.8), channel_id=1, source_target_pairs={{0,16},{16,0},{1,17},{17,1},{2,18},{18,2},{3,19},{19,3},{4,20},{20... | collective-permute-start | bytes 786440 | tf_op jit(solution)/shard_map/ppermute | solution.py:509
  364.0 14.0 %collective-permute-start.7 = (bf16[512,1,256]{0,2,1:T(8,128)(2,1)S(1)}, bf16[512,1,256]{0,2,1:T(8,128)(2,1)S(1)}, u32[]{:S(2)}, u32[]{:S(2)}) collective-permute-start(bf16[512,1,256]{0,2,1:T(8,128)(2,1)S(1)} %select_convert_fusion.7), channel_id=1, source_target_pairs={{0,16},{16,0},{1,17},{17,1},{2,18},{18,2},{3,19},{19,3},{4,20},{20... | collective-permute-start | bytes 786440 | tf_op jit(solution)/shard_map/ppermute | solution.py:509
  384.2 189.2 %reduce-scatter.5.cloned.1.call-start = ((), (), s32[]{:S(2)}) async-start(), calls=%async_computation.10 | async-start | bytes 17825792 | tf_op jit(solution)/shard_map/reduce_scatter | solution.py:415
  460.5 20.3 %collective-permute-start.8 = (bf16[4,256,384]{2,1,0:T(8,128)(2,1)}, bf16[4,256,384]{2,1,0:T(8,128)(2,1)}, u32[]{:S(2)}, u32[]{:S(2)}) collective-permute-start(bf16[4,256,384]{2,1,0:T(8,128)(2,1)} %bitcast.56), channel_id=1, source_target_pairs={{0,32},{32,0},{64,96},{96,64},{1,33},{33,1},{65,97},{97,65},{2,34}... | collective-permute-start | bytes 2359304 | tf_op jit(solution)/shard_map/ppermute | solution.py:509
  463.3 16.2 %all-to-all-start.2 = ((f32[128,1,176]{2,1,0:T(1,128)}), f32[128,1,176]{2,1,0:T(1,128)S(1)}, u32[]{:S(2)}, u32[]{:S(2)}) async-start(f32[128,1,176]{2,1,0:T(1,128)} %copy.44), calls=%async_computation.4 | async-start | bytes 262144 | tf_op jit(solution)/shard_map/all_to_all | solution.py:476
  482.7 14.1 %collective-permute-start.9 = (bf16[2,256,384]{2,1,0:T(8,128)(2,1)S(1)}, bf16[2,256,384]{2,1,0:T(8,128)(2,1)}, u32[]{:S(2)}, u32[]{:S(2)}) collective-permute-start(bf16[2,256,384]{2,1,0:T(8,128)(2,1)S(1)} %select_convert_fusion.5), channel_id=1, source_target_pairs={{0,64},{32,96},{64,0},{96,32},{1,65},{33,97},{65,1},{97,33},{2,66}... | collective-permute-start | bytes 1179656 | tf_op jit(solution)/shard_map/ppermute | solution.py:509
  496.7 1.6 collective-permute-start.11
  498.5 6.4 %collective-permute-start.12 = (bf16[1,128,2,256]{1,3,2,0:T(8,128)(2,1)S(1)}, bf16[1,128,2,256]{1,3,2,0:T(8,128)(2,1)S(1)}, u32[]{:S(2)}, u32[]{:S(2)}) collective-permute-start(bf16[1,128,2,256]{1,3,2,0:T(8,128)(2,1)S(1)} %select_convert_fusion.10), channel_id=1, source_target_pairs={{0,64},{32,96},{64,0},{96,32},{1,65},{33,97},{65,1},{97,33},{2,66}... | collective-permute-start | bytes 393224 | tf_op jit(solution)/shard_map/ppermute | solution.py:509
  499.4 10.7 %collective-permute-start.10 = (bf16[1,256,384]{2,1,0:T(8,128)(2,1)S(1)}, bf16[1,256,384]{2,1,0:T(8,128)(2,1)S(1)}, u32[]{:S(2)}, u32[]{:S(2)}) collective-permute-start(bf16[1,256,384]{2,1,0:T(8,128)(2,1)S(1)} %select_convert_fusion.9), channel_id=1, source_target_pairs={{0,16},{16,0},{1,17},{17,1},{2,18},{18,2},{3,19},{19,3},{4,20},{20... | collective-permute-start | bytes 589832 | tf_op jit(solution)/shard_map/ppermute | solution.py:509
  504.9 6.3 %collective-permute-start.13 = (bf16[1,128,1,256]{1,3,2,0:T(8,128)(2,1)S(1)}, bf16[1,128,1,256]{1,3,2,0:T(8,128)(2,1)S(1)}, u32[]{:S(2)}, u32[]{:S(2)}) collective-permute-start(bf16[1,128,1,256]{1,3,2,0:T(8,128)(2,1)S(1)} %select_convert_fusion.11), channel_id=1, source_target_pairs={{0,16},{16,0},{1,17},{17,1},{2,18},{18,2},{3,19},{19,3},{4,20},{20... | collective-permute-start | bytes 196616 | tf_op jit(solution)/shard_map/ppermute | solution.py:509
  578.6 15.4 %all-to-all-start.3 = ((f32[128,1,16]{2,1,0:T(1,128)}), f32[128,1,16]{2,1,0:T(1,128)S(1)}, u32[]{:S(2)}, u32[]{:S(2)}) async-start(f32[128,1,16]{2,1,0:T(1,128)} %bitcast.65), calls=%async_computation.5 | async-start | bytes 131072 | tf_op jit(solution)/shard_map/all_to_all | solution.py:476
  (34 other events, 698.3 us)
Sparse Core Ops, SparseCore 0:
  13.4 81.5 all-gather.4
  97.1 70.3 all-gather.6
  202.8 68.3 all-gather.8
  291.0 84.6 reduce-scatter.2
  384.3 74.5 all-gather.10
  462.2 111.2 reduce-scatter.4

commit v20 on v16

--- a/solution.py
+++ b/solution.py
@@ -261,7 +261,16 @@
     out_mine = front[:, wide:]
     out_other = lax.ppermute(out_mine, "group", [(g, g ^ 1) for g in range(group_count)])
     upstream, front = lax.optimization_barrier((upstream, front))
-    upstream_full = lax.all_gather(upstream, "tensor", axis=0, tiled=True)
+    tensor_count_static = seq_total // row_count
+    upstream_full = lax.all_to_all(
+        jnp.broadcast_to(upstream[None], (tensor_count_static,) + upstream.shape).reshape(
+            (tensor_count_static * row_count,) + upstream.shape[1:]
+        ),
+        "tensor",
+        0,
+        0,
+        tiled=True,
+    )
     joint_weight = w_qkv.reshape(model_width, 3 * local_width)
     projected = jnp.dot(
         normed_full.reshape(seq_total * seq_count, model_width),
@@ -309,7 +318,6 @@
     middle = inputs + attention
     act_grad = jnp.einsum("rsd,fd->rsf", upstream_full, w_out, preferred_element_type=jnp.float32)
     second_low = layer_norm(middle, ln2_gain, ln2_bias).astype(jnp.bfloat16)
-    second_low, upstream_full = lax.optimization_barrier((second_low, upstream_full))
     second_full = lax.all_gather(second_low, "tensor", axis=0, tiled=True)
     second_full, act_grad = lax.optimization_barrier((second_full, act_grad))
     pre_act = (

time: 597 us -> 702 us (1.18)
  blocking collectives: 20.2 us -> 145 us
  waiting for transfers between devices: 274 us -> 197 us
  local copies, waits for them, and re-layouts: 53.7 us -> 89.6 us
  other arithmetic: 53.7 us -> 65.8 us
  matrix products: 91.1 us -> 101 us
    all_to_all x0 -> x1, blocking collectives: none -> 126 us  [shards(): lax.all_to_all(jnp.broadcast_to(upstream[None], (tensor_count_static,) +...]
    all_gather x1, waiting for transfers between devices: 62.4 us -> 0.01 us  [shards(): second_full = lax.all_gather(second_low, 'tensor', axis=0, tiled=True)]
    unnamed x67 -> x77, local copies, waits for them, and re-layouts: 11 us -> 42 us
    all_gather x1 -> x0, waiting for transfers between devices: 14.6 us -> none  [shards(): upstream_full = lax.all_gather(upstream, 'tensor', axis=0, tiled=True)]
    broadcast_in_dim x0 -> x1, other arithmetic: none -> 12.6 us  [shards(): jnp.broadcast_to(upstream[None], (tensor_count_static,) + upstream.shape)]
  transfers between devices with their start and end apart: 22 -> 21, of which waited for: 12 -> 10; matrix products, arithmetic and copies ran while one was open for 27% -> 30% of each run, Pallas kernels for 7% -> 6%
where the time goes in v20:
time: 702 us; the launch traced here: 691 us
  waiting for transfers between devices  197 us (28%)
  blocking collectives  145 us (21%)
  matrix products  101 us (14%)
  local copies, waits for them, and re-layouts  89.6 us (13%)
  other arithmetic  65.8 us (9%)
  Pallas kernels  41.4 us (6%)
  starting transfers between devices  34.1 us (5%)
  between operations  16.2 us (2%)
    all_to_all x1, blocking collectives, shards(): lax.all_to_all(jnp.broadcast_to(upstream[None], (tensor_count_static,) +...  126 us
    all_gather x1, waiting for transfers between devices, shards(): front = lax.all_gather(front, 'tensor', axis=0, tiled=True)  91.3 us
    reduce_scatter x1, waiting for transfers between devices, shards(): both = lax.psum_scatter(merged, 'tensor', scatter_dimension=0, tiled=True)  62.2 us
    unnamed x77, local copies, waits for them, and re-layouts  42 us
    ppermute x12, waiting for transfers between devices, halving_steps(): got = lax.ppermute(send, axis, [(i, i ^ bit) for i in range(size)])  26.8 us
    pallas_call x1, Pallas kernels, attention_backward(): pl.pallas_call(kernel, out_shape=tuple((jax.ShapeDtypeStruct((n, d), jnp....  24.6 us
    reshape x4, local copies, waits for them, and re-layouts, halving_sum(): value.reshape(shape[:dim] + (groups // 2, 2, dps * rest) + shape[dim + 1:])  19.5 us
    all_to_all x1, blocking collectives, shards(): lax.all_to_all(heads_grad, 'tensor', 1, 0, tiled=True)  19 us
  transfers between devices with their start and end apart: 21, of which 10 were waited for; matrix products, arithmetic and copies ran while one was open for 30% of the time, Pallas kernels for 6%

profile of v20, /device:TPU:96, one launch (start us, length us, event | category | flops | bytes accessed | tf_op | source)
XLA Modules:
  0.0 690.6 jit_solution(3138264302933328665)
XLA Ops:
  13.4 91.3 %all-gather.4.cloned.1.call-done = bf16[2048,3072]{1,0:T(8,128)(2,1)} async-done(((bf16[128,3072]{1,0:T(8,128)(2,1)}), bf16[2048,3072]{1,0:T(8,128)(2,1)}) %all-gather.4.cloned.1.call-update) | async-done | bytes 12582928 | tf_op jit(solution)/shard_map/all_gather | solution.py:258
  112.6 7.4 %fusion.39 = f32[2048,1,3,128]{3,0,2,1:T(8,128)S(1)} fusion(bf16[2048,3072]{1,0:T(8,128)(2,1)} %all-gather.4.cloned.1.call-done, bf16[2048,3,1,128]{0,3,1,2:T(8,128)(2,1)} %copy.48), kind=kOutput, calls=%fused_computation.41 | convolution fusion | flops 3221225472 | bytes 13107200 | tf_op jit(solution)/shard_map/dot_general | solution.py:275
  121.9 16.8 %shard_map.254 = (bf16[2048,128]{1,0:T(8,128)(2,1)}, f32[2048,1]{1,0:T(8,128)}) custom-call(s32[1]{0:T(128)} %dynamic_slice.22.len_ref, bf16[2048,128]{1,0:T(8,128)(2,1)} %get-tuple-element.131.q_ref, bf16[2048,128]{1,0:T(8,128)(2,1)} %fusion.68.k_ref, bf16[2048,128]{1,0:T(8,128)(2,1)} %get-tuple-element.130.v_ref), custom_call_target="tpu_custom_call" | custom-call | flops 1342177280 | bytes 2097152 | tf_op jit(solution)/shard_map/pallas_call | solution.py:85
  146.1 12.1 %all-to-all-done = bf16[16,128,128]{1,2,0:T(8,128)(2,1)S(1)} async-done(((bf16[16,128,128]{1,2,0:T(8,128)(2,1)}), bf16[16,128,128]{1,2,0:T(8,128)(2,1)S(1)}, u32[]{:S(2)}, u32[]{:S(2)}) %all-to-all-start) | async-done | bytes 524320 | tf_op jit(solution)/shard_map/all_to_all | solution.py:301
  172.8 12.6 %reduce.22 = bf16[2048,2048]{1,0:T(8,128)(2,1)} reduce(bf16[2048,1,2048]{2,0,1:T(8,128)(2,1)} %bitcast.158, bf16[]{:T(256)} %broadcast.275), dimensions={1}, to_apply=%copy.50.reduce_sub_computation | reduce | bytes 16777218 | tf_op jit(solution)/shard_map/broadcast_in_dim | solution.py:266
  185.4 14.6 %reshape.534 = bf16[16,2,131072]{2,1,0:T(2,128)(2,1)} reshape(bf16[2048,2048]{1,0:T(8,128)(2,1)} %reduce.22) | data formatting | bytes 16777216
  200.1 126.1 %all_to_all.58 = bf16[16,2,131072]{2,1,0:T(2,128)(2,1)} all-to-all(bf16[16,2,131072]{2,1,0:T(2,128)(2,1)} %reshape.534), channel_id=1, replica_groups=mesh['group'=4,'dp'=2,'tensor'=16] {'tensor'}, dimensions={0} | all-to-all | bytes 16777216 | tf_op jit(solution)/shard_map/all_to_all | solution.py:265
  326.2 16.3 %reshape.535 = bf16[2048,1,2048]{2,1,0:T(2,128)(2,1)} reshape(bf16[16,2,131072]{2,1,0:T(2,128)(2,1)} %all_to_all.58) | data formatting | bytes 16777216
  342.5 14.3 %fusion.31 = f32[2048,1,512]{2,0,1:T(8,128)} fusion(bf16[512,2048]{1,0:T(8,128)(2,1)} %param.28, bf16[2048,1,2048]{2,1,0:T(2,128)(2,1)} %reshape.535), kind=kOutput, calls=%fused_computation.36 | convolution fusion | flops 4294967296 | bytes 14680064 | tf_op jit(solution)/shard_map/rsd,fd->rsf/dot_general | solution.py:319
  356.8 7.0 %fusion.8 = f32[2048,512]{1,0:T(8,128)S(1)} fusion(bf16[2048,512]{1,0:T(8,128)(2,1)S(1)} %copy-done, bf16[2048,1,2048]{2,0,1:T(8,128)(2,1)} %all-gather.6.cloned.1.call-done), kind=kOutput, calls=%fused_computation.9 | convolution fusion | flops 4294967296 | bytes 14680064 | tf_op jit(solution)/shard_map/dot_general | solution.py:324
  369.6 7.1 %convert_bitcast_fusion.1 = bf16[2048,1,2048]{2,0,1:T(8,128)(2,1)} fusion(bf16[2048,512]{1,0:T(8,128)(2,1)S(1)} %get-tuple-element.120, bf16[2048,512]{1,0:T(8,128)(2,1)S(1)} %copy-done), kind=kOutput, calls=%fused_computation.14 | convolution fusion | flops 4299161600 | bytes 12582912 | tf_op jit(solution)/shard_map/rsf,df->rsd/dot_general | solution.py:345
  379.6 7.1 %fusion.28 = f32[2048,512]{1,0:T(8,128)S(1)} fusion(bf16[2048,512]{1,0:T(8,128)(2,1)S(1)} %copy-done.19, bf16[2048,1,2048]{2,0,1:T(8,128)(2,1)} %all-gather.6.cloned.1.call-done, f32[]{:T(128)S(6)} %div.71), kind=kOutput, calls=%fused_computation.35 | convolution fusion | flops 4296015872 | bytes 14680068 | tf_op jit(solution)/shard_map/rd,rf->df/dot_general | solution.py:337
  388.9 16.0 %fusion.25 = f32[512,2048]{1,0:T(8,128)} fusion(bf16[2048,1,2048]{2,1,0:T(2,128)(2,1)} %reshape.535, f32[]{:T(128)S(6)} %div.71, f32[2048,512]{1,0:T(8,128)S(1)} %copy-done.13, f32[512]{0:T(512)S(1)} %copy-done.30), kind=kOutput, calls=%fused_computation.34 | convolution fusion | flops 4306501632 | bytes 16779268 | tf_op jit(solution)/shard_map/rsf,rsd->fd/dot_general | solution.py:333
  411.7 7.3 %copy.51 = f32[512,2,2,512]{0,3,1,2:T(8,128)} copy(f32[512,2,2,512]{3,2,1,0:T(2,128)} %reshape.508) | data formatting | bytes 8388608 | tf_op jit(solution)/shard_map/reshape | solution.py:516
  433.9 10.7 %collective-permute-done.2 = bf16[2,256,512]{2,1,0:T(8,128)(2,1)S(1)} collective-permute-done((bf16[2,256,512]{2,1,0:T(8,128)(2,1)S(1)}, bf16[2,256,512]{2,1,0:T(8,128)(2,1)S(1)}, u32[]{:S(2)}, u32[]{:S(2)}) %collective-permute-start.2) | collective-permute-done | bytes 524320 | tf_op jit(solution)/shard_map/ppermute | solution.py:506
  445.9 9.9 %collective-permute-done.5 = bf16[512,2,256]{0,2,1:T(8,128)(2,1)S(1)} collective-permute-done((bf16[512,2,256]{0,2,1:T(8,128)(2,1)S(1)}, bf16[512,2,256]{0,2,1:T(8,128)(2,1)S(1)}, u32[]{:S(2)}, u32[]{:S(2)}) %collective-permute-start.5) | collective-permute-done | bytes 524320 | tf_op jit(solution)/shard_map/ppermute | solution.py:506
  461.8 6.9 %dynamic_update_slice.12 = bf16[2048,1,4096]{2,0,1:T(8,128)(2,1)} pad(bf16[2048,1,2048]{2,0,1:T(8,128)(2,1)S(1)} %convert_bitcast_fusion, bf16[]{:T(256)} %constant.147.clone.1), padding=0_0x0_0x2048_0 | pad | bytes 25165826 | tf_op jit(solution)/shard_map/dynamic_update_slice | solution.py:354
  482.9 19.0 %all_to_all.59 = bf16[128,16,128]{2,0,1:T(8,128)(2,1)} all-to-all(bf16[128,16,128]{2,0,1:T(8,128)(2,1)S(1)} %bitcast.175), channel_id=1, replica_groups=mesh['group'=4,'dp'=2,'tensor'=16] {'tensor'}, dimensions={1} | all-to-all | bytes 1048576 | tf_op jit(solution)/shard_map/all_to_all | solution.py:386
  501.8 24.6 %shard_map.255 = (bf16[2048,128]{1,0:T(8,128)(2,1)}, bf16[2048,128]{1,0:T(8,128)(2,1)}, bf16[2048,128]{1,0:T(8,128)(2,1)}) custom-call(s32[1]{0:T(128)} %dynamic_slice.22.len_ref, bf16[2048,128]{1,0:T(8,128)(2,1)} %get-tuple-element.131.q_ref, bf16[2048,128]{1,0:T(8,128)(2,1)} %fusion.68.k_ref, bf16[2048,128]{1,0:T(8,128)(2,1)} %get-tuple-element.130.v_ref, ...), custom_call_target="tpu_custom_call" | custom-call | flops 2684354560 | bytes 4194304 | tf_op jit(solution)/shard_map/pallas_call | solution.py:185
  529.9 9.7 %bitcast_dynamic-update-slice_fusion = bf16[2048,1,4096]{2,0,1:T(8,128)(2,1)} fusion(bf16[2048,1,4096]{2,0,1:T(8,128)(2,1)} %dynamic_update_slice.12, bf16[2048,384]{0,1:T(8,128)(2,1)} %bitcast.176, bf16[2048,384]{0,1:T(8,128)(2,1)} %bitcast.169), kind=kOutput, calls=%fused_computation.6 | convolution fusion | flops 3225419776 | bytes 11534336 | tf_op jit(solution)/shard_map/rsc,dc->rsd/dot_general | solution.py:411
  540.3 7.6 %fusion.36 = f32[2048,384]{1,0:T(8,128)S(1)} fusion(bf16[2048,384]{0,1:T(8,128)(2,1)} %bitcast.177, bf16[2048,3072]{1,0:T(8,128)(2,1)} %all-gather.4.cloned.1.call-done, f32[]{:T(128)S(6)} %div.71), kind=kOutput, calls=%fused_computation.40 | convolution fusion | flops 3222011904 | bytes 13107204 | tf_op jit(solution)/shard_map/rd,rc->dc/dot_general | solution.py:405
  551.9 8.0 %all-to-all-start.3 = ((f32[128,1,176]{2,1,0:T(1,128)}), f32[128,1,176]{2,1,0:T(1,128)S(1)}, u32[]{:S(2)}, u32[]{:S(2)}) async-start(f32[128,1,176]{2,1,0:T(1,128)} %copy.55), calls=%async_computation.5 | async-start | bytes 262144 | tf_op jit(solution)/shard_map/all_to_all | solution.py:480
  600.3 62.2 %reduce-scatter.5.cloned.1.call-done = bf16[128,1,4096]{2,0,1:T(8,128)(2,1)} async-done(((bf16[2048,1,4096]{2,0,1:T(8,128)(2,1)}), bf16[128,1,4096]{2,0,1:T(8,128)(2,1)}) %reduce-scatter.5.cloned.1.call-update) | async-done | bytes 1048592 | tf_op jit(solution)/shard_map/reduce_scatter | solution.py:419
  667.8 8.2 %all-to-all-start.4 = ((f32[128,1,16]{2,1,0:T(1,128)}), f32[128,1,16]{2,1,0:T(1,128)S(1)}, u32[]{:S(2)}, u32[]{:S(2)}) async-start(f32[128,1,16]{2,1,0:T(1,128)} %bitcast.61), calls=%async_computation.6 | async-start | bytes 131072 | tf_op jit(solution)/shard_map/all_to_all | solution.py:480
  (223 shorter events, 151.6 us)
Async XLA Ops:
  7.2 349.7 %copy-start = (bf16[2048,512]{1,0:T(8,128)(2,1)S(1)}, bf16[2048,512]{1,0:T(8,128)(2,1)}, u32[]{:S(2)}) copy-start(bf16[2048,512]{1,0:T(8,128)(2,1)} %param.26) | copy-start | bytes 6291460
  7.2 97.5 %all-gather.4.cloned.1.call-start = ((), (), s32[]{:S(2)}) async-start(), calls=%async_computation.7 | async-start | bytes 13369344 | tf_op jit(solution)/shard_map/all_gather | solution.py:258
  8.6 100.7 %copy-start.23 = (f32[128]{0:T(128)}, f32[128]{0:T(128)S(1)}, u32[]{:S(2)}) copy-start(f32[128]{0:T(128)S(1)} %broadcast_multiply_fusion.8) | copy-start | bytes 1540
  10.0 99.4 %copy-start.28 = (f32[128]{0:T(128)}, f32[128]{0:T(128)S(1)}, u32[]{:S(2)}) copy-start(f32[128]{0:T(128)S(1)} %fusion.79) | copy-start | bytes 1540
  109.3 51.9 %collective-permute-start = (bf16[2048,1024]{1,0:T(8,128)(2,1)}, bf16[2048,1024]{1,0:T(8,128)(2,1)}, u32[]{:S(2)}, u32[]{:S(2)}) collective-permute-start(bf16[2048,1024]{1,0:T(8,128)(2,1)} %slice.185), channel_id=1, source_target_pairs={{0,32},{32,0},{64,96},{96,64},{1,33},{33,1},{65,97},{97,65},{2,34}... | collective-permute-start | bytes 12582920 | tf_op jit(solution)/shard_map/ppermute | solution.py:262
  140.8 17.4 %all-to-all-start = ((bf16[16,128,128]{1,2,0:T(8,128)(2,1)}), bf16[16,128,128]{1,2,0:T(8,128)(2,1)S(1)}, u32[]{:S(2)}, u32[]{:S(2)}) async-start(bf16[16,128,128]{1,2,0:T(8,128)(2,1)} %copy.49), calls=%async_computation | async-start | bytes 1048576 | tf_op jit(solution)/shard_map/all_to_all | solution.py:301
  146.0 210.8 %all-gather.6.cloned.1.call-start = ((), (), s32[]{:S(2)}) async-start(), calls=%async_computation.8 | async-start | bytes 8912896 | tf_op jit(solution)/shard_map/all_gather | solution.py:321
  165.8 304.8 %reduce-scatter.3.cloned.1.call-start = ((), (), s32[]{:S(2)}) async-start(), calls=%async_computation.9 | async-start | bytes 8912896 | tf_op jit(solution)/shard_map/reduce_scatter | solution.py:348
  376.8 196.4 %all-gather.8.cloned.1.call-start = ((), (), s32[]{:S(2)}) async-start(), calls=%async_computation.11 | async-start | bytes 8912896 | tf_op jit(solution)/shard_map/all_gather | solution.py:371
  388.8 37.5 %collective-permute-start.1 = (bf16[4,256,512]{2,1,0:T(8,128)(2,1)S(1)}, bf16[4,256,512]{2,1,0:T(8,128)(2,1)S(1)}, u32[]{:S(2)}, u32[]{:S(2)}) collective-permute-start(bf16[4,256,512]{2,1,0:T(8,128)(2,1)S(1)} %bitcast.178), channel_id=1, source_target_pairs={{0,32},{32,0},{64,96},{96,64},{1,33},{33,1},{65,97},{97,65},{2,34}... | collective-permute-start | bytes 3145736 | tf_op jit(solution)/shard_map/ppermute | solution.py:506
  422.5 7.9 %collective-permute-start.4 = (bf16[512,4,256]{0,2,1:T(8,128)(2,1)}, bf16[512,4,256]{0,2,1:T(8,128)(2,1)}, u32[]{:S(2)}, u32[]{:S(2)}) collective-permute-start(bf16[512,4,256]{0,2,1:T(8,128)(2,1)} %select_convert_fusion), channel_id=1, source_target_pairs={{0,32},{32,0},{64,96},{96,64},{1,33},{33,1},{65,97},{97,65},{2,34}... | collective-permute-start | bytes 3145736 | tf_op jit(solution)/shard_map/ppermute | solution.py:506
  429.7 14.9 %collective-permute-start.2 = (bf16[2,256,512]{2,1,0:T(8,128)(2,1)S(1)}, bf16[2,256,512]{2,1,0:T(8,128)(2,1)S(1)}, u32[]{:S(2)}, u32[]{:S(2)}) collective-permute-start(bf16[2,256,512]{2,1,0:T(8,128)(2,1)S(1)} %select_convert_fusion.4), channel_id=1, source_target_pairs={{0,64},{32,96},{64,0},{96,32},{1,65},{33,97},{65,1},{97,33},{2,66}... | collective-permute-start | bytes 1572872 | tf_op jit(solution)/shard_map/ppermute | solution.py:506
  432.5 23.3 %collective-permute-start.5 = (bf16[512,2,256]{0,2,1:T(8,128)(2,1)S(1)}, bf16[512,2,256]{0,2,1:T(8,128)(2,1)S(1)}, u32[]{:S(2)}, u32[]{:S(2)}) collective-permute-start(bf16[512,2,256]{0,2,1:T(8,128)(2,1)S(1)} %select_convert_fusion.3), channel_id=1, source_target_pairs={{0,64},{32,96},{64,0},{96,32},{1,65},{33,97},{65,1},{97,33},{2,66}... | collective-permute-start | bytes 1572872 | tf_op jit(solution)/shard_map/ppermute | solution.py:506
  444.9 23.8 %collective-permute-start.3 = (bf16[1,256,512]{2,1,0:T(8,128)(2,1)S(1)}, bf16[1,256,512]{2,1,0:T(8,128)(2,1)S(1)}, u32[]{:S(2)}, u32[]{:S(2)}) collective-permute-start(bf16[1,256,512]{2,1,0:T(8,128)(2,1)S(1)} %select_convert_fusion.8), channel_id=1, source_target_pairs={{0,16},{16,0},{1,17},{17,1},{2,18},{18,2},{3,19},{19,3},{4,20},{20... | collective-permute-start | bytes 786440 | tf_op jit(solution)/shard_map/ppermute | solution.py:506
  456.1 13.6 %collective-permute-start.6 = (bf16[512,1,256]{0,2,1:T(8,128)(2,1)S(1)}, bf16[512,1,256]{0,2,1:T(8,128)(2,1)S(1)}, u32[]{:S(2)}, u32[]{:S(2)}) collective-permute-start(bf16[512,1,256]{0,2,1:T(8,128)(2,1)S(1)} %select_convert_fusion.7), channel_id=1, source_target_pairs={{0,16},{16,0},{1,17},{17,1},{2,18},{18,2},{3,19},{19,3},{4,20},{20... | collective-permute-start | bytes 786440 | tf_op jit(solution)/shard_map/ppermute | solution.py:506
  475.1 187.5 %reduce-scatter.5.cloned.1.call-start = ((), (), s32[]{:S(2)}) async-start(), calls=%async_computation.10 | async-start | bytes 17825792 | tf_op jit(solution)/shard_map/reduce_scatter | solution.py:419
  549.1 20.8 %collective-permute-start.7 = (bf16[4,256,384]{2,1,0:T(8,128)(2,1)}, bf16[4,256,384]{2,1,0:T(8,128)(2,1)}, u32[]{:S(2)}, u32[]{:S(2)}) collective-permute-start(bf16[4,256,384]{2,1,0:T(8,128)(2,1)} %bitcast.52), channel_id=1, source_target_pairs={{0,32},{32,0},{64,96},{96,64},{1,33},{33,1},{65,97},{97,65},{2,34}... | collective-permute-start | bytes 2359304 | tf_op jit(solution)/shard_map/ppermute | solution.py:506
  551.9 16.7 %all-to-all-start.3 = ((f32[128,1,176]{2,1,0:T(1,128)}), f32[128,1,176]{2,1,0:T(1,128)S(1)}, u32[]{:S(2)}, u32[]{:S(2)}) async-start(f32[128,1,176]{2,1,0:T(1,128)} %copy.55), calls=%async_computation.5 | async-start | bytes 262144 | tf_op jit(solution)/shard_map/all_to_all | solution.py:480
  571.8 14.1 %collective-permute-start.8 = (bf16[2,256,384]{2,1,0:T(8,128)(2,1)S(1)}, bf16[2,256,384]{2,1,0:T(8,128)(2,1)}, u32[]{:S(2)}, u32[]{:S(2)}) collective-permute-start(bf16[2,256,384]{2,1,0:T(8,128)(2,1)S(1)} %select_convert_fusion.5), channel_id=1, source_target_pairs={{0,64},{32,96},{64,0},{96,32},{1,65},{33,97},{65,1},{97,33},{2,66}... | collective-permute-start | bytes 1179656 | tf_op jit(solution)/shard_map/ppermute | solution.py:506
  585.8 1.6 collective-permute-start.10
  587.6 6.4 collective-permute-start.11
  588.5 10.7 %collective-permute-start.9 = (bf16[1,256,384]{2,1,0:T(8,128)(2,1)S(1)}, bf16[1,256,384]{2,1,0:T(8,128)(2,1)S(1)}, u32[]{:S(2)}, u32[]{:S(2)}) collective-permute-start(bf16[1,256,384]{2,1,0:T(8,128)(2,1)S(1)} %select_convert_fusion.9), channel_id=1, source_target_pairs={{0,16},{16,0},{1,17},{17,1},{2,18},{18,2},{3,19},{19,3},{4,20},{20... | collective-permute-start | bytes 589832 | tf_op jit(solution)/shard_map/ppermute | solution.py:506
  594.1 6.2 collective-permute-start.12
  667.8 15.4 %all-to-all-start.4 = ((f32[128,1,16]{2,1,0:T(1,128)}), f32[128,1,16]{2,1,0:T(1,128)S(1)}, u32[]{:S(2)}, u32[]{:S(2)}) async-start(f32[128,1,16]{2,1,0:T(1,128)} %bitcast.61), calls=%async_computation.6 | async-start | bytes 131072 | tf_op jit(solution)/shard_map/all_to_all | solution.py:480
  (33 other events, 829.8 us)
Sparse Core Ops, SparseCore 0:
  13.5 91.1 all-gather.3
  165.9 151.1 all-gather.5
  376.9 82.9 reduce-scatter.2
  475.2 73.0 all-gather.7
  551.5 110.9 reduce-scatter.4

commit v21 on v16

--- a/solution.py
+++ b/solution.py
@@ -204,6 +204,90 @@
             bytes_accessed=8 * n * d * 2,
         ),
     )(length, q, k, v, do, lse)
+
+
+def _attn_bwd1_kernel(len_ref, q_ref, k_ref, v_ref, do_ref, lse_ref, delta_ref, dq_ref, dk_ref, dv_ref,
+                      dk_acc, dv_acc, *, block_q, block_k, scale):
+    i = pl.program_id(0)
+    length = len_ref[0]
+
+    @pl.when(i == 0)
+    def _():
+        dk_acc[...] = jnp.zeros_like(dk_acc)
+        dv_acc[...] = jnp.zeros_like(dv_acc)
+
+    live = i * block_q < length
+
+    @pl.when(live)
+    def _():
+        count = _key_blocks(i, block_q, block_k, length)
+        q = q_ref[...]
+        do = do_ref[...]
+        lse = lse_ref[...]
+        delta = delta_ref[...]
+
+        def step(j, dq):
+            first = pl.multiple_of(j * block_k, block_k)
+            k = k_ref[pl.ds(first, block_k), :]
+            v = v_ref[pl.ds(first, block_k), :]
+            s = lax.dot_general(q, k, (((1,), (1,)), ((), ())), preferred_element_type=jnp.float32)
+            edge = (first + block_k > i * block_q) | (first + block_k > length)
+            p = lax.cond(
+                edge,
+                lambda w: jnp.where(
+                    _valid(i * block_q, first, block_q, block_k, length),
+                    jnp.exp(jnp.where(_valid(i * block_q, first, block_q, block_k, length), w, NEGATIVE) - lse),
+                    0.0,
+                ),
+                lambda w: jnp.exp(w - lse),
+                s * scale,
+            )
+            dp = lax.dot_general(do, v, (((1,), (1,)), ((), ())), preferred_element_type=jnp.float32)
+            ds = (p * (dp - delta)).astype(jnp.bfloat16)
+            dk_acc[pl.ds(first, block_k), :] += lax.dot_general(
+                ds, q, (((0,), (0,)), ((), ())), preferred_element_type=jnp.float32)
+            dv_acc[pl.ds(first, block_k), :] += lax.dot_general(
+                p.astype(jnp.bfloat16), do, (((0,), (0,)), ((), ())), preferred_element_type=jnp.float32)
+            return dq + jnp.dot(ds, k, preferred_element_type=jnp.float32)
+
+        dq = lax.fori_loop(0, count, step, jnp.zeros(dq_ref.shape, jnp.float32))
+        dq_ref[...] = (dq * scale).astype(dq_ref.dtype)
+
+    @pl.when(jnp.logical_not(live))
+    def _():
+        dq_ref[...] = jnp.zeros_like(dq_ref)
+
+    @pl.when(i == pl.num_programs(0) - 1)
+    def _():
+        dk_ref[...] = (dk_acc[...] * scale).astype(dk_ref.dtype)
+        dv_ref[...] = dv_acc[...].astype(dv_ref.dtype)
+
+
+def attention_backward1(q, k, v, do, lse, delta, length, *, block_q=512, block_k=512):
+    n, d = q.shape
+    scale = 1.0 / math.sqrt(d)
+    kernel = partial(_attn_bwd1_kernel, block_q=block_q, block_k=block_k, scale=scale)
+    pairs = (n // block_q) * (n // block_k + 1) // 2
+    full = pl.BlockSpec((n, d), lambda i, lens: (0, 0))
+    rows = pl.BlockSpec((block_q, d), lambda i, lens: (i, 0))
+    col = pl.BlockSpec((block_q, 1), lambda i, lens: (i, 0))
+    return pl.pallas_call(
+        kernel,
+        out_shape=tuple(jax.ShapeDtypeStruct((n, d), jnp.bfloat16) for _ in range(3)),
+        grid_spec=pltpu.PrefetchScalarGridSpec(
+            num_scalar_prefetch=1,
+            grid=(n // block_q,),
+            in_specs=[rows, full, full, rows, col, col],
+            out_specs=[rows, full, full],
+            scratch_shapes=[pltpu.VMEM((n, d), jnp.float32), pltpu.VMEM((n, d), jnp.float32)],
+        ),
+        compiler_params=pltpu.CompilerParams(dimension_semantics=("arbitrary",)),
+        cost_estimate=pl.CostEstimate(
+            flops=10 * pairs * block_q * block_k * d,
+            transcendentals=pairs * block_q * block_k,
+            bytes_accessed=8 * n * d * 2,
+        ),
+    )(length, q, k, v, do, lse, delta)
 
 
 def shards(
@@ -379,15 +463,20 @@
         seq_total, seq_count, local_width
     )
     backward_items = [
-        attention_backward(
+        attention_backward1(
             item(query, s, h),
             item(keys, s, h),
             item(values, s, h),
             item(attended_grad, s, h),
             lse,
+            jnp.sum(
+                item(attended_grad, s, h).astype(jnp.float32) * o.astype(jnp.float32),
+                axis=1,
+                keepdims=True,
+            ),
             seq_lengths[s : s + 1],
         )
-        for (s, h), (_, lse) in zip(pairs, forward_items)
+        for (s, h), (o, lse) in zip(pairs, forward_items)
     ]
     joint_grad = jnp.stack(
         [per_row([grads[kind] for grads in backward_items]) for kind in range(3)], axis=2

time: 597 us -> 596 us (level)
  Pallas kernels: 41.5 us -> 23.6 us
  starting transfers between devices: 35.2 us -> 46.4 us
    pallas_call x1, Pallas kernels: 24.6 us -> 10.4 us  [attention_backward1(): pl.pallas_call(kernel, out_shape=tuple((jax.ShapeDtypeStruct((n, d), jnp....]
    all_to_all x2, starting transfers between devices: 16.3 us -> 26.3 us  [reduce_vectors(): packed = lax.all_to_all(packed, ('group', 'dp', 'tensor'), 0, 0, tiled=True)]
  transfers between devices with their start and end apart: 22 -> 22, of which waited for: 12 -> 12; matrix products, arithmetic and copies ran while one was open for 27% -> 27% of each run, Pallas kernels for 7% -> 4%
where the time goes in v21:
time: 596 us; the launch traced here: 584 us
  waiting for transfers between devices  278 us (47%)
  matrix products  91.4 us (15%)
  local copies, waits for them, and re-layouts  54.7 us (9%)
  other arithmetic  53.4 us (9%)
  starting transfers between devices  46.4 us (8%)
  Pallas kernels  23.6 us (4%)
  blocking collectives  20.4 us (3%)
  between operations  16.6 us (3%)
    all_gather x1, waiting for transfers between devices, shards(): front = lax.all_gather(front, 'tensor', axis=0, tiled=True)  88.1 us
    reduce_scatter x1, waiting for transfers between devices, shards(): both = lax.psum_scatter(merged, 'tensor', scatter_dimension=0, tiled=True)  64 us
    all_gather x1, waiting for transfers between devices, shards(): second_full = lax.all_gather(second_low, 'tensor', axis=0, tiled=True)  62.2 us
    all_to_all x2, starting transfers between devices, reduce_vectors(): packed = lax.all_to_all(packed, ('group', 'dp', 'tensor'), 0, 0, tiled=True)  26.3 us
    ppermute x12, waiting for transfers between devices, halving_steps(): got = lax.ppermute(send, axis, [(i, i ^ bit) for i in range(size)])  26 us
    all_to_all x1, blocking collectives, shards(): lax.all_to_all(heads_grad, 'tensor', 1, 0, tiled=True)  20.4 us
    reshape x4, local copies, waits for them, and re-layouts, halving_sum(): value.reshape(shape[:dim] + (groups // 2, 2, dps * rest) + shape[dim + 1:])  19.3 us
    all_gather x1, waiting for transfers between devices, shards(): upstream_full = lax.all_gather(upstream, 'tensor', axis=0, tiled=True)  17.9 us
  transfers between devices with their start and end apart: 22, of which 12 were waited for; matrix products, arithmetic and copies ran while one was open for 27% of the time, Pallas kernels for 4%

profile of v21, /device:TPU:96, one launch (start us, length us, event | category | flops | bytes accessed | tf_op | source)
XLA Modules:
  0.0 584.3 jit_solution(9063188449145270469)
XLA Ops:
  16.6 88.1 %all-gather.5.cloned.1.call-done = bf16[2048,3072]{1,0:T(8,128)(2,1)} async-done(((bf16[128,3072]{1,0:T(8,128)(2,1)}), bf16[2048,3072]{1,0:T(8,128)(2,1)}) %all-gather.5.cloned.1.call-update) | async-done | bytes 12582928 | tf_op jit(solution)/shard_map/all_gather | solution.py:342
  112.0 7.4 %fusion.37 = f32[2048,1,3,128]{3,0,2,1:T(8,128)S(1)} fusion(bf16[2048,3072]{1,0:T(8,128)(2,1)} %all-gather.5.cloned.1.call-done, bf16[2048,3,1,128]{0,3,1,2:T(8,128)(2,1)} %copy.39), kind=kOutput, calls=%fused_computation.39 | convolution fusion | flops 3221225472 | bytes 13107200 | tf_op jit(solution)/shard_map/dot_general | solution.py:350
  121.4 13.1 %shard_map.254 = (bf16[2048,128]{1,0:T(8,128)(2,1)}, f32[2048,1]{1,0:T(8,128)}) custom-call(s32[1]{0:T(128)} %dynamic_slice.22.len_ref, bf16[2048,128]{1,0:T(8,128)(2,1)} %get-tuple-element.121.q_ref, bf16[2048,128]{1,0:T(8,128)(2,1)} %fusion.66.k_ref, bf16[2048,128]{1,0:T(8,128)(2,1)} %get-tuple-element.120.v_ref), custom_call_target="tpu_custom_call" | custom-call | flops 1342177280 | bytes 2097152 | tf_op jit(solution)/shard_map/pallas_call | solution.py:85
  141.8 15.2 %all-to-all-done = bf16[16,128,128]{1,2,0:T(8,128)(2,1)S(1)} async-done(((bf16[16,128,128]{1,2,0:T(8,128)(2,1)}), bf16[16,128,128]{1,2,0:T(8,128)(2,1)S(1)}, u32[]{:S(2)}, u32[]{:S(2)}) %all-to-all-start) | async-done | bytes 524320 | tf_op jit(solution)/shard_map/all_to_all | solution.py:376
  164.9 17.9 %all-gather.7.cloned.1.call-done = bf16[2048,1,2048]{2,0,1:T(8,128)(2,1)} async-done(((bf16[128,1,2048]{2,0,1:T(8,128)(2,1)}), bf16[2048,1,2048]{2,0,1:T(8,128)(2,1)}) %all-gather.7.cloned.1.call-update) | async-done | bytes 8388624 | tf_op jit(solution)/shard_map/all_gather | solution.py:348
  183.1 10.5 %fusion.31 = f32[2048,1,512]{2,0,1:T(8,128)} fusion(bf16[512,2048]{1,0:T(8,128)(2,1)} %param.28, bf16[2048,1,2048]{2,0,1:T(8,128)(2,1)} %all-gather.7.cloned.1.call-done), kind=kOutput, calls=%fused_computation.36 | convolution fusion | flops 4294967296 | bytes 14680064 | tf_op jit(solution)/shard_map/rsd,fd->rsf/dot_general | solution.py:394
  193.5 62.2 %all-gather.9.cloned.1.call-done = bf16[2048,1,2048]{2,0,1:T(8,128)(2,1)} async-done(((bf16[128,1,2048]{2,0,1:T(8,128)(2,1)}), bf16[2048,1,2048]{2,0,1:T(8,128)(2,1)}) %all-gather.9.cloned.1.call-update) | async-done | bytes 8388624 | tf_op jit(solution)/shard_map/all_gather | solution.py:397
  255.7 7.0 %fusion.6 = f32[2048,512]{1,0:T(8,128)S(1)} fusion(bf16[2048,512]{1,0:T(8,128)(2,1)S(1)} %copy-done, bf16[2048,1,2048]{2,0,1:T(8,128)(2,1)} %all-gather.9.cloned.1.call-done), kind=kOutput, calls=%fused_computation.7 | convolution fusion | flops 4294967296 | bytes 14680064 | tf_op jit(solution)/shard_map/dot_general | solution.py:400
  268.4 6.9 %convert_bitcast_fusion.1 = bf16[2048,1,2048]{2,0,1:T(8,128)(2,1)} fusion(bf16[2048,512]{1,0:T(8,128)(2,1)S(1)} %get-tuple-element.110, bf16[2048,512]{1,0:T(8,128)(2,1)S(1)} %copy-done), kind=kOutput, calls=%fused_computation.14 | convolution fusion | flops 4299161600 | bytes 12582912 | tf_op jit(solution)/shard_map/rsf,df->rsd/dot_general | solution.py:421
  278.2 7.1 %fusion.28 = f32[2048,512]{1,0:T(8,128)S(1)} fusion(bf16[2048,512]{1,0:T(8,128)(2,1)S(1)} %copy-done.19, bf16[2048,1,2048]{2,0,1:T(8,128)(2,1)} %all-gather.9.cloned.1.call-done, f32[]{:T(128)S(6)} %div.71), kind=kOutput, calls=%fused_computation.35 | convolution fusion | flops 4296015872 | bytes 14680068 | tf_op jit(solution)/shard_map/rd,rf->df/dot_general | solution.py:413
  288.0 10.0 %fusion.25 = f32[512,2048]{1,0:T(8,128)} fusion(bf16[2048,1,2048]{2,0,1:T(8,128)(2,1)} %all-gather.7.cloned.1.call-done, f32[]{:T(128)S(6)} %div.71, f32[2048,512]{1,0:T(8,128)S(1)} %copy-done.13, f32[512]{0:T(512)S(1)} %copy-done.26), kind=kOutput, calls=%fused_computation.34 | convolution fusion | flops 4306501632 | bytes 16779268 | tf_op jit(solution)/shard_map/rsf,rsd->fd/dot_general | solution.py:409
  297.9 6.7 %reshape.504 = f32[512,2,2,512]{3,2,1,0:T(2,128)} reshape(f32[512,2048]{1,0:T(8,128)} %fusion.25) | data formatting | bytes 8388608 | tf_op jit(solution)/shard_map/reshape | solution.py:597
  304.6 7.3 %copy.41 = f32[512,2,2,512]{0,3,1,2:T(8,128)} copy(f32[512,2,2,512]{3,2,1,0:T(2,128)} %reshape.504) | data formatting | bytes 8388608 | tf_op jit(solution)/shard_map/reshape | solution.py:597
  326.4 10.6 %collective-permute-done.2 = bf16[2,256,512]{2,1,0:T(8,128)(2,1)S(1)} collective-permute-done((bf16[2,256,512]{2,1,0:T(8,128)(2,1)S(1)}, bf16[2,256,512]{2,1,0:T(8,128)(2,1)S(1)}, u32[]{:S(2)}, u32[]{:S(2)}) %collective-permute-start.2) | collective-permute-done | bytes 524320 | tf_op jit(solution)/shard_map/ppermute | solution.py:587
  338.7 9.5 %collective-permute-done.5 = bf16[512,2,256]{0,2,1:T(8,128)(2,1)S(1)} collective-permute-done((bf16[512,2,256]{0,2,1:T(8,128)(2,1)S(1)}, bf16[512,2,256]{0,2,1:T(8,128)(2,1)S(1)}, u32[]{:S(2)}, u32[]{:S(2)}) %collective-permute-start.5) | collective-permute-done | bytes 524320 | tf_op jit(solution)/shard_map/ppermute | solution.py:587
  354.7 6.9 %dynamic_update_slice.12 = bf16[2048,1,4096]{2,0,1:T(8,128)(2,1)} pad(bf16[2048,1,2048]{2,0,1:T(8,128)(2,1)S(1)} %convert_bitcast_fusion, bf16[]{:T(256)} %constant.147.clone.1), padding=0_0x0_0x2048_0 | pad | bytes 25165826 | tf_op jit(solution)/shard_map/dynamic_update_slice | solution.py:430
  375.8 20.4 %all_to_all.53 = bf16[128,16,128]{2,0,1:T(8,128)(2,1)S(1)} all-to-all(bf16[128,16,128]{2,0,1:T(8,128)(2,1)S(1)} %bitcast.175), channel_id=1, replica_groups=mesh['group'=4,'dp'=2,'tensor'=16] {'tensor'}, dimensions={1} | all-to-all | bytes 1048576 | tf_op jit(solution)/shard_map/all_to_all | solution.py:462
  397.9 10.4 %shard_map.255 = (bf16[2048,128]{1,0:T(8,128)(2,1)}, bf16[2048,128]{1,0:T(8,128)(2,1)}, bf16[2048,128]{1,0:T(8,128)(2,1)}) custom-call(s32[1]{0:T(128)} %dynamic_slice.22.len_ref, bf16[2048,128]{1,0:T(8,128)(2,1)} %get-tuple-element.121.q_ref, bf16[2048,128]{1,0:T(8,128)(2,1)} %fusion.66.k_ref, bf16[2048,128]{1,0:T(8,128)(2,1)} %get-tuple-element.120.v_ref, ...), custom_call_target="tpu_custom_call" | custom-call | flops 3355443200 | bytes 4194304 | tf_op jit(solution)/shard_map/pallas_call | solution.py:274
  411.7 9.8 %bitcast_dynamic-update-slice_fusion = bf16[2048,1,4096]{2,0,1:T(8,128)(2,1)} fusion(bf16[2048,1,4096]{2,0,1:T(8,128)(2,1)} %dynamic_update_slice.12, bf16[2048,384]{0,1:T(8,128)(2,1)} %bitcast.176, bf16[2048,384]{0,1:T(8,128)(2,1)} %bitcast.169), kind=kOutput, calls=%fused_computation.2 | convolution fusion | flops 3225419776 | bytes 11534336 | tf_op jit(solution)/shard_map/rsc,dc->rsd/dot_general | solution.py:492
  422.3 7.8 %fusion.34 = f32[2048,384]{1,0:T(8,128)S(1)} fusion(bf16[2048,384]{0,1:T(8,128)(2,1)} %bitcast.177, bf16[2048,3072]{1,0:T(8,128)(2,1)} %all-gather.5.cloned.1.call-done, f32[]{:T(128)S(6)} %div.71), kind=kOutput, calls=%fused_computation.38 | convolution fusion | flops 3222011904 | bytes 13107204 | tf_op jit(solution)/shard_map/rd,rc->dc/dot_general | solution.py:486
  434.2 18.2 %all-to-all-start.2 = ((f32[128,1,176]{2,1,0:T(1,128)}), f32[128,1,176]{2,1,0:T(1,128)S(1)}, u32[]{:S(2)}, u32[]{:S(2)}) async-start(f32[128,1,176]{2,1,0:T(1,128)} %copy.46), calls=%async_computation.4 | async-start | bytes 262144 | tf_op jit(solution)/shard_map/all_to_all | solution.py:561
  464.4 5.8 fusion.40
  492.0 64.0 %reduce-scatter.5.cloned.1.call-done = bf16[128,1,4096]{2,0,1:T(8,128)(2,1)} async-done(((bf16[2048,1,4096]{2,0,1:T(8,128)(2,1)}), bf16[128,1,4096]{2,0,1:T(8,128)(2,1)}) %reduce-scatter.5.cloned.1.call-update) | async-done | bytes 1048592 | tf_op jit(solution)/shard_map/reduce_scatter | solution.py:500
  561.2 8.2 %all-to-all-start.3 = ((f32[128,1,16]{2,1,0:T(1,128)}), f32[128,1,16]{2,1,0:T(1,128)S(1)}, u32[]{:S(2)}, u32[]{:S(2)}) async-start(f32[128,1,16]{2,1,0:T(1,128)} %bitcast.63), calls=%async_computation.5 | async-start | bytes 131072 | tf_op jit(solution)/shard_map/all_to_all | solution.py:561
  (216 shorter events, 136.8 us)
Async XLA Ops:
  7.2 248.5 %copy-start = (bf16[2048,512]{1,0:T(8,128)(2,1)S(1)}, bf16[2048,512]{1,0:T(8,128)(2,1)}, u32[]{:S(2)}) copy-start(bf16[2048,512]{1,0:T(8,128)(2,1)} %param.26) | copy-start | bytes 6291460
  7.2 97.5 %all-gather.5.cloned.1.call-start = ((), (), s32[]{:S(2)}) async-start(), calls=%async_computation.6 | async-start | bytes 13369344 | tf_op jit(solution)/shard_map/all_gather | solution.py:342
  9.9 99.4 %copy-start.30 = (f32[128]{0:T(128)}, f32[128]{0:T(128)S(1)}, u32[]{:S(2)}) copy-start(f32[128]{0:T(128)S(1)} %fusion.56) | copy-start | bytes 1540
  13.4 169.4 %all-gather.7.cloned.1.call-start = ((), (), s32[]{:S(2)}) async-start(), calls=%async_computation.7 | async-start | bytes 8912896 | tf_op jit(solution)/shard_map/all_gather | solution.py:348
  109.3 50.8 %collective-permute-start = (bf16[2048,1024]{1,0:T(8,128)(2,1)}, bf16[2048,1024]{1,0:T(8,128)(2,1)}, u32[]{:S(2)}, u32[]{:S(2)}) collective-permute-start(bf16[2048,1024]{1,0:T(8,128)(2,1)} %slice.185), channel_id=1, source_target_pairs={{0,32},{32,0},{64,96},{96,64},{1,33},{33,1},{65,97},{97,65},{2,34}... | collective-permute-start | bytes 12582920 | tf_op jit(solution)/shard_map/ppermute | solution.py:346
  136.5 20.6 %all-to-all-start = ((bf16[16,128,128]{1,2,0:T(8,128)(2,1)}), bf16[16,128,128]{1,2,0:T(8,128)(2,1)S(1)}, u32[]{:S(2)}, u32[]{:S(2)}) async-start(bf16[16,128,128]{1,2,0:T(8,128)(2,1)} %copy.40), calls=%async_computation | async-start | bytes 1048576 | tf_op jit(solution)/shard_map/all_to_all | solution.py:376
  141.8 113.9 %all-gather.9.cloned.1.call-start = ((), (), s32[]{:S(2)}) async-start(), calls=%async_computation.8 | async-start | bytes 8912896 | tf_op jit(solution)/shard_map/all_gather | solution.py:397
  182.8 180.6 %reduce-scatter.3.cloned.1.call-start = ((), (), s32[]{:S(2)}) async-start(), calls=%async_computation.9 | async-start | bytes 8912896 | tf_op jit(solution)/shard_map/reduce_scatter | solution.py:424
  275.4 189.0 %all-gather.11.cloned.1.call-start = ((), (), s32[]{:S(2)}) async-start(), calls=%async_computation.11 | async-start | bytes 8912896 | tf_op jit(solution)/shard_map/all_gather | solution.py:447
  287.5 31.3 %collective-permute-start.1 = (bf16[4,256,512]{2,1,0:T(8,128)(2,1)S(1)}, bf16[4,256,512]{2,1,0:T(8,128)(2,1)S(1)}, u32[]{:S(2)}, u32[]{:S(2)}) collective-permute-start(bf16[4,256,512]{2,1,0:T(8,128)(2,1)S(1)} %bitcast.178), channel_id=1, source_target_pairs={{0,32},{32,0},{64,96},{96,64},{1,33},{33,1},{65,97},{97,65},{2,34}... | collective-permute-start | bytes 3145736 | tf_op jit(solution)/shard_map/ppermute | solution.py:587
  315.6 7.4 %collective-permute-start.4 = (bf16[512,4,256]{0,2,1:T(8,128)(2,1)}, bf16[512,4,256]{0,2,1:T(8,128)(2,1)}, u32[]{:S(2)}, u32[]{:S(2)}) collective-permute-start(bf16[512,4,256]{0,2,1:T(8,128)(2,1)} %select_convert_fusion), channel_id=1, source_target_pairs={{0,32},{32,0},{64,96},{96,64},{1,33},{33,1},{65,97},{97,65},{2,34}... | collective-permute-start | bytes 3145736 | tf_op jit(solution)/shard_map/ppermute | solution.py:587
  322.2 14.8 %collective-permute-start.2 = (bf16[2,256,512]{2,1,0:T(8,128)(2,1)S(1)}, bf16[2,256,512]{2,1,0:T(8,128)(2,1)S(1)}, u32[]{:S(2)}, u32[]{:S(2)}) collective-permute-start(bf16[2,256,512]{2,1,0:T(8,128)(2,1)S(1)} %select_convert_fusion.4), channel_id=1, source_target_pairs={{0,64},{32,96},{64,0},{96,32},{1,65},{33,97},{65,1},{97,33},{2,66}... | collective-permute-start | bytes 1572872 | tf_op jit(solution)/shard_map/ppermute | solution.py:587
  325.1 23.1 %collective-permute-start.5 = (bf16[512,2,256]{0,2,1:T(8,128)(2,1)S(1)}, bf16[512,2,256]{0,2,1:T(8,128)(2,1)S(1)}, u32[]{:S(2)}, u32[]{:S(2)}) collective-permute-start(bf16[512,2,256]{0,2,1:T(8,128)(2,1)S(1)} %select_convert_fusion.3), channel_id=1, source_target_pairs={{0,64},{32,96},{64,0},{96,32},{1,65},{33,97},{65,1},{97,33},{2,66}... | collective-permute-start | bytes 1572872 | tf_op jit(solution)/shard_map/ppermute | solution.py:587
  337.4 24.2 %collective-permute-start.3 = (bf16[1,256,512]{2,1,0:T(8,128)(2,1)S(1)}, bf16[1,256,512]{2,1,0:T(8,128)(2,1)S(1)}, u32[]{:S(2)}, u32[]{:S(2)}) collective-permute-start(bf16[1,256,512]{2,1,0:T(8,128)(2,1)S(1)} %select_convert_fusion.8), channel_id=1, source_target_pairs={{0,16},{16,0},{1,17},{17,1},{2,18},{18,2},{3,19},{19,3},{4,20},{20... | collective-permute-start | bytes 786440 | tf_op jit(solution)/shard_map/ppermute | solution.py:587
  348.6 14.0 %collective-permute-start.6 = (bf16[512,1,256]{0,2,1:T(8,128)(2,1)S(1)}, bf16[512,1,256]{0,2,1:T(8,128)(2,1)S(1)}, u32[]{:S(2)}, u32[]{:S(2)}) collective-permute-start(bf16[512,1,256]{0,2,1:T(8,128)(2,1)S(1)} %select_convert_fusion.7), channel_id=1, source_target_pairs={{0,16},{16,0},{1,17},{17,1},{2,18},{18,2},{3,19},{19,3},{4,20},{20... | collective-permute-start | bytes 786440 | tf_op jit(solution)/shard_map/ppermute | solution.py:587
  367.9 188.0 %reduce-scatter.5.cloned.1.call-start = ((), (), s32[]{:S(2)}) async-start(), calls=%async_computation.10 | async-start | bytes 17825792 | tf_op jit(solution)/shard_map/reduce_scatter | solution.py:500
  431.2 29.8 %collective-permute-start.7 = (bf16[4,256,384]{2,1,0:T(8,128)(2,1)}, bf16[4,256,384]{2,1,0:T(8,128)(2,1)}, u32[]{:S(2)}, u32[]{:S(2)}) collective-permute-start(bf16[4,256,384]{2,1,0:T(8,128)(2,1)} %bitcast.54), channel_id=1, source_target_pairs={{0,32},{32,0},{64,96},{96,64},{1,33},{33,1},{65,97},{97,65},{2,34}... | collective-permute-start | bytes 2359304 | tf_op jit(solution)/shard_map/ppermute | solution.py:587
  434.2 25.5 %all-to-all-start.2 = ((f32[128,1,176]{2,1,0:T(1,128)}), f32[128,1,176]{2,1,0:T(1,128)S(1)}, u32[]{:S(2)}, u32[]{:S(2)}) async-start(f32[128,1,176]{2,1,0:T(1,128)} %copy.46), calls=%async_computation.4 | async-start | bytes 262144 | tf_op jit(solution)/shard_map/all_to_all | solution.py:561
  462.9 14.1 %collective-permute-start.8 = (bf16[2,256,384]{2,1,0:T(8,128)(2,1)S(1)}, bf16[2,256,384]{2,1,0:T(8,128)(2,1)}, u32[]{:S(2)}, u32[]{:S(2)}) collective-permute-start(bf16[2,256,384]{2,1,0:T(8,128)(2,1)S(1)} %select_convert_fusion.5), channel_id=1, source_target_pairs={{0,64},{32,96},{64,0},{96,32},{1,65},{33,97},{65,1},{97,33},{2,66}... | collective-permute-start | bytes 1179656 | tf_op jit(solution)/shard_map/ppermute | solution.py:587
  477.0 1.6 collective-permute-start.10
  478.7 6.4 %collective-permute-start.11 = (bf16[1,128,2,256]{1,3,2,0:T(8,128)(2,1)S(1)}, bf16[1,128,2,256]{1,3,2,0:T(8,128)(2,1)S(1)}, u32[]{:S(2)}, u32[]{:S(2)}) collective-permute-start(bf16[1,128,2,256]{1,3,2,0:T(8,128)(2,1)S(1)} %select_convert_fusion.10), channel_id=1, source_target_pairs={{0,64},{32,96},{64,0},{96,32},{1,65},{33,97},{65,1},{97,33},{2,66}... | collective-permute-start | bytes 393224 | tf_op jit(solution)/shard_map/ppermute | solution.py:587
  479.5 11.3 %collective-permute-start.9 = (bf16[1,256,384]{2,1,0:T(8,128)(2,1)S(1)}, bf16[1,256,384]{2,1,0:T(8,128)(2,1)S(1)}, u32[]{:S(2)}, u32[]{:S(2)}) collective-permute-start(bf16[1,256,384]{2,1,0:T(8,128)(2,1)S(1)} %select_convert_fusion.9), channel_id=1, source_target_pairs={{0,16},{16,0},{1,17},{17,1},{2,18},{18,2},{3,19},{19,3},{4,20},{20... | collective-permute-start | bytes 589832 | tf_op jit(solution)/shard_map/ppermute | solution.py:587
  485.2 6.8 %collective-permute-start.12 = (bf16[1,128,1,256]{1,3,2,0:T(8,128)(2,1)S(1)}, bf16[1,128,1,256]{1,3,2,0:T(8,128)(2,1)S(1)}, u32[]{:S(2)}, u32[]{:S(2)}) collective-permute-start(bf16[1,128,1,256]{1,3,2,0:T(8,128)(2,1)S(1)} %select_convert_fusion.11), channel_id=1, source_target_pairs={{0,16},{16,0},{1,17},{17,1},{2,18},{18,2},{3,19},{19,3},{4,20},{20... | collective-permute-start | bytes 196616 | tf_op jit(solution)/shard_map/ppermute | solution.py:587
  561.2 15.4 %all-to-all-start.3 = ((f32[128,1,16]{2,1,0:T(1,128)}), f32[128,1,16]{2,1,0:T(1,128)S(1)}, u32[]{:S(2)}, u32[]{:S(2)}) async-start(f32[128,1,16]{2,1,0:T(1,128)} %bitcast.63), calls=%async_computation.5 | async-start | bytes 131072 | tf_op jit(solution)/shard_map/all_to_all | solution.py:561
  (31 other events, 585.3 us)
Sparse Core Ops, SparseCore 0:
  13.5 91.1 all-gather.4
  106.8 75.9 all-gather.6
  185.5 70.1 all-gather.8
  275.5 84.7 reduce-scatter.2
  368.1 74.3 all-gather.10
  445.7 110.1 reduce-scatter.4
